TPU v7x, 128 devices: a whole 4x4x4 slice. The times are simulated.
128 devices in a mesh: grp: 8 (over y, core), shard: 16 (over x, z).
Axes of the slice: x: 4, y: 4, z: 4, core: 2. Of those that a mesh axis runs over, the one named last changes fastest.
Arguments:
- embed: float32 [131072, 512], P(('grp', 'shard')), may hold values from -6 to 6
- knn_slot: int32 [131072, 80], P(('grp', 'shard')), may hold values from 0 to 4095
- knn_weight: float32 [131072, 80], P(('grp', 'shard')), may hold values from 0.1 to 1
- tile_list: int32 [128, 16, 2], P(('grp', 'shard')), may hold values from 0 to 7, as said below
- send_rows: int32 [128, 128, 8], P(('grp', 'shard')), may hold values from 0 to 1023
- members: int32 [512, 256], P(('grp', 'shard')), may hold values from 0 to 1023
- sub_len: int32 [512], P(('grp', 'shard')), may hold values from 1 to 256, 81920 in all
- w_self: bfloat16 [512, 512], replicated, may hold values from -0.25 to 0.25
- w_nbr: bfloat16 [512, 512], replicated, may hold values from -2 to 2
- bias_v: float32 [512], replicated, may hold values from -6 to 6
- w_conf: bfloat16 [512], replicated, may hold values from -0.25 to 0.25
- w_diff: bfloat16 [512, 512], replicated, may hold values from -0.25 to 0.25
- w_ctx: bfloat16 [512, 512], replicated, may hold values from -0.25 to 0.25
- bias_e: float32 [512], replicated, may hold values from -6 to 6
- w_edge: bfloat16 [512], replicated, may hold values from -0.25 to 0.25
Outputs:
- node_hidden: bfloat16 [131072, 512], P(('grp', 'shard'))
- confidence: float32 [131072], P(('grp', 'shard'))
- edge_scores: float32 [512, 256], P(('grp', 'shard'))
- node_votes: float32 [131072], P(('grp', 'shard'))
Inputs may be any that keep to these rules, and one draw needn't show every extreme that they name: `tile_list`: for each providing device and each device of its group, the 2 tile numbers are distinct local tiles of the provider.
All inputs are finite; a program needn't handle non-finite values. No bound on the sum of `sub_len` on one device may be relied on, other than what follows from the above.
Results may differ from a plain program's by a relative error of at most 0.024.
Values may be sent and summed in bfloat16 or wider, within the bound.
A program may use at most 128 MiB of HBM per device.

v0:
```python
import math

import jax
import jax.numpy as jnp
from jax import lax
from jax.sharding import PartitionSpec as P

TILE = 128


def select_matrix(indices, count, dtype):
    return (indices[:, None] == jnp.arange(count, dtype=jnp.int32)[None, :]).astype(dtype)


def body(
    embed,
    knn_slot,
    knn_weight,
    tile_list,
    send_rows,
    members,
    sub_len,
    w_self,
    w_nbr,
    bias_v,
    w_conf,
    w_diff,
    w_ctx,
    bias_e,
    w_edge,
):
    nodes = embed.shape[0]
    width = embed.shape[1]
    neighbour_count = knn_slot.shape[1]
    shard_count = lax.axis_size("shard")
    list_len = tile_list.shape[2]
    peer_span = list_len * TILE
    column_total = shard_count * peer_span
    embed_bf = embed.astype(jnp.bfloat16)
    weight_sum = jnp.sum(knn_weight, axis=1, keepdims=True)
    coeff_bf = (knn_weight / weight_sum).astype(jnp.bfloat16)
    block_rows = math.gcd(nodes, 256)
    block_count = nodes // block_rows
    peer_part = (knn_slot // peer_span).reshape(block_count, block_rows, neighbour_count)
    row_part = (knn_slot % peer_span).reshape(block_count, block_rows, neighbour_count)
    coeff_blocks = coeff_bf.reshape(block_count, block_rows, neighbour_count)

    def build_block(pieces):
        peer_block, row_block, coeff_block = pieces
        peer_hot = jnp.where(
            peer_block[:, :, None] == jnp.arange(shard_count, dtype=jnp.int32),
            coeff_block[:, :, None],
            jnp.zeros((), jnp.bfloat16),
        )
        row_hot = (row_block[:, :, None] == jnp.arange(peer_span, dtype=jnp.int32)).astype(
            jnp.bfloat16
        )
        joined = jnp.einsum("nkp,nkr->npr", peer_hot, row_hot, preferred_element_type=jnp.float32)
        return joined.reshape(block_rows, column_total)

    adjacency = (
        lax.map(build_block, (peer_part, row_part, coeff_blocks))
        .reshape(nodes, column_total)
        .astype(jnp.bfloat16)
    )
    lists_all = lax.all_gather(tile_list, "shard", axis=0, tiled=True)
    own_lists = lax.dynamic_index_in_dim(lists_all, lax.axis_index("shard"), axis=1, keepdims=False)
    provider_ids = jnp.arange(shard_count, dtype=jnp.int32)[:, None, None]
    tile_rows_in = own_lists[:, :, None] * TILE + jnp.arange(TILE, dtype=jnp.int32)
    group_row = (provider_ids * nodes + tile_rows_in).reshape(column_total)
    initial = jnp.zeros((nodes, width), jnp.float32)
    portion = lax.all_gather(embed_bf, "shard", axis=0, tiled=True)
    length = portion.shape[0]
    trips = min(length // nodes + 2, shard_count)

    def one_provider(step_index, total):
        valid = step_index < shard_count
        clamped = jnp.minimum(step_index, shard_count - 1)
        block = lax.dynamic_slice_in_dim(adjacency, clamped * peer_span, peer_span, 1)
        local_rows = lax.dynamic_slice_in_dim(group_row, clamped * peer_span, peer_span, 0)
        local_rows = jnp.where(valid, local_rows, -1)
        chooser = select_matrix(local_rows, length, jnp.bfloat16)
        picked = jnp.dot(chooser, portion, preferred_element_type=jnp.float32).astype(jnp.bfloat16)
        return total + jnp.dot(block, picked, preferred_element_type=jnp.float32)

    gathered_sum = lax.fori_loop(0, trips, one_provider, initial)
    pre_act = (
        jnp.dot(embed_bf, w_self, preferred_element_type=jnp.float32)
        + jnp.dot(gathered_sum.astype(jnp.bfloat16), w_nbr, preferred_element_type=jnp.float32)
        + bias_v
    )
    node_hidden = jax.nn.relu(pre_act).astype(jnp.bfloat16)
    confidence = jnp.dot(node_hidden, w_conf, preferred_element_type=jnp.float32)
    device_total = send_rows.shape[1]
    capacity = send_rows.shape[2]
    hidden_width = node_hidden.shape[1]
    slot_total = device_total * capacity
    send_flat = send_rows[0].reshape(slot_total)
    send_chooser = select_matrix(send_flat, nodes, jnp.bfloat16)
    outbound = jnp.dot(send_chooser, node_hidden, preferred_element_type=jnp.float32).astype(
        jnp.bfloat16
    )
    outbound = outbound.reshape(device_total, capacity, hidden_width)
    received = lax.all_to_all(outbound, ("grp", "shard"), split_axis=0, concat_axis=0, tiled=True)
    received_rows = received.reshape(slot_total, hidden_width)
    sub_count = members.shape[0]
    member_width = members.shape[1]
    member_flat = members.reshape(sub_count * member_width)
    member_chooser = select_matrix(member_flat, slot_total, jnp.bfloat16)
    member_rows = jnp.dot(member_chooser, received_rows, preferred_element_type=jnp.float32)
    member_rows = member_rows.reshape(sub_count, member_width, hidden_width)
    relative = member_rows - member_rows[:, :1, :]
    alive = jnp.arange(member_width, dtype=jnp.int32)[None, :] < sub_len[:, None]
    masked = jnp.where(alive[:, :, None], relative, 0.0)
    context = (jnp.sum(masked, axis=1) / sub_len[:, None].astype(jnp.float32)).astype(jnp.bfloat16)
    relative_bf = relative.astype(jnp.bfloat16)
    inner = jnp.einsum("smh,hk->smk", relative_bf, w_diff, preferred_element_type=jnp.float32)
    inner = inner + jnp.dot(context, w_ctx, preferred_element_type=jnp.float32)[:, None, :] + bias_e
    edge_hidden = jax.nn.relu(inner).astype(jnp.bfloat16)
    logits = jnp.einsum("smk,k->sm", edge_hidden, w_edge, preferred_element_type=jnp.float32)
    edge_scores = jnp.where(alive, jax.nn.sigmoid(logits), 0.0)
    slot_scores = jnp.dot(
        member_chooser.astype(jnp.float32).T,
        edge_scores.reshape(sub_count * member_width),
        precision=lax.Precision.HIGHEST,
    )
    slot_scores = slot_scores.reshape(device_total, capacity)
    returned = lax.all_to_all(
        slot_scores, ("grp", "shard"), split_axis=0, concat_axis=0, tiled=True
    )
    node_votes = jnp.dot(
        send_chooser.astype(jnp.float32).T,
        returned.reshape(slot_total),
        precision=lax.Precision.HIGHEST,
    )
    return (node_hidden, confidence, edge_scores, node_votes)


def solution(mesh):
    return jax.shard_map(
        body,
        mesh=mesh,
        in_specs=(
            P(("grp", "shard"), None),
            P(("grp", "shard"), None),
            P(("grp", "shard"), None),
            P(("grp", "shard"), None, None),
            P(("grp", "shard"), None, None),
            P(("grp", "shard"), None),
            P(("grp", "shard")),
            P(),
            P(),
            P(),
            P(),
            P(),
            P(),
            P(),
            P(),
        ),
        out_specs=(
            P(("grp", "shard"), None),
            P(("grp", "shard")),
            P(("grp", "shard"), None),
            P(("grp", "shard")),
        ),
        check_vma=False,
    )
```

profile of v0, /device:TPU:1, one launch (start us, length us, event | category | flops | bytes accessed | tf_op | source)
XLA Modules:
  0.0 374.9 jit_solution(17344378188229696888)
XLA Ops:
  7.2 2.8 convert_element_type.49
  10.1 20.5 %all_gather.6 = s32[16,16,2]{1,2,0:T(2,128)S(1)} all-gather(s32[1,16,2]{1,2,0:T(2,128)S(1)} %copy-done.13), channel_id=1, replica_groups=mesh['grp'=8,'shard'=16] {'shard'}, dimensions={0}, use_global_device_ids=true | all-gather | bytes 2176 | tf_op jit(solution)/shard_map/all_gather | solution.py:66
  31.3 1.0 copy.38
  32.9 2.1 fusion.47
  35.0 49.9 %while.24 = (s32[]{:T(128)}, bf16[4,256,4096]{2,1,0:T(8,128)(2,1)}, s32[4,256,80]{2,1,0:T(8,128)S(1)}, bf16[4,256,80]{2,1,0:T(8,128)(2,1)S(1)}, s32[4,256,80]{2,1,0:T(8,128)}, /*index=5*/s32[]{:T(128)}) while((s32[]{:T(128)}, bf16[4,256,4096]{2,1,0:T(8,128)(2,1)}, s32[4,256,80]{2,1,0:T(8,128)S(1)}, bf16[4,256,80]{2,1,0:T(8,128)(2,1)S(1)}, ...), condition=%wide.region_2.3_spmd, body=%wide.region_1.2_spmd.sunk | while | flops 173670400 | bytes 11100749 | solution.py:62
  35.0 0.9 dynamic-slice_bitcast_fusion.5
  36.0 7.0 %fusion.65 = bf16[256,16,256]{2,1,0:T(8,128)(2,1)} fusion(s32[256,80]{1,0:T(8,128)S(1)} %get-tuple-element.228, s32[256,80]{1,0:T(8,128)S(1)} %get-tuple-element.229, bf16[256,80]{1,0:T(8,128)(2,1)S(1)} %dynamic-slice_bitcast_fusion.6), kind=kOutput, calls=%fused_computation.1.clone.1 | convolution fusion | flops 173670400 | bytes 2301952 | tf_op jit(solution)/shard_map/while/body/eval_jaxpr/nkp,nkr->npr/dot_general | solution.py:58
  43.0 2.9 broadcast_in_dim.96
  45.9 1.6 constant_dynamic-update-slice_fusion.2
  48.4 7.0 %fusion.65 = bf16[256,16,256]{2,1,0:T(8,128)(2,1)} fusion(s32[256,80]{1,0:T(8,128)S(1)} %get-tuple-element.228, s32[256,80]{1,0:T(8,128)S(1)} %get-tuple-element.229, bf16[256,80]{1,0:T(8,128)(2,1)S(1)} %dynamic-slice_bitcast_fusion.6), kind=kOutput, calls=%fused_computation.1.clone.1 | convolution fusion | flops 173670400 | bytes 2301952 | tf_op jit(solution)/shard_map/while/body/eval_jaxpr/nkp,nkr->npr/dot_general | solution.py:58
  55.4 3.1 broadcast_in_dim.96
  58.5 1.5 constant_dynamic-update-slice_fusion.2
  61.0 7.0 %fusion.65 = bf16[256,16,256]{2,1,0:T(8,128)(2,1)} fusion(s32[256,80]{1,0:T(8,128)S(1)} %get-tuple-element.228, s32[256,80]{1,0:T(8,128)S(1)} %get-tuple-element.229, bf16[256,80]{1,0:T(8,128)(2,1)S(1)} %dynamic-slice_bitcast_fusion.6), kind=kOutput, calls=%fused_computation.1.clone.1 | convolution fusion | flops 173670400 | bytes 2301952 | tf_op jit(solution)/shard_map/while/body/eval_jaxpr/nkp,nkr->npr/dot_general | solution.py:58
  68.0 2.9 broadcast_in_dim.96
  70.9 1.6 constant_dynamic-update-slice_fusion.2
  73.4 7.0 %fusion.65 = bf16[256,16,256]{2,1,0:T(8,128)(2,1)} fusion(s32[256,80]{1,0:T(8,128)S(1)} %get-tuple-element.228, s32[256,80]{1,0:T(8,128)S(1)} %get-tuple-element.229, bf16[256,80]{1,0:T(8,128)(2,1)S(1)} %dynamic-slice_bitcast_fusion.6), kind=kOutput, calls=%fused_computation.1.clone.1 | convolution fusion | flops 173670400 | bytes 2301952 | tf_op jit(solution)/shard_map/while/body/eval_jaxpr/nkp,nkr->npr/dot_general | solution.py:58
  80.4 2.9 broadcast_in_dim.96
  83.3 1.6 constant_dynamic-update-slice_fusion.2
  84.9 40.6 %all-gather.2.cloned.1.call-done = bf16[16384,512]{1,0:T(8,128)(2,1)} async-done(((bf16[1024,512]{1,0:T(8,128)(2,1)}), bf16[16384,512]{1,0:T(8,128)(2,1)}) %all-gather.2.cloned.1.call-update) | async-done | bytes 16777232 | tf_op jit(solution)/shard_map/all_gather | solution.py:72
  125.5 172.5 %while.25 = (s32[]{:T(128)}, f32[1024,512]{1,0:T(8,128)}, bf16[1024,4096]{1,0:T(8,128)(2,1)}, s32[4096]{0:T(1024)S(1)}, bf16[16384,512]{1,0:T(8,128)(2,1)}, /*in...) while((s32[]{:T(128)}, f32[1024,512]{1,0:T(8,128)}, bf16[1024,4096]{1,0:T(8,128)(2,1)}, ...), condition=%wide.region_4.5_spmd.clone, body=%wide.region_3.4_spmd.clone.sunk | while | flops 4568776704 | bytes 21499056 | solution.py:86
  125.5 10.4 %select_add_fusion.2 = f32[1024,512]{1,0:T(8,128)} fusion(f32[1024,512]{1,0:T(8,128)} %get-tuple-element.264, pred[]{:T(512)S(6)} %compare.6, bf16[16384,512]{1,0:T(8,128)(2,1)} %get-tuple-element.277, s32[256]{0:T(256)S(1)} %dynamic_slice.45, bf16[1024,4096]{1,0:T(8,128)(2,1)} %get-tuple-element.275, s32[]{:T(128)S(6)} %select_n.63), kind=kOutput, calls=%fused_computation.16.clone.1 | convolution fusion | flops 4568776704 | bytes 21496836 | tf_op jit(solution)/shard_map/while/body/eval_jaxpr/dot_general | solution.py:84
  136.1 10.8 %select_add_fusion.2 = f32[1024,512]{1,0:T(8,128)} fusion(f32[1024,512]{1,0:T(8,128)} %get-tuple-element.264, pred[]{:T(512)S(6)} %compare.6, bf16[16384,512]{1,0:T(8,128)(2,1)} %get-tuple-element.277, s32[256]{0:T(256)S(1)} %dynamic_slice.45, bf16[1024,4096]{1,0:T(8,128)(2,1)} %get-tuple-element.275, s32[]{:T(128)S(6)} %select_n.63), kind=kOutput, calls=%fused_computation.16.clone.1 | convolution fusion | flops 4568776704 | bytes 21496836 | tf_op jit(solution)/shard_map/while/body/eval_jaxpr/dot_general | solution.py:84
  146.9 10.6 %select_add_fusion.2 = f32[1024,512]{1,0:T(8,128)} fusion(f32[1024,512]{1,0:T(8,128)} %get-tuple-element.264, pred[]{:T(512)S(6)} %compare.6, bf16[16384,512]{1,0:T(8,128)(2,1)} %get-tuple-element.277, s32[256]{0:T(256)S(1)} %dynamic_slice.45, bf16[1024,4096]{1,0:T(8,128)(2,1)} %get-tuple-element.275, s32[]{:T(128)S(6)} %select_n.63), kind=kOutput, calls=%fused_computation.16.clone.1 | convolution fusion | flops 4568776704 | bytes 21496836 | tf_op jit(solution)/shard_map/while/body/eval_jaxpr/dot_general | solution.py:84
  157.6 10.7 %select_add_fusion.2 = f32[1024,512]{1,0:T(8,128)} fusion(f32[1024,512]{1,0:T(8,128)} %get-tuple-element.264, pred[]{:T(512)S(6)} %compare.6, bf16[16384,512]{1,0:T(8,128)(2,1)} %get-tuple-element.277, s32[256]{0:T(256)S(1)} %dynamic_slice.45, bf16[1024,4096]{1,0:T(8,128)(2,1)} %get-tuple-element.275, s32[]{:T(128)S(6)} %select_n.63), kind=kOutput, calls=%fused_computation.16.clone.1 | convolution fusion | flops 4568776704 | bytes 21496836 | tf_op jit(solution)/shard_map/while/body/eval_jaxpr/dot_general | solution.py:84
  168.4 10.7 %select_add_fusion.2 = f32[1024,512]{1,0:T(8,128)} fusion(f32[1024,512]{1,0:T(8,128)} %get-tuple-element.264, pred[]{:T(512)S(6)} %compare.6, bf16[16384,512]{1,0:T(8,128)(2,1)} %get-tuple-element.277, s32[256]{0:T(256)S(1)} %dynamic_slice.45, bf16[1024,4096]{1,0:T(8,128)(2,1)} %get-tuple-element.275, s32[]{:T(128)S(6)} %select_n.63), kind=kOutput, calls=%fused_computation.16.clone.1 | convolution fusion | flops 4568776704 | bytes 21496836 | tf_op jit(solution)/shard_map/while/body/eval_jaxpr/dot_general | solution.py:84
  179.3 10.7 %select_add_fusion.2 = f32[1024,512]{1,0:T(8,128)} fusion(f32[1024,512]{1,0:T(8,128)} %get-tuple-element.264, pred[]{:T(512)S(6)} %compare.6, bf16[16384,512]{1,0:T(8,128)(2,1)} %get-tuple-element.277, s32[256]{0:T(256)S(1)} %dynamic_slice.45, bf16[1024,4096]{1,0:T(8,128)(2,1)} %get-tuple-element.275, s32[]{:T(128)S(6)} %select_n.63), kind=kOutput, calls=%fused_computation.16.clone.1 | convolution fusion | flops 4568776704 | bytes 21496836 | tf_op jit(solution)/shard_map/while/body/eval_jaxpr/dot_general | solution.py:84
  190.0 10.7 %select_add_fusion.2 = f32[1024,512]{1,0:T(8,128)} fusion(f32[1024,512]{1,0:T(8,128)} %get-tuple-element.264, pred[]{:T(512)S(6)} %compare.6, bf16[16384,512]{1,0:T(8,128)(2,1)} %get-tuple-element.277, s32[256]{0:T(256)S(1)} %dynamic_slice.45, bf16[1024,4096]{1,0:T(8,128)(2,1)} %get-tuple-element.275, s32[]{:T(128)S(6)} %select_n.63), kind=kOutput, calls=%fused_computation.16.clone.1 | convolution fusion | flops 4568776704 | bytes 21496836 | tf_op jit(solution)/shard_map/while/body/eval_jaxpr/dot_general | solution.py:84
  200.8 10.8 %select_add_fusion.2 = f32[1024,512]{1,0:T(8,128)} fusion(f32[1024,512]{1,0:T(8,128)} %get-tuple-element.264, pred[]{:T(512)S(6)} %compare.6, bf16[16384,512]{1,0:T(8,128)(2,1)} %get-tuple-element.277, s32[256]{0:T(256)S(1)} %dynamic_slice.45, bf16[1024,4096]{1,0:T(8,128)(2,1)} %get-tuple-element.275, s32[]{:T(128)S(6)} %select_n.63), kind=kOutput, calls=%fused_computation.16.clone.1 | convolution fusion | flops 4568776704 | bytes 21496836 | tf_op jit(solution)/shard_map/while/body/eval_jaxpr/dot_general | solution.py:84
  211.7 10.7 %select_add_fusion.2 = f32[1024,512]{1,0:T(8,128)} fusion(f32[1024,512]{1,0:T(8,128)} %get-tuple-element.264, pred[]{:T(512)S(6)} %compare.6, bf16[16384,512]{1,0:T(8,128)(2,1)} %get-tuple-element.277, s32[256]{0:T(256)S(1)} %dynamic_slice.45, bf16[1024,4096]{1,0:T(8,128)(2,1)} %get-tuple-element.275, s32[]{:T(128)S(6)} %select_n.63), kind=kOutput, calls=%fused_computation.16.clone.1 | convolution fusion | flops 4568776704 | bytes 21496836 | tf_op jit(solution)/shard_map/while/body/eval_jaxpr/dot_general | solution.py:84
  222.4 10.8 %select_add_fusion.2 = f32[1024,512]{1,0:T(8,128)} fusion(f32[1024,512]{1,0:T(8,128)} %get-tuple-element.264, pred[]{:T(512)S(6)} %compare.6, bf16[16384,512]{1,0:T(8,128)(2,1)} %get-tuple-element.277, s32[256]{0:T(256)S(1)} %dynamic_slice.45, bf16[1024,4096]{1,0:T(8,128)(2,1)} %get-tuple-element.275, s32[]{:T(128)S(6)} %select_n.63), kind=kOutput, calls=%fused_computation.16.clone.1 | convolution fusion | flops 4568776704 | bytes 21496836 | tf_op jit(solution)/shard_map/while/body/eval_jaxpr/dot_general | solution.py:84
  233.3 10.7 %select_add_fusion.2 = f32[1024,512]{1,0:T(8,128)} fusion(f32[1024,512]{1,0:T(8,128)} %get-tuple-element.264, pred[]{:T(512)S(6)} %compare.6, bf16[16384,512]{1,0:T(8,128)(2,1)} %get-tuple-element.277, s32[256]{0:T(256)S(1)} %dynamic_slice.45, bf16[1024,4096]{1,0:T(8,128)(2,1)} %get-tuple-element.275, s32[]{:T(128)S(6)} %select_n.63), kind=kOutput, calls=%fused_computation.16.clone.1 | convolution fusion | flops 4568776704 | bytes 21496836 | tf_op jit(solution)/shard_map/while/body/eval_jaxpr/dot_general | solution.py:84
  244.1 10.8 %select_add_fusion.2 = f32[1024,512]{1,0:T(8,128)} fusion(f32[1024,512]{1,0:T(8,128)} %get-tuple-element.264, pred[]{:T(512)S(6)} %compare.6, bf16[16384,512]{1,0:T(8,128)(2,1)} %get-tuple-element.277, s32[256]{0:T(256)S(1)} %dynamic_slice.45, bf16[1024,4096]{1,0:T(8,128)(2,1)} %get-tuple-element.275, s32[]{:T(128)S(6)} %select_n.63), kind=kOutput, calls=%fused_computation.16.clone.1 | convolution fusion | flops 4568776704 | bytes 21496836 | tf_op jit(solution)/shard_map/while/body/eval_jaxpr/dot_general | solution.py:84
  254.9 10.7 %select_add_fusion.2 = f32[1024,512]{1,0:T(8,128)} fusion(f32[1024,512]{1,0:T(8,128)} %get-tuple-element.264, pred[]{:T(512)S(6)} %compare.6, bf16[16384,512]{1,0:T(8,128)(2,1)} %get-tuple-element.277, s32[256]{0:T(256)S(1)} %dynamic_slice.45, bf16[1024,4096]{1,0:T(8,128)(2,1)} %get-tuple-element.275, s32[]{:T(128)S(6)} %select_n.63), kind=kOutput, calls=%fused_computation.16.clone.1 | convolution fusion | flops 4568776704 | bytes 21496836 | tf_op jit(solution)/shard_map/while/body/eval_jaxpr/dot_general | solution.py:84
  265.7 10.7 %select_add_fusion.2 = f32[1024,512]{1,0:T(8,128)} fusion(f32[1024,512]{1,0:T(8,128)} %get-tuple-element.264, pred[]{:T(512)S(6)} %compare.6, bf16[16384,512]{1,0:T(8,128)(2,1)} %get-tuple-element.277, s32[256]{0:T(256)S(1)} %dynamic_slice.45, bf16[1024,4096]{1,0:T(8,128)(2,1)} %get-tuple-element.275, s32[]{:T(128)S(6)} %select_n.63), kind=kOutput, calls=%fused_computation.16.clone.1 | convolution fusion | flops 4568776704 | bytes 21496836 | tf_op jit(solution)/shard_map/while/body/eval_jaxpr/dot_general | solution.py:84
  276.5 10.7 %select_add_fusion.2 = f32[1024,512]{1,0:T(8,128)} fusion(f32[1024,512]{1,0:T(8,128)} %get-tuple-element.264, pred[]{:T(512)S(6)} %compare.6, bf16[16384,512]{1,0:T(8,128)(2,1)} %get-tuple-element.277, s32[256]{0:T(256)S(1)} %dynamic_slice.45, bf16[1024,4096]{1,0:T(8,128)(2,1)} %get-tuple-element.275, s32[]{:T(128)S(6)} %select_n.63), kind=kOutput, calls=%fused_computation.16.clone.1 | convolution fusion | flops 4568776704 | bytes 21496836 | tf_op jit(solution)/shard_map/while/body/eval_jaxpr/dot_general | solution.py:84
  287.2 10.7 %select_add_fusion.2 = f32[1024,512]{1,0:T(8,128)} fusion(f32[1024,512]{1,0:T(8,128)} %get-tuple-element.264, pred[]{:T(512)S(6)} %compare.6, bf16[16384,512]{1,0:T(8,128)(2,1)} %get-tuple-element.277, s32[256]{0:T(256)S(1)} %dynamic_slice.45, bf16[1024,4096]{1,0:T(8,128)(2,1)} %get-tuple-element.275, s32[]{:T(128)S(6)} %select_n.63), kind=kOutput, calls=%fused_computation.16.clone.1 | convolution fusion | flops 4568776704 | bytes 21496836 | tf_op jit(solution)/shard_map/while/body/eval_jaxpr/dot_general | solution.py:84
  298.0 2.3 maximum_convert_fusion.1
  300.3 1.0 copy-done.3
  301.3 2.3 fusion.26
  303.6 8.4 %all-to-all-start = ((bf16[128,8,512]{2,1,0:T(8,128)(2,1)}), bf16[128,8,512]{2,1,0:T(8,128)(2,1)}, u32[]{:S(2)}, u32[]{:S(2)}) async-start(bf16[128,8,512]{2,1,0:T(8,128)(2,1)} %fusion.26), calls=%async_computation | async-start | bytes 2097152 | tf_op jit(solution)/shard_map/all_to_all | solution.py:104
  312.2 18.1 %all-to-all-done = bf16[128,8,512]{2,1,0:T(8,128)(2,1)} async-done(((bf16[128,8,512]{2,1,0:T(8,128)(2,1)}), bf16[128,8,512]{2,1,0:T(8,128)(2,1)}, u32[]{:S(2)}, u32[]{:S(2)}) %all-to-all-start) | async-done | bytes 1048608 | tf_op jit(solution)/shard_map/all_to_all | solution.py:104
  330.2 2.5 fusion.14
  334.0 0.9 fusion.27
  335.1 14.6 %fusion.28 = f32[128,1,8]{2,1,0:T(1,128)} fusion(f32[1024,1,1]{0,1,2:T(1,128)S(1)} %reshape.146, s32[128,8]{1,0:T(8,128)S(1)} %multiply_add_fusion, s32[1024]{0:T(1024)S(1)} %bitcast.70), kind=kOutput, calls=%fused_computation.41 | convolution fusion | flops 13631488 | bytes 16384 | tf_op jit(solution)/shard_map/dot_general | solution.py:122
  349.6 4.8 %all-to-all-start.1 = ((f32[128,1,8]{2,1,0:T(1,128)}), f32[128,1,8]{2,1,0:T(1,128)S(1)}, u32[]{:S(2)}, u32[]{:S(2)}) async-start(f32[128,1,8]{2,1,0:T(1,128)} %fusion.28), calls=%async_computation.1 | async-start | bytes 131072 | tf_op jit(solution)/shard_map/all_to_all | solution.py:128
  354.5 1.0 fusion.48
  355.5 8.7 %all-to-all-done.1 = f32[128,1,8]{2,1,0:T(1,128)S(1)} async-done(((f32[128,1,8]{2,1,0:T(1,128)}), f32[128,1,8]{2,1,0:T(1,128)S(1)}, u32[]{:S(2)}, u32[]{:S(2)}) %all-to-all-start.1) | async-done | bytes 4128 | tf_op jit(solution)/shard_map/all_to_all | solution.py:128
  365.6 2.5 fusion.17
  (92 shorter events, 8.2 us)
Async XLA Ops:
  7.2 25.8 %copy-start = (bf16[512,512]{1,0:T(8,128)(2,1)S(1)}, bf16[512,512]{1,0:T(8,128)(2,1)}, u32[]{:S(2)}) copy-start(bf16[512,512]{1,0:T(8,128)(2,1)} %param.26) | copy-start | bytes 1572868
  7.2 2.9 copy-start.13
  7.2 23.7 %copy-start.8 = (s32[1024,80]{0,1:T(8,128)S(1)}, s32[1024,80]{0,1:T(8,128)}, u32[]{:S(2)}) copy-start(s32[1024,80]{0,1:T(8,128)} %param.20) | copy-start | bytes 983044
  7.2 118.3 %all-gather.2.cloned.1.call-start = ((), (), s32[]{:S(2)}) async-start(), calls=%async_computation.2 | async-start | bytes 17825792 | tf_op jit(solution)/shard_map/all_gather | solution.py:72
  10.0 22.4 %copy-start.5 = (f32[1024,80]{0,1:T(8,128)S(1)}, f32[1024,80]{0,1:T(8,128)}, u32[]{:S(2)}) copy-start(f32[1024,80]{0,1:T(8,128)} %param.21) | copy-start | bytes 983044
  10.0 22.6 %copy-start.10 = (s32[1,128,8]{1,2,0:T(8,128)S(1)}, s32[1,128,8]{1,2,0:T(8,128)}, u32[]{:S(2)}) copy-start(s32[1,128,8]{1,2,0:T(8,128)} %param.23) | copy-start | bytes 12292
  10.1 22.9 %copy-start.1 = (bf16[1024,512]{1,0:T(8,128)(2,1)S(1)}, bf16[1024,512]{1,0:T(8,128)(2,1)}, u32[]{:S(2)}) copy-start(bf16[1024,512]{1,0:T(8,128)(2,1)} %convert_element_type.49) | copy-start | bytes 3145732
  125.5 172.5 %copy-start.2 = (f32[1024,512]{1,0:T(8,128)S(1)}, f32[1024,512]{1,0:T(8,128)}, u32[]{:S(2)}) copy-start(f32[1024,512]{1,0:T(8,128)} %fusion.47) | copy-start | bytes 6291460
  125.5 172.5 %copy-start.7 = (bf16[512,512]{1,0:T(8,128)(2,1)S(1)}, bf16[512,512]{1,0:T(8,128)(2,1)}, u32[]{:S(2)}) copy-start(bf16[512,512]{1,0:T(8,128)(2,1)} %param.27) | copy-start | bytes 1572868
  125.5 172.5 %copy-start.12 = (f32[512]{0:T(512)S(1)}, f32[512]{0:T(512)}, u32[]{:S(2)}) copy-start(f32[512]{0:T(512)} %param.28) | copy-start | bytes 6148
  300.3 1.0 copy-start.3
  303.6 8.4 %copy-start.16 = (s32[4]{0:T(128)S(1)}, s32[4]{0:T(128)}, u32[]{:S(2)}) copy-start(s32[4]{0:T(128)} %param.25) | copy-start | bytes 52
  303.6 8.4 %copy-start.14 = (bf16[512]{0:T(512)(128)(2,1)S(1)}, bf16[512]{0:T(512)(128)(2,1)}, u32[]{:S(2)}) copy-start(bf16[512]{0:T(512)(128)(2,1)} %param.33) | copy-start | bytes 3076
  303.6 8.4 %copy-start.11 = (s32[4,256]{1,0:T(4,128)S(1)}, s32[4,256]{1,0:T(4,128)}, u32[]{:S(2)}) copy-start(s32[4,256]{1,0:T(4,128)} %param.24) | copy-start | bytes 12292
  303.6 8.5 %copy-start.15 = (bf16[512]{0:T(512)(128)(2,1)S(1)}, bf16[512]{0:T(512)(128)(2,1)}, u32[]{:S(2)}) copy-start(bf16[512]{0:T(512)(128)(2,1)} %param.29) | copy-start | bytes 3076
  303.6 26.6 %all-to-all-start = ((bf16[128,8,512]{2,1,0:T(8,128)(2,1)}), bf16[128,8,512]{2,1,0:T(8,128)(2,1)}, u32[]{:S(2)}, u32[]{:S(2)}) async-start(bf16[128,8,512]{2,1,0:T(8,128)(2,1)} %fusion.26), calls=%async_computation | async-start | bytes 2097152 | tf_op jit(solution)/shard_map/all_to_all | solution.py:104
  332.8 1.0 copy-start.6
  332.8 1.2 copy-start.17
  332.8 1.2 copy-start.18
  334.9 19.5 %copy-start.4 = (bf16[1024,512]{1,0:T(8,128)(2,1)S(1)}, bf16[1024,512]{1,0:T(8,128)(2,1)}, u32[]{:S(2)}) copy-start(bf16[1024,512]{1,0:T(8,128)(2,1)} %copy-done.3) | copy-start | bytes 3145732
  335.0 33.1 %copy-start.9 = (f32[4,256]{1,0:T(4,128)}, f32[4,256]{1,0:T(4,128)S(1)}, u32[]{:S(2)}) copy-start(f32[4,256]{1,0:T(4,128)S(1)} %divide_select_fusion) | copy-start | bytes 12292
  349.6 14.5 %all-to-all-start.1 = ((f32[128,1,8]{2,1,0:T(1,128)}), f32[128,1,8]{2,1,0:T(1,128)S(1)}, u32[]{:S(2)}, u32[]{:S(2)}) async-start(f32[128,1,8]{2,1,0:T(1,128)} %fusion.28), calls=%async_computation.1 | async-start | bytes 131072 | tf_op jit(solution)/shard_map/all_to_all | solution.py:128
Sparse Core Ops, SparseCore 0:
  10.7 114.6 all-gather.1
where the time goes:
time: 376 us; the launch traced here: 375 us
  matrix products  228 us (61%)
  waiting for transfers between devices  67.3 us (18%)
  local copies, waits for them, and re-layouts  27.1 us (7%)
  blocking collectives  20.5 us (5%)
  between operations  14.4 us (4%)
  starting transfers between devices  13.2 us (4%)
  other arithmetic  4.58 us (1%)
    dot_general x16, matrix products, one_provider(): return total + jnp.dot(block, picked, preferred_element_type=jnp.float32)  171 us
    all_gather x1, waiting for transfers between devices, body(): portion = lax.all_gather(embed_bf, 'shard', axis=0, tiled=True)  40.6 us
    dot_general x4, matrix products, build_block(): jnp.einsum('nkp,nkr->npr', peer_hot, row_hot, preferred_element_type=jnp....  28 us
    all_gather x1, blocking collectives, body(): lists_all = lax.all_gather(tile_list, 'shard', axis=0, tiled=True)  20.5 us
    all_to_all x1, waiting for transfers between devices, body(): lax.all_to_all(outbound, ('grp', 'shard'), split_axis=0, concat_axis=0, t...  18.1 us
    dot_general x1, matrix products, body(): jnp.dot(member_chooser.astype(jnp.float32).T, edge_scores.reshape(sub_cou...  14.6 us
    broadcast_in_dim x4, local copies, waits for them, and re-layouts, body(): lax.map(build_block, (peer_part, row_part, coeff_blocks))  11.8 us
    all_to_all x1, waiting for transfers between devices, body(): lax.all_to_all(slot_scores, ('grp', 'shard'), split_axis=0, concat_axis=0...  8.66 us
  transfers between devices with their start and end apart: 3, of which 3 were waited for; matrix products, arithmetic and copies ran while one was open for 15% of the time, Pallas kernels for 0%

commit v1 on v0

--- a/solution.py
+++ b/solution.py
@@ -63,27 +63,13 @@
         .reshape(nodes, column_total)
         .astype(jnp.bfloat16)
     )
-    lists_all = lax.all_gather(tile_list, "shard", axis=0, tiled=True)
-    own_lists = lax.dynamic_index_in_dim(lists_all, lax.axis_index("shard"), axis=1, keepdims=False)
-    provider_ids = jnp.arange(shard_count, dtype=jnp.int32)[:, None, None]
-    tile_rows_in = own_lists[:, :, None] * TILE + jnp.arange(TILE, dtype=jnp.int32)
-    group_row = (provider_ids * nodes + tile_rows_in).reshape(column_total)
-    initial = jnp.zeros((nodes, width), jnp.float32)
-    portion = lax.all_gather(embed_bf, "shard", axis=0, tiled=True)
-    length = portion.shape[0]
-    trips = min(length // nodes + 2, shard_count)
-
-    def one_provider(step_index, total):
-        valid = step_index < shard_count
-        clamped = jnp.minimum(step_index, shard_count - 1)
-        block = lax.dynamic_slice_in_dim(adjacency, clamped * peer_span, peer_span, 1)
-        local_rows = lax.dynamic_slice_in_dim(group_row, clamped * peer_span, peer_span, 0)
-        local_rows = jnp.where(valid, local_rows, -1)
-        chooser = select_matrix(local_rows, length, jnp.bfloat16)
-        picked = jnp.dot(chooser, portion, preferred_element_type=jnp.float32).astype(jnp.bfloat16)
-        return total + jnp.dot(block, picked, preferred_element_type=jnp.float32)
-
-    gathered_sum = lax.fori_loop(0, trips, one_provider, initial)
+    tile_count = nodes // TILE
+    embed_tiles = embed_bf.reshape(tile_count, TILE, width)
+    outgoing = jnp.take(embed_tiles, tile_list[0].reshape(shard_count * list_len), axis=0)
+    outgoing = outgoing.reshape(shard_count, peer_span, width)
+    provided = lax.all_to_all(outgoing, "shard", split_axis=0, concat_axis=0, tiled=True)
+    provided = provided.reshape(column_total, width)
+    gathered_sum = jnp.dot(adjacency, provided, preferred_element_type=jnp.float32)
     pre_act = (
         jnp.dot(embed_bf, w_self, preferred_element_type=jnp.float32)
         + jnp.dot(gathered_sum.astype(jnp.bfloat16), w_nbr, preferred_element_type=jnp.float32)

time: 376 us -> 166 us (0.44)
  matrix products: 228 us -> 64.5 us
  waiting for transfers between devices: 67.3 us -> 35 us
  blocking collectives: 20.5 us -> 0 us
  starting transfers between devices: 13.2 us -> 28.6 us
  between operations: 14.4 us -> 0.96 us
    dot_general x16 -> x0, matrix products: 171 us -> none  [one_provider(): return total + jnp.dot(block, picked, preferred_element_type=jnp.float32)]
    all_gather x1 -> x0, waiting for transfers between devices: 40.6 us -> none  [body(): portion = lax.all_gather(embed_bf, 'shard', axis=0, tiled=True)]
    all_gather x1 -> x0, blocking collectives: 20.5 us -> none  [body(): lists_all = lax.all_gather(tile_list, 'shard', axis=0, tiled=True)]
    all_to_all x0 -> x1, starting transfers between devices: none -> 8.61 us  [body(): lax.all_to_all(outgoing, 'shard', split_axis=0, concat_axis=0, tiled=True)]
    all_to_all x0 -> x1, waiting for transfers between devices: none -> 8.25 us  [body(): lax.all_to_all(outgoing, 'shard', split_axis=0, concat_axis=0, tiled=True)]
    dot_general x1, matrix products: 2.32 us -> 10.4 us  [body(): jnp.dot(gathered_sum.astype(jnp.bfloat16), w_nbr, preferred_element_type=...]
    all_to_all x1, starting transfers between devices: 8.38 us -> 15.1 us  [body(): lax.all_to_all(outbound, ('grp', 'shard'), split_axis=0, concat_axis=0, t...]
    select_n x0 -> x2, other arithmetic: none -> 3.9 us  [body(): jnp.take(embed_tiles, tile_list[0].reshape(shard_count * list_len), axis=0)]
  transfers between devices with their start and end apart: 3 -> 3, of which waited for: 3 -> 3; matrix products, arithmetic and copies ran while one was open for 15% -> 33% of each run, Pallas kernels for 0% -> 0%
where the time goes in v1:
time: 166 us; the launch traced here: 165 us
  matrix products  64.5 us (39%)
  waiting for transfers between devices  35 us (21%)
  starting transfers between devices  28.6 us (17%)
  local copies, waits for them, and re-layouts  27.9 us (17%)
  other arithmetic  8.01 us (5%)
    dot_general x4, matrix products, build_block(): jnp.einsum('nkp,nkr->npr', peer_hot, row_hot, preferred_element_type=jnp....  28 us
    all_to_all x1, waiting for transfers between devices, body(): lax.all_to_all(outbound, ('grp', 'shard'), split_axis=0, concat_axis=0, t...  18.1 us
    all_to_all x1, starting transfers between devices, body(): lax.all_to_all(outbound, ('grp', 'shard'), split_axis=0, concat_axis=0, t...  15.1 us
    dot_general x1, matrix products, body(): jnp.dot(member_chooser.astype(jnp.float32).T, edge_scores.reshape(sub_cou...  14.6 us
    broadcast_in_dim x4, local copies, waits for them, and re-layouts, body(): lax.map(build_block, (peer_part, row_part, coeff_blocks))  11.5 us
    dot_general x1, matrix products, body(): jnp.dot(gathered_sum.astype(jnp.bfloat16), w_nbr, preferred_element_type=...  10.4 us
    all_to_all x1, waiting for transfers between devices, body(): lax.all_to_all(slot_scores, ('grp', 'shard'), split_axis=0, concat_axis=0...  8.68 us
    all_to_all x1, starting transfers between devices, body(): lax.all_to_all(outgoing, 'shard', split_axis=0, concat_axis=0, tiled=True)  8.61 us
  transfers between devices with their start and end apart: 3, of which 3 were waited for; matrix products, arithmetic and copies ran while one was open for 33% of the time, Pallas kernels for 0%

profile of v1, /device:TPU:1, one launch (start us, length us, event | category | flops | bytes accessed | tf_op | source)
XLA Modules:
  0.0 165.1 jit_solution(10998919594268108066)
XLA Ops:
  0.6 0.8 copy.34
  1.5 0.7 compare_and_fusion
  2.1 1.7 %convert_element_type.39 = bf16[1024,512]{1,0:T(8,128)(2,1)S(1)} convert(f32[1024,512]{1,0:T(8,128)} %param.17) | non-fusion elementwise | flops 524288 | bytes 3145728 | tf_op jit(solution)/shard_map/convert_element_type | solution.py:39
  4.0 0.1 copy.33
  4.2 2.8 %gather_fusion = bf16[32,128,512]{2,1,0:T(8,128)(2,1)} fusion(bf16[8,128,512]{2,1,0:T(8,128)(2,1)S(1)} %bitcast.72, s32[1024]{0:T(1024)S(1)} %pad_clamp_fusion), kind=kCustom, calls=%fused_computation | custom fusion | bytes 8388736 | tf_op jit(solution)/shard_map/jit(_take)/gather | solution.py:68
  7.0 3.9 %bitcast_select_fusion = bf16[16,256,512]{2,1,0:T(8,128)(2,1)} fusion(pred[16,256]{1,0:T(8,128)(4,1)S(1)} %bitcast.79, bf16[16,256,512]{2,1,0:T(8,128)(2,1)} %bitcast.73), kind=kLoop, calls=%fused_computation.14 | loop fusion | flops 2097152 | bytes 8392704 | tf_op jit(solution)/shard_map/jit(_take)/select_n | solution.py:68
  10.9 8.6 %all-to-all-start = ((bf16[16,256,512]{2,1,0:T(8,128)(2,1)}), bf16[16,256,512]{2,1,0:T(8,128)(2,1)}, u32[]{:S(2)}, u32[]{:S(2)}) async-start(bf16[16,256,512]{2,1,0:T(8,128)(2,1)} %bitcast_select_fusion), calls=%async_computation | async-start | bytes 8388608 | tf_op jit(solution)/shard_map/all_to_all | solution.py:70
  19.5 0.3 add_select_fusion
  19.8 0.2 copy.30
  20.0 1.0 copy.32
  21.1 0.2 copy.31
  21.3 2.0 %fusion.42 = f32[1024,512]{1,0:T(8,128)} fusion(bf16[1024,512]{1,0:T(8,128)(2,1)S(1)} %convert_element_type.39, bf16[512,512]{1,0:T(8,128)(2,1)S(1)} %copy-done), kind=kOutput, calls=%fused_computation.70 | convolution fusion | flops 536870912 | bytes 3670016 | tf_op jit(solution)/shard_map/dot_general | solution.py:74
  23.3 0.1 copy.35
  23.5 49.2 %while.10 = (s32[]{:T(128)}, bf16[4,256,4096]{2,1,0:T(8,128)(2,1)}, s32[4,256,80]{2,1,0:T(8,128)S(1)}, bf16[4,256,80]{2,1,0:T(8,128)(2,1)S(1)}, s32[4,256,80]{2,1,0:T(8,128)}, /*index=5*/s32[]{:T(128)}) while((s32[]{:T(128)}, bf16[4,256,4096]{2,1,0:T(8,128)(2,1)}, s32[4,256,80]{2,1,0:T(8,128)S(1)}, bf16[4,256,80]{2,1,0:T(8,128)(2,1)S(1)}, ...), condition=%wide.region_2.3_spmd, body=%wide.region_1.2_spmd.sunk | while | flops 173670400 | bytes 11100749 | solution.py:62
  23.5 0.9 dynamic-slice_bitcast_fusion.5
  24.5 7.0 %fusion.59 = bf16[256,16,256]{2,1,0:T(8,128)(2,1)} fusion(s32[256,80]{1,0:T(8,128)S(1)} %get-tuple-element.79, s32[256,80]{1,0:T(8,128)S(1)} %get-tuple-element.80, bf16[256,80]{1,0:T(8,128)(2,1)S(1)} %dynamic-slice_bitcast_fusion.6), kind=kOutput, calls=%fused_computation.2.clone.1 | convolution fusion | flops 173670400 | bytes 2301952 | tf_op jit(solution)/shard_map/while/body/eval_jaxpr/nkp,nkr->npr/dot_general | solution.py:58
  31.5 2.9 %broadcast_in_dim.96 = bf16[1,256,4096]{2,1,0:T(8,128)(2,1)S(1)} reshape(bf16[256,16,256]{2,1,0:T(8,128)(2,1)} %fusion.59) | data formatting | bytes 4194304 | tf_op jit(solution)/shard_map/while/body/jit(dynamic_update_index_in_dim)/broadcast_in_dim | solution.py:62
  34.3 1.5 constant_dynamic-update-slice_fusion.2
  35.8 0.9 dynamic-slice_bitcast_fusion.5
  36.8 7.0 %fusion.59 = bf16[256,16,256]{2,1,0:T(8,128)(2,1)} fusion(s32[256,80]{1,0:T(8,128)S(1)} %get-tuple-element.79, s32[256,80]{1,0:T(8,128)S(1)} %get-tuple-element.80, bf16[256,80]{1,0:T(8,128)(2,1)S(1)} %dynamic-slice_bitcast_fusion.6), kind=kOutput, calls=%fused_computation.2.clone.1 | convolution fusion | flops 173670400 | bytes 2301952 | tf_op jit(solution)/shard_map/while/body/eval_jaxpr/nkp,nkr->npr/dot_general | solution.py:58
  43.8 2.9 %broadcast_in_dim.96 = bf16[1,256,4096]{2,1,0:T(8,128)(2,1)S(1)} reshape(bf16[256,16,256]{2,1,0:T(8,128)(2,1)} %fusion.59) | data formatting | bytes 4194304 | tf_op jit(solution)/shard_map/while/body/jit(dynamic_update_index_in_dim)/broadcast_in_dim | solution.py:62
  46.6 1.5 constant_dynamic-update-slice_fusion.2
  48.1 0.9 dynamic-slice_bitcast_fusion.5
  49.1 7.0 %fusion.59 = bf16[256,16,256]{2,1,0:T(8,128)(2,1)} fusion(s32[256,80]{1,0:T(8,128)S(1)} %get-tuple-element.79, s32[256,80]{1,0:T(8,128)S(1)} %get-tuple-element.80, bf16[256,80]{1,0:T(8,128)(2,1)S(1)} %dynamic-slice_bitcast_fusion.6), kind=kOutput, calls=%fused_computation.2.clone.1 | convolution fusion | flops 173670400 | bytes 2301952 | tf_op jit(solution)/shard_map/while/body/eval_jaxpr/nkp,nkr->npr/dot_general | solution.py:58
  56.0 2.9 %broadcast_in_dim.96 = bf16[1,256,4096]{2,1,0:T(8,128)(2,1)S(1)} reshape(bf16[256,16,256]{2,1,0:T(8,128)(2,1)} %fusion.59) | data formatting | bytes 4194304 | tf_op jit(solution)/shard_map/while/body/jit(dynamic_update_index_in_dim)/broadcast_in_dim | solution.py:62
  58.9 1.5 constant_dynamic-update-slice_fusion.2
  60.4 0.9 dynamic-slice_bitcast_fusion.5
  61.4 7.0 %fusion.59 = bf16[256,16,256]{2,1,0:T(8,128)(2,1)} fusion(s32[256,80]{1,0:T(8,128)S(1)} %get-tuple-element.79, s32[256,80]{1,0:T(8,128)S(1)} %get-tuple-element.80, bf16[256,80]{1,0:T(8,128)(2,1)S(1)} %dynamic-slice_bitcast_fusion.6), kind=kOutput, calls=%fused_computation.2.clone.1 | convolution fusion | flops 173670400 | bytes 2301952 | tf_op jit(solution)/shard_map/while/body/eval_jaxpr/nkp,nkr->npr/dot_general | solution.py:58
  68.4 2.9 %broadcast_in_dim.96 = bf16[1,256,4096]{2,1,0:T(8,128)(2,1)S(1)} reshape(bf16[256,16,256]{2,1,0:T(8,128)(2,1)} %fusion.59) | data formatting | bytes 4194304 | tf_op jit(solution)/shard_map/while/body/jit(dynamic_update_index_in_dim)/broadcast_in_dim | solution.py:62
  71.2 1.5 constant_dynamic-update-slice_fusion.2
  72.7 8.3 %all-to-all-done = bf16[16,256,512]{2,1,0:T(8,128)(2,1)} async-done(((bf16[16,256,512]{2,1,0:T(8,128)(2,1)}), bf16[16,256,512]{2,1,0:T(8,128)(2,1)}, u32[]{:S(2)}, u32[]{:S(2)}) %all-to-all-start) | async-done | bytes 4194336 | tf_op jit(solution)/shard_map/all_to_all | solution.py:70
  81.0 10.4 %maximum_convert_fusion.1 = bf16[1024,512]{1,0:T(8,128)(2,1)S(1)} fusion(f32[1024,512]{1,0:T(8,128)} %fusion.42, bf16[512,512]{1,0:T(8,128)(2,1)} %param.25, f32[512]{0:T(512)S(1)} %copy-done.13, bf16[1024,4096]{1,0:T(8,128)(2,1)} %bitcast.83, bf16[4096,512]{1,0:T(8,128)(2,1)} %bitcast.11), kind=kOutput, calls=%fused_computation.31 | convolution fusion | flops 4834459648 | bytes 16254976 | tf_op jit(solution)/shard_map/dot_general | solution.py:75
  91.4 2.3 %fusion.21 = bf16[128,8,512]{2,1,0:T(8,128)(2,1)} fusion(bf16[1024,512]{1,0:T(8,128)(2,1)S(1)} %maximum_convert_fusion.1, s32[1024]{0:T(1024)S(1)} %eq.107), kind=kOutput, calls=%fused_computation.35 | convolution fusion | flops 1075314688 | bytes 2101248 | tf_op jit(solution)/shard_map/dot_general | solution.py:86
  93.7 15.1 %all-to-all-start.1 = ((bf16[128,8,512]{2,1,0:T(8,128)(2,1)}), bf16[128,8,512]{2,1,0:T(8,128)(2,1)}, u32[]{:S(2)}, u32[]{:S(2)}) async-start(bf16[128,8,512]{2,1,0:T(8,128)(2,1)} %fusion.21), calls=%async_computation.1 | async-start | bytes 2097152 | tf_op jit(solution)/shard_map/all_to_all | solution.py:90
  109.1 18.1 %all-to-all-done.1 = bf16[128,8,512]{2,1,0:T(8,128)(2,1)} async-done(((bf16[128,8,512]{2,1,0:T(8,128)(2,1)}), bf16[128,8,512]{2,1,0:T(8,128)(2,1)}, u32[]{:S(2)}, u32[]{:S(2)}) %all-to-all-start.1) | async-done | bytes 1048608 | tf_op jit(solution)/shard_map/all_to_all | solution.py:90
  127.1 2.5 %fusion.9 = f32[4,256,512]{2,1,0:T(8,128)S(1)} fusion(s32[4,256]{1,0:T(4,128)S(1)} %copy-done.8, bf16[128,8,512]{2,1,0:T(8,128)(2,1)} %all-to-all-done.1), kind=kOutput, calls=%fused_computation.19 | convolution fusion | flops 1074790400 | bytes 3149824 | tf_op jit(solution)/shard_map/dot_general | solution.py:96
  129.7 0.4 select_reduce_fusion
  130.1 0.6 copy-done.4
  130.7 0.2 fusion.36
  130.9 0.9 fusion.22
  132.0 14.6 %fusion.23 = f32[128,1,8]{2,1,0:T(1,128)} fusion(f32[1024,1,1]{0,1,2:T(1,128)S(1)} %reshape.180, s32[128,8]{1,0:T(8,128)S(1)} %multiply_add_fusion, s32[1024]{0:T(1024)S(1)} %bitcast.82), kind=kOutput, calls=%fused_computation.37 | convolution fusion | flops 13631488 | bytes 16384 | tf_op jit(solution)/shard_map/dot_general | solution.py:108
  146.5 4.9 %all-to-all-start.2 = ((f32[128,1,8]{2,1,0:T(1,128)}), f32[128,1,8]{2,1,0:T(1,128)S(1)}, u32[]{:S(2)}, u32[]{:S(2)}) async-start(f32[128,1,8]{2,1,0:T(1,128)} %fusion.23), calls=%async_computation.2 | async-start | bytes 131072 | tf_op jit(solution)/shard_map/all_to_all | solution.py:114
  151.4 1.0 fusion.43
  152.4 8.7 %all-to-all-done.2 = f32[128,1,8]{2,1,0:T(1,128)S(1)} async-done(((f32[128,1,8]{2,1,0:T(1,128)}), f32[128,1,8]{2,1,0:T(1,128)S(1)}, u32[]{:S(2)}, u32[]{:S(2)}) %all-to-all-start.2) | async-done | bytes 4128 | tf_op jit(solution)/shard_map/all_to_all | solution.py:114
  161.1 0.5 broadcast.119
  161.6 0.8 reduce.3
  162.4 0.1 reshape.182
  162.5 2.5 %fusion.12 = f32[1,1024]{1,0:T(1,128)} fusion(f32[1024,1]{0,1:T(1,128)S(1)} %reshape.182, s32[1024]{0:T(1024)S(1)} %eq.107), kind=kOutput, calls=%fused_computation.21 | convolution fusion | flops 13631488 | bytes 12288 | tf_op jit(solution)/shard_map/dot_general | solution.py:117
  (52 shorter events, 0.7 us)
Async XLA Ops:
  0.6 20.6 %copy-start = (bf16[512,512]{1,0:T(8,128)(2,1)S(1)}, bf16[512,512]{1,0:T(8,128)(2,1)}, u32[]{:S(2)}) copy-start(bf16[512,512]{1,0:T(8,128)(2,1)} %param.24) | copy-start | bytes 1572868
  10.9 8.6 %copy-start.5 = (s32[1024,80]{0,1:T(8,128)S(1)}, s32[1024,80]{0,1:T(8,128)}, u32[]{:S(2)}) copy-start(s32[1024,80]{0,1:T(8,128)} %param.18) | copy-start | bytes 983044
  10.9 70.1 %all-to-all-start = ((bf16[16,256,512]{2,1,0:T(8,128)(2,1)}), bf16[16,256,512]{2,1,0:T(8,128)(2,1)}, u32[]{:S(2)}, u32[]{:S(2)}) async-start(bf16[16,256,512]{2,1,0:T(8,128)(2,1)} %bitcast_select_fusion), calls=%async_computation | async-start | bytes 8388608 | tf_op jit(solution)/shard_map/all_to_all | solution.py:70
  19.5 1.5 copy-start.1
  21.1 2.2 %copy-start.7 = (s32[1,128,8]{1,2,0:T(8,128)S(1)}, s32[1,128,8]{1,2,0:T(8,128)}, u32[]{:S(2)}) copy-start(s32[1,128,8]{1,2,0:T(8,128)} %param.21) | copy-start | bytes 12292
  23.5 57.5 %copy-start.13 = (f32[512]{0:T(512)S(1)}, f32[512]{0:T(512)}, u32[]{:S(2)}) copy-start(f32[512]{0:T(512)} %param.26) | copy-start | bytes 6148
  91.4 2.3 %copy-start.2 = (bf16[1024,512]{1,0:T(8,128)(2,1)}, bf16[1024,512]{1,0:T(8,128)(2,1)S(1)}, u32[]{:S(2)}) copy-start(bf16[1024,512]{1,0:T(8,128)(2,1)S(1)} %maximum_convert_fusion.1) | copy-start | bytes 3145732
  93.7 15.2 %copy-start.11 = (s32[4]{0:T(128)S(1)}, s32[4]{0:T(128)}, u32[]{:S(2)}) copy-start(s32[4]{0:T(128)} %param.23) | copy-start | bytes 52
  93.7 15.2 %copy-start.9 = (bf16[512]{0:T(512)(128)(2,1)S(1)}, bf16[512]{0:T(512)(128)(2,1)}, u32[]{:S(2)}) copy-start(bf16[512]{0:T(512)(128)(2,1)} %param.31) | copy-start | bytes 3076
  93.7 15.2 %copy-start.8 = (s32[4,256]{1,0:T(4,128)S(1)}, s32[4,256]{1,0:T(4,128)}, u32[]{:S(2)}) copy-start(s32[4,256]{1,0:T(4,128)} %param.22) | copy-start | bytes 12292
  93.7 15.2 %copy-start.10 = (bf16[512]{0:T(512)(128)(2,1)S(1)}, bf16[512]{0:T(512)(128)(2,1)}, u32[]{:S(2)}) copy-start(bf16[512]{0:T(512)(128)(2,1)} %param.27) | copy-start | bytes 3076
  93.7 33.4 %all-to-all-start.1 = ((bf16[128,8,512]{2,1,0:T(8,128)(2,1)}), bf16[128,8,512]{2,1,0:T(8,128)(2,1)}, u32[]{:S(2)}, u32[]{:S(2)}) async-start(bf16[128,8,512]{2,1,0:T(8,128)(2,1)} %fusion.21), calls=%async_computation.1 | async-start | bytes 2097152 | tf_op jit(solution)/shard_map/all_to_all | solution.py:90
  129.7 1.0 copy-start.4
  129.7 1.2 copy-start.12
  129.7 1.2 copy-start.14
  131.8 19.6 %copy-start.3 = (bf16[1024,512]{1,0:T(8,128)(2,1)S(1)}, bf16[1024,512]{1,0:T(8,128)(2,1)}, u32[]{:S(2)}) copy-start(bf16[1024,512]{1,0:T(8,128)(2,1)} %copy-done.2) | copy-start | bytes 3145732
  131.9 33.1 %copy-start.6 = (f32[4,256]{1,0:T(4,128)}, f32[4,256]{1,0:T(4,128)S(1)}, u32[]{:S(2)}) copy-start(f32[4,256]{1,0:T(4,128)S(1)} %divide_select_fusion) | copy-start | bytes 12292
  146.5 14.6 %all-to-all-start.2 = ((f32[128,1,8]{2,1,0:T(1,128)}), f32[128,1,8]{2,1,0:T(1,128)S(1)}, u32[]{:S(2)}, u32[]{:S(2)}) async-start(f32[128,1,8]{2,1,0:T(1,128)} %fusion.23), calls=%async_computation.2 | async-start | bytes 131072 | tf_op jit(solution)/shard_map/all_to_all | solution.py:114

commit v2 on v1

--- a/solution.py
+++ b/solution.py
@@ -10,6 +10,11 @@
 
 def select_matrix(indices, count, dtype):
     return (indices[:, None] == jnp.arange(count, dtype=jnp.int32)[None, :]).astype(dtype)
+
+
+def scatter_sum(indices, values, count):
+    hit = indices[:, None] == jnp.arange(count, dtype=jnp.int32)[None, :]
+    return jnp.sum(jnp.where(hit, values[:, None], jnp.float32(0.0)), axis=0)
 
 
 def body(
@@ -105,20 +110,12 @@
     edge_hidden = jax.nn.relu(inner).astype(jnp.bfloat16)
     logits = jnp.einsum("smk,k->sm", edge_hidden, w_edge, preferred_element_type=jnp.float32)
     edge_scores = jnp.where(alive, jax.nn.sigmoid(logits), 0.0)
-    slot_scores = jnp.dot(
-        member_chooser.astype(jnp.float32).T,
-        edge_scores.reshape(sub_count * member_width),
-        precision=lax.Precision.HIGHEST,
-    )
+    slot_scores = scatter_sum(member_flat, edge_scores.reshape(sub_count * member_width), slot_total)
     slot_scores = slot_scores.reshape(device_total, capacity)
     returned = lax.all_to_all(
         slot_scores, ("grp", "shard"), split_axis=0, concat_axis=0, tiled=True
     )
-    node_votes = jnp.dot(
-        send_chooser.astype(jnp.float32).T,
-        returned.reshape(slot_total),
-        precision=lax.Precision.HIGHEST,
-    )
+    node_votes = scatter_sum(send_flat, returned.reshape(slot_total), nodes)
     return (node_hidden, confidence, edge_scores, node_votes)
 
 

time: 166 us -> 152 us (0.916)
  matrix products: 64.5 us -> 48.5 us
  other arithmetic: 8.01 us -> 10.4 us
    dot_general x2 -> x0, matrix products: 17.1 us -> none  [the longest x1 14.6 us: body(): jnp.dot(member_chooser.astype(jnp.float32).T, edge_scores.reshape(sub_cou...]
    reduce_sum x0 -> x2, other arithmetic: none -> 1.71 us  [scatter_sum(): return jnp.sum(jnp.where(hit, values[:, None], jnp.float32(0.0)), axis=0)]
  transfers between devices with their start and end apart: 3 -> 3, of which waited for: 3 -> 3; matrix products, arithmetic and copies ran while one was open for 33% -> 36% of each run, Pallas kernels for 0% -> 0%
where the time goes in v2:
time: 152 us; the launch traced here: 151 us
  matrix products  48.5 us (32%)
  waiting for transfers between devices  34.4 us (23%)
  starting transfers between devices  28.6 us (19%)
  local copies, waits for them, and re-layouts  28 us (18%)
  other arithmetic  10.4 us (7%)
    dot_general x4, matrix products, build_block(): jnp.einsum('nkp,nkr->npr', peer_hot, row_hot, preferred_element_type=jnp....  28 us
    all_to_all x1, waiting for transfers between devices, body(): lax.all_to_all(outbound, ('grp', 'shard'), split_axis=0, concat_axis=0, t...  17.1 us
    all_to_all x1, starting transfers between devices, body(): lax.all_to_all(outbound, ('grp', 'shard'), split_axis=0, concat_axis=0, t...  15.1 us
    broadcast_in_dim x4, local copies, waits for them, and re-layouts, body(): lax.map(build_block, (peer_part, row_part, coeff_blocks))  11.5 us
    dot_general x1, matrix products, body(): jnp.dot(gathered_sum.astype(jnp.bfloat16), w_nbr, preferred_element_type=...  10.5 us
    all_to_all x1, waiting for transfers between devices, body(): lax.all_to_all(slot_scores, ('grp', 'shard'), split_axis=0, concat_axis=0...  9 us
    all_to_all x1, starting transfers between devices, body(): lax.all_to_all(outgoing, 'shard', split_axis=0, concat_axis=0, tiled=True)  8.61 us
    all_to_all x1, waiting for transfers between devices, body(): lax.all_to_all(outgoing, 'shard', split_axis=0, concat_axis=0, tiled=True)  8.24 us
  transfers between devices with their start and end apart: 3, of which 3 were waited for; matrix products, arithmetic and copies ran while one was open for 36% of the time, Pallas kernels for 0%

profile of v2, /device:TPU:1, one launch (start us, length us, event | category | flops | bytes accessed | tf_op | source)
XLA Modules:
  0.0 150.8 jit_solution(15093201551236976115)
XLA Ops:
  0.6 0.8 copy.41
  1.5 0.7 compare_and_fusion
  2.1 1.7 %convert_element_type.37 = bf16[1024,512]{1,0:T(8,128)(2,1)S(1)} convert(f32[1024,512]{1,0:T(8,128)} %param.17) | non-fusion elementwise | flops 524288 | bytes 3145728 | tf_op jit(solution)/shard_map/convert_element_type | solution.py:44
  4.0 0.1 copy.40
  4.2 2.8 %gather_fusion = bf16[32,128,512]{2,1,0:T(8,128)(2,1)} fusion(bf16[8,128,512]{2,1,0:T(8,128)(2,1)S(1)} %bitcast.71, s32[1024]{0:T(1024)S(1)} %pad_clamp_fusion), kind=kCustom, calls=%fused_computation | custom fusion | bytes 8388736 | tf_op jit(solution)/shard_map/jit(_take)/gather | solution.py:73
  6.9 3.9 %bitcast_select_fusion = bf16[16,256,512]{2,1,0:T(8,128)(2,1)} fusion(pred[16,256]{1,0:T(8,128)(4,1)S(1)} %bitcast.78, bf16[16,256,512]{2,1,0:T(8,128)(2,1)} %bitcast.72), kind=kLoop, calls=%fused_computation.14 | loop fusion | flops 2097152 | bytes 8392704 | tf_op jit(solution)/shard_map/jit(_take)/select_n | solution.py:73
  10.9 8.6 %all-to-all-start = ((bf16[16,256,512]{2,1,0:T(8,128)(2,1)}), bf16[16,256,512]{2,1,0:T(8,128)(2,1)}, u32[]{:S(2)}, u32[]{:S(2)}) async-start(bf16[16,256,512]{2,1,0:T(8,128)(2,1)} %bitcast_select_fusion), calls=%async_computation | async-start | bytes 8388608 | tf_op jit(solution)/shard_map/all_to_all | solution.py:75
  19.5 0.3 add_select_fusion
  19.8 0.2 copy.37
  20.0 1.0 copy.39
  21.1 0.2 copy.38
  21.3 2.1 %fusion.33 = f32[1024,512]{1,0:T(8,128)} fusion(bf16[1024,512]{1,0:T(8,128)(2,1)S(1)} %convert_element_type.37, bf16[512,512]{1,0:T(8,128)(2,1)S(1)} %copy-done), kind=kOutput, calls=%fused_computation.64 | convolution fusion | flops 536870912 | bytes 3670016 | tf_op jit(solution)/shard_map/dot_general | solution.py:79
  23.3 0.1 copy.42
  23.5 49.2 %while.10 = (s32[]{:T(128)}, bf16[4,256,4096]{2,1,0:T(8,128)(2,1)}, s32[4,256,80]{2,1,0:T(8,128)S(1)}, bf16[4,256,80]{2,1,0:T(8,128)(2,1)S(1)}, s32[4,256,80]{2,1,0:T(8,128)}, /*index=5*/s32[]{:T(128)}) while((s32[]{:T(128)}, bf16[4,256,4096]{2,1,0:T(8,128)(2,1)}, s32[4,256,80]{2,1,0:T(8,128)S(1)}, bf16[4,256,80]{2,1,0:T(8,128)(2,1)S(1)}, ...), condition=%wide.region_2.3_spmd, body=%wide.region_1.2_spmd.sunk | while | flops 173670400 | bytes 11100749 | solution.py:67
  23.5 0.9 dynamic-slice_bitcast_fusion.5
  24.5 7.0 %fusion.49 = bf16[256,16,256]{2,1,0:T(8,128)(2,1)} fusion(s32[256,80]{1,0:T(8,128)S(1)} %get-tuple-element.79, s32[256,80]{1,0:T(8,128)S(1)} %get-tuple-element.80, bf16[256,80]{1,0:T(8,128)(2,1)S(1)} %dynamic-slice_bitcast_fusion.6), kind=kOutput, calls=%fused_computation.2.clone.1 | convolution fusion | flops 173670400 | bytes 2301952 | tf_op jit(solution)/shard_map/while/body/eval_jaxpr/nkp,nkr->npr/dot_general | solution.py:63
  31.5 2.9 %broadcast_in_dim.131 = bf16[1,256,4096]{2,1,0:T(8,128)(2,1)S(1)} reshape(bf16[256,16,256]{2,1,0:T(8,128)(2,1)} %fusion.49) | data formatting | bytes 4194304 | tf_op jit(solution)/shard_map/while/body/jit(dynamic_update_index_in_dim)/broadcast_in_dim | solution.py:67
  34.4 1.5 constant_dynamic-update-slice_fusion.2
  35.9 0.9 dynamic-slice_bitcast_fusion.5
  36.8 7.0 %fusion.49 = bf16[256,16,256]{2,1,0:T(8,128)(2,1)} fusion(s32[256,80]{1,0:T(8,128)S(1)} %get-tuple-element.79, s32[256,80]{1,0:T(8,128)S(1)} %get-tuple-element.80, bf16[256,80]{1,0:T(8,128)(2,1)S(1)} %dynamic-slice_bitcast_fusion.6), kind=kOutput, calls=%fused_computation.2.clone.1 | convolution fusion | flops 173670400 | bytes 2301952 | tf_op jit(solution)/shard_map/while/body/eval_jaxpr/nkp,nkr->npr/dot_general | solution.py:63
  43.8 2.9 %broadcast_in_dim.131 = bf16[1,256,4096]{2,1,0:T(8,128)(2,1)S(1)} reshape(bf16[256,16,256]{2,1,0:T(8,128)(2,1)} %fusion.49) | data formatting | bytes 4194304 | tf_op jit(solution)/shard_map/while/body/jit(dynamic_update_index_in_dim)/broadcast_in_dim | solution.py:67
  46.7 1.5 constant_dynamic-update-slice_fusion.2
  48.1 0.9 dynamic-slice_bitcast_fusion.5
  49.1 7.0 %fusion.49 = bf16[256,16,256]{2,1,0:T(8,128)(2,1)} fusion(s32[256,80]{1,0:T(8,128)S(1)} %get-tuple-element.79, s32[256,80]{1,0:T(8,128)S(1)} %get-tuple-element.80, bf16[256,80]{1,0:T(8,128)(2,1)S(1)} %dynamic-slice_bitcast_fusion.6), kind=kOutput, calls=%fused_computation.2.clone.1 | convolution fusion | flops 173670400 | bytes 2301952 | tf_op jit(solution)/shard_map/while/body/eval_jaxpr/nkp,nkr->npr/dot_general | solution.py:63
  56.1 2.9 %broadcast_in_dim.131 = bf16[1,256,4096]{2,1,0:T(8,128)(2,1)S(1)} reshape(bf16[256,16,256]{2,1,0:T(8,128)(2,1)} %fusion.49) | data formatting | bytes 4194304 | tf_op jit(solution)/shard_map/while/body/jit(dynamic_update_index_in_dim)/broadcast_in_dim | solution.py:67
  59.0 1.5 constant_dynamic-update-slice_fusion.2
  60.4 0.9 dynamic-slice_bitcast_fusion.5
  61.4 7.0 %fusion.49 = bf16[256,16,256]{2,1,0:T(8,128)(2,1)} fusion(s32[256,80]{1,0:T(8,128)S(1)} %get-tuple-element.79, s32[256,80]{1,0:T(8,128)S(1)} %get-tuple-element.80, bf16[256,80]{1,0:T(8,128)(2,1)S(1)} %dynamic-slice_bitcast_fusion.6), kind=kOutput, calls=%fused_computation.2.clone.1 | convolution fusion | flops 173670400 | bytes 2301952 | tf_op jit(solution)/shard_map/while/body/eval_jaxpr/nkp,nkr->npr/dot_general | solution.py:63
  68.4 2.9 %broadcast_in_dim.131 = bf16[1,256,4096]{2,1,0:T(8,128)(2,1)S(1)} reshape(bf16[256,16,256]{2,1,0:T(8,128)(2,1)} %fusion.49) | data formatting | bytes 4194304 | tf_op jit(solution)/shard_map/while/body/jit(dynamic_update_index_in_dim)/broadcast_in_dim | solution.py:67
  71.2 1.5 constant_dynamic-update-slice_fusion.2
  72.7 8.2 %all-to-all-done = bf16[16,256,512]{2,1,0:T(8,128)(2,1)} async-done(((bf16[16,256,512]{2,1,0:T(8,128)(2,1)}), bf16[16,256,512]{2,1,0:T(8,128)(2,1)}, u32[]{:S(2)}, u32[]{:S(2)}) %all-to-all-start) | async-done | bytes 4194336 | tf_op jit(solution)/shard_map/all_to_all | solution.py:75
  81.0 10.5 %maximum_convert_fusion.1 = bf16[1024,512]{1,0:T(8,128)(2,1)S(1)} fusion(f32[1024,512]{1,0:T(8,128)} %fusion.33, bf16[512,512]{1,0:T(8,128)(2,1)} %param.25, f32[512]{0:T(512)S(1)} %copy-done.10, bf16[1024,4096]{1,0:T(8,128)(2,1)} %bitcast.83, bf16[4096,512]{1,0:T(8,128)(2,1)} %bitcast.11), kind=kOutput, calls=%fused_computation.27 | convolution fusion | flops 4834459648 | bytes 16254976 | tf_op jit(solution)/shard_map/dot_general | solution.py:80
  91.5 2.3 %fusion.15 = bf16[128,8,512]{2,1,0:T(8,128)(2,1)} fusion(bf16[1024,512]{1,0:T(8,128)(2,1)S(1)} %maximum_convert_fusion.1, s32[1024]{0:T(1024)S(1)} %eq.102), kind=kOutput, calls=%fused_computation.31 | convolution fusion | flops 1075314688 | bytes 2101248 | tf_op jit(solution)/shard_map/dot_general | solution.py:91
  93.8 15.1 %all-to-all-start.1 = ((bf16[128,8,512]{2,1,0:T(8,128)(2,1)}), bf16[128,8,512]{2,1,0:T(8,128)(2,1)}, u32[]{:S(2)}, u32[]{:S(2)}) async-start(bf16[128,8,512]{2,1,0:T(8,128)(2,1)} %fusion.15), calls=%async_computation.1 | async-start | bytes 2097152 | tf_op jit(solution)/shard_map/all_to_all | solution.py:95
  109.1 1.0 fusion.34
  110.1 17.1 %all-to-all-done.1 = bf16[128,8,512]{2,1,0:T(8,128)(2,1)} async-done(((bf16[128,8,512]{2,1,0:T(8,128)(2,1)}), bf16[128,8,512]{2,1,0:T(8,128)(2,1)}, u32[]{:S(2)}, u32[]{:S(2)}) %all-to-all-start.1) | async-done | bytes 1048608 | tf_op jit(solution)/shard_map/all_to_all | solution.py:95
  127.2 2.5 %fusion.10 = f32[4,256,512]{2,1,0:T(8,128)S(1)} fusion(s32[4,256]{1,0:T(4,128)S(1)} %copy-done.6, bf16[128,8,512]{2,1,0:T(8,128)(2,1)} %all-to-all-done.1), kind=kOutput, calls=%fused_computation.22 | convolution fusion | flops 1074790400 | bytes 3149824 | tf_op jit(solution)/shard_map/dot_general | solution.py:101
  129.8 0.4 select_reduce_fusion.2
  130.1 0.2 fusion.27
  130.4 2.0 %fusion.16 = f32[1,4,256]{2,0,1:T(1,128)S(1)} fusion(bf16[512,1,1]{0,1,2:T(2,128)(2,1)S(1)} %reshape.155, f32[4,256,512]{2,1,0:T(8,128)S(1)} %fusion.10, f32[512]{0:T(512)S(1)} %copy-done.11, f32[4,512]{1,0:T(4,128)S(1)} %fusion.27, f32[4,512]{1,0:T(4,128)S(1)} %bitcast.76, bf16[512,512]{1,0:T(8,128)(2,1)} %param.28), kind=kOutput, calls=%fused_computation.32 | convolution fusion | flops 541065216 | bytes 2644992 | tf_op jit(solution)/shard_map/smk,k->sm/dot_general | solution.py:111
  132.4 0.6 select_reduce_fusion.1
  133.0 0.7 all_to_all.14
  133.7 4.9 %all-to-all-start.2 = ((f32[128,1,8]{2,1,0:T(1,128)}), f32[128,1,8]{2,1,0:T(1,128)S(1)}, u32[]{:S(2)}, u32[]{:S(2)}) async-start(f32[128,1,8]{2,1,0:T(1,128)} %bitcast.19), calls=%async_computation.2 | async-start | bytes 131072 | tf_op jit(solution)/shard_map/all_to_all | solution.py:115
  138.6 0.7 divide_select_fusion
  139.3 9.0 %all-to-all-done.2 = f32[128,1,8]{2,1,0:T(1,128)S(1)} async-done(((f32[128,1,8]{2,1,0:T(1,128)}), f32[128,1,8]{2,1,0:T(1,128)S(1)}, u32[]{:S(2)}, u32[]{:S(2)}) %all-to-all-start.2) | async-done | bytes 4128 | tf_op jit(solution)/shard_map/all_to_all | solution.py:115
  148.3 0.5 broadcast.97
  148.8 0.8 reduce.3
  149.7 1.1 select_reduce_fusion
  (47 shorter events, 0.7 us)
Async XLA Ops:
  0.6 20.6 %copy-start = (bf16[512,512]{1,0:T(8,128)(2,1)S(1)}, bf16[512,512]{1,0:T(8,128)(2,1)}, u32[]{:S(2)}) copy-start(bf16[512,512]{1,0:T(8,128)(2,1)} %param.24) | copy-start | bytes 1572868
  10.9 8.6 %copy-start.4 = (s32[1024,80]{0,1:T(8,128)S(1)}, s32[1024,80]{0,1:T(8,128)}, u32[]{:S(2)}) copy-start(s32[1024,80]{0,1:T(8,128)} %param.18) | copy-start | bytes 983044
  10.9 10.1 %copy-start.1 = (f32[1024,80]{0,1:T(8,128)S(1)}, f32[1024,80]{0,1:T(8,128)}, u32[]{:S(2)}) copy-start(f32[1024,80]{0,1:T(8,128)} %param.19) | copy-start | bytes 983044
  10.9 70.1 %all-to-all-start = ((bf16[16,256,512]{2,1,0:T(8,128)(2,1)}), bf16[16,256,512]{2,1,0:T(8,128)(2,1)}, u32[]{:S(2)}, u32[]{:S(2)}) async-start(bf16[16,256,512]{2,1,0:T(8,128)(2,1)} %bitcast_select_fusion), calls=%async_computation | async-start | bytes 8388608 | tf_op jit(solution)/shard_map/all_to_all | solution.py:75
  19.5 3.8 %copy-start.5 = (s32[1,128,8]{1,2,0:T(8,128)S(1)}, s32[1,128,8]{1,2,0:T(8,128)}, u32[]{:S(2)}) copy-start(s32[1,128,8]{1,2,0:T(8,128)} %param.21) | copy-start | bytes 12292
  23.5 57.5 %copy-start.10 = (f32[512]{0:T(512)S(1)}, f32[512]{0:T(512)}, u32[]{:S(2)}) copy-start(f32[512]{0:T(512)} %param.26) | copy-start | bytes 6148
  91.4 17.7 %copy-start.2 = (bf16[1024,512]{1,0:T(8,128)(2,1)}, bf16[1024,512]{1,0:T(8,128)(2,1)S(1)}, u32[]{:S(2)}) copy-start(bf16[1024,512]{1,0:T(8,128)(2,1)S(1)} %maximum_convert_fusion.1) | copy-start | bytes 3145732
  91.4 17.5 %copy-start.7 = (s32[4]{0:T(128)S(1)}, s32[4]{0:T(128)}, u32[]{:S(2)}) copy-start(s32[4]{0:T(128)} %param.23) | copy-start | bytes 52
  91.5 17.5 %copy-start.8 = (bf16[512]{0:T(512)(128)(2,1)S(1)}, bf16[512]{0:T(512)(128)(2,1)}, u32[]{:S(2)}) copy-start(bf16[512]{0:T(512)(128)(2,1)} %param.31) | copy-start | bytes 3076
  91.5 17.5 %copy-start.6 = (s32[4,256]{1,0:T(4,128)S(1)}, s32[4,256]{1,0:T(4,128)}, u32[]{:S(2)}) copy-start(s32[4,256]{1,0:T(4,128)} %param.22) | copy-start | bytes 12292
  91.5 17.5 %copy-start.9 = (bf16[512]{0:T(512)(128)(2,1)S(1)}, bf16[512]{0:T(512)(128)(2,1)}, u32[]{:S(2)}) copy-start(bf16[512]{0:T(512)(128)(2,1)} %param.27) | copy-start | bytes 3076
  93.8 33.4 %all-to-all-start.1 = ((bf16[128,8,512]{2,1,0:T(8,128)(2,1)}), bf16[128,8,512]{2,1,0:T(8,128)(2,1)}, u32[]{:S(2)}, u32[]{:S(2)}) async-start(bf16[128,8,512]{2,1,0:T(8,128)(2,1)} %fusion.15), calls=%async_computation.1 | async-start | bytes 2097152 | tf_op jit(solution)/shard_map/all_to_all | solution.py:95
  110.1 20.1 %copy-start.3 = (bf16[512,512]{1,0:T(8,128)(2,1)S(1)}, bf16[512,512]{1,0:T(8,128)(2,1)}, u32[]{:S(2)}) copy-start(bf16[512,512]{1,0:T(8,128)(2,1)} %param.29) | copy-start | bytes 1572868
  110.1 20.3 %copy-start.11 = (f32[512]{0:T(512)S(1)}, f32[512]{0:T(512)}, u32[]{:S(2)}) copy-start(f32[512]{0:T(512)} %param.30) | copy-start | bytes 6148
  133.7 14.6 %all-to-all-start.2 = ((f32[128,1,8]{2,1,0:T(1,128)}), f32[128,1,8]{2,1,0:T(1,128)S(1)}, u32[]{:S(2)}, u32[]{:S(2)}) async-start(f32[128,1,8]{2,1,0:T(1,128)} %bitcast.19), calls=%async_computation.2 | async-start | bytes 131072 | tf_op jit(solution)/shard_map/all_to_all | solution.py:115

commit v3 on v2

--- a/solution.py
+++ b/solution.py
@@ -3,9 +3,81 @@
 import jax
 import jax.numpy as jnp
 from jax import lax
+from jax.experimental import pallas as pl
+from jax.experimental.pallas import tpu as pltpu
 from jax.sharding import PartitionSpec as P
 
 TILE = 128
+
+
+SUB = 8
+
+
+def node_kernel(slot_ref, coef_ref, table_ref, embed_ref, w_self_ref, w_nbr_ref, bias_ref, out_ref, adj_ref):
+    rows_in_block = out_ref.shape[0]
+    peers = adj_ref.shape[0]
+    span = adj_ref.shape[2]
+    sub_count = rows_in_block // SUB
+    width = slot_ref.shape[1]
+    row_hit = lax.broadcasted_iota(jnp.int32, (span, width), 0)
+    lane_node = lax.broadcasted_iota(jnp.int32, (peers * SUB, width), 1) // (width // SUB)
+    pair_row = lax.broadcasted_iota(jnp.int32, (peers * SUB, width), 0)
+    pair_peer = pair_row // SUB
+    pair_node = pair_row % SUB
+
+    def one_sub(s, carry):
+        slots = slot_ref[pl.ds(s, 1), :]
+        coefs = coef_ref[pl.ds(s, 1), :]
+        peer = slots // span
+        row = slots % span
+        onehot = jnp.where(row_hit == row, 1.0, 0.0).astype(jnp.bfloat16)
+        picked = (pair_peer == peer) & (pair_node == lane_node)
+        weights = jnp.where(picked, coefs, 0.0).astype(jnp.bfloat16)
+        block = lax.dot_general(
+            weights, onehot, (((1,), (1,)), ((), ())), preferred_element_type=jnp.float32
+        )
+        start = pl.multiple_of(s * SUB, SUB)
+        adj_ref[:, pl.ds(start, SUB), :] = block.astype(jnp.bfloat16).astype(jnp.float32).reshape(peers, SUB, span)
+        return carry
+
+    lax.fori_loop(0, sub_count, one_sub, 0)
+    total = jnp.zeros((rows_in_block, table_ref.shape[1]), jnp.float32)
+    for p in range(peers):
+        total = total + jnp.dot(
+            adj_ref[p].astype(jnp.bfloat16),
+            table_ref[pl.ds(p * span, span), :],
+            preferred_element_type=jnp.float32,
+        )
+    pre = (
+        jnp.dot(embed_ref[...], w_self_ref[...], preferred_element_type=jnp.float32)
+        + jnp.dot(total.astype(jnp.bfloat16), w_nbr_ref[...], preferred_element_type=jnp.float32)
+        + bias_ref[...]
+    )
+    out_ref[...] = jnp.maximum(pre, 0.0).astype(out_ref.dtype)
+
+
+def node_layer(slot_rows, coef_rows, table, embed_bf, w_self, w_nbr, bias, peers, span):
+    nodes, width = embed_bf.shape
+    hidden = w_self.shape[1]
+    block_rows = 128
+    subs_per_block = block_rows // SUB
+    row_width = slot_rows.shape[1]
+    return pl.pallas_call(
+        node_kernel,
+        grid=(nodes // block_rows,),
+        in_specs=[
+            pl.BlockSpec((subs_per_block, row_width), lambda b: (b, 0)),
+            pl.BlockSpec((subs_per_block, row_width), lambda b: (b, 0)),
+            pl.BlockSpec(table.shape, lambda b: (0, 0)),
+            pl.BlockSpec((block_rows, width), lambda b: (b, 0)),
+            pl.BlockSpec(w_self.shape, lambda b: (0, 0)),
+            pl.BlockSpec(w_nbr.shape, lambda b: (0, 0)),
+            pl.BlockSpec((1, hidden), lambda b: (0, 0)),
+        ],
+        out_specs=pl.BlockSpec((block_rows, hidden), lambda b: (b, 0)),
+        out_shape=jax.ShapeDtypeStruct((nodes, hidden), jnp.bfloat16),
+        scratch_shapes=[pltpu.VMEM((peers, block_rows, span), jnp.float32)],
+    )(slot_rows, coef_rows, table, embed_bf, w_self, w_nbr, bias.reshape(1, hidden))
 
 
 def select_matrix(indices, count, dtype):
@@ -44,43 +116,16 @@
     embed_bf = embed.astype(jnp.bfloat16)
     weight_sum = jnp.sum(knn_weight, axis=1, keepdims=True)
     coeff_bf = (knn_weight / weight_sum).astype(jnp.bfloat16)
-    block_rows = math.gcd(nodes, 256)
-    block_count = nodes // block_rows
-    peer_part = (knn_slot // peer_span).reshape(block_count, block_rows, neighbour_count)
-    row_part = (knn_slot % peer_span).reshape(block_count, block_rows, neighbour_count)
-    coeff_blocks = coeff_bf.reshape(block_count, block_rows, neighbour_count)
-
-    def build_block(pieces):
-        peer_block, row_block, coeff_block = pieces
-        peer_hot = jnp.where(
-            peer_block[:, :, None] == jnp.arange(shard_count, dtype=jnp.int32),
-            coeff_block[:, :, None],
-            jnp.zeros((), jnp.bfloat16),
-        )
-        row_hot = (row_block[:, :, None] == jnp.arange(peer_span, dtype=jnp.int32)).astype(
-            jnp.bfloat16
-        )
-        joined = jnp.einsum("nkp,nkr->npr", peer_hot, row_hot, preferred_element_type=jnp.float32)
-        return joined.reshape(block_rows, column_total)
-
-    adjacency = (
-        lax.map(build_block, (peer_part, row_part, coeff_blocks))
-        .reshape(nodes, column_total)
-        .astype(jnp.bfloat16)
-    )
     tile_count = nodes // TILE
     embed_tiles = embed_bf.reshape(tile_count, TILE, width)
     outgoing = jnp.take(embed_tiles, tile_list[0].reshape(shard_count * list_len), axis=0)
     outgoing = outgoing.reshape(shard_count, peer_span, width)
     provided = lax.all_to_all(outgoing, "shard", split_axis=0, concat_axis=0, tiled=True)
     provided = provided.reshape(column_total, width)
-    gathered_sum = jnp.dot(adjacency, provided, preferred_element_type=jnp.float32)
-    pre_act = (
-        jnp.dot(embed_bf, w_self, preferred_element_type=jnp.float32)
-        + jnp.dot(gathered_sum.astype(jnp.bfloat16), w_nbr, preferred_element_type=jnp.float32)
-        + bias_v
-    )
-    node_hidden = jax.nn.relu(pre_act).astype(jnp.bfloat16)
+    sub_rows = nodes // SUB
+    slot_rows = knn_slot.reshape(sub_rows, SUB * neighbour_count)
+    coef_rows = coeff_bf.astype(jnp.float32).reshape(sub_rows, SUB * neighbour_count)
+    node_hidden = node_layer(slot_rows, coef_rows, provided, embed_bf, w_self, w_nbr, bias_v, shard_count, peer_span)
     confidence = jnp.dot(node_hidden, w_conf, preferred_element_type=jnp.float32)
     device_total = send_rows.shape[1]
     capacity = send_rows.shape[2]

time: 152 us -> 187 us (1.23)
  waiting for transfers between devices: 34.4 us -> 85.1 us
  Pallas kernels: 0 us -> 45.9 us
  matrix products: 48.5 us -> 8.25 us
  local copies, waits for them, and re-layouts: 28 us -> 7.65 us
    all_to_all x1, waiting for transfers between devices: 8.24 us -> 59 us  [body(): lax.all_to_all(outgoing, 'shard', split_axis=0, concat_axis=0, tiled=True)]
    pallas_call x0 -> x1, Pallas kernels: none -> 45.9 us  [node_layer(): pl.pallas_call(node_kernel, grid=(nodes // block_rows,), in_specs=[pl.Blo...]
    dot_general x6 -> x0, matrix products: 40.5 us -> none  [the longest x4 28 us: build_block(): jnp.einsum('nkp,nkr->npr', peer_hot, row_hot, preferred_element_type=jnp....]
    broadcast_in_dim x8 -> x0, local copies, waits for them, and re-layouts: 11.5 us -> none  [the longest x4 11.5 us: body(): lax.map(build_block, (peer_part, row_part, coeff_blocks))]
    dynamic_update_slice x4 -> x0, local copies, waits for them, and re-layouts: 5.89 us -> none  [body(): lax.map(build_block, (peer_part, row_part, coeff_blocks))]
    eq x4 -> x0, local copies, waits for them, and re-layouts: 3.69 us -> none  [build_block(): row_block[:, :, None] == jnp.arange(peer_span, dtype=jnp.int32)]
    reshape x0 -> x3, local copies, waits for them, and re-layouts: none -> 2.03 us  [the longest x2 1.12 us: body(): coeff_bf.astype(jnp.float32).reshape(sub_rows, SUB * neighbour_count)]
  transfers between devices with their start and end apart: 3 -> 3, of which waited for: 3 -> 3; matrix products, arithmetic and copies ran while one was open for 36% -> 2% of each run, Pallas kernels for 0% -> 0%
where the time goes in v3:
time: 187 us; the launch traced here: 186 us
  waiting for transfers between devices  85.1 us (46%)
  Pallas kernels  45.9 us (25%)
  starting transfers between devices  28.6 us (15%)
  other arithmetic  10.1 us (5%)
  matrix products  8.25 us (4%)
  local copies, waits for them, and re-layouts  7.65 us (4%)
    all_to_all x1, waiting for transfers between devices, body(): lax.all_to_all(outgoing, 'shard', split_axis=0, concat_axis=0, tiled=True)  59 us
    pallas_call x1, Pallas kernels, node_layer(): pl.pallas_call(node_kernel, grid=(nodes // block_rows,), in_specs=[pl.Blo...  45.9 us
    all_to_all x1, waiting for transfers between devices, body(): lax.all_to_all(outbound, ('grp', 'shard'), split_axis=0, concat_axis=0, t...  17.1 us
    all_to_all x1, starting transfers between devices, body(): lax.all_to_all(outbound, ('grp', 'shard'), split_axis=0, concat_axis=0, t...  15.1 us
    all_to_all x1, waiting for transfers between devices, body(): lax.all_to_all(slot_scores, ('grp', 'shard'), split_axis=0, concat_axis=0...  9 us
    all_to_all x1, starting transfers between devices, body(): lax.all_to_all(outgoing, 'shard', split_axis=0, concat_axis=0, tiled=True)  8.61 us
    all_to_all x1, starting transfers between devices, body(): lax.all_to_all(slot_scores, ('grp', 'shard'), split_axis=0, concat_axis=0...  4.85 us
    select_n x2, other arithmetic, body(): jnp.take(embed_tiles, tile_list[0].reshape(shard_count * list_len), axis=0)  3.91 us
  transfers between devices with their start and end apart: 3, of which 3 were waited for; matrix products, arithmetic and copies ran while one was open for 2% of the time, Pallas kernels for 0%

profile of v3, /device:TPU:1, one launch (start us, length us, event | category | flops | bytes accessed | tf_op | source)
XLA Modules:
  0.0 186.5 jit_solution(5724291682164305386)
XLA Ops:
  0.6 0.0 copy-start
  0.6 0.8 copy.37
  1.5 0.7 compare_and_fusion
  2.1 1.7 convert_element_type.26.embed_ref
  3.9 0.0 copy-start.1
  3.9 0.1 reshape_squeeze.6
  4.0 0.1 copy.36
  4.1 0.1 broadcast_in_dim.63
  4.2 2.8 %gather_fusion = bf16[32,128,512]{2,1,0:T(8,128)(2,1)} fusion(bf16[8,128,512]{2,1,0:T(8,128)(2,1)S(1)} %bitcast.53, s32[1024]{0:T(1024)S(1)} %pad_clamp_fusion), kind=kCustom, calls=%fused_computation | custom fusion | bytes 8388736 | tf_op jit(solution)/shard_map/jit(_take)/gather | solution.py:121
  7.0 0.0 copy-done.1
  7.0 3.9 %bitcast_select_fusion = bf16[16,256,512]{2,1,0:T(8,128)(2,1)} fusion(pred[16,256]{1,0:T(8,128)(4,1)S(1)} %bitcast.58, bf16[16,256,512]{2,1,0:T(8,128)(2,1)} %bitcast.54), kind=kLoop, calls=%fused_computation.1 | loop fusion | flops 2097152 | bytes 8392704 | tf_op jit(solution)/shard_map/jit(_take)/select_n | solution.py:121
  10.9 8.6 %all-to-all-start = ((bf16[16,256,512]{2,1,0:T(8,128)(2,1)}), bf16[16,256,512]{2,1,0:T(8,128)(2,1)}, u32[]{:S(2)}, u32[]{:S(2)}) async-start(bf16[16,256,512]{2,1,0:T(8,128)(2,1)} %bitcast_select_fusion), calls=%async_computation | async-start | bytes 8388608 | tf_op jit(solution)/shard_map/all_to_all | solution.py:123
  19.5 0.0 copy-done.3
  19.5 0.0 copy-start.5
  19.6 0.2 copy.35
  19.8 0.9 reshape.136.coef_ref
  20.7 0.0 copy-done.4
  20.7 0.2 copy.34
  20.9 0.9 reshape.127.slot_ref
  21.8 0.0 copy-done.5
  21.8 0.1 copy.38
  21.9 0.1 eq.70
  22.0 59.0 %all-to-all-done = bf16[16,256,512]{2,1,0:T(8,128)(2,1)} async-done(((bf16[16,256,512]{2,1,0:T(8,128)(2,1)}), bf16[16,256,512]{2,1,0:T(8,128)(2,1)}, u32[]{:S(2)}, u32[]{:S(2)}) %all-to-all-start) | async-done | bytes 4194336 | tf_op jit(solution)/shard_map/all_to_all | solution.py:123
  81.0 45.9 %shard_map.174 = bf16[1024,512]{1,0:T(8,128)(2,1)} custom-call(s32[128,640]{1,0:T(8,128)} %reshape.127.slot_ref, f32[128,640]{1,0:T(8,128)} %reshape.136.coef_ref, bf16[4096,512]{1,0:T(8,128)(2,1)} %bitcast.4.table_ref, bf16[1024,512]{1,0:T(8,128)(2,1)} %copy-done.1, bf16[512,512]{1,0:T(8,128)(2,1)} %w_self_ref.1, bf16[512,512]{1,0:T(8,128)(2,1)} %w_nbr_ref.1, ...), custom_call_target="tpu_custom_call" | custom-call | tf_op jit(solution)/shard_map/pallas_call | solution.py:65
  126.9 0.0 copy-start.6
  126.9 0.0 copy-start.9
  126.9 0.0 copy-start.2
  126.9 3.6 %fusion.7 = bf16[128,8,512]{2,1,0:T(8,128)(2,1)} fusion(bf16[1024,512]{1,0:T(8,128)(2,1)} %shard_map.174, s32[1024]{0:T(1024)S(1)} %eq.70), kind=kOutput, calls=%fused_computation.16 | convolution fusion | flops 1075314688 | bytes 2101248 | tf_op jit(solution)/shard_map/dot_general | solution.py:136
  130.5 15.1 %all-to-all-start.1 = ((bf16[128,8,512]{2,1,0:T(8,128)(2,1)}), bf16[128,8,512]{2,1,0:T(8,128)(2,1)}, u32[]{:S(2)}, u32[]{:S(2)}) async-start(bf16[128,8,512]{2,1,0:T(8,128)(2,1)} %fusion.7), calls=%async_computation.1 | async-start | bytes 2097152 | tf_op jit(solution)/shard_map/all_to_all | solution.py:140
  145.7 0.0 copy-done.7
  145.7 0.1 iota_compare_fusion.8
  145.8 1.0 fusion.24
  146.8 17.1 %all-to-all-done.1 = bf16[128,8,512]{2,1,0:T(8,128)(2,1)} async-done(((bf16[128,8,512]{2,1,0:T(8,128)(2,1)}), bf16[128,8,512]{2,1,0:T(8,128)(2,1)}, u32[]{:S(2)}, u32[]{:S(2)}) %all-to-all-start.1) | async-done | bytes 1048608 | tf_op jit(solution)/shard_map/all_to_all | solution.py:140
  163.9 2.5 %fusion.2 = f32[4,256,512]{2,1,0:T(8,128)S(1)} fusion(s32[4,256]{1,0:T(4,128)S(1)} %copy-done.6, bf16[128,8,512]{2,1,0:T(8,128)(2,1)} %all-to-all-done.1), kind=kOutput, calls=%fused_computation.9 | convolution fusion | flops 1074790400 | bytes 3149824 | tf_op jit(solution)/shard_map/dot_general | solution.py:146
  166.5 0.4 select_reduce_fusion.2
  166.9 0.2 fusion.18
  167.1 0.0 copy-done.11
  167.1 0.9 fusion.8
  168.0 0.1 fusion.30
  168.1 0.6 select_reduce_fusion.1
  168.7 0.7 all_to_all.14
  169.4 4.8 %all-to-all-start.2 = ((f32[128,1,8]{2,1,0:T(1,128)}), f32[128,1,8]{2,1,0:T(1,128)S(1)}, u32[]{:S(2)}, u32[]{:S(2)}) async-start(f32[128,1,8]{2,1,0:T(1,128)} %bitcast.13), calls=%async_computation.2 | async-start | bytes 131072 | tf_op jit(solution)/shard_map/all_to_all | solution.py:160
  174.2 0.7 divide_select_fusion
  174.9 9.0 %all-to-all-done.2 = f32[128,1,8]{2,1,0:T(1,128)S(1)} async-done(((f32[128,1,8]{2,1,0:T(1,128)}), f32[128,1,8]{2,1,0:T(1,128)S(1)}, u32[]{:S(2)}, u32[]{:S(2)}) %all-to-all-start.2) | async-done | bytes 4128 | tf_op jit(solution)/shard_map/all_to_all | solution.py:160
  183.9 0.5 broadcast.82
  184.4 0.8 reduce.3
  185.2 0.1 broadcast_in_dim.73
  185.3 1.1 select_reduce_fusion
  (24 shorter events, 0.1 us)
Async XLA Ops:
  0.6 166.2 %copy-start = (bf16[512,512]{1,0:T(8,128)(2,1)S(1)}, bf16[512,512]{1,0:T(8,128)(2,1)}, u32[]{:S(2)}) copy-start(bf16[512,512]{1,0:T(8,128)(2,1)} %param.27) | copy-start | bytes 1572868
  3.9 3.1 %copy-start.1 = (bf16[1024,512]{1,0:T(8,128)(2,1)}, bf16[1024,512]{1,0:T(8,128)(2,1)S(1)}, u32[]{:S(2)}) copy-start(bf16[1024,512]{1,0:T(8,128)(2,1)S(1)} %convert_element_type.26.embed_ref) | copy-start | bytes 3145732
  10.9 8.6 %copy-start.3 = (f32[1024,80]{0,1:T(8,128)S(1)}, f32[1024,80]{0,1:T(8,128)}, u32[]{:S(2)}) copy-start(f32[1024,80]{0,1:T(8,128)} %param.17) | copy-start | bytes 983044
  10.9 9.8 %copy-start.4 = (s32[1024,80]{0,1:T(8,128)S(1)}, s32[1024,80]{0,1:T(8,128)}, u32[]{:S(2)}) copy-start(s32[1024,80]{0,1:T(8,128)} %param.16) | copy-start | bytes 983044
  10.9 70.1 %all-to-all-start = ((bf16[16,256,512]{2,1,0:T(8,128)(2,1)}), bf16[16,256,512]{2,1,0:T(8,128)(2,1)}, u32[]{:S(2)}, u32[]{:S(2)}) async-start(bf16[16,256,512]{2,1,0:T(8,128)(2,1)} %bitcast_select_fusion), calls=%async_computation | async-start | bytes 8388608 | tf_op jit(solution)/shard_map/all_to_all | solution.py:123
  19.5 2.3 %copy-start.5 = (s32[1,128,8]{1,2,0:T(8,128)S(1)}, s32[1,128,8]{1,2,0:T(8,128)}, u32[]{:S(2)}) copy-start(s32[1,128,8]{1,2,0:T(8,128)} %param.19) | copy-start | bytes 12292
  126.9 18.8 %copy-start.7 = (s32[4]{0:T(128)S(1)}, s32[4]{0:T(128)}, u32[]{:S(2)}) copy-start(s32[4]{0:T(128)} %param.21) | copy-start | bytes 52
  126.9 18.8 %copy-start.8 = (bf16[512]{0:T(512)(128)(2,1)S(1)}, bf16[512]{0:T(512)(128)(2,1)}, u32[]{:S(2)}) copy-start(bf16[512]{0:T(512)(128)(2,1)} %param.29) | copy-start | bytes 3076
  126.9 18.8 %copy-start.6 = (s32[4,256]{1,0:T(4,128)S(1)}, s32[4,256]{1,0:T(4,128)}, u32[]{:S(2)}) copy-start(s32[4,256]{1,0:T(4,128)} %param.20) | copy-start | bytes 12292
  126.9 18.8 %copy-start.9 = (bf16[512]{0:T(512)(128)(2,1)S(1)}, bf16[512]{0:T(512)(128)(2,1)}, u32[]{:S(2)}) copy-start(bf16[512]{0:T(512)(128)(2,1)} %param.25) | copy-start | bytes 3076
  126.9 18.9 %copy-start.2 = (bf16[1024,512]{1,0:T(8,128)(2,1)S(1)}, bf16[1024,512]{1,0:T(8,128)(2,1)}, u32[]{:S(2)}) copy-start(bf16[1024,512]{1,0:T(8,128)(2,1)} %shard_map.174) | copy-start | bytes 3145732
  130.5 33.4 %all-to-all-start.1 = ((bf16[128,8,512]{2,1,0:T(8,128)(2,1)}), bf16[128,8,512]{2,1,0:T(8,128)(2,1)}, u32[]{:S(2)}, u32[]{:S(2)}) async-start(bf16[128,8,512]{2,1,0:T(8,128)(2,1)} %fusion.7), calls=%async_computation.1 | async-start | bytes 2097152 | tf_op jit(solution)/shard_map/all_to_all | solution.py:140
  146.8 20.3 %copy-start.10 = (bf16[512,512]{1,0:T(8,128)(2,1)S(1)}, bf16[512,512]{1,0:T(8,128)(2,1)}, u32[]{:S(2)}) copy-start(bf16[512,512]{1,0:T(8,128)(2,1)} %param.26) | copy-start | bytes 1572868
  146.8 20.3 %copy-start.11 = (f32[512]{0:T(512)S(1)}, f32[512]{0:T(512)}, u32[]{:S(2)}) copy-start(f32[512]{0:T(512)} %param.28) | copy-start | bytes 6148
  169.4 14.5 %all-to-all-start.2 = ((f32[128,1,8]{2,1,0:T(1,128)}), f32[128,1,8]{2,1,0:T(1,128)S(1)}, u32[]{:S(2)}, u32[]{:S(2)}) async-start(f32[128,1,8]{2,1,0:T(1,128)} %bitcast.13), calls=%async_computation.2 | async-start | bytes 131072 | tf_op jit(solution)/shard_map/all_to_all | solution.py:160

commit v4 on v3

--- a/solution.py
+++ b/solution.py
@@ -13,11 +13,10 @@
 SUB = 8
 
 
-def node_kernel(slot_ref, coef_ref, table_ref, embed_ref, w_self_ref, w_nbr_ref, bias_ref, out_ref, adj_ref):
-    rows_in_block = out_ref.shape[0]
+def build_adjacency(slot_ref, coef_ref, adj_ref):
     peers = adj_ref.shape[0]
     span = adj_ref.shape[2]
-    sub_count = rows_in_block // SUB
+    sub_count = adj_ref.shape[1] // SUB
     width = slot_ref.shape[1]
     row_hit = lax.broadcasted_iota(jnp.int32, (span, width), 0)
     lane_node = lax.broadcasted_iota(jnp.int32, (peers * SUB, width), 1) // (width // SUB)
@@ -41,43 +40,88 @@
         return carry
 
     lax.fori_loop(0, sub_count, one_sub, 0)
-    total = jnp.zeros((rows_in_block, table_ref.shape[1]), jnp.float32)
-    for p in range(peers):
-        total = total + jnp.dot(
-            adj_ref[p].astype(jnp.bfloat16),
-            table_ref[pl.ds(p * span, span), :],
-            preferred_element_type=jnp.float32,
+
+
+def node_kernel(
+    outgoing_ref, slot_ref, coef_ref, embed_ref, w_self_ref, w_nbr_ref, bias_ref,
+    out_ref, table_ref, adj_ref, send_sems, recv_sems, self_sem,
+):
+    peers = adj_ref.shape[0]
+    span = adj_ref.shape[2]
+    block_rows = 128
+    group = lax.axis_index("grp")
+    me = lax.axis_index("shard")
+    barrier = pltpu.get_barrier_semaphore()
+    for d in range(1, peers):
+        pl.semaphore_signal(barrier, 1, device_id=(group, lax.rem(me + d, peers)), device_id_type=pl.DeviceIdType.MESH)
+    pl.semaphore_wait(barrier, peers - 1)
+
+    def link(target, slot):
+        return pltpu.make_async_remote_copy(
+            src_ref=outgoing_ref.at[target],
+            dst_ref=table_ref.at[slot],
+            send_sem=send_sems.at[target],
+            recv_sem=recv_sems.at[slot],
+            device_id=(group, target),
+            device_id_type=pl.DeviceIdType.MESH,
         )
-    pre = (
-        jnp.dot(embed_ref[...], w_self_ref[...], preferred_element_type=jnp.float32)
-        + jnp.dot(total.astype(jnp.bfloat16), w_nbr_ref[...], preferred_element_type=jnp.float32)
-        + bias_ref[...]
-    )
-    out_ref[...] = jnp.maximum(pre, 0.0).astype(out_ref.dtype)
-
-
-def node_layer(slot_rows, coef_rows, table, embed_bf, w_self, w_nbr, bias, peers, span):
+
+    own = pltpu.make_async_copy(outgoing_ref.at[me], table_ref.at[me], self_sem)
+    own.start()
+    sends = []
+    for d in range(1, peers):
+        copy = link(lax.rem(me + d, peers), me)
+        copy.start()
+        sends.append(copy)
+    build_adjacency(slot_ref, coef_ref, adj_ref)
+    own.wait()
+    for d in range(1, peers):
+        source = lax.rem(me + peers - d, peers)
+        link(source, source).wait_recv()
+    for copy in sends:
+        copy.wait_send()
+
+    def one_block(b, carry):
+        rows = pl.ds(pl.multiple_of(b * block_rows, block_rows), block_rows)
+        total = jnp.zeros((block_rows, table_ref.shape[2]), jnp.float32)
+        for p in range(peers):
+            total = total + jnp.dot(
+                adj_ref[p, rows, :].astype(jnp.bfloat16),
+                table_ref[p],
+                preferred_element_type=jnp.float32,
+            )
+        pre = (
+            jnp.dot(embed_ref[rows, :], w_self_ref[...], preferred_element_type=jnp.float32)
+            + jnp.dot(total.astype(jnp.bfloat16), w_nbr_ref[...], preferred_element_type=jnp.float32)
+            + bias_ref[...]
+        )
+        out_ref[rows, :] = jnp.maximum(pre, 0.0).astype(out_ref.dtype)
+        return carry
+
+    lax.fori_loop(0, out_ref.shape[0] // block_rows, one_block, 0)
+
+
+def node_layer(outgoing, slot_rows, coef_rows, embed_bf, w_self, w_nbr, bias):
     nodes, width = embed_bf.shape
     hidden = w_self.shape[1]
-    block_rows = 128
-    subs_per_block = block_rows // SUB
-    row_width = slot_rows.shape[1]
+    peers, span, _ = outgoing.shape
+    vmem = pl.BlockSpec(memory_space=pltpu.VMEM)
     return pl.pallas_call(
         node_kernel,
-        grid=(nodes // block_rows,),
-        in_specs=[
-            pl.BlockSpec((subs_per_block, row_width), lambda b: (b, 0)),
-            pl.BlockSpec((subs_per_block, row_width), lambda b: (b, 0)),
-            pl.BlockSpec(table.shape, lambda b: (0, 0)),
-            pl.BlockSpec((block_rows, width), lambda b: (b, 0)),
-            pl.BlockSpec(w_self.shape, lambda b: (0, 0)),
-            pl.BlockSpec(w_nbr.shape, lambda b: (0, 0)),
-            pl.BlockSpec((1, hidden), lambda b: (0, 0)),
+        in_specs=[pl.BlockSpec(memory_space=pl.ANY)] + [vmem] * 6,
+        out_specs=vmem,
+        out_shape=jax.ShapeDtypeStruct((nodes, hidden), jnp.bfloat16),
+        scratch_shapes=[
+            pltpu.VMEM((peers, span, width), jnp.bfloat16),
+            pltpu.VMEM((peers, nodes, span), jnp.float32),
+            pltpu.SemaphoreType.DMA((peers,)),
+            pltpu.SemaphoreType.DMA((peers,)),
+            pltpu.SemaphoreType.DMA,
         ],
-        out_specs=pl.BlockSpec((block_rows, hidden), lambda b: (b, 0)),
-        out_shape=jax.ShapeDtypeStruct((nodes, hidden), jnp.bfloat16),
-        scratch_shapes=[pltpu.VMEM((peers, block_rows, span), jnp.float32)],
-    )(slot_rows, coef_rows, table, embed_bf, w_self, w_nbr, bias.reshape(1, hidden))
+        compiler_params=pltpu.CompilerParams(
+            collective_id=0, has_side_effects=True, vmem_limit_bytes=60 * 1024 * 1024
+        ),
+    )(outgoing, slot_rows, coef_rows, embed_bf, w_self, w_nbr, bias.reshape(1, hidden))
 
 
 def select_matrix(indices, count, dtype):
@@ -120,12 +164,10 @@
     embed_tiles = embed_bf.reshape(tile_count, TILE, width)
     outgoing = jnp.take(embed_tiles, tile_list[0].reshape(shard_count * list_len), axis=0)
     outgoing = outgoing.reshape(shard_count, peer_span, width)
-    provided = lax.all_to_all(outgoing, "shard", split_axis=0, concat_axis=0, tiled=True)
-    provided = provided.reshape(column_total, width)
     sub_rows = nodes // SUB
     slot_rows = knn_slot.reshape(sub_rows, SUB * neighbour_count)
     coef_rows = coeff_bf.astype(jnp.float32).reshape(sub_rows, SUB * neighbour_count)
-    node_hidden = node_layer(slot_rows, coef_rows, provided, embed_bf, w_self, w_nbr, bias_v, shard_count, peer_span)
+    node_hidden = node_layer(outgoing, slot_rows, coef_rows, embed_bf, w_self, w_nbr, bias_v)
     confidence = jnp.dot(node_hidden, w_conf, preferred_element_type=jnp.float32)
     device_total = send_rows.shape[1]
     capacity = send_rows.shape[2]

time: 187 us -> 177 us (0.947)
  waiting for transfers between devices: 85.1 us -> 26.4 us
  Pallas kernels: 45.9 us -> 90.7 us
  local copies, waits for them, and re-layouts: 7.65 us -> 10 us
  other arithmetic: 10.1 us -> 12.1 us
    all_to_all x1 -> x0, waiting for transfers between devices: 59 us -> none  [body(): lax.all_to_all(outgoing, 'shard', split_axis=0, concat_axis=0, tiled=True)]
    pallas_call x1, Pallas kernels: 45.9 us -> 90.7 us  [node_layer(): pl.pallas_call(node_kernel, in_specs=[pl.BlockSpec(memory_space=pl.ANY)]...]
    all_to_all x1 -> x0, starting transfers between devices: 8.61 us -> none  [body(): lax.all_to_all(outgoing, 'shard', split_axis=0, concat_axis=0, tiled=True)]
    all_to_all x1, starting transfers between devices: 15.1 us -> 23.3 us  [body(): lax.all_to_all(outbound, ('grp', 'shard'), split_axis=0, concat_axis=0, t...]
    unnamed x33 -> x34, local copies, waits for them, and re-layouts: 1.2 us -> 3.49 us
  transfers between devices with their start and end apart: 3 -> 2, of which waited for: 3 -> 2; matrix products, arithmetic and copies ran while one was open for 2% -> 1% of each run, Pallas kernels for 0% -> 0%
where the time goes in v4:
time: 177 us
  Pallas kernels  90.7 us (51%)
  starting transfers between devices  28.2 us (16%)
  waiting for transfers between devices  26.4 us (15%)
  other arithmetic  12.1 us (7%)
  local copies, waits for them, and re-layouts  10 us (6%)
  matrix products  8.58 us (5%)
    pallas_call x1, Pallas kernels, node_layer(): pl.pallas_call(node_kernel, in_specs=[pl.BlockSpec(memory_space=pl.ANY)]...  90.7 us
    all_to_all x1, starting transfers between devices, body(): lax.all_to_all(outbound, ('grp', 'shard'), split_axis=0, concat_axis=0, t...  23.3 us
    all_to_all x1, waiting for transfers between devices, body(): lax.all_to_all(outbound, ('grp', 'shard'), split_axis=0, concat_axis=0, t...  17.5 us
    all_to_all x1, waiting for transfers between devices, body(): lax.all_to_all(slot_scores, ('grp', 'shard'), split_axis=0, concat_axis=0...  8.93 us
    all_to_all x1, starting transfers between devices, body(): lax.all_to_all(slot_scores, ('grp', 'shard'), split_axis=0, concat_axis=0...  4.87 us
    select_n x2, other arithmetic, body(): jnp.take(embed_tiles, tile_list[0].reshape(shard_count * list_len), axis=0)  3.87 us
    dot_general x1, matrix products, body(): jnp.dot(send_chooser, node_hidden, preferred_element_type=jnp.float32)  3.58 us
  transfers between devices with their start and end apart: 2, of which 2 were waited for; matrix products, arithmetic and copies ran while one was open for 1% of the time, Pallas kernels for 0%

profile of v4, /device:TPU:1, one launch (start us, length us, event | category | flops | bytes accessed | tf_op | source)
XLA Modules:
  0.0 176.9 jit_solution(7916438544075796228)
XLA Ops:
  0.6 0.0 copy-start
  0.6 0.0 copy-start.4
  0.7 0.0 copy-start.5
  0.7 0.8 copy.35
  1.5 0.7 compare_and_fusion
  2.2 1.7 convert_element_type.25.embed_ref
  3.9 0.0 copy-start.1
  3.9 0.1 reshape_squeeze.6
  4.0 0.1 copy.34
  4.1 0.1 broadcast_in_dim.63
  4.2 1.0 reduce_sum.36
  5.3 1.0 fusion.17
  6.3 0.2 copy.37
  6.5 0.9 reshape.132.coef_ref
  7.4 0.2 copy.36
  7.6 1.0 reshape.125.slot_ref
  8.6 0.1 copy.38
  8.7 0.1 eq.70
  8.8 2.8 %gather_fusion = bf16[32,128,512]{2,1,0:T(8,128)(2,1)} fusion(bf16[8,128,512]{2,1,0:T(8,128)(2,1)S(1)} %bitcast.52, s32[1024]{0:T(1024)S(1)} %pad_clamp_fusion), kind=kCustom, calls=%fused_computation | custom fusion | bytes 8388736 | tf_op jit(solution)/shard_map/jit(_take)/gather | solution.py:165
  11.6 0.0 copy-done.1
  11.6 3.9 %bitcast_select_fusion.outgoing_ref = bf16[16,256,512]{2,1,0:T(8,128)(2,1)} fusion(pred[16,256]{1,0:T(8,128)(4,1)S(1)} %bitcast.57, bf16[16,256,512]{2,1,0:T(8,128)(2,1)} %bitcast.53), kind=kLoop, calls=%fused_computation.1 | loop fusion | flops 2097152 | bytes 8392704 | tf_op jit(solution)/shard_map/jit(_take)/select_n | solution.py:165
  15.4 90.7 %shard_map.174 = bf16[1024,512]{1,0:T(8,128)(2,1)} custom-call(bf16[16,256,512]{2,1,0:T(8,128)(2,1)} %bitcast_select_fusion.outgoing_ref, s32[128,640]{1,0:T(8,128)} %reshape.125.slot_ref, f32[128,640]{1,0:T(8,128)} %reshape.132.coef_ref, bf16[1024,512]{1,0:T(8,128)(2,1)} %copy-done.1, bf16[512,512]{1,0:T(8,128)(2,1)} %w_self_ref.1, ...), custom_call_target="tpu_custom_call" | custom-call | tf_op jit(solution)/shard_map/pallas_call | solution.py:109
  106.2 0.0 copy-start.7
  106.2 0.0 copy-start.8
  106.2 0.0 copy-start.6
  106.2 0.0 copy-start.9
  106.2 3.6 %fusion.7 = bf16[128,8,512]{2,1,0:T(8,128)(2,1)} fusion(bf16[1024,512]{1,0:T(8,128)(2,1)} %shard_map.174, s32[1024]{0:T(1024)S(1)} %eq.70), kind=kOutput, calls=%fused_computation.16 | convolution fusion | flops 1075314688 | bytes 2101248 | tf_op jit(solution)/shard_map/dot_general | solution.py:178
  109.8 23.3 %all-to-all-start = ((bf16[128,8,512]{2,1,0:T(8,128)(2,1)}), bf16[128,8,512]{2,1,0:T(8,128)(2,1)S(1)}, u32[]{:S(2)}, u32[]{:S(2)}) async-start(bf16[128,8,512]{2,1,0:T(8,128)(2,1)} %fusion.7), calls=%async_computation | async-start | bytes 2097152 | tf_op jit(solution)/shard_map/all_to_all | solution.py:182
  133.2 0.1 iota_compare_fusion.8
  133.3 1.0 fusion.24
  134.3 17.5 %all-to-all-done = bf16[128,8,512]{2,1,0:T(8,128)(2,1)S(1)} async-done(((bf16[128,8,512]{2,1,0:T(8,128)(2,1)}), bf16[128,8,512]{2,1,0:T(8,128)(2,1)S(1)}, u32[]{:S(2)}, u32[]{:S(2)}) %all-to-all-start) | async-done | bytes 1048608 | tf_op jit(solution)/shard_map/all_to_all | solution.py:182
  151.8 1.3 fusion.2
  153.1 1.3 copy-done.3
  154.4 0.4 select_reduce_fusion.2
  154.8 0.2 fusion.18
  155.0 0.0 copy-done.10
  155.0 2.5 %fusion.8 = f32[1,4,256]{2,0,1:T(1,128)S(1)} fusion(bf16[512,1,1]{0,1,2:T(2,128)(2,1)S(1)} %reshape.145, f32[4,256,512]{2,1,0:T(8,128)} %copy-done.3, f32[512]{0:T(512)S(1)} %copy-done.11, f32[4,512]{1,0:T(4,128)S(1)} %fusion.18, f32[4,512]{1,0:T(4,128)S(1)} %bitcast.55, bf16[512,512]{1,0:T(8,128)(2,1)S(1)} %copy-done.10), kind=kOutput, calls=%fused_computation.17 | convolution fusion | flops 541065216 | bytes 2644992 | tf_op jit(solution)/shard_map/smk,k->sm/dot_general | solution.py:198
  157.5 0.1 fusion.30
  157.6 0.6 select_reduce_fusion.1
  158.2 0.7 all_to_all.10
  158.9 4.9 %all-to-all-start.1 = ((f32[128,1,8]{2,1,0:T(1,128)}), f32[128,1,8]{2,1,0:T(1,128)S(1)}, u32[]{:S(2)}, u32[]{:S(2)}) async-start(f32[128,1,8]{2,1,0:T(1,128)} %bitcast.12), calls=%async_computation.1 | async-start | bytes 131072 | tf_op jit(solution)/shard_map/all_to_all | solution.py:202
  163.8 0.7 divide_select_fusion
  164.5 8.9 %all-to-all-done.1 = f32[128,1,8]{2,1,0:T(1,128)S(1)} async-done(((f32[128,1,8]{2,1,0:T(1,128)}), f32[128,1,8]{2,1,0:T(1,128)S(1)}, u32[]{:S(2)}, u32[]{:S(2)}) %all-to-all-start.1) | async-done | bytes 4128 | tf_op jit(solution)/shard_map/all_to_all | solution.py:202
  173.4 0.5 broadcast.82
  173.9 0.8 reduce.3
  174.7 0.1 broadcast_in_dim.73
  174.8 1.1 select_reduce_fusion
  175.9 1.0 copy.53
  (23 shorter events, 0.1 us)
Async XLA Ops:
  0.6 154.2 %copy-start = (bf16[512,512]{1,0:T(8,128)(2,1)S(1)}, bf16[512,512]{1,0:T(8,128)(2,1)}, u32[]{:S(2)}) copy-start(bf16[512,512]{1,0:T(8,128)(2,1)} %param.27) | copy-start | bytes 1572868
  0.6 6.8 %copy-start.4 = (s32[1024,80]{0,1:T(8,128)S(1)}, s32[1024,80]{0,1:T(8,128)}, u32[]{:S(2)}) copy-start(s32[1024,80]{0,1:T(8,128)} %param.16) | copy-start | bytes 983044
  0.7 7.9 %copy-start.5 = (s32[1,128,8]{1,2,0:T(8,128)S(1)}, s32[1,128,8]{1,2,0:T(8,128)}, u32[]{:S(2)}) copy-start(s32[1,128,8]{1,2,0:T(8,128)} %param.19) | copy-start | bytes 12292
  3.9 7.7 %copy-start.1 = (bf16[1024,512]{1,0:T(8,128)(2,1)}, bf16[1024,512]{1,0:T(8,128)(2,1)S(1)}, u32[]{:S(2)}) copy-start(bf16[1024,512]{1,0:T(8,128)(2,1)S(1)} %convert_element_type.25.embed_ref) | copy-start | bytes 3145732
  106.2 27.0 %copy-start.7 = (s32[4]{0:T(128)S(1)}, s32[4]{0:T(128)}, u32[]{:S(2)}) copy-start(s32[4]{0:T(128)} %param.21) | copy-start | bytes 52
  106.2 27.0 %copy-start.8 = (bf16[512]{0:T(512)(128)(2,1)S(1)}, bf16[512]{0:T(512)(128)(2,1)}, u32[]{:S(2)}) copy-start(bf16[512]{0:T(512)(128)(2,1)} %param.29) | copy-start | bytes 3076
  106.2 27.0 %copy-start.6 = (s32[4,256]{1,0:T(4,128)S(1)}, s32[4,256]{1,0:T(4,128)}, u32[]{:S(2)}) copy-start(s32[4,256]{1,0:T(4,128)} %param.20) | copy-start | bytes 12292
  106.2 27.0 %copy-start.9 = (bf16[512]{0:T(512)(128)(2,1)S(1)}, bf16[512]{0:T(512)(128)(2,1)}, u32[]{:S(2)}) copy-start(bf16[512]{0:T(512)(128)(2,1)} %param.25) | copy-start | bytes 3076
  106.2 27.1 %copy-start.2 = (bf16[1024,512]{1,0:T(8,128)(2,1)S(1)}, bf16[1024,512]{1,0:T(8,128)(2,1)}, u32[]{:S(2)}) copy-start(bf16[1024,512]{1,0:T(8,128)(2,1)} %shard_map.174) | copy-start | bytes 3145732
  109.8 42.0 %all-to-all-start = ((bf16[128,8,512]{2,1,0:T(8,128)(2,1)}), bf16[128,8,512]{2,1,0:T(8,128)(2,1)S(1)}, u32[]{:S(2)}, u32[]{:S(2)}) async-start(bf16[128,8,512]{2,1,0:T(8,128)(2,1)} %fusion.7), calls=%async_computation | async-start | bytes 2097152 | tf_op jit(solution)/shard_map/all_to_all | solution.py:182
  134.3 20.7 %copy-start.10 = (bf16[512,512]{1,0:T(8,128)(2,1)S(1)}, bf16[512,512]{1,0:T(8,128)(2,1)}, u32[]{:S(2)}) copy-start(bf16[512,512]{1,0:T(8,128)(2,1)} %param.26) | copy-start | bytes 1572868
  134.3 20.7 %copy-start.11 = (f32[512]{0:T(512)S(1)}, f32[512]{0:T(512)}, u32[]{:S(2)}) copy-start(f32[512]{0:T(512)} %param.28) | copy-start | bytes 6148
  153.1 1.3 copy-start.3
  158.9 14.5 %all-to-all-start.1 = ((f32[128,1,8]{2,1,0:T(1,128)}), f32[128,1,8]{2,1,0:T(1,128)S(1)}, u32[]{:S(2)}, u32[]{:S(2)}) async-start(f32[128,1,8]{2,1,0:T(1,128)} %bitcast.12), calls=%async_computation.1 | async-start | bytes 131072 | tf_op jit(solution)/shard_map/all_to_all | solution.py:202

commit v5 on v2

--- a/solution.py
+++ b/solution.py
@@ -70,16 +70,13 @@
     )
     tile_count = nodes // TILE
     embed_tiles = embed_bf.reshape(tile_count, TILE, width)
-    outgoing = jnp.take(embed_tiles, tile_list[0].reshape(shard_count * list_len), axis=0)
+    outgoing = embed_tiles.at[tile_list[0].reshape(shard_count * list_len)].get(mode="promise_in_bounds")
     outgoing = outgoing.reshape(shard_count, peer_span, width)
     provided = lax.all_to_all(outgoing, "shard", split_axis=0, concat_axis=0, tiled=True)
     provided = provided.reshape(column_total, width)
     gathered_sum = jnp.dot(adjacency, provided, preferred_element_type=jnp.float32)
-    pre_act = (
-        jnp.dot(embed_bf, w_self, preferred_element_type=jnp.float32)
-        + jnp.dot(gathered_sum.astype(jnp.bfloat16), w_nbr, preferred_element_type=jnp.float32)
-        + bias_v
-    )
+    self_term = jnp.dot(embed_bf, w_self, preferred_element_type=jnp.float32) + bias_v
+    pre_act = self_term + jnp.dot(gathered_sum.astype(jnp.bfloat16), w_nbr, preferred_element_type=jnp.float32)
     node_hidden = jax.nn.relu(pre_act).astype(jnp.bfloat16)
     confidence = jnp.dot(node_hidden, w_conf, preferred_element_type=jnp.float32)
     device_total = send_rows.shape[1]

time: 152 us -> 147 us (0.967)
  other arithmetic: 10.4 us -> 5.84 us
    select_n x2 -> x1, other arithmetic: 3.91 us -> 0.01 us  [body(): embed_tiles.at[tile_list[0].reshape(shard_count * list_len)]]
  transfers between devices with their start and end apart: 3 -> 3, of which waited for: 3 -> 3; matrix products, arithmetic and copies ran while one was open for 36% -> 38% of each run, Pallas kernels for 0% -> 0%
where the time goes in v5:
time: 147 us; the launch traced here: 146 us
  matrix products  48.5 us (33%)
  waiting for transfers between devices  34.4 us (23%)
  starting transfers between devices  28.6 us (19%)
  local copies, waits for them, and re-layouts  27.7 us (19%)
  other arithmetic  5.84 us (4%)
    dot_general x4, matrix products, build_block(): jnp.einsum('nkp,nkr->npr', peer_hot, row_hot, preferred_element_type=jnp....  28 us
    all_to_all x1, waiting for transfers between devices, body(): lax.all_to_all(outbound, ('grp', 'shard'), split_axis=0, concat_axis=0, t...  17.1 us
    all_to_all x1, starting transfers between devices, body(): lax.all_to_all(outbound, ('grp', 'shard'), split_axis=0, concat_axis=0, t...  15.1 us
    broadcast_in_dim x4, local copies, waits for them, and re-layouts, body(): lax.map(build_block, (peer_part, row_part, coeff_blocks))  11.5 us
    dot_general x1, matrix products, body(): jnp.dot(gathered_sum.astype(jnp.bfloat16), w_nbr, preferred_element_type=...  10.4 us
    all_to_all x1, waiting for transfers between devices, body(): lax.all_to_all(slot_scores, ('grp', 'shard'), split_axis=0, concat_axis=0...  9 us
    all_to_all x1, starting transfers between devices, body(): lax.all_to_all(outgoing, 'shard', split_axis=0, concat_axis=0, tiled=True)  8.61 us
    all_to_all x1, waiting for transfers between devices, body(): lax.all_to_all(outgoing, 'shard', split_axis=0, concat_axis=0, tiled=True)  8.24 us
  transfers between devices with their start and end apart: 3, of which 3 were waited for; matrix products, arithmetic and copies ran while one was open for 38% of the time, Pallas kernels for 0%

profile of v5, /device:TPU:1, one launch (start us, length us, event | category | flops | bytes accessed | tf_op | source)
XLA Modules:
  0.0 146.0 jit_solution(9828292942205431604)
XLA Ops:
  0.6 1.8 %convert_element_type.37 = bf16[1024,512]{1,0:T(8,128)(2,1)S(1)} convert(f32[1024,512]{1,0:T(8,128)} %param.17) | non-fusion elementwise | flops 524288 | bytes 3145728 | tf_op jit(solution)/shard_map/convert_element_type | solution.py:44
  2.4 0.8 copy.37
  3.2 0.1 reshape_squeeze.3
  3.3 2.8 %gather_fusion = bf16[32,128,512]{2,1,0:T(8,128)(2,1)} fusion(bf16[8,128,512]{2,1,0:T(8,128)(2,1)S(1)} %bitcast.63, s32[1024]{0:T(1024)S(1)} %pad_clamp_fusion), kind=kCustom, calls=%fused_computation | custom fusion | bytes 8388736 | tf_op jit(solution)/shard_map/gather | solution.py:73
  6.1 8.6 %all-to-all-start = ((bf16[16,256,512]{2,1,0:T(8,128)(2,1)}), bf16[16,256,512]{2,1,0:T(8,128)(2,1)}, u32[]{:S(2)}, u32[]{:S(2)}) async-start(bf16[16,256,512]{2,1,0:T(8,128)(2,1)} %bitcast.64), calls=%async_computation | async-start | bytes 8388608 | tf_op jit(solution)/shard_map/all_to_all | solution.py:75
  14.7 0.3 add_select_fusion
  15.0 0.2 copy.34
  15.2 1.0 copy.36
  16.3 0.2 copy.35
  16.5 2.1 %fusion.33 = f32[1024,512]{1,0:T(8,128)} fusion(bf16[1024,512]{1,0:T(8,128)(2,1)S(1)} %convert_element_type.37, bf16[512,512]{1,0:T(8,128)(2,1)S(1)} %copy-done), kind=kOutput, calls=%fused_computation.60 | convolution fusion | flops 536870912 | bytes 3670016 | tf_op jit(solution)/shard_map/dot_general | solution.py:78
  18.5 0.1 copy.38
  18.6 0.1 eq.102
  18.7 49.2 %while.10 = (s32[]{:T(128)}, bf16[4,256,4096]{2,1,0:T(8,128)(2,1)}, s32[4,256,80]{2,1,0:T(8,128)S(1)}, bf16[4,256,80]{2,1,0:T(8,128)(2,1)S(1)}, s32[4,256,80]{2,1,0:T(8,128)}, /*index=5*/s32[]{:T(128)}) while((s32[]{:T(128)}, bf16[4,256,4096]{2,1,0:T(8,128)(2,1)}, s32[4,256,80]{2,1,0:T(8,128)S(1)}, bf16[4,256,80]{2,1,0:T(8,128)(2,1)S(1)}, ...), condition=%wide.region_2.3_spmd, body=%wide.region_1.2_spmd.sunk | while | flops 173670400 | bytes 11100749 | solution.py:67
  18.7 0.9 dynamic-slice_bitcast_fusion.5
  19.7 7.0 %fusion.49 = bf16[256,16,256]{2,1,0:T(8,128)(2,1)} fusion(s32[256,80]{1,0:T(8,128)S(1)} %get-tuple-element.79, s32[256,80]{1,0:T(8,128)S(1)} %get-tuple-element.80, bf16[256,80]{1,0:T(8,128)(2,1)S(1)} %dynamic-slice_bitcast_fusion.6), kind=kOutput, calls=%fused_computation.2.clone.1 | convolution fusion | flops 173670400 | bytes 2301952 | tf_op jit(solution)/shard_map/while/body/eval_jaxpr/nkp,nkr->npr/dot_general | solution.py:63
  26.7 2.9 %broadcast_in_dim.112 = bf16[1,256,4096]{2,1,0:T(8,128)(2,1)S(1)} reshape(bf16[256,16,256]{2,1,0:T(8,128)(2,1)} %fusion.49) | data formatting | bytes 4194304 | tf_op jit(solution)/shard_map/while/body/jit(dynamic_update_index_in_dim)/broadcast_in_dim | solution.py:67
  29.6 1.5 %constant_dynamic-update-slice_fusion.2 = bf16[4,256,4096]{2,1,0:T(8,128)(2,1)} fusion(bf16[4,256,4096]{2,1,0:T(8,128)(2,1)} %get-tuple-element.88, bf16[1,256,4096]{2,1,0:T(8,128)(2,1)S(1)} %broadcast_in_dim.112, s32[]{:T(128)} %get-tuple-element.87), kind=kLoop, calls=%fused_computation.12.clone.1 | loop fusion | bytes 4194816 | tf_op jit(solution)/shard_map/while/body/jit(dynamic_update_index_in_dim)/dynamic_update_slice | solution.py:67
  31.1 0.9 dynamic-slice_bitcast_fusion.5
  32.0 7.0 %fusion.49 = bf16[256,16,256]{2,1,0:T(8,128)(2,1)} fusion(s32[256,80]{1,0:T(8,128)S(1)} %get-tuple-element.79, s32[256,80]{1,0:T(8,128)S(1)} %get-tuple-element.80, bf16[256,80]{1,0:T(8,128)(2,1)S(1)} %dynamic-slice_bitcast_fusion.6), kind=kOutput, calls=%fused_computation.2.clone.1 | convolution fusion | flops 173670400 | bytes 2301952 | tf_op jit(solution)/shard_map/while/body/eval_jaxpr/nkp,nkr->npr/dot_general | solution.py:63
  39.0 2.9 %broadcast_in_dim.112 = bf16[1,256,4096]{2,1,0:T(8,128)(2,1)S(1)} reshape(bf16[256,16,256]{2,1,0:T(8,128)(2,1)} %fusion.49) | data formatting | bytes 4194304 | tf_op jit(solution)/shard_map/while/body/jit(dynamic_update_index_in_dim)/broadcast_in_dim | solution.py:67
  41.9 1.5 constant_dynamic-update-slice_fusion.2
  43.3 0.9 dynamic-slice_bitcast_fusion.5
  44.3 7.0 %fusion.49 = bf16[256,16,256]{2,1,0:T(8,128)(2,1)} fusion(s32[256,80]{1,0:T(8,128)S(1)} %get-tuple-element.79, s32[256,80]{1,0:T(8,128)S(1)} %get-tuple-element.80, bf16[256,80]{1,0:T(8,128)(2,1)S(1)} %dynamic-slice_bitcast_fusion.6), kind=kOutput, calls=%fused_computation.2.clone.1 | convolution fusion | flops 173670400 | bytes 2301952 | tf_op jit(solution)/shard_map/while/body/eval_jaxpr/nkp,nkr->npr/dot_general | solution.py:63
  51.3 2.9 %broadcast_in_dim.112 = bf16[1,256,4096]{2,1,0:T(8,128)(2,1)S(1)} reshape(bf16[256,16,256]{2,1,0:T(8,128)(2,1)} %fusion.49) | data formatting | bytes 4194304 | tf_op jit(solution)/shard_map/while/body/jit(dynamic_update_index_in_dim)/broadcast_in_dim | solution.py:67
  54.2 1.5 constant_dynamic-update-slice_fusion.2
  55.6 0.9 dynamic-slice_bitcast_fusion.5
  56.6 7.0 %fusion.49 = bf16[256,16,256]{2,1,0:T(8,128)(2,1)} fusion(s32[256,80]{1,0:T(8,128)S(1)} %get-tuple-element.79, s32[256,80]{1,0:T(8,128)S(1)} %get-tuple-element.80, bf16[256,80]{1,0:T(8,128)(2,1)S(1)} %dynamic-slice_bitcast_fusion.6), kind=kOutput, calls=%fused_computation.2.clone.1 | convolution fusion | flops 173670400 | bytes 2301952 | tf_op jit(solution)/shard_map/while/body/eval_jaxpr/nkp,nkr->npr/dot_general | solution.py:63
  63.6 2.9 %broadcast_in_dim.112 = bf16[1,256,4096]{2,1,0:T(8,128)(2,1)S(1)} reshape(bf16[256,16,256]{2,1,0:T(8,128)(2,1)} %fusion.49) | data formatting | bytes 4194304 | tf_op jit(solution)/shard_map/while/body/jit(dynamic_update_index_in_dim)/broadcast_in_dim | solution.py:67
  66.4 1.5 %constant_dynamic-update-slice_fusion.2 = bf16[4,256,4096]{2,1,0:T(8,128)(2,1)} fusion(bf16[4,256,4096]{2,1,0:T(8,128)(2,1)} %get-tuple-element.88, bf16[1,256,4096]{2,1,0:T(8,128)(2,1)S(1)} %broadcast_in_dim.112, s32[]{:T(128)} %get-tuple-element.87), kind=kLoop, calls=%fused_computation.12.clone.1 | loop fusion | bytes 4194816 | tf_op jit(solution)/shard_map/while/body/jit(dynamic_update_index_in_dim)/dynamic_update_slice | solution.py:67
  67.9 8.2 %all-to-all-done = bf16[16,256,512]{2,1,0:T(8,128)(2,1)} async-done(((bf16[16,256,512]{2,1,0:T(8,128)(2,1)}), bf16[16,256,512]{2,1,0:T(8,128)(2,1)}, u32[]{:S(2)}, u32[]{:S(2)}) %all-to-all-start) | async-done | bytes 4194336 | tf_op jit(solution)/shard_map/all_to_all | solution.py:75
  76.2 10.4 %maximum_convert_fusion.1 = bf16[1024,512]{1,0:T(8,128)(2,1)S(1)} fusion(f32[1024,512]{1,0:T(8,128)} %fusion.33, bf16[512,512]{1,0:T(8,128)(2,1)} %param.25, f32[512]{0:T(512)S(1)} %copy-done.10, bf16[1024,4096]{1,0:T(8,128)(2,1)} %bitcast.73, bf16[4096,512]{1,0:T(8,128)(2,1)} %bitcast.10), kind=kOutput, calls=%fused_computation.26 | convolution fusion | flops 4834459648 | bytes 16254976 | tf_op jit(solution)/shard_map/dot_general | solution.py:79
  86.7 2.3 %fusion.15 = bf16[128,8,512]{2,1,0:T(8,128)(2,1)} fusion(bf16[1024,512]{1,0:T(8,128)(2,1)S(1)} %maximum_convert_fusion.1, s32[1024]{0:T(1024)S(1)} %eq.102), kind=kOutput, calls=%fused_computation.30 | convolution fusion | flops 1075314688 | bytes 2101248 | tf_op jit(solution)/shard_map/dot_general | solution.py:88
  89.0 15.1 %all-to-all-start.1 = ((bf16[128,8,512]{2,1,0:T(8,128)(2,1)}), bf16[128,8,512]{2,1,0:T(8,128)(2,1)}, u32[]{:S(2)}, u32[]{:S(2)}) async-start(bf16[128,8,512]{2,1,0:T(8,128)(2,1)} %fusion.15), calls=%async_computation.1 | async-start | bytes 2097152 | tf_op jit(solution)/shard_map/all_to_all | solution.py:92
  104.3 1.0 fusion.34
  105.3 17.1 %all-to-all-done.1 = bf16[128,8,512]{2,1,0:T(8,128)(2,1)} async-done(((bf16[128,8,512]{2,1,0:T(8,128)(2,1)}), bf16[128,8,512]{2,1,0:T(8,128)(2,1)}, u32[]{:S(2)}, u32[]{:S(2)}) %all-to-all-start.1) | async-done | bytes 1048608 | tf_op jit(solution)/shard_map/all_to_all | solution.py:92
  122.4 2.5 %fusion.10 = f32[4,256,512]{2,1,0:T(8,128)S(1)} fusion(s32[4,256]{1,0:T(4,128)S(1)} %copy-done.6, bf16[128,8,512]{2,1,0:T(8,128)(2,1)} %all-to-all-done.1), kind=kOutput, calls=%fused_computation.21 | convolution fusion | flops 1074790400 | bytes 3149824 | tf_op jit(solution)/shard_map/dot_general | solution.py:98
  125.0 0.4 select_reduce_fusion.2
  125.3 0.2 fusion.27
  125.6 2.0 %fusion.16 = f32[1,4,256]{2,0,1:T(1,128)S(1)} fusion(bf16[512,1,1]{0,1,2:T(2,128)(2,1)S(1)} %reshape.147, f32[4,256,512]{2,1,0:T(8,128)S(1)} %fusion.10, f32[512]{0:T(512)S(1)} %copy-done.11, f32[4,512]{1,0:T(4,128)S(1)} %fusion.27, f32[4,512]{1,0:T(4,128)S(1)} %bitcast.68, bf16[512,512]{1,0:T(8,128)(2,1)} %param.28), kind=kOutput, calls=%fused_computation.31 | convolution fusion | flops 541065216 | bytes 2644992 | tf_op jit(solution)/shard_map/smk,k->sm/dot_general | solution.py:108
  127.6 0.6 select_reduce_fusion.1
  128.2 0.7 all_to_all.14
  128.9 4.9 %all-to-all-start.2 = ((f32[128,1,8]{2,1,0:T(1,128)}), f32[128,1,8]{2,1,0:T(1,128)S(1)}, u32[]{:S(2)}, u32[]{:S(2)}) async-start(f32[128,1,8]{2,1,0:T(1,128)} %bitcast.18), calls=%async_computation.2 | async-start | bytes 131072 | tf_op jit(solution)/shard_map/all_to_all | solution.py:112
  133.8 0.7 divide_select_fusion
  134.5 9.0 %all-to-all-done.2 = f32[128,1,8]{2,1,0:T(1,128)S(1)} async-done(((f32[128,1,8]{2,1,0:T(1,128)}), f32[128,1,8]{2,1,0:T(1,128)S(1)}, u32[]{:S(2)}, u32[]{:S(2)}) %all-to-all-start.2) | async-done | bytes 4128 | tf_op jit(solution)/shard_map/all_to_all | solution.py:112
  143.5 0.5 broadcast.79
  144.0 0.8 reduce.3
  144.8 0.1 broadcast_in_dim.84
  144.9 1.1 select_reduce_fusion
  (42 shorter events, 0.4 us)
Async XLA Ops:
  0.6 15.8 %copy-start = (bf16[512,512]{1,0:T(8,128)(2,1)S(1)}, bf16[512,512]{1,0:T(8,128)(2,1)}, u32[]{:S(2)}) copy-start(bf16[512,512]{1,0:T(8,128)(2,1)} %param.24) | copy-start | bytes 1572868
  6.1 8.6 %copy-start.4 = (s32[1024,80]{0,1:T(8,128)S(1)}, s32[1024,80]{0,1:T(8,128)}, u32[]{:S(2)}) copy-start(s32[1024,80]{0,1:T(8,128)} %param.18) | copy-start | bytes 983044
  6.1 10.1 %copy-start.1 = (f32[1024,80]{0,1:T(8,128)S(1)}, f32[1024,80]{0,1:T(8,128)}, u32[]{:S(2)}) copy-start(f32[1024,80]{0,1:T(8,128)} %param.19) | copy-start | bytes 983044
  6.1 70.1 %all-to-all-start = ((bf16[16,256,512]{2,1,0:T(8,128)(2,1)}), bf16[16,256,512]{2,1,0:T(8,128)(2,1)}, u32[]{:S(2)}, u32[]{:S(2)}) async-start(bf16[16,256,512]{2,1,0:T(8,128)(2,1)} %bitcast.64), calls=%async_computation | async-start | bytes 8388608 | tf_op jit(solution)/shard_map/all_to_all | solution.py:75
  14.7 3.8 %copy-start.5 = (s32[1,128,8]{1,2,0:T(8,128)S(1)}, s32[1,128,8]{1,2,0:T(8,128)}, u32[]{:S(2)}) copy-start(s32[1,128,8]{1,2,0:T(8,128)} %param.21) | copy-start | bytes 12292
  18.7 57.5 %copy-start.10 = (f32[512]{0:T(512)S(1)}, f32[512]{0:T(512)}, u32[]{:S(2)}) copy-start(f32[512]{0:T(512)} %param.26) | copy-start | bytes 6148
  86.6 17.7 %copy-start.2 = (bf16[1024,512]{1,0:T(8,128)(2,1)}, bf16[1024,512]{1,0:T(8,128)(2,1)S(1)}, u32[]{:S(2)}) copy-start(bf16[1024,512]{1,0:T(8,128)(2,1)S(1)} %maximum_convert_fusion.1) | copy-start | bytes 3145732
  86.6 17.5 %copy-start.7 = (s32[4]{0:T(128)S(1)}, s32[4]{0:T(128)}, u32[]{:S(2)}) copy-start(s32[4]{0:T(128)} %param.23) | copy-start | bytes 52
  86.6 17.5 %copy-start.8 = (bf16[512]{0:T(512)(128)(2,1)S(1)}, bf16[512]{0:T(512)(128)(2,1)}, u32[]{:S(2)}) copy-start(bf16[512]{0:T(512)(128)(2,1)} %param.31) | copy-start | bytes 3076
  86.7 17.5 %copy-start.6 = (s32[4,256]{1,0:T(4,128)S(1)}, s32[4,256]{1,0:T(4,128)}, u32[]{:S(2)}) copy-start(s32[4,256]{1,0:T(4,128)} %param.22) | copy-start | bytes 12292
  86.7 17.5 %copy-start.9 = (bf16[512]{0:T(512)(128)(2,1)S(1)}, bf16[512]{0:T(512)(128)(2,1)}, u32[]{:S(2)}) copy-start(bf16[512]{0:T(512)(128)(2,1)} %param.27) | copy-start | bytes 3076
  89.0 33.4 %all-to-all-start.1 = ((bf16[128,8,512]{2,1,0:T(8,128)(2,1)}), bf16[128,8,512]{2,1,0:T(8,128)(2,1)}, u32[]{:S(2)}, u32[]{:S(2)}) async-start(bf16[128,8,512]{2,1,0:T(8,128)(2,1)} %fusion.15), calls=%async_computation.1 | async-start | bytes 2097152 | tf_op jit(solution)/shard_map/all_to_all | solution.py:92
  105.3 20.1 %copy-start.3 = (bf16[512,512]{1,0:T(8,128)(2,1)S(1)}, bf16[512,512]{1,0:T(8,128)(2,1)}, u32[]{:S(2)}) copy-start(bf16[512,512]{1,0:T(8,128)(2,1)} %param.29) | copy-start | bytes 1572868
  105.3 20.3 %copy-start.11 = (f32[512]{0:T(512)S(1)}, f32[512]{0:T(512)}, u32[]{:S(2)}) copy-start(f32[512]{0:T(512)} %param.30) | copy-start | bytes 6148
  128.9 14.6 %all-to-all-start.2 = ((f32[128,1,8]{2,1,0:T(1,128)}), f32[128,1,8]{2,1,0:T(1,128)S(1)}, u32[]{:S(2)}, u32[]{:S(2)}) async-start(f32[128,1,8]{2,1,0:T(1,128)} %bitcast.18), calls=%async_computation.2 | async-start | bytes 131072 | tf_op jit(solution)/shard_map/all_to_all | solution.py:112

commit v6 on v5

--- a/solution.py
+++ b/solution.py
@@ -84,18 +84,14 @@
     hidden_width = node_hidden.shape[1]
     slot_total = device_total * capacity
     send_flat = send_rows[0].reshape(slot_total)
-    send_chooser = select_matrix(send_flat, nodes, jnp.bfloat16)
-    outbound = jnp.dot(send_chooser, node_hidden, preferred_element_type=jnp.float32).astype(
-        jnp.bfloat16
-    )
+    outbound = node_hidden.at[send_flat].get(mode="promise_in_bounds")
     outbound = outbound.reshape(device_total, capacity, hidden_width)
     received = lax.all_to_all(outbound, ("grp", "shard"), split_axis=0, concat_axis=0, tiled=True)
     received_rows = received.reshape(slot_total, hidden_width)
     sub_count = members.shape[0]
     member_width = members.shape[1]
     member_flat = members.reshape(sub_count * member_width)
-    member_chooser = select_matrix(member_flat, slot_total, jnp.bfloat16)
-    member_rows = jnp.dot(member_chooser, received_rows, preferred_element_type=jnp.float32)
+    member_rows = received_rows.at[member_flat].get(mode="promise_in_bounds").astype(jnp.float32)
     member_rows = member_rows.reshape(sub_count, member_width, hidden_width)
     relative = member_rows - member_rows[:, :1, :]
     alive = jnp.arange(member_width, dtype=jnp.int32)[None, :] < sub_len[:, None]

time: 147 us -> 151 us (1.027)
  local copies, waits for them, and re-layouts: 27.7 us -> 36.8 us
  matrix products: 48.5 us -> 43.6 us
    gather x0 -> x2, local copies, waits for them, and re-layouts: none -> 9.01 us  [the longest x1 5.06 us: body(): outbound = node_hidden.at[send_flat].get(mode='promise_in_bounds')]
    dot_general x2 -> x0, matrix products: 4.85 us -> none  [the longest x1 2.52 us: body(): jnp.dot(member_chooser, received_rows, preferred_element_type=jnp.float32)]
  transfers between devices with their start and end apart: 3 -> 3, of which waited for: 3 -> 3; matrix products, arithmetic and copies ran while one was open for 38% -> 37% of each run, Pallas kernels for 0% -> 0%
where the time goes in v6:
time: 151 us; the launch traced here: 150 us
  matrix products  43.6 us (29%)
  local copies, waits for them, and re-layouts  36.8 us (24%)
  waiting for transfers between devices  34.6 us (23%)
  starting transfers between devices  28.2 us (19%)
  other arithmetic  5.85 us (4%)
    dot_general x4, matrix products, build_block(): jnp.einsum('nkp,nkr->npr', peer_hot, row_hot, preferred_element_type=jnp....  28 us
    all_to_all x1, waiting for transfers between devices, body(): lax.all_to_all(outbound, ('grp', 'shard'), split_axis=0, concat_axis=0, t...  17.4 us
    all_to_all x1, starting transfers between devices, body(): lax.all_to_all(outbound, ('grp', 'shard'), split_axis=0, concat_axis=0, t...  14.7 us
    broadcast_in_dim x4, local copies, waits for them, and re-layouts, body(): lax.map(build_block, (peer_part, row_part, coeff_blocks))  11.5 us
    dot_general x1, matrix products, body(): jnp.dot(gathered_sum.astype(jnp.bfloat16), w_nbr, preferred_element_type=...  10.4 us
    all_to_all x1, waiting for transfers between devices, body(): lax.all_to_all(slot_scores, ('grp', 'shard'), split_axis=0, concat_axis=0...  9 us
    all_to_all x1, starting transfers between devices, body(): lax.all_to_all(outgoing, 'shard', split_axis=0, concat_axis=0, tiled=True)  8.61 us
    all_to_all x1, waiting for transfers between devices, body(): lax.all_to_all(outgoing, 'shard', split_axis=0, concat_axis=0, tiled=True)  8.21 us
  transfers between devices with their start and end apart: 3, of which 3 were waited for; matrix products, arithmetic and copies ran while one was open for 37% of the time, Pallas kernels for 0%

profile of v6, /device:TPU:1, one launch (start us, length us, event | category | flops | bytes accessed | tf_op | source)
XLA Modules:
  0.0 150.1 jit_solution(11979412568214636673)
XLA Ops:
  0.6 1.8 %convert_element_type.39 = bf16[1024,512]{1,0:T(8,128)(2,1)S(1)} convert(f32[1024,512]{1,0:T(8,128)} %param.17) | non-fusion elementwise | flops 524288 | bytes 3145728 | tf_op jit(solution)/shard_map/convert_element_type | solution.py:44
  2.4 0.8 copy.39
  3.3 2.8 %gather_fusion = bf16[32,128,512]{2,1,0:T(8,128)(2,1)} fusion(bf16[8,128,512]{2,1,0:T(8,128)(2,1)S(1)} %bitcast.64, s32[1024]{0:T(1024)S(1)} %pad_clamp_fusion), kind=kCustom, calls=%fused_computation | custom fusion | bytes 8388736 | tf_op jit(solution)/shard_map/gather | solution.py:73
  6.1 8.6 %all-to-all-start = ((bf16[16,256,512]{2,1,0:T(8,128)(2,1)}), bf16[16,256,512]{2,1,0:T(8,128)(2,1)}, u32[]{:S(2)}, u32[]{:S(2)}) async-start(bf16[16,256,512]{2,1,0:T(8,128)(2,1)} %bitcast.65), calls=%async_computation | async-start | bytes 8388608 | tf_op jit(solution)/shard_map/all_to_all | solution.py:75
  14.7 0.3 add_select_fusion
  15.0 0.2 copy.36
  15.2 1.0 copy.38
  16.3 0.2 copy.37
  16.5 2.1 %fusion.26 = f32[1024,512]{1,0:T(8,128)} fusion(bf16[1024,512]{1,0:T(8,128)(2,1)S(1)} %convert_element_type.39, bf16[512,512]{1,0:T(8,128)(2,1)S(1)} %copy-done), kind=kOutput, calls=%fused_computation.58 | convolution fusion | flops 536870912 | bytes 3670016 | tf_op jit(solution)/shard_map/dot_general | solution.py:78
  18.5 0.1 copy.40
  18.6 0.1 reshape_squeeze.7
  18.8 49.2 %while.10 = (s32[]{:T(128)}, bf16[4,256,4096]{2,1,0:T(8,128)(2,1)}, s32[4,256,80]{2,1,0:T(8,128)S(1)}, bf16[4,256,80]{2,1,0:T(8,128)(2,1)S(1)}, s32[4,256,80]{2,1,0:T(8,128)}, /*index=5*/s32[]{:T(128)}) while((s32[]{:T(128)}, bf16[4,256,4096]{2,1,0:T(8,128)(2,1)}, s32[4,256,80]{2,1,0:T(8,128)S(1)}, bf16[4,256,80]{2,1,0:T(8,128)(2,1)S(1)}, ...), condition=%wide.region_2.3_spmd, body=%wide.region_1.2_spmd.sunk | while | flops 173670400 | bytes 11100749 | solution.py:67
  18.8 0.9 dynamic-slice_bitcast_fusion.5
  19.7 7.0 %fusion.41 = bf16[256,16,256]{2,1,0:T(8,128)(2,1)} fusion(s32[256,80]{1,0:T(8,128)S(1)} %get-tuple-element.79, s32[256,80]{1,0:T(8,128)S(1)} %get-tuple-element.80, bf16[256,80]{1,0:T(8,128)(2,1)S(1)} %dynamic-slice_bitcast_fusion.6), kind=kOutput, calls=%fused_computation.4.clone.1 | convolution fusion | flops 173670400 | bytes 2301952 | tf_op jit(solution)/shard_map/while/body/eval_jaxpr/nkp,nkr->npr/dot_general | solution.py:63
  26.7 2.9 %broadcast_in_dim.112 = bf16[1,256,4096]{2,1,0:T(8,128)(2,1)S(1)} reshape(bf16[256,16,256]{2,1,0:T(8,128)(2,1)} %fusion.41) | data formatting | bytes 4194304 | tf_op jit(solution)/shard_map/while/body/jit(dynamic_update_index_in_dim)/broadcast_in_dim | solution.py:67
  29.6 1.5 constant_dynamic-update-slice_fusion.2
  31.1 0.9 dynamic-slice_bitcast_fusion.5
  32.0 7.0 %fusion.41 = bf16[256,16,256]{2,1,0:T(8,128)(2,1)} fusion(s32[256,80]{1,0:T(8,128)S(1)} %get-tuple-element.79, s32[256,80]{1,0:T(8,128)S(1)} %get-tuple-element.80, bf16[256,80]{1,0:T(8,128)(2,1)S(1)} %dynamic-slice_bitcast_fusion.6), kind=kOutput, calls=%fused_computation.4.clone.1 | convolution fusion | flops 173670400 | bytes 2301952 | tf_op jit(solution)/shard_map/while/body/eval_jaxpr/nkp,nkr->npr/dot_general | solution.py:63
  39.0 2.9 %broadcast_in_dim.112 = bf16[1,256,4096]{2,1,0:T(8,128)(2,1)S(1)} reshape(bf16[256,16,256]{2,1,0:T(8,128)(2,1)} %fusion.41) | data formatting | bytes 4194304 | tf_op jit(solution)/shard_map/while/body/jit(dynamic_update_index_in_dim)/broadcast_in_dim | solution.py:67
  41.9 1.5 constant_dynamic-update-slice_fusion.2
  43.4 0.9 dynamic-slice_bitcast_fusion.5
  44.3 7.0 %fusion.41 = bf16[256,16,256]{2,1,0:T(8,128)(2,1)} fusion(s32[256,80]{1,0:T(8,128)S(1)} %get-tuple-element.79, s32[256,80]{1,0:T(8,128)S(1)} %get-tuple-element.80, bf16[256,80]{1,0:T(8,128)(2,1)S(1)} %dynamic-slice_bitcast_fusion.6), kind=kOutput, calls=%fused_computation.4.clone.1 | convolution fusion | flops 173670400 | bytes 2301952 | tf_op jit(solution)/shard_map/while/body/eval_jaxpr/nkp,nkr->npr/dot_general | solution.py:63
  51.3 2.9 %broadcast_in_dim.112 = bf16[1,256,4096]{2,1,0:T(8,128)(2,1)S(1)} reshape(bf16[256,16,256]{2,1,0:T(8,128)(2,1)} %fusion.41) | data formatting | bytes 4194304 | tf_op jit(solution)/shard_map/while/body/jit(dynamic_update_index_in_dim)/broadcast_in_dim | solution.py:67
  54.2 1.5 constant_dynamic-update-slice_fusion.2
  55.7 0.9 dynamic-slice_bitcast_fusion.5
  56.6 7.0 %fusion.41 = bf16[256,16,256]{2,1,0:T(8,128)(2,1)} fusion(s32[256,80]{1,0:T(8,128)S(1)} %get-tuple-element.79, s32[256,80]{1,0:T(8,128)S(1)} %get-tuple-element.80, bf16[256,80]{1,0:T(8,128)(2,1)S(1)} %dynamic-slice_bitcast_fusion.6), kind=kOutput, calls=%fused_computation.4.clone.1 | convolution fusion | flops 173670400 | bytes 2301952 | tf_op jit(solution)/shard_map/while/body/eval_jaxpr/nkp,nkr->npr/dot_general | solution.py:63
  63.6 2.9 %broadcast_in_dim.112 = bf16[1,256,4096]{2,1,0:T(8,128)(2,1)S(1)} reshape(bf16[256,16,256]{2,1,0:T(8,128)(2,1)} %fusion.41) | data formatting | bytes 4194304 | tf_op jit(solution)/shard_map/while/body/jit(dynamic_update_index_in_dim)/broadcast_in_dim | solution.py:67
  66.5 1.5 constant_dynamic-update-slice_fusion.2
  68.0 8.2 %all-to-all-done = bf16[16,256,512]{2,1,0:T(8,128)(2,1)} async-done(((bf16[16,256,512]{2,1,0:T(8,128)(2,1)}), bf16[16,256,512]{2,1,0:T(8,128)(2,1)}, u32[]{:S(2)}, u32[]{:S(2)}) %all-to-all-start) | async-done | bytes 4194336 | tf_op jit(solution)/shard_map/all_to_all | solution.py:75
  76.2 10.4 %maximum_convert_fusion.1 = bf16[1024,512]{1,0:T(8,128)(2,1)S(1)} fusion(f32[1024,512]{1,0:T(8,128)} %fusion.26, bf16[512,512]{1,0:T(8,128)(2,1)} %param.25, f32[512]{0:T(512)S(1)} %copy-done.10, bf16[1024,4096]{1,0:T(8,128)(2,1)} %bitcast.81, bf16[4096,512]{1,0:T(8,128)(2,1)} %bitcast.10), kind=kOutput, calls=%fused_computation.22 | convolution fusion | flops 4834459648 | bytes 16254976 | tf_op jit(solution)/shard_map/dot_general | solution.py:79
  86.7 5.1 %gather_fusion.1 = bf16[1024,512]{1,0:T(8,128)(2,1)} fusion(bf16[1024,512]{1,0:T(8,128)(2,1)S(1)} %maximum_convert_fusion.1, s32[1024]{0:T(1024)S(1)} %broadcast_clamp_fusion.1), kind=kCustom, calls=%fused_computation.1 | custom fusion | bytes 2101248 | tf_op jit(solution)/shard_map/gather | solution.py:87
  91.7 14.7 %all-to-all-start.1 = ((bf16[128,8,512]{2,1,0:T(8,128)(2,1)}), bf16[128,8,512]{2,1,0:T(8,128)(2,1)S(1)}, u32[]{:S(2)}, u32[]{:S(2)}) async-start(bf16[128,8,512]{2,1,0:T(8,128)(2,1)} %bitcast.68), calls=%async_computation.1 | async-start | bytes 2097152 | tf_op jit(solution)/shard_map/all_to_all | solution.py:89
  106.4 0.1 eq.62
  106.7 1.0 fusion.27
  107.7 17.4 %all-to-all-done.1 = bf16[128,8,512]{2,1,0:T(8,128)(2,1)S(1)} async-done(((bf16[128,8,512]{2,1,0:T(8,128)(2,1)}), bf16[128,8,512]{2,1,0:T(8,128)(2,1)S(1)}, u32[]{:S(2)}, u32[]{:S(2)}) %all-to-all-start.1) | async-done | bytes 1048608 | tf_op jit(solution)/shard_map/all_to_all | solution.py:89
  125.0 4.0 %gather_fusion.2 = bf16[1024,512]{1,0:T(8,128)(2,1)S(1)} fusion(bf16[1024,512]{1,0:T(8,128)(2,1)S(1)} %bitcast.63, s32[1024]{0:T(1024)S(1)} %broadcast_clamp_fusion), kind=kCustom, calls=%fused_computation.2 | custom fusion | bytes 2101248 | tf_op jit(solution)/shard_map/gather | solution.py:94
  129.0 0.4 select_reduce_fusion.2
  129.4 0.2 fusion.20
  129.6 2.0 %fusion.8 = f32[1,4,256]{2,0,1:T(1,128)S(1)} fusion(bf16[512,1,1]{0,1,2:T(2,128)(2,1)S(1)} %reshape.205, bf16[4,256,512]{2,1,0:T(8,128)(2,1)S(1)} %bitcast.67, f32[512]{0:T(512)S(1)} %copy-done.11, f32[4,512]{1,0:T(4,128)S(1)} %fusion.20, f32[4,512]{1,0:T(4,128)S(1)} %bitcast.72, bf16[512,512]{1,0:T(8,128)(2,1)} %param.28), kind=kOutput, calls=%fused_computation.25 | convolution fusion | flops 541589504 | bytes 1596416 | tf_op jit(solution)/shard_map/smk,k->sm/dot_general | solution.py:104
  131.7 0.6 select_reduce_fusion.1
  132.2 0.7 all_to_all.14
  132.9 4.9 %all-to-all-start.2 = ((f32[128,1,8]{2,1,0:T(1,128)}), f32[128,1,8]{2,1,0:T(1,128)S(1)}, u32[]{:S(2)}, u32[]{:S(2)}) async-start(f32[128,1,8]{2,1,0:T(1,128)} %bitcast.20), calls=%async_computation.2 | async-start | bytes 131072 | tf_op jit(solution)/shard_map/all_to_all | solution.py:108
  137.8 0.7 divide_select_fusion
  138.5 9.0 %all-to-all-done.2 = f32[128,1,8]{2,1,0:T(1,128)S(1)} async-done(((f32[128,1,8]{2,1,0:T(1,128)}), f32[128,1,8]{2,1,0:T(1,128)S(1)}, u32[]{:S(2)}, u32[]{:S(2)}) %all-to-all-start.2) | async-done | bytes 4128 | tf_op jit(solution)/shard_map/all_to_all | solution.py:108
  147.5 0.5 broadcast.108
  148.0 0.8 reduce.3
  148.8 0.1 broadcast_in_dim.84
  148.9 1.1 select_reduce_fusion
  (48 shorter events, 0.5 us)
Async XLA Ops:
  0.6 15.8 %copy-start = (bf16[512,512]{1,0:T(8,128)(2,1)S(1)}, bf16[512,512]{1,0:T(8,128)(2,1)}, u32[]{:S(2)}) copy-start(bf16[512,512]{1,0:T(8,128)(2,1)} %param.24) | copy-start | bytes 1572868
  6.1 8.6 %copy-start.4 = (s32[1024,80]{0,1:T(8,128)S(1)}, s32[1024,80]{0,1:T(8,128)}, u32[]{:S(2)}) copy-start(s32[1024,80]{0,1:T(8,128)} %param.18) | copy-start | bytes 983044
  6.1 10.1 %copy-start.2 = (f32[1024,80]{0,1:T(8,128)S(1)}, f32[1024,80]{0,1:T(8,128)}, u32[]{:S(2)}) copy-start(f32[1024,80]{0,1:T(8,128)} %param.19) | copy-start | bytes 983044
  6.1 70.1 %all-to-all-start = ((bf16[16,256,512]{2,1,0:T(8,128)(2,1)}), bf16[16,256,512]{2,1,0:T(8,128)(2,1)}, u32[]{:S(2)}, u32[]{:S(2)}) async-start(bf16[16,256,512]{2,1,0:T(8,128)(2,1)} %bitcast.65), calls=%async_computation | async-start | bytes 8388608 | tf_op jit(solution)/shard_map/all_to_all | solution.py:75
  14.7 3.8 %copy-start.6 = (s32[1,128,8]{1,2,0:T(8,128)S(1)}, s32[1,128,8]{1,2,0:T(8,128)}, u32[]{:S(2)}) copy-start(s32[1,128,8]{1,2,0:T(8,128)} %param.21) | copy-start | bytes 12292
  18.8 57.4 %copy-start.10 = (f32[512]{0:T(512)S(1)}, f32[512]{0:T(512)}, u32[]{:S(2)}) copy-start(f32[512]{0:T(512)} %param.26) | copy-start | bytes 6148
  86.6 20.1 %copy-start.1 = (bf16[1024,512]{1,0:T(8,128)(2,1)}, bf16[1024,512]{1,0:T(8,128)(2,1)S(1)}, u32[]{:S(2)}) copy-start(bf16[1024,512]{1,0:T(8,128)(2,1)S(1)} %maximum_convert_fusion.1) | copy-start | bytes 3145732
  86.6 19.9 %copy-start.5 = (s32[4,256]{1,0:T(4,128)S(1)}, s32[4,256]{1,0:T(4,128)}, u32[]{:S(2)}) copy-start(s32[4,256]{1,0:T(4,128)} %param.22) | copy-start | bytes 12292
  86.6 19.9 %copy-start.7 = (s32[4]{0:T(128)S(1)}, s32[4]{0:T(128)}, u32[]{:S(2)}) copy-start(s32[4]{0:T(128)} %param.23) | copy-start | bytes 52
  86.7 19.9 %copy-start.8 = (bf16[512]{0:T(512)(128)(2,1)S(1)}, bf16[512]{0:T(512)(128)(2,1)}, u32[]{:S(2)}) copy-start(bf16[512]{0:T(512)(128)(2,1)} %param.31) | copy-start | bytes 3076
  86.7 19.9 %copy-start.9 = (bf16[512]{0:T(512)(128)(2,1)S(1)}, bf16[512]{0:T(512)(128)(2,1)}, u32[]{:S(2)}) copy-start(bf16[512]{0:T(512)(128)(2,1)} %param.27) | copy-start | bytes 3076
  91.7 33.3 %all-to-all-start.1 = ((bf16[128,8,512]{2,1,0:T(8,128)(2,1)}), bf16[128,8,512]{2,1,0:T(8,128)(2,1)S(1)}, u32[]{:S(2)}, u32[]{:S(2)}) async-start(bf16[128,8,512]{2,1,0:T(8,128)(2,1)} %bitcast.68), calls=%async_computation.1 | async-start | bytes 2097152 | tf_op jit(solution)/shard_map/all_to_all | solution.py:89
  125.0 4.4 %copy-start.3 = (bf16[512,512]{1,0:T(8,128)(2,1)S(1)}, bf16[512,512]{1,0:T(8,128)(2,1)}, u32[]{:S(2)}) copy-start(bf16[512,512]{1,0:T(8,128)(2,1)} %param.29) | copy-start | bytes 1572868
  125.0 4.6 %copy-start.11 = (f32[512]{0:T(512)S(1)}, f32[512]{0:T(512)}, u32[]{:S(2)}) copy-start(f32[512]{0:T(512)} %param.30) | copy-start | bytes 6148
  132.9 14.6 %all-to-all-start.2 = ((f32[128,1,8]{2,1,0:T(1,128)}), f32[128,1,8]{2,1,0:T(1,128)S(1)}, u32[]{:S(2)}, u32[]{:S(2)}) async-start(f32[128,1,8]{2,1,0:T(1,128)} %bitcast.20), calls=%async_computation.2 | async-start | bytes 131072 | tf_op jit(solution)/shard_map/all_to_all | solution.py:108

commit v7 on v6

--- a/solution.py
+++ b/solution.py
@@ -3,9 +3,66 @@
 import jax
 import jax.numpy as jnp
 from jax import lax
+from jax.experimental import pallas as pl
+from jax.experimental.pallas import tpu as pltpu
 from jax.sharding import PartitionSpec as P
 
 TILE = 128
+
+
+def node_kernel(adj_ref, table_ref, embed_ref, w_self_ref, w_nbr_ref, bias_ref, send_ref, out_ref, outbound_ref, held_ref):
+    b = pl.program_id(0)
+    rows = out_ref.shape[0]
+    total = jnp.dot(adj_ref[...], table_ref[...], preferred_element_type=jnp.float32)
+    pre = (
+        jnp.dot(embed_ref[...], w_self_ref[...], preferred_element_type=jnp.float32)
+        + bias_ref[...]
+        + jnp.dot(total.astype(jnp.bfloat16), w_nbr_ref[...], preferred_element_type=jnp.float32)
+    )
+    hidden = jnp.maximum(pre, 0.0).astype(out_ref.dtype)
+    out_ref[...] = hidden
+    held_ref[pl.ds(pl.multiple_of(b * rows, rows), rows), :] = hidden
+
+    @pl.when(b == pl.num_programs(0) - 1)
+    def _():
+        nodes = held_ref.shape[0]
+        chooser = jnp.where(
+            send_ref[...] == lax.broadcasted_iota(jnp.int32, (send_ref.shape[0], nodes), 1), 1.0, 0.0
+        ).astype(jnp.bfloat16)
+        outbound_ref[...] = jnp.dot(chooser, held_ref[...], preferred_element_type=jnp.float32).astype(
+            outbound_ref.dtype
+        )
+
+
+def node_layer(adjacency, table, embed_bf, w_self, w_nbr, bias, send_flat):
+    nodes, width = embed_bf.shape
+    hidden = w_self.shape[1]
+    columns = adjacency.shape[1]
+    rows = 128
+    slots = send_flat.shape[0]
+    return pl.pallas_call(
+        node_kernel,
+        grid=(nodes // rows,),
+        in_specs=[
+            pl.BlockSpec((rows, columns), lambda b: (b, 0)),
+            pl.BlockSpec(table.shape, lambda b: (0, 0)),
+            pl.BlockSpec((rows, width), lambda b: (b, 0)),
+            pl.BlockSpec(w_self.shape, lambda b: (0, 0)),
+            pl.BlockSpec(w_nbr.shape, lambda b: (0, 0)),
+            pl.BlockSpec((1, hidden), lambda b: (0, 0)),
+            pl.BlockSpec((slots, 1), lambda b: (0, 0)),
+        ],
+        out_specs=[
+            pl.BlockSpec((rows, hidden), lambda b: (b, 0)),
+            pl.BlockSpec((slots, hidden), lambda b: (0, 0)),
+        ],
+        out_shape=[
+            jax.ShapeDtypeStruct((nodes, hidden), jnp.bfloat16),
+            jax.ShapeDtypeStruct((slots, hidden), jnp.bfloat16),
+        ],
+        scratch_shapes=[pltpu.VMEM((nodes, hidden), jnp.bfloat16)],
+        compiler_params=pltpu.CompilerParams(vmem_limit_bytes=48 * 1024 * 1024),
+    )(adjacency, table, embed_bf, w_self, w_nbr, bias.reshape(1, hidden), send_flat.reshape(slots, 1))
 
 
 def select_matrix(indices, count, dtype):
@@ -74,24 +131,21 @@
     outgoing = outgoing.reshape(shard_count, peer_span, width)
     provided = lax.all_to_all(outgoing, "shard", split_axis=0, concat_axis=0, tiled=True)
     provided = provided.reshape(column_total, width)
-    gathered_sum = jnp.dot(adjacency, provided, preferred_element_type=jnp.float32)
-    self_term = jnp.dot(embed_bf, w_self, preferred_element_type=jnp.float32) + bias_v
-    pre_act = self_term + jnp.dot(gathered_sum.astype(jnp.bfloat16), w_nbr, preferred_element_type=jnp.float32)
-    node_hidden = jax.nn.relu(pre_act).astype(jnp.bfloat16)
+    send_flat = send_rows[0].reshape(send_rows.shape[1] * send_rows.shape[2])
+    node_hidden, outbound = node_layer(adjacency, provided, embed_bf, w_self, w_nbr, bias_v, send_flat)
     confidence = jnp.dot(node_hidden, w_conf, preferred_element_type=jnp.float32)
     device_total = send_rows.shape[1]
     capacity = send_rows.shape[2]
     hidden_width = node_hidden.shape[1]
     slot_total = device_total * capacity
-    send_flat = send_rows[0].reshape(slot_total)
-    outbound = node_hidden.at[send_flat].get(mode="promise_in_bounds")
     outbound = outbound.reshape(device_total, capacity, hidden_width)
     received = lax.all_to_all(outbound, ("grp", "shard"), split_axis=0, concat_axis=0, tiled=True)
     received_rows = received.reshape(slot_total, hidden_width)
     sub_count = members.shape[0]
     member_width = members.shape[1]
     member_flat = members.reshape(sub_count * member_width)
-    member_rows = received_rows.at[member_flat].get(mode="promise_in_bounds").astype(jnp.float32)
+    member_chooser = select_matrix(member_flat, slot_total, jnp.bfloat16)
+    member_rows = jnp.dot(member_chooser, received_rows, preferred_element_type=jnp.float32)
     member_rows = member_rows.reshape(sub_count, member_width, hidden_width)
     relative = member_rows - member_rows[:, :1, :]
     alive = jnp.arange(member_width, dtype=jnp.int32)[None, :] < sub_len[:, None]

time: 151 us -> 148 us (0.980)
  Pallas kernels: 0 us -> 13.5 us
  waiting for transfers between devices: 34.6 us -> 24.8 us
  matrix products: 43.6 us -> 34.9 us
  local copies, waits for them, and re-layouts: 36.8 us -> 41 us
  starting transfers between devices: 28.2 us -> 25.7 us
    pallas_call x0 -> x1, Pallas kernels: none -> 13.5 us  [node_layer(): pl.pallas_call(node_kernel, grid=(nodes // rows,), in_specs=[pl.BlockSpec...]
    dot_general x2 -> x1, matrix products: 12.5 us -> 2.52 us  [body(): jnp.dot(member_chooser, received_rows, preferred_element_type=jnp.float32)]
    gather x2 -> x0, local copies, waits for them, and re-layouts: 9.01 us -> none  [the longest x1 5.06 us: body(): outbound = node_hidden.at[send_flat].get(mode='promise_in_bounds')]
    all_to_all x1, waiting for transfers between devices: 8.21 us -> 0.01 us  [body(): lax.all_to_all(outgoing, 'shard', split_axis=0, concat_axis=0, tiled=True)]
    dynamic_update_slice x4, local copies, waits for them, and re-layouts: 5.89 us -> 12.6 us  [body(): lax.map(build_block, (peer_part, row_part, coeff_blocks))]
    broadcast_in_dim x4, local copies, waits for them, and re-layouts: 11.5 us -> 16.8 us  [body(): lax.map(build_block, (peer_part, row_part, coeff_blocks))]
    all_to_all x1, starting transfers between devices: 14.7 us -> 12.2 us  [body(): lax.all_to_all(outbound, ('grp', 'shard'), split_axis=0, concat_axis=0, t...]
    all_to_all x1, waiting for transfers between devices: 17.4 us -> 15.8 us  [body(): lax.all_to_all(outbound, ('grp', 'shard'), split_axis=0, concat_axis=0, t...]
  transfers between devices with their start and end apart: 3 -> 3, of which waited for: 3 -> 2; matrix products, arithmetic and copies ran while one was open for 37% -> 46% of each run, Pallas kernels for 0% -> 0%
where the time goes in v7:
time: 148 us; the launch traced here: 147 us
  local copies, waits for them, and re-layouts  41 us (28%)
  matrix products  34.9 us (24%)
  starting transfers between devices  25.7 us (17%)
  waiting for transfers between devices  24.8 us (17%)
  Pallas kernels  13.5 us (9%)
  other arithmetic  5.84 us (4%)
    dot_general x4, matrix products, build_block(): jnp.einsum('nkp,nkr->npr', peer_hot, row_hot, preferred_element_type=jnp....  28 us
    broadcast_in_dim x4, local copies, waits for them, and re-layouts, body(): lax.map(build_block, (peer_part, row_part, coeff_blocks))  16.8 us
    all_to_all x1, waiting for transfers between devices, body(): lax.all_to_all(outbound, ('grp', 'shard'), split_axis=0, concat_axis=0, t...  15.8 us
    pallas_call x1, Pallas kernels, node_layer(): pl.pallas_call(node_kernel, grid=(nodes // rows,), in_specs=[pl.BlockSpec...  13.5 us
    dynamic_update_slice x4, local copies, waits for them, and re-layouts, body(): lax.map(build_block, (peer_part, row_part, coeff_blocks))  12.6 us
    all_to_all x1, starting transfers between devices, body(): lax.all_to_all(outbound, ('grp', 'shard'), split_axis=0, concat_axis=0, t...  12.2 us
    all_to_all x1, waiting for transfers between devices, body(): lax.all_to_all(slot_scores, ('grp', 'shard'), split_axis=0, concat_axis=0...  8.99 us
    all_to_all x1, starting transfers between devices, body(): lax.all_to_all(outgoing, 'shard', split_axis=0, concat_axis=0, tiled=True)  8.61 us
  transfers between devices with their start and end apart: 3, of which 2 were waited for; matrix products, arithmetic and copies ran while one was open for 46% of the time, Pallas kernels for 0%

profile of v7, /device:TPU:1, one launch (start us, length us, event | category | flops | bytes accessed | tf_op | source)
XLA Modules:
  0.0 146.6 jit_solution(6473547913611017140)
XLA Ops:
  0.6 1.8 %convert_element_type.29.embed_ref = bf16[1024,512]{1,0:T(8,128)(2,1)S(1)} convert(f32[1024,512]{1,0:T(8,128)} %param.17) | non-fusion elementwise | flops 524288 | bytes 3145728 | tf_op jit(solution)/shard_map/convert_element_type | solution.py:101
  2.4 0.8 copy.42
  3.2 0.1 reshape_squeeze.3
  3.3 2.8 %gather_fusion = bf16[32,128,512]{2,1,0:T(8,128)(2,1)} fusion(bf16[8,128,512]{2,1,0:T(8,128)(2,1)S(1)} %bitcast.57, s32[1024]{0:T(1024)S(1)} %pad_clamp_fusion), kind=kCustom, calls=%fused_computation | custom fusion | bytes 8388736 | tf_op jit(solution)/shard_map/gather | solution.py:130
  6.1 8.6 %all-to-all-start = ((bf16[16,256,512]{2,1,0:T(8,128)(2,1)}), bf16[16,256,512]{2,1,0:T(8,128)(2,1)}, u32[]{:S(2)}, u32[]{:S(2)}) async-start(bf16[16,256,512]{2,1,0:T(8,128)(2,1)} %bitcast.59), calls=%async_computation | async-start | bytes 8388608 | tf_op jit(solution)/shard_map/all_to_all | solution.py:132
  14.7 0.3 add_select_fusion
  15.0 1.0 copy.39
  16.0 1.0 copy.41
  17.1 0.2 copy.40
  17.3 0.1 copy.43
  17.4 0.2 reshape_reshape_squeeze.4.send_ref
  17.6 61.5 %while.10 = (s32[]{:T(128)}, bf16[4,256,4096]{2,1,0:T(8,128)(2,1)}, s32[4,256,80]{2,1,0:T(8,128)}, bf16[4,256,80]{2,1,0:T(8,128)(2,1)S(1)}, s32[4,256,80]{2,1,0:T(8,128)}, /*index=5*/s32[]{:T(128)}) while((s32[]{:T(128)}, bf16[4,256,4096]{2,1,0:T(8,128)(2,1)}, s32[4,256,80]{2,1,0:T(8,128)}, bf16[4,256,80]{2,1,0:T(8,128)(2,1)S(1)}, ...), condition=%wide.region_2.3_spmd, body=%wide.region_1.2_spmd.sunk | while | flops 173670400 | bytes 11100749 | solution.py:124
  17.6 1.1 dynamic-slice_bitcast_fusion.5
  18.7 7.0 %fusion.38 = bf16[256,16,256]{2,1,0:T(8,128)(2,1)} fusion(s32[256,80]{1,0:T(8,128)S(1)} %get-tuple-element.83, s32[256,80]{1,0:T(8,128)S(1)} %get-tuple-element.84, bf16[256,80]{1,0:T(8,128)(2,1)S(1)} %dynamic-slice_bitcast_fusion.6), kind=kOutput, calls=%fused_computation.2.clone.1 | convolution fusion | flops 173670400 | bytes 2301952 | tf_op jit(solution)/shard_map/while/body/eval_jaxpr/nkp,nkr->npr/dot_general | solution.py:120
  25.7 4.2 %broadcast_in_dim.110 = bf16[1,256,4096]{2,1,0:T(8,128)(2,1)} reshape(bf16[256,16,256]{2,1,0:T(8,128)(2,1)} %fusion.38) | data formatting | bytes 4194304 | tf_op jit(solution)/shard_map/while/body/jit(dynamic_update_index_in_dim)/broadcast_in_dim | solution.py:124
  29.9 3.2 %constant_dynamic-update-slice_fusion.2 = bf16[4,256,4096]{2,1,0:T(8,128)(2,1)} fusion(bf16[4,256,4096]{2,1,0:T(8,128)(2,1)} %get-tuple-element.92, bf16[1,256,4096]{2,1,0:T(8,128)(2,1)} %broadcast_in_dim.110, s32[]{:T(128)} %get-tuple-element.91), kind=kLoop, calls=%fused_computation.12.clone.1 | loop fusion | bytes 4194816 | tf_op jit(solution)/shard_map/while/body/jit(dynamic_update_index_in_dim)/dynamic_update_slice | solution.py:124
  33.0 1.0 dynamic-slice_bitcast_fusion.5
  34.0 7.0 %fusion.38 = bf16[256,16,256]{2,1,0:T(8,128)(2,1)} fusion(s32[256,80]{1,0:T(8,128)S(1)} %get-tuple-element.83, s32[256,80]{1,0:T(8,128)S(1)} %get-tuple-element.84, bf16[256,80]{1,0:T(8,128)(2,1)S(1)} %dynamic-slice_bitcast_fusion.6), kind=kOutput, calls=%fused_computation.2.clone.1 | convolution fusion | flops 173670400 | bytes 2301952 | tf_op jit(solution)/shard_map/while/body/eval_jaxpr/nkp,nkr->npr/dot_general | solution.py:120
  41.0 4.2 %broadcast_in_dim.110 = bf16[1,256,4096]{2,1,0:T(8,128)(2,1)} reshape(bf16[256,16,256]{2,1,0:T(8,128)(2,1)} %fusion.38) | data formatting | bytes 4194304 | tf_op jit(solution)/shard_map/while/body/jit(dynamic_update_index_in_dim)/broadcast_in_dim | solution.py:124
  45.2 3.1 %constant_dynamic-update-slice_fusion.2 = bf16[4,256,4096]{2,1,0:T(8,128)(2,1)} fusion(bf16[4,256,4096]{2,1,0:T(8,128)(2,1)} %get-tuple-element.92, bf16[1,256,4096]{2,1,0:T(8,128)(2,1)} %broadcast_in_dim.110, s32[]{:T(128)} %get-tuple-element.91), kind=kLoop, calls=%fused_computation.12.clone.1 | loop fusion | bytes 4194816 | tf_op jit(solution)/shard_map/while/body/jit(dynamic_update_index_in_dim)/dynamic_update_slice | solution.py:124
  48.3 1.0 dynamic-slice_bitcast_fusion.5
  49.4 7.0 %fusion.38 = bf16[256,16,256]{2,1,0:T(8,128)(2,1)} fusion(s32[256,80]{1,0:T(8,128)S(1)} %get-tuple-element.83, s32[256,80]{1,0:T(8,128)S(1)} %get-tuple-element.84, bf16[256,80]{1,0:T(8,128)(2,1)S(1)} %dynamic-slice_bitcast_fusion.6), kind=kOutput, calls=%fused_computation.2.clone.1 | convolution fusion | flops 173670400 | bytes 2301952 | tf_op jit(solution)/shard_map/while/body/eval_jaxpr/nkp,nkr->npr/dot_general | solution.py:120
  56.4 4.2 %broadcast_in_dim.110 = bf16[1,256,4096]{2,1,0:T(8,128)(2,1)} reshape(bf16[256,16,256]{2,1,0:T(8,128)(2,1)} %fusion.38) | data formatting | bytes 4194304 | tf_op jit(solution)/shard_map/while/body/jit(dynamic_update_index_in_dim)/broadcast_in_dim | solution.py:124
  60.5 3.1 %constant_dynamic-update-slice_fusion.2 = bf16[4,256,4096]{2,1,0:T(8,128)(2,1)} fusion(bf16[4,256,4096]{2,1,0:T(8,128)(2,1)} %get-tuple-element.92, bf16[1,256,4096]{2,1,0:T(8,128)(2,1)} %broadcast_in_dim.110, s32[]{:T(128)} %get-tuple-element.91), kind=kLoop, calls=%fused_computation.12.clone.1 | loop fusion | bytes 4194816 | tf_op jit(solution)/shard_map/while/body/jit(dynamic_update_index_in_dim)/dynamic_update_slice | solution.py:124
  63.7 1.0 dynamic-slice_bitcast_fusion.5
  64.7 7.0 %fusion.38 = bf16[256,16,256]{2,1,0:T(8,128)(2,1)} fusion(s32[256,80]{1,0:T(8,128)S(1)} %get-tuple-element.83, s32[256,80]{1,0:T(8,128)S(1)} %get-tuple-element.84, bf16[256,80]{1,0:T(8,128)(2,1)S(1)} %dynamic-slice_bitcast_fusion.6), kind=kOutput, calls=%fused_computation.2.clone.1 | convolution fusion | flops 173670400 | bytes 2301952 | tf_op jit(solution)/shard_map/while/body/eval_jaxpr/nkp,nkr->npr/dot_general | solution.py:120
  71.7 4.2 %broadcast_in_dim.110 = bf16[1,256,4096]{2,1,0:T(8,128)(2,1)} reshape(bf16[256,16,256]{2,1,0:T(8,128)(2,1)} %fusion.38) | data formatting | bytes 4194304 | tf_op jit(solution)/shard_map/while/body/jit(dynamic_update_index_in_dim)/broadcast_in_dim | solution.py:124
  75.9 3.2 %constant_dynamic-update-slice_fusion.2 = bf16[4,256,4096]{2,1,0:T(8,128)(2,1)} fusion(bf16[4,256,4096]{2,1,0:T(8,128)(2,1)} %get-tuple-element.92, bf16[1,256,4096]{2,1,0:T(8,128)(2,1)} %broadcast_in_dim.110, s32[]{:T(128)} %get-tuple-element.91), kind=kLoop, calls=%fused_computation.12.clone.1 | loop fusion | bytes 4194816 | tf_op jit(solution)/shard_map/while/body/jit(dynamic_update_index_in_dim)/dynamic_update_slice | solution.py:124
  79.1 13.5 %shard_map.174 = (bf16[1024,512]{1,0:T(8,128)(2,1)}, bf16[1024,512]{1,0:T(8,128)(2,1)}) custom-call(bf16[1024,4096]{1,0:T(8,128)(2,1)} %bitcast.60, bf16[4096,512]{1,0:T(8,128)(2,1)} %bitcast.10.table_ref, bf16[1024,512]{1,0:T(8,128)(2,1)S(1)} %convert_element_type.29.embed_ref, bf16[512,512]{1,0:T(8,128)(2,1)S(1)} %copy-done.1, ...), custom_call_target="tpu_custom_call" | custom-call | tf_op jit(solution)/shard_map/pallas_call | solution.py:43
  92.6 12.2 %all-to-all-start.1 = ((bf16[128,8,512]{2,1,0:T(8,128)(2,1)}), bf16[128,8,512]{2,1,0:T(8,128)(2,1)}, u32[]{:S(2)}, u32[]{:S(2)}) async-start(bf16[128,8,512]{2,1,0:T(8,128)(2,1)} %bitcast.14), calls=%async_computation.1 | async-start | bytes 2097152 | tf_op jit(solution)/shard_map/all_to_all | solution.py:142
  104.8 0.1 eq.95
  105.0 0.1 iota_compare_fusion.6
  105.1 2.2 %fusion.29 = f32[1,1024]{1,0:T(1,128)} fusion(bf16[1024,512]{1,0:T(8,128)(2,1)} %get-tuple-element.29, bf16[512,1]{0,1:T(2,128)(2,1)S(1)} %reshape.146), kind=kOutput, calls=%fused_computation.54 | convolution fusion | flops 1048576 | bytes 1053696 | tf_op jit(solution)/shard_map/dot_general | solution.py:136
  107.3 15.8 %all-to-all-done.1 = bf16[128,8,512]{2,1,0:T(8,128)(2,1)} async-done(((bf16[128,8,512]{2,1,0:T(8,128)(2,1)}), bf16[128,8,512]{2,1,0:T(8,128)(2,1)}, u32[]{:S(2)}, u32[]{:S(2)}) %all-to-all-start.1) | async-done | bytes 1048608 | tf_op jit(solution)/shard_map/all_to_all | solution.py:142
  123.1 2.5 %fusion.9 = f32[4,256,512]{2,1,0:T(8,128)S(1)} fusion(s32[4,256]{1,0:T(4,128)S(1)} %copy-done.7, bf16[128,8,512]{2,1,0:T(8,128)(2,1)} %all-to-all-done.1), kind=kOutput, calls=%fused_computation.20 | convolution fusion | flops 1074790400 | bytes 3149824 | tf_op jit(solution)/shard_map/dot_general | solution.py:148
  125.6 0.4 select_reduce_fusion.2
  126.0 0.2 fusion.23
  126.2 2.0 %fusion.12 = f32[1,4,256]{2,0,1:T(1,128)S(1)} fusion(bf16[512,1,1]{0,1,2:T(2,128)(2,1)S(1)} %reshape.150, f32[4,256,512]{2,1,0:T(8,128)S(1)} %fusion.9, f32[512]{0:T(512)S(1)} %copy-done.11, f32[4,512]{1,0:T(4,128)S(1)} %fusion.23, f32[4,512]{1,0:T(4,128)S(1)} %bitcast.65, bf16[512,512]{1,0:T(8,128)(2,1)} %param.28), kind=kOutput, calls=%fused_computation.25 | convolution fusion | flops 541065216 | bytes 2644992 | tf_op jit(solution)/shard_map/smk,k->sm/dot_general | solution.py:158
  128.2 0.1 fusion.34
  128.3 0.6 select_reduce_fusion.1
  128.9 0.7 all_to_all.14
  129.6 4.8 %all-to-all-start.2 = ((f32[128,1,8]{2,1,0:T(1,128)}), f32[128,1,8]{2,1,0:T(1,128)S(1)}, u32[]{:S(2)}, u32[]{:S(2)}) async-start(f32[128,1,8]{2,1,0:T(1,128)} %bitcast.19), calls=%async_computation.2 | async-start | bytes 131072 | tf_op jit(solution)/shard_map/all_to_all | solution.py:162
  134.4 0.7 divide_select_fusion
  135.1 9.0 %all-to-all-done.2 = f32[128,1,8]{2,1,0:T(1,128)S(1)} async-done(((f32[128,1,8]{2,1,0:T(1,128)}), f32[128,1,8]{2,1,0:T(1,128)S(1)}, u32[]{:S(2)}, u32[]{:S(2)}) %all-to-all-start.2) | async-done | bytes 4128 | tf_op jit(solution)/shard_map/all_to_all | solution.py:162
  144.0 0.5 broadcast.78
  144.6 0.8 reduce.3
  145.4 0.1 broadcast_in_dim.82
  145.5 1.1 select_reduce_fusion
  (41 shorter events, 0.2 us)
Async XLA Ops:
  0.6 125.4 %copy-start = (bf16[512,512]{1,0:T(8,128)(2,1)S(1)}, bf16[512,512]{1,0:T(8,128)(2,1)}, u32[]{:S(2)}) copy-start(bf16[512,512]{1,0:T(8,128)(2,1)} %param.29) | copy-start | bytes 1572868
  6.1 8.6 %copy-start.5 = (s32[1024,80]{0,1:T(8,128)S(1)}, s32[1024,80]{0,1:T(8,128)}, u32[]{:S(2)}) copy-start(s32[1024,80]{0,1:T(8,128)} %param.18) | copy-start | bytes 983044
  6.1 10.9 %copy-start.4 = (f32[1024,80]{0,1:T(8,128)S(1)}, f32[1024,80]{0,1:T(8,128)}, u32[]{:S(2)}) copy-start(f32[1024,80]{0,1:T(8,128)} %param.19) | copy-start | bytes 983044
  6.1 11.2 %copy-start.6 = (s32[1,128,8]{1,2,0:T(8,128)S(1)}, s32[1,128,8]{1,2,0:T(8,128)}, u32[]{:S(2)}) copy-start(s32[1,128,8]{1,2,0:T(8,128)} %param.21) | copy-start | bytes 12292
  6.1 73.0 %all-to-all-start = ((bf16[16,256,512]{2,1,0:T(8,128)(2,1)}), bf16[16,256,512]{2,1,0:T(8,128)(2,1)}, u32[]{:S(2)}, u32[]{:S(2)}) async-start(bf16[16,256,512]{2,1,0:T(8,128)(2,1)} %bitcast.59), calls=%async_computation | async-start | bytes 8388608 | tf_op jit(solution)/shard_map/all_to_all | solution.py:132
  17.5 61.5 %copy-start.1 = (bf16[512,512]{1,0:T(8,128)(2,1)S(1)}, bf16[512,512]{1,0:T(8,128)(2,1)}, u32[]{:S(2)}) copy-start(bf16[512,512]{1,0:T(8,128)(2,1)} %w_self_ref.1) | copy-start | bytes 1572868
  17.6 61.5 %copy-start.2 = (bf16[512,512]{1,0:T(8,128)(2,1)S(1)}, bf16[512,512]{1,0:T(8,128)(2,1)}, u32[]{:S(2)}) copy-start(bf16[512,512]{1,0:T(8,128)(2,1)} %w_nbr_ref.1) | copy-start | bytes 1572868
  17.6 61.5 %copy-start.3 = (f32[512]{0:T(512)S(1)}, f32[512]{0:T(512)}, u32[]{:S(2)}) copy-start(f32[512]{0:T(512)} %param.26) | copy-start | bytes 6148
  79.1 25.9 %copy-start.8 = (s32[4]{0:T(128)S(1)}, s32[4]{0:T(128)}, u32[]{:S(2)}) copy-start(s32[4]{0:T(128)} %param.23) | copy-start | bytes 52
  79.1 25.9 %copy-start.9 = (bf16[512]{0:T(512)(128)(2,1)S(1)}, bf16[512]{0:T(512)(128)(2,1)}, u32[]{:S(2)}) copy-start(bf16[512]{0:T(512)(128)(2,1)} %param.31) | copy-start | bytes 3076
  79.1 25.9 %copy-start.7 = (s32[4,256]{1,0:T(4,128)S(1)}, s32[4,256]{1,0:T(4,128)}, u32[]{:S(2)}) copy-start(s32[4,256]{1,0:T(4,128)} %param.22) | copy-start | bytes 12292
  79.1 25.9 %copy-start.10 = (bf16[512]{0:T(512)(128)(2,1)S(1)}, bf16[512]{0:T(512)(128)(2,1)}, u32[]{:S(2)}) copy-start(bf16[512]{0:T(512)(128)(2,1)} %param.27) | copy-start | bytes 3076
  92.6 30.5 %all-to-all-start.1 = ((bf16[128,8,512]{2,1,0:T(8,128)(2,1)}), bf16[128,8,512]{2,1,0:T(8,128)(2,1)}, u32[]{:S(2)}, u32[]{:S(2)}) async-start(bf16[128,8,512]{2,1,0:T(8,128)(2,1)} %bitcast.14), calls=%async_computation.1 | async-start | bytes 2097152 | tf_op jit(solution)/shard_map/all_to_all | solution.py:142
  107.3 19.0 %copy-start.11 = (f32[512]{0:T(512)S(1)}, f32[512]{0:T(512)}, u32[]{:S(2)}) copy-start(f32[512]{0:T(512)} %param.30) | copy-start | bytes 6148
  129.6 14.5 %all-to-all-start.2 = ((f32[128,1,8]{2,1,0:T(1,128)}), f32[128,1,8]{2,1,0:T(1,128)S(1)}, u32[]{:S(2)}, u32[]{:S(2)}) async-start(f32[128,1,8]{2,1,0:T(1,128)} %bitcast.19), calls=%async_computation.2 | async-start | bytes 131072 | tf_op jit(solution)/shard_map/all_to_all | solution.py:162

commit v8 on v7

--- a/solution.py
+++ b/solution.py
@@ -8,6 +8,55 @@
 from jax.sharding import PartitionSpec as P
 
 TILE = 128
+
+
+SUB = 8
+
+
+def adjacency_kernel(slot_ref, coef_ref, out_ref, acc_ref):
+    span = 256
+    peers = out_ref.shape[1] // span
+    sub_count = out_ref.shape[0] // SUB
+    width = slot_ref.shape[1]
+    row_hit = lax.broadcasted_iota(jnp.int32, (span, width), 0)
+    lane_node = lax.broadcasted_iota(jnp.int32, (peers * SUB, width), 1) // (width // SUB)
+    pair_row = lax.broadcasted_iota(jnp.int32, (peers * SUB, width), 0)
+    pair_peer = pair_row // SUB
+    pair_node = pair_row % SUB
+
+    def one_sub(s, carry):
+        slots = slot_ref[pl.ds(s, 1), :]
+        coefs = coef_ref[pl.ds(s, 1), :]
+        onehot = jnp.where(row_hit == slots % span, 1.0, 0.0).astype(jnp.bfloat16)
+        picked = (pair_peer == slots // span) & (pair_node == lane_node)
+        weights = jnp.where(picked, coefs, 0.0).astype(jnp.bfloat16)
+        block = lax.dot_general(
+            weights, onehot, (((1,), (1,)), ((), ())), preferred_element_type=jnp.float32
+        )
+        block = block.astype(jnp.bfloat16).astype(jnp.float32)
+        rows = pl.ds(pl.multiple_of(s * SUB, SUB), SUB)
+        for p in range(peers):
+            acc_ref[rows, p * span:(p + 1) * span] = block[p * SUB:(p + 1) * SUB, :]
+        return carry
+
+    lax.fori_loop(0, sub_count, one_sub, 0)
+    out_ref[...] = acc_ref[...].astype(out_ref.dtype)
+
+
+def build_adjacency(slot_rows, coef_rows, nodes, columns):
+    rows = 128
+    subs = rows // SUB
+    return pl.pallas_call(
+        adjacency_kernel,
+        grid=(nodes // rows,),
+        in_specs=[
+            pl.BlockSpec((subs, slot_rows.shape[1]), lambda b: (b, 0)),
+            pl.BlockSpec((subs, coef_rows.shape[1]), lambda b: (b, 0)),
+        ],
+        out_specs=pl.BlockSpec((rows, columns), lambda b: (b, 0)),
+        out_shape=jax.ShapeDtypeStruct((nodes, columns), jnp.bfloat16),
+        scratch_shapes=[pltpu.VMEM((rows, columns), jnp.float32)],
+    )(slot_rows, coef_rows)
 
 
 def node_kernel(adj_ref, table_ref, embed_ref, w_self_ref, w_nbr_ref, bias_ref, send_ref, out_ref, outbound_ref, held_ref):
@@ -101,29 +150,12 @@
     embed_bf = embed.astype(jnp.bfloat16)
     weight_sum = jnp.sum(knn_weight, axis=1, keepdims=True)
     coeff_bf = (knn_weight / weight_sum).astype(jnp.bfloat16)
-    block_rows = math.gcd(nodes, 256)
-    block_count = nodes // block_rows
-    peer_part = (knn_slot // peer_span).reshape(block_count, block_rows, neighbour_count)
-    row_part = (knn_slot % peer_span).reshape(block_count, block_rows, neighbour_count)
-    coeff_blocks = coeff_bf.reshape(block_count, block_rows, neighbour_count)
-
-    def build_block(pieces):
-        peer_block, row_block, coeff_block = pieces
-        peer_hot = jnp.where(
-            peer_block[:, :, None] == jnp.arange(shard_count, dtype=jnp.int32),
-            coeff_block[:, :, None],
-            jnp.zeros((), jnp.bfloat16),
-        )
-        row_hot = (row_block[:, :, None] == jnp.arange(peer_span, dtype=jnp.int32)).astype(
-            jnp.bfloat16
-        )
-        joined = jnp.einsum("nkp,nkr->npr", peer_hot, row_hot, preferred_element_type=jnp.float32)
-        return joined.reshape(block_rows, column_total)
-
-    adjacency = (
-        lax.map(build_block, (peer_part, row_part, coeff_blocks))
-        .reshape(nodes, column_total)
-        .astype(jnp.bfloat16)
+    sub_rows = nodes // SUB
+    adjacency = build_adjacency(
+        knn_slot.reshape(sub_rows, SUB * neighbour_count),
+        coeff_bf.astype(jnp.float32).reshape(sub_rows, SUB * neighbour_count),
+        nodes,
+        column_total,
     )
     tile_count = nodes // TILE
     embed_tiles = embed_bf.reshape(tile_count, TILE, width)

time: 148 us -> 147 us (level)
  Pallas kernels: 13.5 us -> 50.9 us
  local copies, waits for them, and re-layouts: 41 us -> 8.09 us
  matrix products: 34.9 us -> 4.61 us
  waiting for transfers between devices: 24.8 us -> 47.4 us
  starting transfers between devices: 25.7 us -> 28.6 us
    pallas_call x0 -> x1, Pallas kernels: none -> 37.5 us  [build_adjacency(): pl.pallas_call(adjacency_kernel, grid=(nodes // rows,), in_specs=[pl.Bloc...]
    dot_general x4 -> x0, matrix products: 28 us -> none  [build_block(): jnp.einsum('nkp,nkr->npr', peer_hot, row_hot, preferred_element_type=jnp....]
    all_to_all x1, waiting for transfers between devices: 0.01 us -> 21.3 us  [body(): lax.all_to_all(outgoing, 'shard', split_axis=0, concat_axis=0, tiled=True)]
    broadcast_in_dim x8 -> x0, local copies, waits for them, and re-layouts: 16.8 us -> none  [the longest x4 16.8 us: body(): lax.map(build_block, (peer_part, row_part, coeff_blocks))]
    dynamic_update_slice x4 -> x0, local copies, waits for them, and re-layouts: 12.6 us -> none  [body(): lax.map(build_block, (peer_part, row_part, coeff_blocks))]
    eq x4 -> x0, local copies, waits for them, and re-layouts: 4.03 us -> none  [build_block(): row_block[:, :, None] == jnp.arange(peer_span, dtype=jnp.int32)]
    all_to_all x1, starting transfers between devices: 12.2 us -> 15.1 us  [body(): lax.all_to_all(outbound, ('grp', 'shard'), split_axis=0, concat_axis=0, t...]
    reshape x0 -> x3, local copies, waits for them, and re-layouts: none -> 2.06 us  [the longest x2 1.14 us: body(): coeff_bf.astype(jnp.float32).reshape(sub_rows, SUB * neighbour_count)]
  transfers between devices with their start and end apart: 3 -> 3, of which waited for: 2 -> 3; matrix products, arithmetic and copies ran while one was open for 46% -> 3% of each run, Pallas kernels for 0% -> 26%
where the time goes in v8:
time: 147 us; the launch traced here: 146 us
  Pallas kernels  50.9 us (35%)
  waiting for transfers between devices  47.4 us (32%)
  starting transfers between devices  28.6 us (19%)
  local copies, waits for them, and re-layouts  8.09 us (6%)
  other arithmetic  5.52 us (4%)
  matrix products  4.61 us (3%)
    pallas_call x1, Pallas kernels, build_adjacency(): pl.pallas_call(adjacency_kernel, grid=(nodes // rows,), in_specs=[pl.Bloc...  37.5 us
    all_to_all x1, waiting for transfers between devices, body(): lax.all_to_all(outgoing, 'shard', split_axis=0, concat_axis=0, tiled=True)  21.3 us
    all_to_all x1, waiting for transfers between devices, body(): lax.all_to_all(outbound, ('grp', 'shard'), split_axis=0, concat_axis=0, t...  17 us
    all_to_all x1, starting transfers between devices, body(): lax.all_to_all(outbound, ('grp', 'shard'), split_axis=0, concat_axis=0, t...  15.1 us
    pallas_call x1, Pallas kernels, node_layer(): pl.pallas_call(node_kernel, grid=(nodes // rows,), in_specs=[pl.BlockSpec...  13.5 us
    all_to_all x1, waiting for transfers between devices, body(): lax.all_to_all(slot_scores, ('grp', 'shard'), split_axis=0, concat_axis=0...  9 us
    all_to_all x1, starting transfers between devices, body(): lax.all_to_all(outgoing, 'shard', split_axis=0, concat_axis=0, tiled=True)  8.61 us
    all_to_all x1, starting transfers between devices, body(): lax.all_to_all(slot_scores, ('grp', 'shard'), split_axis=0, concat_axis=0...  4.89 us
  transfers between devices with their start and end apart: 3, of which 3 were waited for; matrix products, arithmetic and copies ran while one was open for 3% of the time, Pallas kernels for 26%

profile of v8, /device:TPU:1, one launch (start us, length us, event | category | flops | bytes accessed | tf_op | source)
XLA Modules:
  0.0 146.1 jit_solution(16451910782368580796)
XLA Ops:
  0.6 0.0 copy-start
  0.6 0.8 copy.38
  1.5 0.1 reshape_squeeze.3
  1.6 1.7 %convert_element_type.22.embed_ref = bf16[1024,512]{1,0:T(8,128)(2,1)S(1)} convert(f32[1024,512]{1,0:T(8,128)} %param.15) | non-fusion elementwise | flops 524288 | bytes 3145728 | tf_op jit(solution)/shard_map/convert_element_type | solution.py:150
  3.3 2.8 %gather_fusion = bf16[32,128,512]{2,1,0:T(8,128)(2,1)} fusion(bf16[8,128,512]{2,1,0:T(8,128)(2,1)S(1)} %bitcast.43, s32[1024]{0:T(1024)S(1)} %pad_clamp_fusion), kind=kCustom, calls=%fused_computation | custom fusion | bytes 8388736 | tf_op jit(solution)/shard_map/gather | solution.py:162
  6.1 8.6 %all-to-all-start = ((bf16[16,256,512]{2,1,0:T(8,128)(2,1)}), bf16[16,256,512]{2,1,0:T(8,128)(2,1)}, u32[]{:S(2)}, u32[]{:S(2)}) async-start(bf16[16,256,512]{2,1,0:T(8,128)(2,1)} %bitcast.45), calls=%async_computation | async-start | bytes 8388608 | tf_op jit(solution)/shard_map/all_to_all | solution.py:164
  14.7 0.0 copy-done.7
  14.7 0.0 copy-start.6
  14.7 0.1 copy.39
  14.8 0.0 copy-done.4
  14.9 0.2 copy.37
  15.1 0.9 reshape.128.coef_ref
  16.0 0.2 reshape_reshape_squeeze.4.send_ref
  16.2 0.0 copy-done.6
  16.2 0.2 copy.36
  16.4 0.9 reshape.118.slot_ref
  17.4 37.5 %shard_map.174.adj_ref = bf16[1024,4096]{1,0:T(8,128)(2,1)} custom-call(s32[128,640]{1,0:T(8,128)} %reshape.118.slot_ref, f32[128,640]{1,0:T(8,128)} %reshape.128.coef_ref), custom_call_target="tpu_custom_call" | custom-call | tf_op jit(solution)/shard_map/pallas_call | solution.py:49
  54.8 21.3 %all-to-all-done = bf16[16,256,512]{2,1,0:T(8,128)(2,1)} async-done(((bf16[16,256,512]{2,1,0:T(8,128)(2,1)}), bf16[16,256,512]{2,1,0:T(8,128)(2,1)}, u32[]{:S(2)}, u32[]{:S(2)}) %all-to-all-start) | async-done | bytes 4194336 | tf_op jit(solution)/shard_map/all_to_all | solution.py:164
  76.2 0.0 copy-done.1
  76.2 0.0 copy-done.2
  76.2 0.0 copy-done.3
  76.2 13.5 %shard_map.175 = (bf16[1024,512]{1,0:T(8,128)(2,1)}, bf16[1024,512]{1,0:T(8,128)(2,1)}) custom-call(bf16[1024,4096]{1,0:T(8,128)(2,1)} %shard_map.174.adj_ref, bf16[4096,512]{1,0:T(8,128)(2,1)} %bitcast.3.table_ref, bf16[1024,512]{1,0:T(8,128)(2,1)S(1)} %convert_element_type.22.embed_ref, bf16[512,512]{1,0:T(8,128)(2,1)S(1)} %copy-done.1, ...), custom_call_target="tpu_custom_call" | custom-call | tf_op jit(solution)/shard_map/pallas_call | solution.py:92
  89.6 0.0 copy-start.11
  89.7 0.0 copy-start.8
  89.7 0.0 copy-start.5
  89.7 15.1 %all-to-all-start.1 = ((bf16[128,8,512]{2,1,0:T(8,128)(2,1)}), bf16[128,8,512]{2,1,0:T(8,128)(2,1)}, u32[]{:S(2)}, u32[]{:S(2)}) async-start(bf16[128,8,512]{2,1,0:T(8,128)(2,1)} %bitcast.7), calls=%async_computation.1 | async-start | bytes 2097152 | tf_op jit(solution)/shard_map/all_to_all | solution.py:174
  104.8 0.1 eq.63
  105.0 0.1 iota_compare_fusion.3
  105.1 1.0 fusion.20
  106.1 17.0 %all-to-all-done.1 = bf16[128,8,512]{2,1,0:T(8,128)(2,1)} async-done(((bf16[128,8,512]{2,1,0:T(8,128)(2,1)}), bf16[128,8,512]{2,1,0:T(8,128)(2,1)}, u32[]{:S(2)}, u32[]{:S(2)}) %all-to-all-start.1) | async-done | bytes 1048608 | tf_op jit(solution)/shard_map/all_to_all | solution.py:174
  123.1 2.5 %fusion.1 = f32[4,256,512]{2,1,0:T(8,128)S(1)} fusion(s32[4,256]{1,0:T(4,128)S(1)} %copy-done.8, bf16[128,8,512]{2,1,0:T(8,128)(2,1)} %all-to-all-done.1), kind=kOutput, calls=%fused_computation.7 | convolution fusion | flops 1074790400 | bytes 3149824 | tf_op jit(solution)/shard_map/dot_general | solution.py:180
  125.6 0.0 copy-start.12
  125.6 0.0 copy-start.13
  125.7 0.4 select_reduce_fusion.2
  126.1 0.2 fusion.14
  126.3 0.4 copy-done.12
  126.7 0.0 copy-done.13
  126.7 0.9 fusion.4
  127.6 0.1 fusion.25
  127.6 0.6 select_reduce_fusion.1
  128.2 0.7 all_to_all.14
  129.0 4.9 %all-to-all-start.2 = ((f32[128,1,8]{2,1,0:T(1,128)}), f32[128,1,8]{2,1,0:T(1,128)S(1)}, u32[]{:S(2)}, u32[]{:S(2)}) async-start(f32[128,1,8]{2,1,0:T(1,128)} %bitcast.12), calls=%async_computation.2 | async-start | bytes 131072 | tf_op jit(solution)/shard_map/all_to_all | solution.py:194
  133.9 0.7 divide_select_fusion
  134.5 9.0 %all-to-all-done.2 = f32[128,1,8]{2,1,0:T(1,128)S(1)} async-done(((f32[128,1,8]{2,1,0:T(1,128)}), f32[128,1,8]{2,1,0:T(1,128)S(1)}, u32[]{:S(2)}, u32[]{:S(2)}) %all-to-all-start.2) | async-done | bytes 4128 | tf_op jit(solution)/shard_map/all_to_all | solution.py:194
  143.5 0.5 broadcast.64
  144.0 0.8 reduce.3
  144.8 0.1 broadcast_in_dim.55
  144.9 1.1 select_reduce_fusion
  (24 shorter events, 0.1 us)
Async XLA Ops:
  0.6 125.4 %copy-start = (bf16[512,512]{1,0:T(8,128)(2,1)S(1)}, bf16[512,512]{1,0:T(8,128)(2,1)}, u32[]{:S(2)}) copy-start(bf16[512,512]{1,0:T(8,128)(2,1)} %param.27) | copy-start | bytes 1572868
  6.1 8.6 %copy-start.7 = (s32[1,128,8]{1,2,0:T(8,128)S(1)}, s32[1,128,8]{1,2,0:T(8,128)}, u32[]{:S(2)}) copy-start(s32[1,128,8]{1,2,0:T(8,128)} %param.19) | copy-start | bytes 12292
  6.1 8.7 %copy-start.4 = (f32[1024,80]{0,1:T(8,128)S(1)}, f32[1024,80]{0,1:T(8,128)}, u32[]{:S(2)}) copy-start(f32[1024,80]{0,1:T(8,128)} %param.17) | copy-start | bytes 983044
  6.1 70.1 %all-to-all-start = ((bf16[16,256,512]{2,1,0:T(8,128)(2,1)}), bf16[16,256,512]{2,1,0:T(8,128)(2,1)}, u32[]{:S(2)}, u32[]{:S(2)}) async-start(bf16[16,256,512]{2,1,0:T(8,128)(2,1)} %bitcast.45), calls=%async_computation | async-start | bytes 8388608 | tf_op jit(solution)/shard_map/all_to_all | solution.py:164
  14.7 1.5 %copy-start.6 = (s32[1024,80]{0,1:T(8,128)S(1)}, s32[1024,80]{0,1:T(8,128)}, u32[]{:S(2)}) copy-start(s32[1024,80]{0,1:T(8,128)} %param.16) | copy-start | bytes 983044
  17.4 58.8 %copy-start.1 = (bf16[512,512]{1,0:T(8,128)(2,1)S(1)}, bf16[512,512]{1,0:T(8,128)(2,1)}, u32[]{:S(2)}) copy-start(bf16[512,512]{1,0:T(8,128)(2,1)} %w_self_ref.1) | copy-start | bytes 1572868
  17.4 58.8 %copy-start.2 = (bf16[512,512]{1,0:T(8,128)(2,1)S(1)}, bf16[512,512]{1,0:T(8,128)(2,1)}, u32[]{:S(2)}) copy-start(bf16[512,512]{1,0:T(8,128)(2,1)} %w_nbr_ref.1) | copy-start | bytes 1572868
  17.4 58.8 %copy-start.3 = (f32[512]{0:T(512)S(1)}, f32[512]{0:T(512)}, u32[]{:S(2)}) copy-start(f32[512]{0:T(512)} %param.24) | copy-start | bytes 6148
  89.6 15.3 %copy-start.9 = (s32[4]{0:T(128)S(1)}, s32[4]{0:T(128)}, u32[]{:S(2)}) copy-start(s32[4]{0:T(128)} %param.21) | copy-start | bytes 52
  89.6 15.3 %copy-start.10 = (bf16[512]{0:T(512)(128)(2,1)S(1)}, bf16[512]{0:T(512)(128)(2,1)}, u32[]{:S(2)}) copy-start(bf16[512]{0:T(512)(128)(2,1)} %param.25) | copy-start | bytes 3076
  89.6 15.3 %copy-start.11 = (bf16[512]{0:T(512)(128)(2,1)S(1)}, bf16[512]{0:T(512)(128)(2,1)}, u32[]{:S(2)}) copy-start(bf16[512]{0:T(512)(128)(2,1)} %param.29) | copy-start | bytes 3076
  89.7 15.3 %copy-start.8 = (s32[4,256]{1,0:T(4,128)S(1)}, s32[4,256]{1,0:T(4,128)}, u32[]{:S(2)}) copy-start(s32[4,256]{1,0:T(4,128)} %param.20) | copy-start | bytes 12292
  89.7 15.4 %copy-start.5 = (bf16[1024,512]{1,0:T(8,128)(2,1)S(1)}, bf16[1024,512]{1,0:T(8,128)(2,1)}, u32[]{:S(2)}) copy-start(bf16[1024,512]{1,0:T(8,128)(2,1)} %get-tuple-element.2) | copy-start | bytes 3145732
  89.7 33.4 %all-to-all-start.1 = ((bf16[128,8,512]{2,1,0:T(8,128)(2,1)}), bf16[128,8,512]{2,1,0:T(8,128)(2,1)}, u32[]{:S(2)}, u32[]{:S(2)}) async-start(bf16[128,8,512]{2,1,0:T(8,128)(2,1)} %bitcast.7), calls=%async_computation.1 | async-start | bytes 2097152 | tf_op jit(solution)/shard_map/all_to_all | solution.py:174
  125.6 1.0 copy-start.12
  125.6 1.0 copy-start.13
  129.0 14.6 %all-to-all-start.2 = ((f32[128,1,8]{2,1,0:T(1,128)}), f32[128,1,8]{2,1,0:T(1,128)S(1)}, u32[]{:S(2)}, u32[]{:S(2)}) async-start(f32[128,1,8]{2,1,0:T(1,128)} %bitcast.12), calls=%async_computation.2 | async-start | bytes 131072 | tf_op jit(solution)/shard_map/all_to_all | solution.py:194

commit v9 on v8

--- a/solution.py
+++ b/solution.py
@@ -59,59 +59,29 @@
     )(slot_rows, coef_rows)
 
 
-def node_kernel(adj_ref, table_ref, embed_ref, w_self_ref, w_nbr_ref, bias_ref, send_ref, out_ref, outbound_ref, held_ref):
-    b = pl.program_id(0)
-    rows = out_ref.shape[0]
+def node_kernel(adj_ref, table_ref, self_ref, w_nbr_ref, out_ref):
     total = jnp.dot(adj_ref[...], table_ref[...], preferred_element_type=jnp.float32)
-    pre = (
-        jnp.dot(embed_ref[...], w_self_ref[...], preferred_element_type=jnp.float32)
-        + bias_ref[...]
-        + jnp.dot(total.astype(jnp.bfloat16), w_nbr_ref[...], preferred_element_type=jnp.float32)
-    )
-    hidden = jnp.maximum(pre, 0.0).astype(out_ref.dtype)
-    out_ref[...] = hidden
-    held_ref[pl.ds(pl.multiple_of(b * rows, rows), rows), :] = hidden
-
-    @pl.when(b == pl.num_programs(0) - 1)
-    def _():
-        nodes = held_ref.shape[0]
-        chooser = jnp.where(
-            send_ref[...] == lax.broadcasted_iota(jnp.int32, (send_ref.shape[0], nodes), 1), 1.0, 0.0
-        ).astype(jnp.bfloat16)
-        outbound_ref[...] = jnp.dot(chooser, held_ref[...], preferred_element_type=jnp.float32).astype(
-            outbound_ref.dtype
-        )
-
-
-def node_layer(adjacency, table, embed_bf, w_self, w_nbr, bias, send_flat):
-    nodes, width = embed_bf.shape
-    hidden = w_self.shape[1]
-    columns = adjacency.shape[1]
+    pre = self_ref[...] + jnp.dot(total.astype(jnp.bfloat16), w_nbr_ref[...], preferred_element_type=jnp.float32)
+    out_ref[...] = jnp.maximum(pre, 0.0).astype(out_ref.dtype)
+
+
+def node_layer(adjacency, table, self_term, w_nbr):
+    count, columns = adjacency.shape
+    hidden = w_nbr.shape[1]
     rows = 128
-    slots = send_flat.shape[0]
     return pl.pallas_call(
         node_kernel,
-        grid=(nodes // rows,),
+        grid=(count // rows,),
         in_specs=[
             pl.BlockSpec((rows, columns), lambda b: (b, 0)),
             pl.BlockSpec(table.shape, lambda b: (0, 0)),
-            pl.BlockSpec((rows, width), lambda b: (b, 0)),
-            pl.BlockSpec(w_self.shape, lambda b: (0, 0)),
+            pl.BlockSpec((rows, hidden), lambda b: (b, 0)),
             pl.BlockSpec(w_nbr.shape, lambda b: (0, 0)),
-            pl.BlockSpec((1, hidden), lambda b: (0, 0)),
-            pl.BlockSpec((slots, 1), lambda b: (0, 0)),
         ],
-        out_specs=[
-            pl.BlockSpec((rows, hidden), lambda b: (b, 0)),
-            pl.BlockSpec((slots, hidden), lambda b: (0, 0)),
-        ],
-        out_shape=[
-            jax.ShapeDtypeStruct((nodes, hidden), jnp.bfloat16),
-            jax.ShapeDtypeStruct((slots, hidden), jnp.bfloat16),
-        ],
-        scratch_shapes=[pltpu.VMEM((nodes, hidden), jnp.bfloat16)],
+        out_specs=pl.BlockSpec((rows, hidden), lambda b: (b, 0)),
+        out_shape=jax.ShapeDtypeStruct((count, hidden), jnp.bfloat16),
         compiler_params=pltpu.CompilerParams(vmem_limit_bytes=48 * 1024 * 1024),
-    )(adjacency, table, embed_bf, w_self, w_nbr, bias.reshape(1, hidden), send_flat.reshape(slots, 1))
+    )(adjacency, table, self_term, w_nbr)
 
 
 def select_matrix(indices, count, dtype):
@@ -164,7 +134,11 @@
     provided = lax.all_to_all(outgoing, "shard", split_axis=0, concat_axis=0, tiled=True)
     provided = provided.reshape(column_total, width)
     send_flat = send_rows[0].reshape(send_rows.shape[1] * send_rows.shape[2])
-    node_hidden, outbound = node_layer(adjacency, provided, embed_bf, w_self, w_nbr, bias_v, send_flat)
+    self_term = jnp.dot(embed_bf, w_self, preferred_element_type=jnp.float32) + bias_v
+    send_adjacency = adjacency.at[send_flat].get(mode="promise_in_bounds")
+    send_self = self_term.at[send_flat].get(mode="promise_in_bounds")
+    outbound = node_layer(send_adjacency, provided, send_self, w_nbr)
+    node_hidden = node_layer(adjacency, provided, self_term, w_nbr)
     confidence = jnp.dot(node_hidden, w_conf, preferred_element_type=jnp.float32)
     device_total = send_rows.shape[1]
     capacity = send_rows.shape[2]

time: 147 us -> 150 us (1.020)
  waiting for transfers between devices: 47.4 us -> 13 us
  local copies, waits for them, and re-layouts: 8.09 us -> 35.4 us
  Pallas kernels: 50.9 us -> 60 us
  matrix products: 4.61 us -> 8.82 us
  starting transfers between devices: 28.6 us -> 25 us
    gather x0 -> x2, local copies, waits for them, and re-layouts: none -> 24.5 us  [the longest x1 19.6 us: body(): send_adjacency = adjacency.at[send_flat].get(mode='promise_in_bounds')]
    all_to_all x1, waiting for transfers between devices: 21.3 us -> 0.01 us  [body(): lax.all_to_all(outgoing, 'shard', split_axis=0, concat_axis=0, tiled=True)]
    all_to_all x1, waiting for transfers between devices: 17 us -> 4.09 us  [body(): lax.all_to_all(outbound, ('grp', 'shard'), split_axis=0, concat_axis=0, t...]
    pallas_call x1 -> x2, Pallas kernels: 13.5 us -> 22.6 us  [node_layer(): pl.pallas_call(node_kernel, grid=(count // rows,), in_specs=[pl.BlockSpec...]
    all_to_all x1, starting transfers between devices: 15.1 us -> 10.7 us  [body(): lax.all_to_all(outbound, ('grp', 'shard'), split_axis=0, concat_axis=0, t...]
    unnamed x36 -> x38, local copies, waits for them, and re-layouts: 1.6 us -> 4.36 us
    dot_general x0 -> x1, matrix products: none -> 1.92 us  [body(): jnp.dot(embed_bf, w_self, preferred_element_type=jnp.float32) + bias_v]
  transfers between devices with their start and end apart: 3 -> 3, of which waited for: 3 -> 2; matrix products, arithmetic and copies ran while one was open for 3% -> 22% of each run, Pallas kernels for 26% -> 33%
where the time goes in v9:
time: 150 us; the launch traced here: 149 us
  Pallas kernels  60 us (40%)
  local copies, waits for them, and re-layouts  35.4 us (24%)
  starting transfers between devices  25 us (17%)
  waiting for transfers between devices  13 us (9%)
  matrix products  8.82 us (6%)
  other arithmetic  5.52 us (4%)
    pallas_call x1, Pallas kernels, build_adjacency(): pl.pallas_call(adjacency_kernel, grid=(nodes // rows,), in_specs=[pl.Bloc...  37.4 us
    pallas_call x2, Pallas kernels, node_layer(): pl.pallas_call(node_kernel, grid=(count // rows,), in_specs=[pl.BlockSpec...  22.6 us
    gather x1, local copies, waits for them, and re-layouts, body(): send_adjacency = adjacency.at[send_flat].get(mode='promise_in_bounds')  19.6 us
    all_to_all x1, starting transfers between devices, body(): lax.all_to_all(outbound, ('grp', 'shard'), split_axis=0, concat_axis=0, t...  10.7 us
    all_to_all x1, waiting for transfers between devices, body(): lax.all_to_all(slot_scores, ('grp', 'shard'), split_axis=0, concat_axis=0...  8.87 us
    all_to_all x1, starting transfers between devices, body(): lax.all_to_all(outgoing, 'shard', split_axis=0, concat_axis=0, tiled=True)  8.61 us
    all_to_all x1, starting transfers between devices, body(): lax.all_to_all(slot_scores, ('grp', 'shard'), split_axis=0, concat_axis=0...  5.68 us
    gather x1, local copies, waits for them, and re-layouts, body(): send_self = self_term.at[send_flat].get(mode='promise_in_bounds')  4.91 us
  transfers between devices with their start and end apart: 3, of which 2 were waited for; matrix products, arithmetic and copies ran while one was open for 22% of the time, Pallas kernels for 33%

profile of v9, /device:TPU:1, one launch (start us, length us, event | category | flops | bytes accessed | tf_op | source)
XLA Modules:
  0.0 148.6 jit_solution(14595469202491663815)
XLA Ops:
  0.6 0.0 copy-start
  0.6 0.8 copy.35
  1.5 0.1 reshape_squeeze.6
  1.6 1.7 %convert_element_type.22 = bf16[1024,512]{1,0:T(8,128)(2,1)S(1)} convert(f32[1024,512]{1,0:T(8,128)} %param.15) | non-fusion elementwise | flops 524288 | bytes 3145728 | tf_op jit(solution)/shard_map/convert_element_type | solution.py:120
  3.3 0.0 copy-start.4
  3.3 2.8 %gather_fusion = bf16[32,128,512]{2,1,0:T(8,128)(2,1)} fusion(bf16[8,128,512]{2,1,0:T(8,128)(2,1)S(1)} %bitcast.46, s32[1024]{0:T(1024)S(1)} %pad_clamp_fusion), kind=kCustom, calls=%fused_computation | custom fusion | bytes 8388736 | tf_op jit(solution)/shard_map/gather | solution.py:132
  6.1 8.6 %all-to-all-start = ((bf16[16,256,512]{2,1,0:T(8,128)(2,1)}), bf16[16,256,512]{2,1,0:T(8,128)(2,1)}, u32[]{:S(2)}, u32[]{:S(2)}) async-start(bf16[16,256,512]{2,1,0:T(8,128)(2,1)} %bitcast.47), calls=%async_computation | async-start | bytes 8388608 | tf_op jit(solution)/shard_map/all_to_all | solution.py:134
  14.7 0.0 copy-start.7
  14.7 0.1 copy.36
  14.9 0.1 reshape_squeeze.7
  15.0 0.0 copy-done.5
  15.0 0.0 copy-start.13
  15.0 0.2 copy.34
  15.2 0.9 reshape.153.coef_ref
  16.2 0.2 copy.33
  16.4 1.0 reshape.144.slot_ref
  17.4 0.0 copy-done
  17.4 1.9 %convolution_add_fusion.self_ref = f32[1024,512]{1,0:T(8,128)S(1)} fusion(bf16[1024,512]{1,0:T(8,128)(2,1)} %copy-done.4, bf16[512,512]{1,0:T(8,128)(2,1)S(1)} %copy-done, f32[512]{0:T(512)S(1)} %copy-done.13), kind=kOutput, calls=%fused_computation.14 | convolution fusion | flops 537395200 | bytes 3672064 | tf_op jit(solution)/shard_map/dot_general | solution.py:137
  19.3 4.9 %gather_fusion.2 = f32[1024,512]{1,0:T(8,128)} fusion(f32[1024,512]{1,0:T(8,128)S(1)} %convolution_add_fusion.self_ref, s32[1024]{0:T(1024)S(1)} %broadcast_clamp_fusion), kind=kCustom, calls=%fused_computation.2 | custom fusion | bytes 4198400 | tf_op jit(solution)/shard_map/gather | solution.py:139
  24.3 37.4 %shard_map.174.adj_ref = bf16[1024,4096]{1,0:T(8,128)(2,1)} custom-call(s32[128,640]{1,0:T(8,128)} %reshape.144.slot_ref, f32[128,640]{1,0:T(8,128)} %reshape.153.coef_ref), custom_call_target="tpu_custom_call" | custom-call | tf_op jit(solution)/shard_map/pallas_call | solution.py:49
  61.7 19.6 %gather_fusion.1 = bf16[1024,4096]{1,0:T(8,128)(2,1)} fusion(bf16[1024,4096]{1,0:T(8,128)(2,1)} %shard_map.174.adj_ref, s32[1024]{0:T(1024)S(1)} %broadcast_clamp_fusion), kind=kCustom, calls=%fused_computation.1 | custom fusion | bytes 16781312 | tf_op jit(solution)/shard_map/gather | solution.py:138
  81.2 0.0 all-to-all-done
  81.3 1.6 %copy-done.1 = f32[1024,512]{1,0:T(8,128)S(1)} copy-done((f32[1024,512]{1,0:T(8,128)S(1)}, f32[1024,512]{1,0:T(8,128)}, u32[]{:S(2)}) %copy-start.1) | copy-done | bytes 2097176
  82.8 10.9 %shard_map.176 = bf16[1024,512]{1,0:T(8,128)(2,1)S(1)} custom-call(bf16[1024,4096]{1,0:T(8,128)(2,1)} %gather_fusion.1, bf16[4096,512]{1,0:T(8,128)(2,1)} %bitcast.3.table_ref, f32[1024,512]{1,0:T(8,128)S(1)} %copy-done.1, bf16[512,512]{1,0:T(8,128)(2,1)S(1)} %copy-done.3), custom_call_target="tpu_custom_call" | custom-call | tf_op jit(solution)/shard_map/pallas_call | solution.py:72
  93.8 1.0 copy-done.2
  94.7 10.7 %all-to-all-start.1 = ((bf16[128,8,512]{2,1,0:T(8,128)(2,1)}), bf16[128,8,512]{2,1,0:T(8,128)(2,1)}, u32[]{:S(2)}, u32[]{:S(2)}) async-start(bf16[128,8,512]{2,1,0:T(8,128)(2,1)} %bitcast.45), calls=%async_computation.1 | async-start | bytes 2097152 | tf_op jit(solution)/shard_map/all_to_all | solution.py:148
  105.4 0.1 eq.63
  105.6 0.1 iota_compare_fusion.3
  105.7 11.7 %shard_map.175 = bf16[1024,512]{1,0:T(8,128)(2,1)} custom-call(bf16[1024,4096]{1,0:T(8,128)(2,1)} %shard_map.174.adj_ref, bf16[4096,512]{1,0:T(8,128)(2,1)} %bitcast.3.table_ref, f32[1024,512]{1,0:T(8,128)S(1)} %convolution_add_fusion.self_ref, bf16[512,512]{1,0:T(8,128)(2,1)S(1)} %copy-done.3), custom_call_target="tpu_custom_call" | custom-call | tf_op jit(solution)/shard_map/pallas_call | solution.py:72
  117.4 2.2 %fusion.20 = f32[1,1024]{1,0:T(1,128)} fusion(bf16[1024,512]{1,0:T(8,128)(2,1)} %shard_map.175, bf16[512,1]{0,1:T(2,128)(2,1)S(1)} %reshape.178), kind=kOutput, calls=%fused_computation.39 | convolution fusion | flops 1048576 | bytes 1053696 | tf_op jit(solution)/shard_map/dot_general | solution.py:142
  119.6 4.1 %all-to-all-done.1 = bf16[128,8,512]{2,1,0:T(8,128)(2,1)} async-done(((bf16[128,8,512]{2,1,0:T(8,128)(2,1)}), bf16[128,8,512]{2,1,0:T(8,128)(2,1)}, u32[]{:S(2)}, u32[]{:S(2)}) %all-to-all-start.1) | async-done | bytes 1048608 | tf_op jit(solution)/shard_map/all_to_all | solution.py:148
  123.7 2.5 %fusion.1 = f32[4,256,512]{2,1,0:T(8,128)S(1)} fusion(s32[4,256]{1,0:T(4,128)S(1)} %copy-done.9, bf16[128,8,512]{2,1,0:T(8,128)(2,1)} %all-to-all-done.1), kind=kOutput, calls=%fused_computation.9 | convolution fusion | flops 1074790400 | bytes 3149824 | tf_op jit(solution)/shard_map/dot_general | solution.py:154
  126.2 0.0 copy-start.6
  126.3 0.0 copy-start.14
  126.3 0.4 select_reduce_fusion.2
  126.7 0.6 copy-done.6
  127.3 0.2 fusion.14
  127.5 2.0 %fusion.4 = f32[1,4,256]{2,0,1:T(1,128)S(1)} fusion(bf16[512,1,1]{0,1,2:T(2,128)(2,1)S(1)} %reshape.182, f32[4,256,512]{2,1,0:T(8,128)S(1)} %fusion.1, f32[512]{0:T(512)S(1)} %copy-done.14, f32[4,512]{1,0:T(4,128)S(1)} %fusion.14, f32[4,512]{1,0:T(4,128)S(1)} %bitcast.49, bf16[512,512]{1,0:T(8,128)(2,1)} %param.26), kind=kOutput, calls=%fused_computation.15 | convolution fusion | flops 541065216 | bytes 2644992 | tf_op jit(solution)/shard_map/smk,k->sm/dot_general | solution.py:164
  129.5 0.1 fusion.27
  129.5 0.6 select_reduce_fusion.1
  130.1 0.7 all_to_all.14
  130.8 5.7 %all-to-all-start.2 = ((f32[128,1,8]{2,1,0:T(1,128)}), f32[128,1,8]{2,1,0:T(1,128)S(1)}, u32[]{:S(2)}, u32[]{:S(2)}) async-start(f32[128,1,8]{2,1,0:T(1,128)} %bitcast.12), calls=%async_computation.2 | async-start | bytes 131072 | tf_op jit(solution)/shard_map/all_to_all | solution.py:168
  136.5 0.7 divide_select_fusion
  137.2 8.9 %all-to-all-done.2 = f32[128,1,8]{2,1,0:T(1,128)S(1)} async-done(((f32[128,1,8]{2,1,0:T(1,128)}), f32[128,1,8]{2,1,0:T(1,128)S(1)}, u32[]{:S(2)}, u32[]{:S(2)}) %all-to-all-start.2) | async-done | bytes 4128 | tf_op jit(solution)/shard_map/all_to_all | solution.py:168
  146.1 0.5 broadcast.95
  146.6 0.8 reduce.3
  147.4 0.1 broadcast_in_dim.58
  147.5 1.1 select_reduce_fusion
  (32 shorter events, 0.2 us)
Async XLA Ops:
  0.6 16.8 %copy-start = (bf16[512,512]{1,0:T(8,128)(2,1)S(1)}, bf16[512,512]{1,0:T(8,128)(2,1)}, u32[]{:S(2)}) copy-start(bf16[512,512]{1,0:T(8,128)(2,1)} %param.22) | copy-start | bytes 1572868
  3.3 2.8 %copy-start.4 = (bf16[1024,512]{1,0:T(8,128)(2,1)}, bf16[1024,512]{1,0:T(8,128)(2,1)S(1)}, u32[]{:S(2)}) copy-start(bf16[1024,512]{1,0:T(8,128)(2,1)S(1)} %convert_element_type.22) | copy-start | bytes 3145732
  6.1 8.6 %copy-start.8 = (s32[1,128,8]{1,2,0:T(8,128)S(1)}, s32[1,128,8]{1,2,0:T(8,128)}, u32[]{:S(2)}) copy-start(s32[1,128,8]{1,2,0:T(8,128)} %param.19) | copy-start | bytes 12292
  6.1 8.8 %copy-start.5 = (f32[1024,80]{0,1:T(8,128)S(1)}, f32[1024,80]{0,1:T(8,128)}, u32[]{:S(2)}) copy-start(f32[1024,80]{0,1:T(8,128)} %param.17) | copy-start | bytes 983044
  6.1 75.1 %all-to-all-start = ((bf16[16,256,512]{2,1,0:T(8,128)(2,1)}), bf16[16,256,512]{2,1,0:T(8,128)(2,1)}, u32[]{:S(2)}, u32[]{:S(2)}) async-start(bf16[16,256,512]{2,1,0:T(8,128)(2,1)} %bitcast.47), calls=%async_computation | async-start | bytes 8388608 | tf_op jit(solution)/shard_map/all_to_all | solution.py:134
  14.7 1.5 copy-start.7
  15.0 2.4 %copy-start.13 = (f32[512]{0:T(512)S(1)}, f32[512]{0:T(512)}, u32[]{:S(2)}) copy-start(f32[512]{0:T(512)} %param.24) | copy-start | bytes 6148
  61.6 19.6 %copy-start.3 = (bf16[512,512]{1,0:T(8,128)(2,1)S(1)}, bf16[512,512]{1,0:T(8,128)(2,1)}, u32[]{:S(2)}) copy-start(bf16[512,512]{1,0:T(8,128)(2,1)} %w_nbr_ref.3) | copy-start | bytes 1572868
  81.2 1.6 %copy-start.1 = (f32[1024,512]{1,0:T(8,128)S(1)}, f32[1024,512]{1,0:T(8,128)}, u32[]{:S(2)}) copy-start(f32[1024,512]{1,0:T(8,128)} %gather_fusion.2) | copy-start | bytes 6291460
  93.8 1.0 copy-start.2
  94.7 10.8 %copy-start.10 = (s32[4]{0:T(128)S(1)}, s32[4]{0:T(128)}, u32[]{:S(2)}) copy-start(s32[4]{0:T(128)} %param.21) | copy-start | bytes 52
  94.7 10.8 %copy-start.11 = (bf16[512]{0:T(512)(128)(2,1)S(1)}, bf16[512]{0:T(512)(128)(2,1)}, u32[]{:S(2)}) copy-start(bf16[512]{0:T(512)(128)(2,1)} %param.25) | copy-start | bytes 3076
  94.7 10.9 %copy-start.12 = (bf16[512]{0:T(512)(128)(2,1)S(1)}, bf16[512]{0:T(512)(128)(2,1)}, u32[]{:S(2)}) copy-start(bf16[512]{0:T(512)(128)(2,1)} %param.29) | copy-start | bytes 3076
  94.7 10.9 %copy-start.9 = (s32[4,256]{1,0:T(4,128)S(1)}, s32[4,256]{1,0:T(4,128)}, u32[]{:S(2)}) copy-start(s32[4,256]{1,0:T(4,128)} %param.20) | copy-start | bytes 12292
  94.7 29.0 %all-to-all-start.1 = ((bf16[128,8,512]{2,1,0:T(8,128)(2,1)}), bf16[128,8,512]{2,1,0:T(8,128)(2,1)}, u32[]{:S(2)}, u32[]{:S(2)}) async-start(bf16[128,8,512]{2,1,0:T(8,128)(2,1)} %bitcast.45), calls=%async_computation.1 | async-start | bytes 2097152 | tf_op jit(solution)/shard_map/all_to_all | solution.py:148
  126.2 1.0 copy-start.6
  126.3 1.2 copy-start.14
  130.8 15.2 %all-to-all-start.2 = ((f32[128,1,8]{2,1,0:T(1,128)}), f32[128,1,8]{2,1,0:T(1,128)S(1)}, u32[]{:S(2)}, u32[]{:S(2)}) async-start(f32[128,1,8]{2,1,0:T(1,128)} %bitcast.12), calls=%async_computation.2 | async-start | bytes 131072 | tf_op jit(solution)/shard_map/all_to_all | solution.py:168

commit v10 on v9

--- a/solution.py
+++ b/solution.py
@@ -135,8 +135,10 @@
     provided = provided.reshape(column_total, width)
     send_flat = send_rows[0].reshape(send_rows.shape[1] * send_rows.shape[2])
     self_term = jnp.dot(embed_bf, w_self, preferred_element_type=jnp.float32) + bias_v
-    send_adjacency = adjacency.at[send_flat].get(mode="promise_in_bounds")
-    send_self = self_term.at[send_flat].get(mode="promise_in_bounds")
+    send_chooser = select_matrix(send_flat, nodes, jnp.bfloat16)
+    send_adjacency = jnp.dot(send_chooser, adjacency, preferred_element_type=jnp.float32).astype(jnp.bfloat16)
+    send_embed = jnp.dot(send_chooser, embed_bf, preferred_element_type=jnp.float32).astype(jnp.bfloat16)
+    send_self = jnp.dot(send_embed, w_self, preferred_element_type=jnp.float32) + bias_v
     outbound = node_layer(send_adjacency, provided, send_self, w_nbr)
     node_hidden = node_layer(adjacency, provided, self_term, w_nbr)
     confidence = jnp.dot(node_hidden, w_conf, preferred_element_type=jnp.float32)

time: 150 us -> 147 us (0.980)
  local copies, waits for them, and re-layouts: 35.4 us -> 7.5 us
  matrix products: 8.82 us -> 25.1 us
  starting transfers between devices: 25 us -> 30 us
  waiting for transfers between devices: 13 us -> 16.2 us
    gather x2 -> x0, local copies, waits for them, and re-layouts: 24.5 us -> none  [the longest x1 19.6 us: body(): send_adjacency = adjacency.at[send_flat].get(mode='promise_in_bounds')]
    dot_general x0 -> x2, matrix products: none -> 17.5 us  [the longest x1 14.4 us: body(): jnp.dot(send_chooser, adjacency, preferred_element_type=jnp.float32)]
    all_to_all x1, starting transfers between devices: 10.7 us -> 15.1 us  [body(): lax.all_to_all(outbound, ('grp', 'shard'), split_axis=0, concat_axis=0, t...]
    all_to_all x1, waiting for transfers between devices: 0.01 us -> 3.94 us  [body(): lax.all_to_all(outgoing, 'shard', split_axis=0, concat_axis=0, tiled=True)]
    unnamed x38, local copies, waits for them, and re-layouts: 4.36 us -> 1.1 us
  transfers between devices with their start and end apart: 3 -> 3, of which waited for: 2 -> 3; matrix products, arithmetic and copies ran while one was open for 22% -> 16% of each run, Pallas kernels for 33% -> 34%
where the time goes in v10:
time: 147 us; the launch traced here: 146 us
  Pallas kernels  60.9 us (41%)
  starting transfers between devices  30 us (20%)
  matrix products  25.1 us (17%)
  waiting for transfers between devices  16.2 us (11%)
  local copies, waits for them, and re-layouts  7.5 us (5%)
  other arithmetic  5.57 us (4%)
    pallas_call x1, Pallas kernels, build_adjacency(): pl.pallas_call(adjacency_kernel, grid=(nodes // rows,), in_specs=[pl.Bloc...  37.4 us
    pallas_call x2, Pallas kernels, node_layer(): pl.pallas_call(node_kernel, grid=(count // rows,), in_specs=[pl.BlockSpec...  23.5 us
    all_to_all x1, starting transfers between devices, body(): lax.all_to_all(outbound, ('grp', 'shard'), split_axis=0, concat_axis=0, t...  15.1 us
    dot_general x1, matrix products, body(): jnp.dot(send_chooser, adjacency, preferred_element_type=jnp.float32)  14.4 us
    all_to_all x1, waiting for transfers between devices, body(): lax.all_to_all(slot_scores, ('grp', 'shard'), split_axis=0, concat_axis=0...  8.87 us
    all_to_all x1, starting transfers between devices, body(): lax.all_to_all(outgoing, 'shard', split_axis=0, concat_axis=0, tiled=True)  8.61 us
    all_to_all x1, starting transfers between devices, body(): lax.all_to_all(slot_scores, ('grp', 'shard'), split_axis=0, concat_axis=0...  6.31 us
    all_to_all x1, waiting for transfers between devices, body(): lax.all_to_all(outgoing, 'shard', split_axis=0, concat_axis=0, tiled=True)  3.94 us
  transfers between devices with their start and end apart: 3, of which 3 were waited for; matrix products, arithmetic and copies ran while one was open for 16% of the time, Pallas kernels for 34%

profile of v10, /device:TPU:1, one launch (start us, length us, event | category | flops | bytes accessed | tf_op | source)
XLA Modules:
  0.0 146.3 jit_solution(13127251094422819917)
XLA Ops:
  0.6 0.0 copy-start
  0.7 1.8 %convert_element_type.29 = bf16[1024,512]{1,0:T(8,128)(2,1)S(1)} convert(f32[1024,512]{1,0:T(8,128)} %param.15) | non-fusion elementwise | flops 524288 | bytes 3145728 | tf_op jit(solution)/shard_map/convert_element_type | solution.py:120
  2.4 0.0 copy-done.10
  2.5 0.0 copy-start.2
  2.5 0.1 copy.33
  2.6 0.1 reshape_squeeze.3
  2.7 2.8 %gather_fusion = bf16[32,128,512]{2,1,0:T(8,128)(2,1)} fusion(bf16[8,128,512]{2,1,0:T(8,128)(2,1)S(1)} %bitcast.47, s32[1024]{0:T(1024)S(1)} %pad_clamp_fusion), kind=kCustom, calls=%fused_computation | custom fusion | bytes 8388736 | tf_op jit(solution)/shard_map/gather | solution.py:132
  5.5 8.6 %all-to-all-start = ((bf16[16,256,512]{2,1,0:T(8,128)(2,1)}), bf16[16,256,512]{2,1,0:T(8,128)(2,1)}, u32[]{:S(2)}, u32[]{:S(2)}) async-start(bf16[16,256,512]{2,1,0:T(8,128)(2,1)} %bitcast.48), calls=%async_computation | async-start | bytes 8388608 | tf_op jit(solution)/shard_map/all_to_all | solution.py:134
  14.1 0.0 copy-start.7
  14.1 0.2 copy.31
  14.3 1.0 reshape.116.slot_ref
  15.4 0.2 copy.32
  15.6 0.9 reshape.125.coef_ref
  16.5 0.0 copy-done.7
  16.5 0.1 copy.34
  16.6 0.1 eq.70
  16.7 0.0 copy-start.13
  16.7 37.4 %shard_map.174.adj_ref = bf16[1024,4096]{1,0:T(8,128)(2,1)} custom-call(s32[128,640]{1,0:T(8,128)} %reshape.116.slot_ref, f32[128,640]{1,0:T(8,128)} %reshape.125.coef_ref), custom_call_target="tpu_custom_call" | custom-call | tf_op jit(solution)/shard_map/pallas_call | solution.py:49
  54.1 3.1 %convolution_add_fusion.self_ref = f32[1024,512]{1,0:T(8,128)S(1)} fusion(bf16[512,512]{1,0:T(8,128)(2,1)S(1)} %copy-done, f32[512]{0:T(512)S(1)} %copy-done.13, bf16[1024,512]{1,0:T(8,128)(2,1)} %copy-done.2, s32[1024]{0:T(1024)S(1)} %eq.70), kind=kOutput, calls=%fused_computation.16 | convolution fusion | flops 1612709888 | bytes 3676160 | tf_op jit(solution)/shard_map/dot_general | solution.py:141
  57.2 0.0 copy-start.1
  57.2 14.4 %convolution_convert_fusion.adj_ref = bf16[1024,4096]{1,0:T(8,128)(2,1)} fusion(bf16[1024,4096]{1,0:T(8,128)(2,1)} %shard_map.174.adj_ref, s32[1024]{0:T(1024)S(1)} %eq.70), kind=kOutput, calls=%fused_computation.1 | convolution fusion | flops 8595177472 | bytes 16781312 | tf_op jit(solution)/shard_map/dot_general | solution.py:139
  71.6 3.9 %all-to-all-done = bf16[16,256,512]{2,1,0:T(8,128)(2,1)} async-done(((bf16[16,256,512]{2,1,0:T(8,128)(2,1)}), bf16[16,256,512]{2,1,0:T(8,128)(2,1)}, u32[]{:S(2)}, u32[]{:S(2)}) %all-to-all-start) | async-done | bytes 4194336 | tf_op jit(solution)/shard_map/all_to_all | solution.py:134
  75.6 11.7 %shard_map.176 = bf16[1024,512]{1,0:T(8,128)(2,1)} custom-call(bf16[1024,4096]{1,0:T(8,128)(2,1)} %convolution_convert_fusion.adj_ref, bf16[4096,512]{1,0:T(8,128)(2,1)} %bitcast.3.table_ref, f32[1024,512]{1,0:T(8,128)S(1)} %convolution_add_fusion.self_ref, bf16[512,512]{1,0:T(8,128)(2,1)S(1)} %copy-done.1), custom_call_target="tpu_custom_call" | custom-call | tf_op jit(solution)/shard_map/pallas_call | solution.py:72
  87.3 0.0 copy-start.8
  87.3 0.0 copy-start.3
  87.4 15.1 %all-to-all-start.1 = ((bf16[128,8,512]{2,1,0:T(8,128)(2,1)}), bf16[128,8,512]{2,1,0:T(8,128)(2,1)}, u32[]{:S(2)}, u32[]{:S(2)}) async-start(bf16[128,8,512]{2,1,0:T(8,128)(2,1)} %bitcast.6), calls=%async_computation.1 | async-start | bytes 2097152 | tf_op jit(solution)/shard_map/all_to_all | solution.py:150
  102.6 0.1 iota_compare_fusion.9
  102.6 0.7 convolution_add_fusion.1.self_ref
  103.4 11.8 %shard_map.175 = bf16[1024,512]{1,0:T(8,128)(2,1)} custom-call(bf16[1024,4096]{1,0:T(8,128)(2,1)} %shard_map.174.adj_ref, bf16[4096,512]{1,0:T(8,128)(2,1)} %bitcast.3.table_ref, f32[1024,512]{1,0:T(8,128)S(1)} %convolution_add_fusion.1.self_ref, bf16[512,512]{1,0:T(8,128)(2,1)S(1)} %copy-done.1), custom_call_target="tpu_custom_call" | custom-call | tf_op jit(solution)/shard_map/pallas_call | solution.py:72
  115.1 2.2 %fusion.24 = f32[1,1024]{1,0:T(1,128)} fusion(bf16[1024,512]{1,0:T(8,128)(2,1)} %shard_map.175, bf16[512,1]{0,1:T(2,128)(2,1)S(1)} %reshape.134), kind=kOutput, calls=%fused_computation.41 | convolution fusion | flops 1048576 | bytes 1053696 | tf_op jit(solution)/shard_map/dot_general | solution.py:144
  117.3 3.4 %all-to-all-done.1 = bf16[128,8,512]{2,1,0:T(8,128)(2,1)} async-done(((bf16[128,8,512]{2,1,0:T(8,128)(2,1)}), bf16[128,8,512]{2,1,0:T(8,128)(2,1)}, u32[]{:S(2)}, u32[]{:S(2)}) %all-to-all-start.1) | async-done | bytes 1048608 | tf_op jit(solution)/shard_map/all_to_all | solution.py:150
  120.8 2.5 %fusion.2 = f32[4,256,512]{2,1,0:T(8,128)S(1)} fusion(s32[4,256]{1,0:T(4,128)S(1)} %copy-done.8, bf16[128,8,512]{2,1,0:T(8,128)(2,1)} %all-to-all-done.1), kind=kOutput, calls=%fused_computation.9 | convolution fusion | flops 1074790400 | bytes 3149824 | tf_op jit(solution)/shard_map/dot_general | solution.py:156
  123.3 0.0 copy-start.5
  123.3 0.0 copy-start.14
  123.3 0.4 select_reduce_fusion.2
  123.7 0.6 copy-done.5
  124.3 0.2 fusion.18
  124.5 2.0 %fusion.8 = f32[1,4,256]{2,0,1:T(1,128)S(1)} fusion(bf16[512,1,1]{0,1,2:T(2,128)(2,1)S(1)} %reshape.138, f32[4,256,512]{2,1,0:T(8,128)S(1)} %fusion.2, f32[512]{0:T(512)S(1)} %copy-done.14, f32[4,512]{1,0:T(4,128)S(1)} %fusion.18, f32[4,512]{1,0:T(4,128)S(1)} %bitcast.50, bf16[512,512]{1,0:T(8,128)(2,1)} %param.26), kind=kOutput, calls=%fused_computation.19 | convolution fusion | flops 541065216 | bytes 2644992 | tf_op jit(solution)/shard_map/smk,k->sm/dot_general | solution.py:166
  126.5 0.1 fusion.34
  126.6 0.6 select_reduce_fusion.1
  127.2 0.7 all_to_all.14
  127.9 6.3 %all-to-all-start.2 = ((f32[128,1,8]{2,1,0:T(1,128)}), f32[128,1,8]{2,1,0:T(1,128)S(1)}, u32[]{:S(2)}, u32[]{:S(2)}) async-start(f32[128,1,8]{2,1,0:T(1,128)} %bitcast.11), calls=%async_computation.2 | async-start | bytes 131072 | tf_op jit(solution)/shard_map/all_to_all | solution.py:170
  134.2 0.7 divide_select_fusion
  134.9 8.9 %all-to-all-done.2 = f32[128,1,8]{2,1,0:T(1,128)S(1)} async-done(((f32[128,1,8]{2,1,0:T(1,128)}), f32[128,1,8]{2,1,0:T(1,128)S(1)}, u32[]{:S(2)}, u32[]{:S(2)}) %all-to-all-start.2) | async-done | bytes 4128 | tf_op jit(solution)/shard_map/all_to_all | solution.py:170
  143.7 0.5 broadcast.65
  144.2 0.8 reduce.3
  145.0 0.1 broadcast_in_dim.58
  145.1 1.1 select_reduce_fusion
  (29 shorter events, 0.1 us)
Async XLA Ops:
  0.6 53.5 %copy-start = (bf16[512,512]{1,0:T(8,128)(2,1)S(1)}, bf16[512,512]{1,0:T(8,128)(2,1)}, u32[]{:S(2)}) copy-start(bf16[512,512]{1,0:T(8,128)(2,1)} %param.22) | copy-start | bytes 1572868
  0.6 1.8 %copy-start.10 = (s32[1,16,2]{1,2,0:T(2,128)S(1)}, s32[1,16,2]{1,2,0:T(2,128)}, u32[]{:S(2)}) copy-start(s32[1,16,2]{1,2,0:T(2,128)} %param.18) | copy-start | bytes 388
  2.5 3.0 %copy-start.2 = (bf16[1024,512]{1,0:T(8,128)(2,1)}, bf16[1024,512]{1,0:T(8,128)(2,1)S(1)}, u32[]{:S(2)}) copy-start(bf16[1024,512]{1,0:T(8,128)(2,1)S(1)} %convert_element_type.29) | copy-start | bytes 3145732
  5.5 8.6 %copy-start.6 = (s32[1024,80]{0,1:T(8,128)S(1)}, s32[1024,80]{0,1:T(8,128)}, u32[]{:S(2)}) copy-start(s32[1024,80]{0,1:T(8,128)} %param.16) | copy-start | bytes 983044
  5.5 9.8 %copy-start.4 = (f32[1024,80]{0,1:T(8,128)S(1)}, f32[1024,80]{0,1:T(8,128)}, u32[]{:S(2)}) copy-start(f32[1024,80]{0,1:T(8,128)} %param.17) | copy-start | bytes 983044
  5.5 70.1 %all-to-all-start = ((bf16[16,256,512]{2,1,0:T(8,128)(2,1)}), bf16[16,256,512]{2,1,0:T(8,128)(2,1)}, u32[]{:S(2)}, u32[]{:S(2)}) async-start(bf16[16,256,512]{2,1,0:T(8,128)(2,1)} %bitcast.48), calls=%async_computation | async-start | bytes 8388608 | tf_op jit(solution)/shard_map/all_to_all | solution.py:134
  14.1 2.4 %copy-start.7 = (s32[1,128,8]{1,2,0:T(8,128)S(1)}, s32[1,128,8]{1,2,0:T(8,128)}, u32[]{:S(2)}) copy-start(s32[1,128,8]{1,2,0:T(8,128)} %param.19) | copy-start | bytes 12292
  16.7 37.4 %copy-start.13 = (f32[512]{0:T(512)S(1)}, f32[512]{0:T(512)}, u32[]{:S(2)}) copy-start(f32[512]{0:T(512)} %param.24) | copy-start | bytes 6148
  57.2 18.4 %copy-start.1 = (bf16[512,512]{1,0:T(8,128)(2,1)S(1)}, bf16[512,512]{1,0:T(8,128)(2,1)}, u32[]{:S(2)}) copy-start(bf16[512,512]{1,0:T(8,128)(2,1)} %w_nbr_ref.3) | copy-start | bytes 1572868
  87.3 15.2 %copy-start.11 = (bf16[512]{0:T(512)(128)(2,1)S(1)}, bf16[512]{0:T(512)(128)(2,1)}, u32[]{:S(2)}) copy-start(bf16[512]{0:T(512)(128)(2,1)} %param.25) | copy-start | bytes 3076
  87.3 15.2 %copy-start.12 = (bf16[512]{0:T(512)(128)(2,1)S(1)}, bf16[512]{0:T(512)(128)(2,1)}, u32[]{:S(2)}) copy-start(bf16[512]{0:T(512)(128)(2,1)} %param.29) | copy-start | bytes 3076
  87.3 15.2 %copy-start.9 = (s32[4]{0:T(128)S(1)}, s32[4]{0:T(128)}, u32[]{:S(2)}) copy-start(s32[4]{0:T(128)} %param.21) | copy-start | bytes 52
  87.3 15.2 %copy-start.8 = (s32[4,256]{1,0:T(4,128)S(1)}, s32[4,256]{1,0:T(4,128)}, u32[]{:S(2)}) copy-start(s32[4,256]{1,0:T(4,128)} %param.20) | copy-start | bytes 12292
  87.3 15.3 %copy-start.3 = (bf16[1024,512]{1,0:T(8,128)(2,1)S(1)}, bf16[1024,512]{1,0:T(8,128)(2,1)}, u32[]{:S(2)}) copy-start(bf16[1024,512]{1,0:T(8,128)(2,1)} %copy-done.2) | copy-start | bytes 3145732
  87.4 33.4 %all-to-all-start.1 = ((bf16[128,8,512]{2,1,0:T(8,128)(2,1)}), bf16[128,8,512]{2,1,0:T(8,128)(2,1)}, u32[]{:S(2)}, u32[]{:S(2)}) async-start(bf16[128,8,512]{2,1,0:T(8,128)(2,1)} %bitcast.6), calls=%async_computation.1 | async-start | bytes 2097152 | tf_op jit(solution)/shard_map/all_to_all | solution.py:150
  123.3 1.0 copy-start.5
  123.3 1.2 copy-start.14
  127.9 15.9 %all-to-all-start.2 = ((f32[128,1,8]{2,1,0:T(1,128)}), f32[128,1,8]{2,1,0:T(1,128)S(1)}, u32[]{:S(2)}, u32[]{:S(2)}) async-start(f32[128,1,8]{2,1,0:T(1,128)} %bitcast.11), calls=%async_computation.2 | async-start | bytes 131072 | tf_op jit(solution)/shard_map/all_to_all | solution.py:170

commit v11 on v10

--- a/solution.py
+++ b/solution.py
@@ -82,6 +82,54 @@
         out_shape=jax.ShapeDtypeStruct((count, hidden), jnp.bfloat16),
         compiler_params=pltpu.CompilerParams(vmem_limit_bytes=48 * 1024 * 1024),
     )(adjacency, table, self_term, w_nbr)
+
+
+def edge_kernel(len_ref, rows_ref, member_ref, w_diff_ref, w_ctx_ref, bias_ref, w_edge_ref, scores_ref):
+    slots = rows_ref.shape[0]
+    subs, width = scores_ref.shape
+    hidden = w_diff_ref.shape[1]
+    chooser = jnp.where(
+        member_ref[...] == lax.broadcasted_iota(jnp.int32, (subs * width, slots), 1), 1.0, 0.0
+    ).astype(jnp.bfloat16)
+    member_rows = jnp.dot(chooser, rows_ref[...], preferred_element_type=jnp.float32)
+    for s in range(subs):
+        block = member_rows[s * width:(s + 1) * width, :]
+        relative = block - block[0:1, :]
+        length = len_ref[s]
+        alive = lax.broadcasted_iota(jnp.int32, (width, 1), 0) < length
+        total = jnp.sum(jnp.where(alive, relative, 0.0), axis=0, keepdims=True)
+        count = jnp.full((1, hidden), length, jnp.int32).astype(jnp.float32)
+        context = jnp.broadcast_to((total / count).astype(jnp.bfloat16), (8, hidden))
+        inner = (
+            jnp.dot(relative.astype(jnp.bfloat16), w_diff_ref[...], preferred_element_type=jnp.float32)
+            + jnp.dot(context, w_ctx_ref[...], preferred_element_type=jnp.float32)[0:1, :]
+            + bias_ref[...]
+        )
+        edge_hidden = jnp.maximum(inner, 0.0).astype(jnp.bfloat16)
+        logits = lax.dot_general(
+            w_edge_ref[...], edge_hidden, (((1,), (1,)), ((), ())), preferred_element_type=jnp.float32
+        )[0:1, :]
+        live = lax.broadcasted_iota(jnp.int32, (1, width), 1) < length
+        scores_ref[s:s + 1, :] = jnp.where(live, 1.0 / (1.0 + jnp.exp(-logits)), 0.0)
+
+
+def edge_layer(sub_len, rows, member_flat, w_diff, w_ctx, bias, w_edge, subs, width):
+    vmem = pl.BlockSpec(memory_space=pltpu.VMEM)
+    hidden = w_diff.shape[1]
+    return pl.pallas_call(
+        edge_kernel,
+        in_specs=[pl.BlockSpec(memory_space=pltpu.SMEM)] + [vmem] * 6,
+        out_specs=vmem,
+        out_shape=jax.ShapeDtypeStruct((subs, width), jnp.float32),
+    )(
+        sub_len,
+        rows,
+        member_flat.reshape(subs * width, 1),
+        w_diff,
+        w_ctx,
+        bias.reshape(1, hidden),
+        jnp.broadcast_to(w_edge.reshape(1, hidden), (8, hidden)),
+    )
 
 
 def select_matrix(indices, count, dtype):
@@ -152,19 +200,7 @@
     sub_count = members.shape[0]
     member_width = members.shape[1]
     member_flat = members.reshape(sub_count * member_width)
-    member_chooser = select_matrix(member_flat, slot_total, jnp.bfloat16)
-    member_rows = jnp.dot(member_chooser, received_rows, preferred_element_type=jnp.float32)
-    member_rows = member_rows.reshape(sub_count, member_width, hidden_width)
-    relative = member_rows - member_rows[:, :1, :]
-    alive = jnp.arange(member_width, dtype=jnp.int32)[None, :] < sub_len[:, None]
-    masked = jnp.where(alive[:, :, None], relative, 0.0)
-    context = (jnp.sum(masked, axis=1) / sub_len[:, None].astype(jnp.float32)).astype(jnp.bfloat16)
-    relative_bf = relative.astype(jnp.bfloat16)
-    inner = jnp.einsum("smh,hk->smk", relative_bf, w_diff, preferred_element_type=jnp.float32)
-    inner = inner + jnp.dot(context, w_ctx, preferred_element_type=jnp.float32)[:, None, :] + bias_e
-    edge_hidden = jax.nn.relu(inner).astype(jnp.bfloat16)
-    logits = jnp.einsum("smk,k->sm", edge_hidden, w_edge, preferred_element_type=jnp.float32)
-    edge_scores = jnp.where(alive, jax.nn.sigmoid(logits), 0.0)
+    edge_scores = edge_layer(sub_len, received_rows, member_flat, w_diff, w_ctx, bias_e, w_edge, sub_count, member_width)
     slot_scores = scatter_sum(member_flat, edge_scores.reshape(sub_count * member_width), slot_total)
     slot_scores = slot_scores.reshape(device_total, capacity)
     returned = lax.all_to_all(

time: 147 us -> 148 us (level)
  Pallas kernels: 60.9 us -> 66 us
  matrix products: 25.1 us -> 21.6 us
  local copies, waits for them, and re-layouts: 7.5 us -> 10.2 us
    pallas_call x0 -> x1, Pallas kernels: none -> 5.12 us  [edge_layer(): pl.pallas_call(edge_kernel, in_specs=[pl.BlockSpec(memory_space=pltpu.SME...]
    dot_general x3 -> x0, matrix products: 4.69 us -> none  [the longest x1 2.52 us: body(): jnp.dot(member_chooser, received_rows, preferred_element_type=jnp.float32)]
    unnamed x38 -> x30, local copies, waits for them, and re-layouts: 1.1 us -> 3.23 us
    all_to_all x1, waiting for transfers between devices: 8.87 us -> 7.31 us  [body(): lax.all_to_all(slot_scores, ('grp', 'shard'), split_axis=0, concat_axis=0...]
  transfers between devices with their start and end apart: 3 -> 3, of which waited for: 3 -> 3; matrix products, arithmetic and copies ran while one was open for 16% -> 17% of each run, Pallas kernels for 34% -> 33%
where the time goes in v11:
time: 148 us; the launch traced here: 147 us
  Pallas kernels  66 us (45%)
  starting transfers between devices  29.2 us (20%)
  matrix products  21.6 us (15%)
  waiting for transfers between devices  15.1 us (10%)
  local copies, waits for them, and re-layouts  10.2 us (7%)
  other arithmetic  4.35 us (3%)
    pallas_call x1, Pallas kernels, build_adjacency(): pl.pallas_call(adjacency_kernel, grid=(nodes // rows,), in_specs=[pl.Bloc...  37.4 us
    pallas_call x2, Pallas kernels, node_layer(): pl.pallas_call(node_kernel, grid=(count // rows,), in_specs=[pl.BlockSpec...  23.5 us
    all_to_all x1, starting transfers between devices, body(): lax.all_to_all(outbound, ('grp', 'shard'), split_axis=0, concat_axis=0, t...  14.7 us
    dot_general x1, matrix products, body(): jnp.dot(send_chooser, adjacency, preferred_element_type=jnp.float32)  14.4 us
    all_to_all x1, starting transfers between devices, body(): lax.all_to_all(outgoing, 'shard', split_axis=0, concat_axis=0, tiled=True)  8.61 us
    all_to_all x1, waiting for transfers between devices, body(): lax.all_to_all(slot_scores, ('grp', 'shard'), split_axis=0, concat_axis=0...  7.31 us
    all_to_all x1, starting transfers between devices, body(): lax.all_to_all(slot_scores, ('grp', 'shard'), split_axis=0, concat_axis=0...  5.95 us
    pallas_call x1, Pallas kernels, edge_layer(): pl.pallas_call(edge_kernel, in_specs=[pl.BlockSpec(memory_space=pltpu.SME...  5.12 us
  transfers between devices with their start and end apart: 3, of which 3 were waited for; matrix products, arithmetic and copies ran while one was open for 17% of the time, Pallas kernels for 33%

profile of v11, /device:TPU:1, one launch (start us, length us, event | category | flops | bytes accessed | tf_op | source)
XLA Modules:
  0.0 147.4 jit_solution(12600174333370735363)
XLA Ops:
  0.6 0.0 copy-start
  0.6 1.8 %convert_element_type.15 = bf16[1024,512]{1,0:T(8,128)(2,1)S(1)} convert(f32[1024,512]{1,0:T(8,128)} %param.15) | non-fusion elementwise | flops 524288 | bytes 3145728 | tf_op jit(solution)/shard_map/convert_element_type | solution.py:168
  2.4 0.0 copy-start.2
  2.4 0.8 copy.35
  3.2 0.1 reshape_squeeze.3
  3.3 2.8 %gather_fusion = bf16[32,128,512]{2,1,0:T(8,128)(2,1)} fusion(bf16[8,128,512]{2,1,0:T(8,128)(2,1)S(1)} %bitcast.25, s32[1024]{0:T(1024)S(1)} %pad_clamp_fusion), kind=kCustom, calls=%fused_computation | custom fusion | bytes 8388736 | tf_op jit(solution)/shard_map/gather | solution.py:180
  6.1 0.0 copy-done.2
  6.1 8.6 %all-to-all-start = ((bf16[16,256,512]{2,1,0:T(8,128)(2,1)}), bf16[16,256,512]{2,1,0:T(8,128)(2,1)}, u32[]{:S(2)}, u32[]{:S(2)}) async-start(bf16[16,256,512]{2,1,0:T(8,128)(2,1)} %bitcast.26), calls=%async_computation | async-start | bytes 8388608 | tf_op jit(solution)/shard_map/all_to_all | solution.py:182
  14.8 0.0 copy-done.5
  14.8 0.0 copy-start.7
  14.8 0.2 copy.33
  15.0 1.0 reshape.75.slot_ref
  15.9 0.0 copy-done.4
  16.0 0.2 copy.34
  16.2 0.9 reshape.85.coef_ref
  17.2 0.0 copy-done.7
  17.2 0.1 copy.36
  17.3 0.1 eq.16
  17.4 0.0 copy-start.10
  17.4 37.4 %shard_map.174.adj_ref = bf16[1024,4096]{1,0:T(8,128)(2,1)} custom-call(s32[128,640]{1,0:T(8,128)} %reshape.75.slot_ref, f32[128,640]{1,0:T(8,128)} %reshape.85.coef_ref), custom_call_target="tpu_custom_call" | custom-call | tf_op jit(solution)/shard_map/pallas_call | solution.py:49
  54.8 0.0 copy-done
  54.8 0.0 copy-done.10
  54.8 3.1 %convolution_add_fusion.self_ref = f32[1024,512]{1,0:T(8,128)S(1)} fusion(bf16[512,512]{1,0:T(8,128)(2,1)S(1)} %copy-done, f32[512]{0:T(512)S(1)} %copy-done.10, bf16[1024,512]{1,0:T(8,128)(2,1)} %copy-done.2, s32[1024]{0:T(1024)S(1)} %eq.16), kind=kOutput, calls=%fused_computation.9 | convolution fusion | flops 1612709888 | bytes 3676160 | tf_op jit(solution)/shard_map/dot_general | solution.py:189
  57.8 0.0 copy-start.1
  57.9 14.4 %convolution_convert_fusion.adj_ref = bf16[1024,4096]{1,0:T(8,128)(2,1)} fusion(bf16[1024,4096]{1,0:T(8,128)(2,1)} %shard_map.174.adj_ref, s32[1024]{0:T(1024)S(1)} %eq.16), kind=kOutput, calls=%fused_computation.1 | convolution fusion | flops 8595177472 | bytes 16781312 | tf_op jit(solution)/shard_map/dot_general | solution.py:187
  72.3 3.9 %all-to-all-done = bf16[16,256,512]{2,1,0:T(8,128)(2,1)} async-done(((bf16[16,256,512]{2,1,0:T(8,128)(2,1)}), bf16[16,256,512]{2,1,0:T(8,128)(2,1)}, u32[]{:S(2)}, u32[]{:S(2)}) %all-to-all-start) | async-done | bytes 4194336 | tf_op jit(solution)/shard_map/all_to_all | solution.py:182
  76.2 0.0 copy-done.1
  76.3 11.8 %shard_map.176 = bf16[1024,512]{1,0:T(8,128)(2,1)} custom-call(bf16[1024,4096]{1,0:T(8,128)(2,1)} %convolution_convert_fusion.adj_ref, bf16[4096,512]{1,0:T(8,128)(2,1)} %bitcast.3.table_ref, f32[1024,512]{1,0:T(8,128)S(1)} %convolution_add_fusion.self_ref, bf16[512,512]{1,0:T(8,128)(2,1)S(1)} %copy-done.1), custom_call_target="tpu_custom_call" | custom-call | tf_op jit(solution)/shard_map/pallas_call | solution.py:72
  88.0 14.7 %all-to-all-start.1 = ((bf16[128,8,512]{2,1,0:T(8,128)(2,1)}), bf16[128,8,512]{2,1,0:T(8,128)(2,1)S(1)}, u32[]{:S(2)}, u32[]{:S(2)}) async-start(bf16[128,8,512]{2,1,0:T(8,128)(2,1)} %bitcast.5), calls=%async_computation.1 | async-start | bytes 2097152 | tf_op jit(solution)/shard_map/all_to_all | solution.py:198
  102.7 0.0 copy-done.8
  102.7 1.1 copy.40
  103.8 1.9 %convolution_add_fusion.1.self_ref = f32[1024,512]{1,0:T(8,128)S(1)} fusion(bf16[1024,512]{1,0:T(8,128)(2,1)} %copy-done.2, bf16[512,512]{1,0:T(8,128)(2,1)S(1)} %copy-done, f32[512]{0:T(512)S(1)} %copy-done.10), kind=kOutput, calls=%fused_computation.10 | convolution fusion | flops 537395200 | bytes 3672064 | tf_op jit(solution)/shard_map/dot_general | solution.py:185
  105.7 0.0 copy-start.9
  105.8 11.7 %shard_map.175 = bf16[1024,512]{1,0:T(8,128)(2,1)} custom-call(bf16[1024,4096]{1,0:T(8,128)(2,1)} %shard_map.174.adj_ref, bf16[4096,512]{1,0:T(8,128)(2,1)} %bitcast.3.table_ref, f32[1024,512]{1,0:T(8,128)S(1)} %convolution_add_fusion.1.self_ref, bf16[512,512]{1,0:T(8,128)(2,1)S(1)} %copy-done.1), custom_call_target="tpu_custom_call" | custom-call | tf_op jit(solution)/shard_map/pallas_call | solution.py:72
  117.5 3.8 %all-to-all-done.1 = bf16[128,8,512]{2,1,0:T(8,128)(2,1)S(1)} async-done(((bf16[128,8,512]{2,1,0:T(8,128)(2,1)}), bf16[128,8,512]{2,1,0:T(8,128)(2,1)S(1)}, u32[]{:S(2)}, u32[]{:S(2)}) %all-to-all-start.1) | async-done | bytes 1048608 | tf_op jit(solution)/shard_map/all_to_all | solution.py:198
  121.3 0.6 broadcast_in_dim.34.w_edge_ref
  122.0 0.3 copy-done.3
  122.3 5.1 %shard_map.177 = f32[4,256]{1,0:T(4,128)} custom-call(s32[4]{0:T(128)} %len_ref.1, bf16[1024,512]{1,0:T(8,128)(2,1)} %bitcast.27, s32[1024,1]{1,0:T(8,128)} %bitcast.28, bf16[512,512]{1,0:T(8,128)(2,1)} %w_diff_ref.1, bf16[512,512]{1,0:T(8,128)(2,1)} %w_ctx_ref.1, f32[1,512]{1,0:T(1,128)} %bitcast.36, bf16[8,512]{1,0:T(8,128)(2,1)} %broadcast_in_dim.34.w_edge_ref), custom_call_target="tpu_custom_call" | custom-call | tf_op jit(solution)/shard_map/pallas_call | solution.py:119
  127.4 0.7 copy.42
  128.1 0.5 select_reduce_fusion.1
  128.7 0.7 all_to_all.14
  129.4 6.0 %all-to-all-start.2 = ((f32[128,1,8]{2,1,0:T(1,128)}), f32[128,1,8]{2,1,0:T(1,128)S(1)}, u32[]{:S(2)}, u32[]{:S(2)}) async-start(f32[128,1,8]{2,1,0:T(1,128)} %bitcast.8), calls=%async_computation.2 | async-start | bytes 131072 | tf_op jit(solution)/shard_map/all_to_all | solution.py:206
  135.3 2.2 %fusion.6 = f32[1,1024]{1,0:T(1,128)} fusion(bf16[1024,512]{1,0:T(8,128)(2,1)} %shard_map.175, bf16[512,1]{0,1:T(2,128)(2,1)S(1)} %reshape.94), kind=kOutput, calls=%fused_computation.17 | convolution fusion | flops 1048576 | bytes 1053696 | tf_op jit(solution)/shard_map/dot_general | solution.py:192
  137.5 7.3 %all-to-all-done.2 = f32[128,1,8]{2,1,0:T(1,128)S(1)} async-done(((f32[128,1,8]{2,1,0:T(1,128)}), f32[128,1,8]{2,1,0:T(1,128)S(1)}, u32[]{:S(2)}, u32[]{:S(2)}) %all-to-all-start.2) | async-done | bytes 4128 | tf_op jit(solution)/shard_map/all_to_all | solution.py:206
  144.8 0.5 broadcast.24
  145.3 0.8 reduce.3
  146.2 0.1 broadcast_in_dim.38
  146.2 1.1 select_reduce_fusion
  (14 shorter events, 0.1 us)
Async XLA Ops:
  0.6 54.1 %copy-start = (bf16[512,512]{1,0:T(8,128)(2,1)S(1)}, bf16[512,512]{1,0:T(8,128)(2,1)}, u32[]{:S(2)}) copy-start(bf16[512,512]{1,0:T(8,128)(2,1)} %param.22) | copy-start | bytes 1572868
  2.4 3.7 %copy-start.2 = (bf16[1024,512]{1,0:T(8,128)(2,1)}, bf16[1024,512]{1,0:T(8,128)(2,1)S(1)}, u32[]{:S(2)}) copy-start(bf16[1024,512]{1,0:T(8,128)(2,1)S(1)} %convert_element_type.15) | copy-start | bytes 3145732
  6.1 8.6 %copy-start.5 = (s32[1024,80]{0,1:T(8,128)S(1)}, s32[1024,80]{0,1:T(8,128)}, u32[]{:S(2)}) copy-start(s32[1024,80]{0,1:T(8,128)} %param.16) | copy-start | bytes 983044
  6.1 9.8 %copy-start.4 = (f32[1024,80]{0,1:T(8,128)S(1)}, f32[1024,80]{0,1:T(8,128)}, u32[]{:S(2)}) copy-start(f32[1024,80]{0,1:T(8,128)} %param.17) | copy-start | bytes 983044
  6.1 70.1 %all-to-all-start = ((bf16[16,256,512]{2,1,0:T(8,128)(2,1)}), bf16[16,256,512]{2,1,0:T(8,128)(2,1)}, u32[]{:S(2)}, u32[]{:S(2)}) async-start(bf16[16,256,512]{2,1,0:T(8,128)(2,1)} %bitcast.26), calls=%async_computation | async-start | bytes 8388608 | tf_op jit(solution)/shard_map/all_to_all | solution.py:182
  14.8 2.4 %copy-start.7 = (s32[1,128,8]{1,2,0:T(8,128)S(1)}, s32[1,128,8]{1,2,0:T(8,128)}, u32[]{:S(2)}) copy-start(s32[1,128,8]{1,2,0:T(8,128)} %param.19) | copy-start | bytes 12292
  17.4 37.4 %copy-start.10 = (f32[512]{0:T(512)S(1)}, f32[512]{0:T(512)}, u32[]{:S(2)}) copy-start(f32[512]{0:T(512)} %param.24) | copy-start | bytes 6148
  57.8 18.4 %copy-start.1 = (bf16[512,512]{1,0:T(8,128)(2,1)S(1)}, bf16[512,512]{1,0:T(8,128)(2,1)}, u32[]{:S(2)}) copy-start(bf16[512,512]{1,0:T(8,128)(2,1)} %w_nbr_ref.3) | copy-start | bytes 1572868
  76.3 26.4 %copy-start.8 = (bf16[512]{0:T(512)(128)(2,1)S(1)}, bf16[512]{0:T(512)(128)(2,1)}, u32[]{:S(2)}) copy-start(bf16[512]{0:T(512)(128)(2,1)} %param.25) | copy-start | bytes 3076
  76.3 26.5 %copy-start.6 = (s32[4,256]{1,0:T(4,128)S(1)}, s32[4,256]{1,0:T(4,128)}, u32[]{:S(2)}) copy-start(s32[4,256]{1,0:T(4,128)} %param.20) | copy-start | bytes 12292
  88.0 33.3 %all-to-all-start.1 = ((bf16[128,8,512]{2,1,0:T(8,128)(2,1)}), bf16[128,8,512]{2,1,0:T(8,128)(2,1)S(1)}, u32[]{:S(2)}, u32[]{:S(2)}) async-start(bf16[128,8,512]{2,1,0:T(8,128)(2,1)} %bitcast.5), calls=%async_computation.1 | async-start | bytes 2097152 | tf_op jit(solution)/shard_map/all_to_all | solution.py:198
  105.7 15.6 %copy-start.9 = (bf16[512]{0:T(512)(128)(2,1)S(1)}, bf16[512]{0:T(512)(128)(2,1)}, u32[]{:S(2)}) copy-start(bf16[512]{0:T(512)(128)(2,1)} %param.29) | copy-start | bytes 3076
  121.3 1.0 copy-start.3
  129.4 15.5 %all-to-all-start.2 = ((f32[128,1,8]{2,1,0:T(1,128)}), f32[128,1,8]{2,1,0:T(1,128)S(1)}, u32[]{:S(2)}, u32[]{:S(2)}) async-start(f32[128,1,8]{2,1,0:T(1,128)} %bitcast.8), calls=%async_computation.2 | async-start | bytes 131072 | tf_op jit(solution)/shard_map/all_to_all | solution.py:206

commit v12 on v8

--- a/solution.py
+++ b/solution.py
@@ -158,8 +158,9 @@
         column_total,
     )
     tile_count = nodes // TILE
-    embed_tiles = embed_bf.reshape(tile_count, TILE, width)
+    embed_tiles = embed.reshape(tile_count, TILE, width)
     outgoing = embed_tiles.at[tile_list[0].reshape(shard_count * list_len)].get(mode="promise_in_bounds")
+    outgoing = outgoing.astype(jnp.bfloat16)
     outgoing = outgoing.reshape(shard_count, peer_span, width)
     provided = lax.all_to_all(outgoing, "shard", split_axis=0, concat_axis=0, tiled=True)
     provided = provided.reshape(column_total, width)

time: 147 us -> 147 us (level)
  waiting for transfers between devices: 47.4 us -> 45.6 us
  local copies, waits for them, and re-layouts: 8.09 us -> 9.83 us
    all_to_all x1, waiting for transfers between devices: 21.3 us -> 19.5 us  [body(): lax.all_to_all(outgoing, 'shard', split_axis=0, concat_axis=0, tiled=True)]
    gather x1, local copies, waits for them, and re-layouts: 2.76 us -> 4.49 us  [body(): embed_tiles.at[tile_list[0].reshape(shard_count * list_len)]]
  transfers between devices with their start and end apart: 3 -> 3, of which waited for: 3 -> 3; matrix products, arithmetic and copies ran while one was open for 3% -> 4% of each run, Pallas kernels for 26% -> 26%
where the time goes in v12:
time: 147 us; the launch traced here: 146 us
  Pallas kernels  50.9 us (35%)
  waiting for transfers between devices  45.6 us (31%)
  starting transfers between devices  28.5 us (19%)
  local copies, waits for them, and re-layouts  9.83 us (7%)
  other arithmetic  5.56 us (4%)
  matrix products  4.61 us (3%)
    pallas_call x1, Pallas kernels, build_adjacency(): pl.pallas_call(adjacency_kernel, grid=(nodes // rows,), in_specs=[pl.Bloc...  37.5 us
    all_to_all x1, waiting for transfers between devices, body(): lax.all_to_all(outgoing, 'shard', split_axis=0, concat_axis=0, tiled=True)  19.5 us
    all_to_all x1, waiting for transfers between devices, body(): lax.all_to_all(outbound, ('grp', 'shard'), split_axis=0, concat_axis=0, t...  17 us
    all_to_all x1, starting transfers between devices, body(): lax.all_to_all(outbound, ('grp', 'shard'), split_axis=0, concat_axis=0, t...  15.1 us
    pallas_call x1, Pallas kernels, node_layer(): pl.pallas_call(node_kernel, grid=(nodes // rows,), in_specs=[pl.BlockSpec...  13.4 us
    all_to_all x1, waiting for transfers between devices, body(): lax.all_to_all(slot_scores, ('grp', 'shard'), split_axis=0, concat_axis=0...  9 us
    all_to_all x1, starting transfers between devices, body(): lax.all_to_all(outgoing, 'shard', split_axis=0, concat_axis=0, tiled=True)  8.48 us
    all_to_all x1, starting transfers between devices, body(): lax.all_to_all(slot_scores, ('grp', 'shard'), split_axis=0, concat_axis=0...  4.9 us
  transfers between devices with their start and end apart: 3, of which 3 were waited for; matrix products, arithmetic and copies ran while one was open for 4% of the time, Pallas kernels for 26%

profile of v12, /device:TPU:1, one launch (start us, length us, event | category | flops | bytes accessed | tf_op | source)
XLA Modules:
  0.0 146.0 jit_solution(933326449662430407)
XLA Ops:
  0.6 0.0 copy-start
  0.6 0.8 copy.38
  1.5 0.1 reshape_squeeze.3
  1.6 4.5 %gather_fusion = bf16[32,128,512]{2,1,0:T(8,128)(2,1)} fusion(f32[8,128,512]{2,1,0:T(8,128)} %bitcast.44, s32[1024]{0:T(1024)S(1)} %pad_clamp_fusion), kind=kCustom, calls=%fused_computation | custom fusion | bytes 8388736 | tf_op jit(solution)/shard_map/gather | solution.py:162
  6.1 8.5 %all-to-all-start = ((bf16[16,256,512]{2,1,0:T(8,128)(2,1)}), bf16[16,256,512]{2,1,0:T(8,128)(2,1)}, u32[]{:S(2)}, u32[]{:S(2)}) async-start(bf16[16,256,512]{2,1,0:T(8,128)(2,1)} %bitcast.45), calls=%async_computation | async-start | bytes 8388608 | tf_op jit(solution)/shard_map/all_to_all | solution.py:165
  14.5 0.0 copy-start.7
  14.6 0.0 copy-start.4
  14.6 1.8 %convert_element_type.31.embed_ref = bf16[1024,512]{1,0:T(8,128)(2,1)S(1)} convert(f32[1024,512]{1,0:T(8,128)} %param.15) | non-fusion elementwise | flops 524288 | bytes 3145728 | tf_op jit(solution)/shard_map/convert_element_type | solution.py:150
  16.4 0.0 copy-start.6
  16.4 0.1 copy.39
  16.5 0.0 copy-done.4
  16.6 0.2 copy.37
  16.8 0.9 reshape.127.coef_ref
  17.7 0.2 reshape_reshape_squeeze.4.send_ref
  17.9 0.2 copy.36
  18.1 0.9 reshape.118.slot_ref
  19.0 37.5 %shard_map.174.adj_ref = bf16[1024,4096]{1,0:T(8,128)(2,1)} custom-call(s32[128,640]{1,0:T(8,128)} %reshape.118.slot_ref, f32[128,640]{1,0:T(8,128)} %reshape.127.coef_ref), custom_call_target="tpu_custom_call" | custom-call | tf_op jit(solution)/shard_map/pallas_call | solution.py:49
  56.5 19.5 %all-to-all-done = bf16[16,256,512]{2,1,0:T(8,128)(2,1)} async-done(((bf16[16,256,512]{2,1,0:T(8,128)(2,1)}), bf16[16,256,512]{2,1,0:T(8,128)(2,1)}, u32[]{:S(2)}, u32[]{:S(2)}) %all-to-all-start) | async-done | bytes 4194336 | tf_op jit(solution)/shard_map/all_to_all | solution.py:165
  76.0 13.4 %shard_map.175 = (bf16[1024,512]{1,0:T(8,128)(2,1)}, bf16[1024,512]{1,0:T(8,128)(2,1)}) custom-call(bf16[1024,4096]{1,0:T(8,128)(2,1)} %shard_map.174.adj_ref, bf16[4096,512]{1,0:T(8,128)(2,1)} %bitcast.3.table_ref, bf16[1024,512]{1,0:T(8,128)(2,1)S(1)} %convert_element_type.31.embed_ref, bf16[512,512]{1,0:T(8,128)(2,1)S(1)} %copy-done.1, ...), custom_call_target="tpu_custom_call" | custom-call | tf_op jit(solution)/shard_map/pallas_call | solution.py:92
  89.5 0.0 copy-start.11
  89.5 0.0 copy-start.8
  89.5 0.0 copy-start.5
  89.5 15.1 %all-to-all-start.1 = ((bf16[128,8,512]{2,1,0:T(8,128)(2,1)}), bf16[128,8,512]{2,1,0:T(8,128)(2,1)}, u32[]{:S(2)}, u32[]{:S(2)}) async-start(bf16[128,8,512]{2,1,0:T(8,128)(2,1)} %bitcast.7), calls=%async_computation.1 | async-start | bytes 2097152 | tf_op jit(solution)/shard_map/all_to_all | solution.py:175
  104.7 0.1 eq.63
  104.8 0.0 copy-done.10
  104.8 0.0 copy-done.11
  104.8 0.0 copy-done.8
  104.9 0.1 iota_compare_fusion.3
  104.9 1.0 fusion.20
  105.9 17.0 %all-to-all-done.1 = bf16[128,8,512]{2,1,0:T(8,128)(2,1)} async-done(((bf16[128,8,512]{2,1,0:T(8,128)(2,1)}), bf16[128,8,512]{2,1,0:T(8,128)(2,1)}, u32[]{:S(2)}, u32[]{:S(2)}) %all-to-all-start.1) | async-done | bytes 1048608 | tf_op jit(solution)/shard_map/all_to_all | solution.py:175
  123.0 2.5 %fusion.1 = f32[4,256,512]{2,1,0:T(8,128)S(1)} fusion(s32[4,256]{1,0:T(4,128)S(1)} %copy-done.8, bf16[128,8,512]{2,1,0:T(8,128)(2,1)} %all-to-all-done.1), kind=kOutput, calls=%fused_computation.7 | convolution fusion | flops 1074790400 | bytes 3149824 | tf_op jit(solution)/shard_map/dot_general | solution.py:181
  125.5 0.0 copy-start.12
  125.5 0.0 copy-start.13
  125.5 0.4 select_reduce_fusion.2
  125.9 0.0 copy-done
  125.9 0.2 fusion.14
  126.1 0.4 copy-done.12
  126.5 0.9 fusion.4
  127.4 0.1 fusion.25
  127.5 0.6 select_reduce_fusion.1
  128.1 0.7 all_to_all.14
  128.8 4.9 %all-to-all-start.2 = ((f32[128,1,8]{2,1,0:T(1,128)}), f32[128,1,8]{2,1,0:T(1,128)S(1)}, u32[]{:S(2)}, u32[]{:S(2)}) async-start(f32[128,1,8]{2,1,0:T(1,128)} %bitcast.12), calls=%async_computation.2 | async-start | bytes 131072 | tf_op jit(solution)/shard_map/all_to_all | solution.py:195
  133.7 0.7 divide_select_fusion
  134.4 9.0 %all-to-all-done.2 = f32[128,1,8]{2,1,0:T(1,128)S(1)} async-done(((f32[128,1,8]{2,1,0:T(1,128)}), f32[128,1,8]{2,1,0:T(1,128)S(1)}, u32[]{:S(2)}, u32[]{:S(2)}) %all-to-all-start.2) | async-done | bytes 4128 | tf_op jit(solution)/shard_map/all_to_all | solution.py:195
  143.4 0.5 broadcast.64
  143.9 0.8 reduce.3
  144.7 0.1 broadcast_in_dim.55
  144.8 1.1 select_reduce_fusion
  (24 shorter events, 0.1 us)
Async XLA Ops:
  0.6 125.3 %copy-start = (bf16[512,512]{1,0:T(8,128)(2,1)S(1)}, bf16[512,512]{1,0:T(8,128)(2,1)}, u32[]{:S(2)}) copy-start(bf16[512,512]{1,0:T(8,128)(2,1)} %param.27) | copy-start | bytes 1572868
  6.1 70.0 %all-to-all-start = ((bf16[16,256,512]{2,1,0:T(8,128)(2,1)}), bf16[16,256,512]{2,1,0:T(8,128)(2,1)}, u32[]{:S(2)}, u32[]{:S(2)}) async-start(bf16[16,256,512]{2,1,0:T(8,128)(2,1)} %bitcast.45), calls=%async_computation | async-start | bytes 8388608 | tf_op jit(solution)/shard_map/all_to_all | solution.py:165
  14.5 1.8 %copy-start.7 = (s32[1,128,8]{1,2,0:T(8,128)S(1)}, s32[1,128,8]{1,2,0:T(8,128)}, u32[]{:S(2)}) copy-start(s32[1,128,8]{1,2,0:T(8,128)} %param.19) | copy-start | bytes 12292
  14.6 1.9 %copy-start.4 = (f32[1024,80]{0,1:T(8,128)S(1)}, f32[1024,80]{0,1:T(8,128)}, u32[]{:S(2)}) copy-start(f32[1024,80]{0,1:T(8,128)} %param.17) | copy-start | bytes 983044
  16.4 1.5 %copy-start.6 = (s32[1024,80]{0,1:T(8,128)S(1)}, s32[1024,80]{0,1:T(8,128)}, u32[]{:S(2)}) copy-start(s32[1024,80]{0,1:T(8,128)} %param.16) | copy-start | bytes 983044
  19.0 57.0 %copy-start.1 = (bf16[512,512]{1,0:T(8,128)(2,1)S(1)}, bf16[512,512]{1,0:T(8,128)(2,1)}, u32[]{:S(2)}) copy-start(bf16[512,512]{1,0:T(8,128)(2,1)} %w_self_ref.1) | copy-start | bytes 1572868
  19.0 57.0 %copy-start.2 = (bf16[512,512]{1,0:T(8,128)(2,1)S(1)}, bf16[512,512]{1,0:T(8,128)(2,1)}, u32[]{:S(2)}) copy-start(bf16[512,512]{1,0:T(8,128)(2,1)} %w_nbr_ref.1) | copy-start | bytes 1572868
  19.0 57.0 %copy-start.3 = (f32[512]{0:T(512)S(1)}, f32[512]{0:T(512)}, u32[]{:S(2)}) copy-start(f32[512]{0:T(512)} %param.24) | copy-start | bytes 6148
  89.5 15.3 %copy-start.9 = (s32[4]{0:T(128)S(1)}, s32[4]{0:T(128)}, u32[]{:S(2)}) copy-start(s32[4]{0:T(128)} %param.21) | copy-start | bytes 52
  89.5 15.3 %copy-start.10 = (bf16[512]{0:T(512)(128)(2,1)S(1)}, bf16[512]{0:T(512)(128)(2,1)}, u32[]{:S(2)}) copy-start(bf16[512]{0:T(512)(128)(2,1)} %param.25) | copy-start | bytes 3076
  89.5 15.3 %copy-start.11 = (bf16[512]{0:T(512)(128)(2,1)S(1)}, bf16[512]{0:T(512)(128)(2,1)}, u32[]{:S(2)}) copy-start(bf16[512]{0:T(512)(128)(2,1)} %param.29) | copy-start | bytes 3076
  89.5 15.3 %copy-start.8 = (s32[4,256]{1,0:T(4,128)S(1)}, s32[4,256]{1,0:T(4,128)}, u32[]{:S(2)}) copy-start(s32[4,256]{1,0:T(4,128)} %param.20) | copy-start | bytes 12292
  89.5 15.4 %copy-start.5 = (bf16[1024,512]{1,0:T(8,128)(2,1)S(1)}, bf16[1024,512]{1,0:T(8,128)(2,1)}, u32[]{:S(2)}) copy-start(bf16[1024,512]{1,0:T(8,128)(2,1)} %get-tuple-element.2) | copy-start | bytes 3145732
  89.5 33.4 %all-to-all-start.1 = ((bf16[128,8,512]{2,1,0:T(8,128)(2,1)}), bf16[128,8,512]{2,1,0:T(8,128)(2,1)}, u32[]{:S(2)}, u32[]{:S(2)}) async-start(bf16[128,8,512]{2,1,0:T(8,128)(2,1)} %bitcast.7), calls=%async_computation.1 | async-start | bytes 2097152 | tf_op jit(solution)/shard_map/all_to_all | solution.py:175
  125.5 1.0 copy-start.12
  125.5 1.0 copy-start.13
  128.8 14.6 %all-to-all-start.2 = ((f32[128,1,8]{2,1,0:T(1,128)}), f32[128,1,8]{2,1,0:T(1,128)S(1)}, u32[]{:S(2)}, u32[]{:S(2)}) async-start(f32[128,1,8]{2,1,0:T(1,128)} %bitcast.12), calls=%async_computation.2 | async-start | bytes 131072 | tf_op jit(solution)/shard_map/all_to_all | solution.py:195

commit v13 on v12

--- a/solution.py
+++ b/solution.py
@@ -59,15 +59,11 @@
     )(slot_rows, coef_rows)
 
 
-def node_kernel(adj_ref, table_ref, embed_ref, w_self_ref, w_nbr_ref, bias_ref, send_ref, out_ref, outbound_ref, held_ref):
+def node_kernel(adj_ref, table_ref, self_ref, w_nbr_ref, send_ref, out_ref, outbound_ref, held_ref):
     b = pl.program_id(0)
     rows = out_ref.shape[0]
     total = jnp.dot(adj_ref[...], table_ref[...], preferred_element_type=jnp.float32)
-    pre = (
-        jnp.dot(embed_ref[...], w_self_ref[...], preferred_element_type=jnp.float32)
-        + bias_ref[...]
-        + jnp.dot(total.astype(jnp.bfloat16), w_nbr_ref[...], preferred_element_type=jnp.float32)
-    )
+    pre = self_ref[...] + jnp.dot(total.astype(jnp.bfloat16), w_nbr_ref[...], preferred_element_type=jnp.float32)
     hidden = jnp.maximum(pre, 0.0).astype(out_ref.dtype)
     out_ref[...] = hidden
     held_ref[pl.ds(pl.multiple_of(b * rows, rows), rows), :] = hidden
@@ -83,9 +79,8 @@
         )
 
 
-def node_layer(adjacency, table, embed_bf, w_self, w_nbr, bias, send_flat):
-    nodes, width = embed_bf.shape
-    hidden = w_self.shape[1]
+def node_layer(adjacency, table, self_term, w_nbr, send_flat):
+    nodes, hidden = self_term.shape
     columns = adjacency.shape[1]
     rows = 128
     slots = send_flat.shape[0]
@@ -95,10 +90,8 @@
         in_specs=[
             pl.BlockSpec((rows, columns), lambda b: (b, 0)),
             pl.BlockSpec(table.shape, lambda b: (0, 0)),
-            pl.BlockSpec((rows, width), lambda b: (b, 0)),
-            pl.BlockSpec(w_self.shape, lambda b: (0, 0)),
+            pl.BlockSpec((rows, hidden), lambda b: (b, 0)),
             pl.BlockSpec(w_nbr.shape, lambda b: (0, 0)),
-            pl.BlockSpec((1, hidden), lambda b: (0, 0)),
             pl.BlockSpec((slots, 1), lambda b: (0, 0)),
         ],
         out_specs=[
@@ -111,7 +104,7 @@
         ],
         scratch_shapes=[pltpu.VMEM((nodes, hidden), jnp.bfloat16)],
         compiler_params=pltpu.CompilerParams(vmem_limit_bytes=48 * 1024 * 1024),
-    )(adjacency, table, embed_bf, w_self, w_nbr, bias.reshape(1, hidden), send_flat.reshape(slots, 1))
+    )(adjacency, table, self_term, w_nbr, send_flat.reshape(slots, 1))
 
 
 def select_matrix(indices, count, dtype):
@@ -165,7 +158,8 @@
     provided = lax.all_to_all(outgoing, "shard", split_axis=0, concat_axis=0, tiled=True)
     provided = provided.reshape(column_total, width)
     send_flat = send_rows[0].reshape(send_rows.shape[1] * send_rows.shape[2])
-    node_hidden, outbound = node_layer(adjacency, provided, embed_bf, w_self, w_nbr, bias_v, send_flat)
+    self_term = jnp.dot(embed_bf, w_self, preferred_element_type=jnp.float32) + bias_v
+    node_hidden, outbound = node_layer(adjacency, provided, self_term, w_nbr, send_flat)
     confidence = jnp.dot(node_hidden, w_conf, preferred_element_type=jnp.float32)
     device_total = send_rows.shape[1]
     capacity = send_rows.shape[2]

time: 147 us -> 149 us (1.014)
  matrix products: 4.61 us -> 6.91 us
  local copies, waits for them, and re-layouts: 9.83 us -> 12.1 us
  other arithmetic: 5.56 us -> 3.79 us
    dot_general x0 -> x1, matrix products: none -> 2.3 us  [body(): jnp.dot(embed_bf, w_self, preferred_element_type=jnp.float32) + bias_v]
    unnamed x36 -> x38, local copies, waits for them, and re-layouts: 1.61 us -> 3.87 us
    convert_element_type x1 -> x0, other arithmetic: 1.77 us -> none  [body(): embed_bf = embed.astype(jnp.bfloat16)]
  transfers between devices with their start and end apart: 3 -> 3, of which waited for: 3 -> 3; matrix products, arithmetic and copies ran while one was open for 4% -> 5% of each run, Pallas kernels for 26% -> 25%
where the time goes in v13:
time: 149 us; the launch traced here: 148 us
  Pallas kernels  50.4 us (34%)
  waiting for transfers between devices  45.2 us (30%)
  starting transfers between devices  28.6 us (19%)
  local copies, waits for them, and re-layouts  12.1 us (8%)
  matrix products  6.91 us (5%)
  other arithmetic  3.79 us (3%)
    pallas_call x1, Pallas kernels, build_adjacency(): pl.pallas_call(adjacency_kernel, grid=(nodes // rows,), in_specs=[pl.Bloc...  37.4 us
    all_to_all x1, waiting for transfers between devices, body(): lax.all_to_all(outgoing, 'shard', split_axis=0, concat_axis=0, tiled=True)  19.1 us
    all_to_all x1, waiting for transfers between devices, body(): lax.all_to_all(outbound, ('grp', 'shard'), split_axis=0, concat_axis=0, t...  17 us
    all_to_all x1, starting transfers between devices, body(): lax.all_to_all(outbound, ('grp', 'shard'), split_axis=0, concat_axis=0, t...  15.1 us
    pallas_call x1, Pallas kernels, node_layer(): pl.pallas_call(node_kernel, grid=(nodes // rows,), in_specs=[pl.BlockSpec...  13 us
    all_to_all x1, waiting for transfers between devices, body(): lax.all_to_all(slot_scores, ('grp', 'shard'), split_axis=0, concat_axis=0...  8.99 us
    all_to_all x1, starting transfers between devices, body(): lax.all_to_all(outgoing, 'shard', split_axis=0, concat_axis=0, tiled=True)  8.61 us
    all_to_all x1, starting transfers between devices, body(): lax.all_to_all(slot_scores, ('grp', 'shard'), split_axis=0, concat_axis=0...  4.81 us
  transfers between devices with their start and end apart: 3, of which 3 were waited for; matrix products, arithmetic and copies ran while one was open for 5% of the time, Pallas kernels for 25%

profile of v13, /device:TPU:1, one launch (start us, length us, event | category | flops | bytes accessed | tf_op | source)
XLA Modules:
  0.0 147.8 jit_solution(10241756800150212939)
XLA Ops:
  0.6 0.0 copy-start
  0.6 0.8 copy.38
  1.5 0.1 reshape_squeeze.3
  1.6 4.5 %gather_fusion = bf16[32,128,512]{2,1,0:T(8,128)(2,1)} fusion(f32[8,128,512]{2,1,0:T(8,128)} %bitcast.44, s32[1024]{0:T(1024)S(1)} %pad_clamp_fusion), kind=kCustom, calls=%fused_computation | custom fusion | bytes 8388736 | tf_op jit(solution)/shard_map/gather | solution.py:155
  6.1 8.6 %all-to-all-start = ((bf16[16,256,512]{2,1,0:T(8,128)(2,1)}), bf16[16,256,512]{2,1,0:T(8,128)(2,1)}, u32[]{:S(2)}, u32[]{:S(2)}) async-start(bf16[16,256,512]{2,1,0:T(8,128)(2,1)} %bitcast.45), calls=%async_computation | async-start | bytes 8388608 | tf_op jit(solution)/shard_map/all_to_all | solution.py:158
  14.7 0.0 copy-done.7
  14.7 0.0 copy-start.6
  14.7 0.1 copy.39
  14.8 0.0 copy-done.3
  14.9 0.2 copy.37
  15.1 0.9 reshape.124.coef_ref
  16.0 0.2 reshape_reshape_squeeze.4.send_ref
  16.2 0.0 copy-done.6
  16.2 0.2 copy.36
  16.4 0.9 reshape.116.slot_ref
  17.3 37.4 %shard_map.174.adj_ref = bf16[1024,4096]{1,0:T(8,128)(2,1)} custom-call(s32[128,640]{1,0:T(8,128)} %reshape.116.slot_ref, f32[128,640]{1,0:T(8,128)} %reshape.124.coef_ref), custom_call_target="tpu_custom_call" | custom-call | tf_op jit(solution)/shard_map/pallas_call | solution.py:49
  54.7 2.3 %convolution_add_fusion.self_ref = f32[1024,512]{1,0:T(8,128)S(1)} fusion(bf16[512,512]{1,0:T(8,128)(2,1)S(1)} %copy-done, f32[512]{0:T(512)S(1)} %copy-done.9, f32[1024,512]{1,0:T(8,128)} %param.15), kind=kOutput, calls=%fused_computation.12 | convolution fusion | flops 537919488 | bytes 4720640 | tf_op jit(solution)/shard_map/dot_general | solution.py:161
  57.0 19.1 %all-to-all-done = bf16[16,256,512]{2,1,0:T(8,128)(2,1)} async-done(((bf16[16,256,512]{2,1,0:T(8,128)(2,1)}), bf16[16,256,512]{2,1,0:T(8,128)(2,1)}, u32[]{:S(2)}, u32[]{:S(2)}) %all-to-all-start) | async-done | bytes 4194336 | tf_op jit(solution)/shard_map/all_to_all | solution.py:158
  76.2 1.0 copy-done.2
  77.2 13.0 %shard_map.175 = (bf16[1024,512]{1,0:T(8,128)(2,1)}, bf16[1024,512]{1,0:T(8,128)(2,1)S(1)}) custom-call(bf16[1024,4096]{1,0:T(8,128)(2,1)} %shard_map.174.adj_ref, bf16[4096,512]{1,0:T(8,128)(2,1)} %bitcast.3.table_ref, f32[1024,512]{1,0:T(8,128)S(1)} %convolution_add_fusion.self_ref, bf16[512,512]{1,0:T(8,128)(2,1)S(1)} %copy-done.2, ...), custom_call_target="tpu_custom_call" | custom-call | tf_op jit(solution)/shard_map/pallas_call | solution.py:87
  90.2 1.0 copy-done.1
  91.3 0.0 copy-start.4
  91.3 15.1 %all-to-all-start.1 = ((bf16[128,8,512]{2,1,0:T(8,128)(2,1)}), bf16[128,8,512]{2,1,0:T(8,128)(2,1)}, u32[]{:S(2)}, u32[]{:S(2)}) async-start(bf16[128,8,512]{2,1,0:T(8,128)(2,1)} %bitcast.43), calls=%async_computation.1 | async-start | bytes 2097152 | tf_op jit(solution)/shard_map/all_to_all | solution.py:169
  106.4 0.1 eq.63
  106.6 0.0 copy-done.11
  106.6 0.0 copy-done.12
  106.6 0.0 copy-done.8
  106.6 0.1 iota_compare_fusion.3
  106.7 1.0 fusion.21
  107.7 17.0 %all-to-all-done.1 = bf16[128,8,512]{2,1,0:T(8,128)(2,1)} async-done(((bf16[128,8,512]{2,1,0:T(8,128)(2,1)}), bf16[128,8,512]{2,1,0:T(8,128)(2,1)}, u32[]{:S(2)}, u32[]{:S(2)}) %all-to-all-start.1) | async-done | bytes 1048608 | tf_op jit(solution)/shard_map/all_to_all | solution.py:169
  124.7 2.5 %fusion.1 = f32[4,256,512]{2,1,0:T(8,128)S(1)} fusion(s32[4,256]{1,0:T(4,128)S(1)} %copy-done.8, bf16[128,8,512]{2,1,0:T(8,128)(2,1)} %all-to-all-done.1), kind=kOutput, calls=%fused_computation.7 | convolution fusion | flops 1074790400 | bytes 3149824 | tf_op jit(solution)/shard_map/dot_general | solution.py:175
  127.2 0.0 copy-start.5
  127.2 0.0 copy-start.13
  127.3 0.0 copy-start.14
  127.3 0.4 select_reduce_fusion.2
  127.7 0.6 copy-done.5
  128.3 0.2 fusion.15
  128.5 0.9 fusion.4
  129.4 0.1 fusion.27
  129.5 0.6 select_reduce_fusion.1
  130.1 0.7 all_to_all.14
  130.8 4.8 %all-to-all-start.2 = ((f32[128,1,8]{2,1,0:T(1,128)}), f32[128,1,8]{2,1,0:T(1,128)S(1)}, u32[]{:S(2)}, u32[]{:S(2)}) async-start(f32[128,1,8]{2,1,0:T(1,128)} %bitcast.11), calls=%async_computation.2 | async-start | bytes 131072 | tf_op jit(solution)/shard_map/all_to_all | solution.py:189
  135.6 0.7 divide_select_fusion
  136.3 9.0 %all-to-all-done.2 = f32[128,1,8]{2,1,0:T(1,128)S(1)} async-done(((f32[128,1,8]{2,1,0:T(1,128)}), f32[128,1,8]{2,1,0:T(1,128)S(1)}, u32[]{:S(2)}, u32[]{:S(2)}) %all-to-all-start.2) | async-done | bytes 4128 | tf_op jit(solution)/shard_map/all_to_all | solution.py:189
  145.3 0.5 broadcast.65
  145.8 0.8 reduce.3
  146.6 0.1 broadcast_in_dim.56
  146.7 1.1 select_reduce_fusion
  (26 shorter events, 0.1 us)
Async XLA Ops:
  0.6 54.1 %copy-start = (bf16[512,512]{1,0:T(8,128)(2,1)S(1)}, bf16[512,512]{1,0:T(8,128)(2,1)}, u32[]{:S(2)}) copy-start(bf16[512,512]{1,0:T(8,128)(2,1)} %param.22) | copy-start | bytes 1572868
  6.1 8.6 %copy-start.7 = (s32[1,128,8]{1,2,0:T(8,128)S(1)}, s32[1,128,8]{1,2,0:T(8,128)}, u32[]{:S(2)}) copy-start(s32[1,128,8]{1,2,0:T(8,128)} %param.19) | copy-start | bytes 12292
  6.1 8.7 %copy-start.3 = (f32[1024,80]{0,1:T(8,128)S(1)}, f32[1024,80]{0,1:T(8,128)}, u32[]{:S(2)}) copy-start(f32[1024,80]{0,1:T(8,128)} %param.17) | copy-start | bytes 983044
  6.1 70.1 %all-to-all-start = ((bf16[16,256,512]{2,1,0:T(8,128)(2,1)}), bf16[16,256,512]{2,1,0:T(8,128)(2,1)}, u32[]{:S(2)}, u32[]{:S(2)}) async-start(bf16[16,256,512]{2,1,0:T(8,128)(2,1)} %bitcast.45), calls=%async_computation | async-start | bytes 8388608 | tf_op jit(solution)/shard_map/all_to_all | solution.py:158
  14.7 1.5 %copy-start.6 = (s32[1024,80]{0,1:T(8,128)S(1)}, s32[1024,80]{0,1:T(8,128)}, u32[]{:S(2)}) copy-start(s32[1024,80]{0,1:T(8,128)} %param.16) | copy-start | bytes 983044
  17.3 37.4 %copy-start.9 = (f32[512]{0:T(512)S(1)}, f32[512]{0:T(512)}, u32[]{:S(2)}) copy-start(f32[512]{0:T(512)} %param.24) | copy-start | bytes 6148
  76.2 1.0 copy-start.2
  90.2 1.0 copy-start.1
  91.3 15.3 %copy-start.10 = (s32[4]{0:T(128)S(1)}, s32[4]{0:T(128)}, u32[]{:S(2)}) copy-start(s32[4]{0:T(128)} %param.21) | copy-start | bytes 52
  91.3 15.3 %copy-start.11 = (bf16[512]{0:T(512)(128)(2,1)S(1)}, bf16[512]{0:T(512)(128)(2,1)}, u32[]{:S(2)}) copy-start(bf16[512]{0:T(512)(128)(2,1)} %param.25) | copy-start | bytes 3076
  91.3 15.3 %copy-start.12 = (bf16[512]{0:T(512)(128)(2,1)S(1)}, bf16[512]{0:T(512)(128)(2,1)}, u32[]{:S(2)}) copy-start(bf16[512]{0:T(512)(128)(2,1)} %param.29) | copy-start | bytes 3076
  91.3 15.3 %copy-start.8 = (s32[4,256]{1,0:T(4,128)S(1)}, s32[4,256]{1,0:T(4,128)}, u32[]{:S(2)}) copy-start(s32[4,256]{1,0:T(4,128)} %param.20) | copy-start | bytes 12292
  91.3 15.4 %copy-start.4 = (bf16[1024,512]{1,0:T(8,128)(2,1)S(1)}, bf16[1024,512]{1,0:T(8,128)(2,1)}, u32[]{:S(2)}) copy-start(bf16[1024,512]{1,0:T(8,128)(2,1)} %get-tuple-element.2) | copy-start | bytes 3145732
  91.3 33.4 %all-to-all-start.1 = ((bf16[128,8,512]{2,1,0:T(8,128)(2,1)}), bf16[128,8,512]{2,1,0:T(8,128)(2,1)}, u32[]{:S(2)}, u32[]{:S(2)}) async-start(bf16[128,8,512]{2,1,0:T(8,128)(2,1)} %bitcast.43), calls=%async_computation.1 | async-start | bytes 2097152 | tf_op jit(solution)/shard_map/all_to_all | solution.py:169
  127.2 1.0 copy-start.5
  127.2 1.2 copy-start.13
  127.3 1.2 copy-start.14
  130.8 14.5 %all-to-all-start.2 = ((f32[128,1,8]{2,1,0:T(1,128)}), f32[128,1,8]{2,1,0:T(1,128)S(1)}, u32[]{:S(2)}, u32[]{:S(2)}) async-start(f32[128,1,8]{2,1,0:T(1,128)} %bitcast.11), calls=%async_computation.2 | async-start | bytes 131072 | tf_op jit(solution)/shard_map/all_to_all | solution.py:189

commit v14 on v12

--- a/solution.py
+++ b/solution.py
@@ -87,7 +87,7 @@
     nodes, width = embed_bf.shape
     hidden = w_self.shape[1]
     columns = adjacency.shape[1]
-    rows = 128
+    rows = 256
     slots = send_flat.shape[0]
     return pl.pallas_call(
         node_kernel,

time: 147 us -> 145 us (0.986)
  Pallas kernels: 50.9 us -> 49.1 us
    pallas_call x1, Pallas kernels: 13.4 us -> 11.6 us  [node_layer(): pl.pallas_call(node_kernel, grid=(nodes // rows,), in_specs=[pl.BlockSpec...]
where the time goes in v14:
time: 145 us; the launch traced here: 144 us
  Pallas kernels  49.1 us (34%)
  waiting for transfers between devices  45.6 us (31%)
  starting transfers between devices  28.5 us (20%)
  local copies, waits for them, and re-layouts  9.83 us (7%)
  other arithmetic  5.56 us (4%)
  matrix products  4.6 us (3%)
    pallas_call x1, Pallas kernels, build_adjacency(): pl.pallas_call(adjacency_kernel, grid=(nodes // rows,), in_specs=[pl.Bloc...  37.5 us
    all_to_all x1, waiting for transfers between devices, body(): lax.all_to_all(outgoing, 'shard', split_axis=0, concat_axis=0, tiled=True)  19.5 us
    all_to_all x1, waiting for transfers between devices, body(): lax.all_to_all(outbound, ('grp', 'shard'), split_axis=0, concat_axis=0, t...  17 us
    all_to_all x1, starting transfers between devices, body(): lax.all_to_all(outbound, ('grp', 'shard'), split_axis=0, concat_axis=0, t...  15.1 us
    pallas_call x1, Pallas kernels, node_layer(): pl.pallas_call(node_kernel, grid=(nodes // rows,), in_specs=[pl.BlockSpec...  11.6 us
    all_to_all x1, waiting for transfers between devices, body(): lax.all_to_all(slot_scores, ('grp', 'shard'), split_axis=0, concat_axis=0...  9 us
    all_to_all x1, starting transfers between devices, body(): lax.all_to_all(outgoing, 'shard', split_axis=0, concat_axis=0, tiled=True)  8.48 us
    all_to_all x1, starting transfers between devices, body(): lax.all_to_all(slot_scores, ('grp', 'shard'), split_axis=0, concat_axis=0...  4.9 us
  transfers between devices with their start and end apart: 3, of which 3 were waited for; matrix products, arithmetic and copies ran while one was open for 4% of the time, Pallas kernels for 26%

profile of v14, /device:TPU:1, one launch (start us, length us, event | category | flops | bytes accessed | tf_op | source)
XLA Modules:
  0.0 144.1 jit_solution(17886056141851518724)
XLA Ops:
  0.6 0.0 copy-start
  0.6 0.8 copy.38
  1.5 0.1 reshape_squeeze.3
  1.6 4.5 %gather_fusion = bf16[32,128,512]{2,1,0:T(8,128)(2,1)} fusion(f32[8,128,512]{2,1,0:T(8,128)} %bitcast.44, s32[1024]{0:T(1024)S(1)} %pad_clamp_fusion), kind=kCustom, calls=%fused_computation | custom fusion | bytes 8388736 | tf_op jit(solution)/shard_map/gather | solution.py:162
  6.1 8.5 %all-to-all-start = ((bf16[16,256,512]{2,1,0:T(8,128)(2,1)}), bf16[16,256,512]{2,1,0:T(8,128)(2,1)}, u32[]{:S(2)}, u32[]{:S(2)}) async-start(bf16[16,256,512]{2,1,0:T(8,128)(2,1)} %bitcast.45), calls=%async_computation | async-start | bytes 8388608 | tf_op jit(solution)/shard_map/all_to_all | solution.py:165
  14.5 0.0 copy-start.7
  14.6 0.0 copy-start.4
  14.6 1.8 %convert_element_type.31.embed_ref = bf16[1024,512]{1,0:T(8,128)(2,1)S(1)} convert(f32[1024,512]{1,0:T(8,128)} %param.15) | non-fusion elementwise | flops 524288 | bytes 3145728 | tf_op jit(solution)/shard_map/convert_element_type | solution.py:150
  16.3 0.0 copy-done.7
  16.4 0.0 copy-start.6
  16.4 0.1 copy.39
  16.5 0.0 copy-done.4
  16.6 0.2 copy.37
  16.8 0.9 reshape.127.coef_ref
  17.7 0.2 reshape_reshape_squeeze.4.send_ref
  17.9 0.0 copy-done.6
  17.9 0.2 copy.36
  18.1 0.9 reshape.118.slot_ref
  19.0 37.5 %shard_map.174.adj_ref = bf16[1024,4096]{1,0:T(8,128)(2,1)} custom-call(s32[128,640]{1,0:T(8,128)} %reshape.118.slot_ref, f32[128,640]{1,0:T(8,128)} %reshape.127.coef_ref), custom_call_target="tpu_custom_call" | custom-call | tf_op jit(solution)/shard_map/pallas_call | solution.py:49
  56.5 19.5 %all-to-all-done = bf16[16,256,512]{2,1,0:T(8,128)(2,1)} async-done(((bf16[16,256,512]{2,1,0:T(8,128)(2,1)}), bf16[16,256,512]{2,1,0:T(8,128)(2,1)}, u32[]{:S(2)}, u32[]{:S(2)}) %all-to-all-start) | async-done | bytes 4194336 | tf_op jit(solution)/shard_map/all_to_all | solution.py:165
  76.0 0.0 copy-done.1
  76.0 11.6 %shard_map.175 = (bf16[1024,512]{1,0:T(8,128)(2,1)}, bf16[1024,512]{1,0:T(8,128)(2,1)}) custom-call(bf16[1024,4096]{1,0:T(8,128)(2,1)} %shard_map.174.adj_ref, bf16[4096,512]{1,0:T(8,128)(2,1)} %bitcast.3.table_ref, bf16[1024,512]{1,0:T(8,128)(2,1)S(1)} %convert_element_type.31.embed_ref, bf16[512,512]{1,0:T(8,128)(2,1)S(1)} %copy-done.1, ...), custom_call_target="tpu_custom_call" | custom-call | tf_op jit(solution)/shard_map/pallas_call | solution.py:92
  87.6 0.0 copy-start.11
  87.6 0.0 copy-start.8
  87.7 0.0 copy-start.5
  87.7 15.1 %all-to-all-start.1 = ((bf16[128,8,512]{2,1,0:T(8,128)(2,1)}), bf16[128,8,512]{2,1,0:T(8,128)(2,1)}, u32[]{:S(2)}, u32[]{:S(2)}) async-start(bf16[128,8,512]{2,1,0:T(8,128)(2,1)} %bitcast.7), calls=%async_computation.1 | async-start | bytes 2097152 | tf_op jit(solution)/shard_map/all_to_all | solution.py:175
  102.8 0.1 eq.63
  103.0 0.1 iota_compare_fusion.3
  103.1 1.0 fusion.20
  104.1 17.0 %all-to-all-done.1 = bf16[128,8,512]{2,1,0:T(8,128)(2,1)} async-done(((bf16[128,8,512]{2,1,0:T(8,128)(2,1)}), bf16[128,8,512]{2,1,0:T(8,128)(2,1)}, u32[]{:S(2)}, u32[]{:S(2)}) %all-to-all-start.1) | async-done | bytes 1048608 | tf_op jit(solution)/shard_map/all_to_all | solution.py:175
  121.1 2.5 %fusion.1 = f32[4,256,512]{2,1,0:T(8,128)S(1)} fusion(s32[4,256]{1,0:T(4,128)S(1)} %copy-done.8, bf16[128,8,512]{2,1,0:T(8,128)(2,1)} %all-to-all-done.1), kind=kOutput, calls=%fused_computation.7 | convolution fusion | flops 1074790400 | bytes 3149824 | tf_op jit(solution)/shard_map/dot_general | solution.py:181
  123.6 0.0 copy-start.12
  123.6 0.0 copy-start.13
  123.7 0.4 select_reduce_fusion.2
  124.0 0.0 copy-done
  124.1 0.2 fusion.14
  124.3 0.4 copy-done.12
  124.7 0.9 fusion.4
  125.6 0.1 fusion.25
  125.6 0.6 select_reduce_fusion.1
  126.2 0.7 all_to_all.14
  126.9 4.9 %all-to-all-start.2 = ((f32[128,1,8]{2,1,0:T(1,128)}), f32[128,1,8]{2,1,0:T(1,128)S(1)}, u32[]{:S(2)}, u32[]{:S(2)}) async-start(f32[128,1,8]{2,1,0:T(1,128)} %bitcast.12), calls=%async_computation.2 | async-start | bytes 131072 | tf_op jit(solution)/shard_map/all_to_all | solution.py:195
  131.9 0.7 divide_select_fusion
  132.5 9.0 %all-to-all-done.2 = f32[128,1,8]{2,1,0:T(1,128)S(1)} async-done(((f32[128,1,8]{2,1,0:T(1,128)}), f32[128,1,8]{2,1,0:T(1,128)S(1)}, u32[]{:S(2)}, u32[]{:S(2)}) %all-to-all-start.2) | async-done | bytes 4128 | tf_op jit(solution)/shard_map/all_to_all | solution.py:195
  141.5 0.5 broadcast.64
  142.0 0.8 reduce.3
  142.8 0.1 broadcast_in_dim.55
  142.9 1.1 select_reduce_fusion
  (24 shorter events, 0.1 us)
Async XLA Ops:
  0.6 123.4 %copy-start = (bf16[512,512]{1,0:T(8,128)(2,1)S(1)}, bf16[512,512]{1,0:T(8,128)(2,1)}, u32[]{:S(2)}) copy-start(bf16[512,512]{1,0:T(8,128)(2,1)} %param.27) | copy-start | bytes 1572868
  6.1 70.0 %all-to-all-start = ((bf16[16,256,512]{2,1,0:T(8,128)(2,1)}), bf16[16,256,512]{2,1,0:T(8,128)(2,1)}, u32[]{:S(2)}, u32[]{:S(2)}) async-start(bf16[16,256,512]{2,1,0:T(8,128)(2,1)} %bitcast.45), calls=%async_computation | async-start | bytes 8388608 | tf_op jit(solution)/shard_map/all_to_all | solution.py:165
  14.5 1.8 %copy-start.7 = (s32[1,128,8]{1,2,0:T(8,128)S(1)}, s32[1,128,8]{1,2,0:T(8,128)}, u32[]{:S(2)}) copy-start(s32[1,128,8]{1,2,0:T(8,128)} %param.19) | copy-start | bytes 12292
  14.6 1.9 %copy-start.4 = (f32[1024,80]{0,1:T(8,128)S(1)}, f32[1024,80]{0,1:T(8,128)}, u32[]{:S(2)}) copy-start(f32[1024,80]{0,1:T(8,128)} %param.17) | copy-start | bytes 983044
  16.4 1.5 %copy-start.6 = (s32[1024,80]{0,1:T(8,128)S(1)}, s32[1024,80]{0,1:T(8,128)}, u32[]{:S(2)}) copy-start(s32[1024,80]{0,1:T(8,128)} %param.16) | copy-start | bytes 983044
  19.0 57.0 %copy-start.1 = (bf16[512,512]{1,0:T(8,128)(2,1)S(1)}, bf16[512,512]{1,0:T(8,128)(2,1)}, u32[]{:S(2)}) copy-start(bf16[512,512]{1,0:T(8,128)(2,1)} %w_self_ref.1) | copy-start | bytes 1572868
  19.0 57.0 %copy-start.2 = (bf16[512,512]{1,0:T(8,128)(2,1)S(1)}, bf16[512,512]{1,0:T(8,128)(2,1)}, u32[]{:S(2)}) copy-start(bf16[512,512]{1,0:T(8,128)(2,1)} %w_nbr_ref.1) | copy-start | bytes 1572868
  19.0 57.0 %copy-start.3 = (f32[512]{0:T(512)S(1)}, f32[512]{0:T(512)}, u32[]{:S(2)}) copy-start(f32[512]{0:T(512)} %param.24) | copy-start | bytes 6148
  87.6 15.3 %copy-start.9 = (s32[4]{0:T(128)S(1)}, s32[4]{0:T(128)}, u32[]{:S(2)}) copy-start(s32[4]{0:T(128)} %param.21) | copy-start | bytes 52
  87.6 15.3 %copy-start.10 = (bf16[512]{0:T(512)(128)(2,1)S(1)}, bf16[512]{0:T(512)(128)(2,1)}, u32[]{:S(2)}) copy-start(bf16[512]{0:T(512)(128)(2,1)} %param.25) | copy-start | bytes 3076
  87.6 15.3 %copy-start.11 = (bf16[512]{0:T(512)(128)(2,1)S(1)}, bf16[512]{0:T(512)(128)(2,1)}, u32[]{:S(2)}) copy-start(bf16[512]{0:T(512)(128)(2,1)} %param.29) | copy-start | bytes 3076
  87.6 15.3 %copy-start.8 = (s32[4,256]{1,0:T(4,128)S(1)}, s32[4,256]{1,0:T(4,128)}, u32[]{:S(2)}) copy-start(s32[4,256]{1,0:T(4,128)} %param.20) | copy-start | bytes 12292
  87.7 15.4 %copy-start.5 = (bf16[1024,512]{1,0:T(8,128)(2,1)S(1)}, bf16[1024,512]{1,0:T(8,128)(2,1)}, u32[]{:S(2)}) copy-start(bf16[1024,512]{1,0:T(8,128)(2,1)} %get-tuple-element.2) | copy-start | bytes 3145732
  87.7 33.4 %all-to-all-start.1 = ((bf16[128,8,512]{2,1,0:T(8,128)(2,1)}), bf16[128,8,512]{2,1,0:T(8,128)(2,1)}, u32[]{:S(2)}, u32[]{:S(2)}) async-start(bf16[128,8,512]{2,1,0:T(8,128)(2,1)} %bitcast.7), calls=%async_computation.1 | async-start | bytes 2097152 | tf_op jit(solution)/shard_map/all_to_all | solution.py:175
  123.6 1.0 copy-start.12
  123.6 1.0 copy-start.13
  126.9 14.6 %all-to-all-start.2 = ((f32[128,1,8]{2,1,0:T(1,128)}), f32[128,1,8]{2,1,0:T(1,128)S(1)}, u32[]{:S(2)}, u32[]{:S(2)}) async-start(f32[128,1,8]{2,1,0:T(1,128)} %bitcast.12), calls=%async_computation.2 | async-start | bytes 131072 | tf_op jit(solution)/shard_map/all_to_all | solution.py:195

commit v15 on v14

--- a/solution.py
+++ b/solution.py
@@ -87,7 +87,7 @@
     nodes, width = embed_bf.shape
     hidden = w_self.shape[1]
     columns = adjacency.shape[1]
-    rows = 256
+    rows = 512
     slots = send_flat.shape[0]
     return pl.pallas_call(
         node_kernel,

time: 145 us -> 145 us (level)
  no operation moved by 1% of the time
where the time goes in v15:
time: 145 us; the launch traced here: 144 us
  Pallas kernels  49.2 us (34%)
  waiting for transfers between devices  45.6 us (31%)
  starting transfers between devices  28.5 us (20%)
  local copies, waits for them, and re-layouts  9.83 us (7%)
  other arithmetic  5.56 us (4%)
  matrix products  4.61 us (3%)
    pallas_call x1, Pallas kernels, build_adjacency(): pl.pallas_call(adjacency_kernel, grid=(nodes // rows,), in_specs=[pl.Bloc...  37.5 us
    all_to_all x1, waiting for transfers between devices, body(): lax.all_to_all(outgoing, 'shard', split_axis=0, concat_axis=0, tiled=True)  19.5 us
    all_to_all x1, waiting for transfers between devices, body(): lax.all_to_all(outbound, ('grp', 'shard'), split_axis=0, concat_axis=0, t...  17 us
    all_to_all x1, starting transfers between devices, body(): lax.all_to_all(outbound, ('grp', 'shard'), split_axis=0, concat_axis=0, t...  15.1 us
    pallas_call x1, Pallas kernels, node_layer(): pl.pallas_call(node_kernel, grid=(nodes // rows,), in_specs=[pl.BlockSpec...  11.8 us
    all_to_all x1, waiting for transfers between devices, body(): lax.all_to_all(slot_scores, ('grp', 'shard'), split_axis=0, concat_axis=0...  9 us
    all_to_all x1, starting transfers between devices, body(): lax.all_to_all(outgoing, 'shard', split_axis=0, concat_axis=0, tiled=True)  8.48 us
    all_to_all x1, starting transfers between devices, body(): lax.all_to_all(slot_scores, ('grp', 'shard'), split_axis=0, concat_axis=0...  4.9 us
  transfers between devices with their start and end apart: 3, of which 3 were waited for; matrix products, arithmetic and copies ran while one was open for 4% of the time, Pallas kernels for 26%

profile of v15, /device:TPU:1, one launch (start us, length us, event | category | flops | bytes accessed | tf_op | source)
XLA Modules:
  0.0 144.3 jit_solution(6088484021178668368)
XLA Ops:
  0.6 0.0 copy-start
  0.6 0.8 copy.38
  1.5 0.1 reshape_squeeze.3
  1.6 4.5 %gather_fusion = bf16[32,128,512]{2,1,0:T(8,128)(2,1)} fusion(f32[8,128,512]{2,1,0:T(8,128)} %bitcast.44, s32[1024]{0:T(1024)S(1)} %pad_clamp_fusion), kind=kCustom, calls=%fused_computation | custom fusion | bytes 8388736 | tf_op jit(solution)/shard_map/gather | solution.py:162
  6.1 8.5 %all-to-all-start = ((bf16[16,256,512]{2,1,0:T(8,128)(2,1)}), bf16[16,256,512]{2,1,0:T(8,128)(2,1)}, u32[]{:S(2)}, u32[]{:S(2)}) async-start(bf16[16,256,512]{2,1,0:T(8,128)(2,1)} %bitcast.45), calls=%async_computation | async-start | bytes 8388608 | tf_op jit(solution)/shard_map/all_to_all | solution.py:165
  14.5 0.0 copy-start.7
  14.6 0.0 copy-start.4
  14.6 1.8 %convert_element_type.31.embed_ref = bf16[1024,512]{1,0:T(8,128)(2,1)S(1)} convert(f32[1024,512]{1,0:T(8,128)} %param.15) | non-fusion elementwise | flops 524288 | bytes 3145728 | tf_op jit(solution)/shard_map/convert_element_type | solution.py:150
  16.3 0.0 copy-done.7
  16.4 0.0 copy-start.6
  16.4 0.1 copy.39
  16.5 0.0 copy-done.4
  16.6 0.2 copy.37
  16.8 0.9 reshape.127.coef_ref
  17.7 0.2 reshape_reshape_squeeze.4.send_ref
  17.9 0.0 copy-done.6
  17.9 0.2 copy.36
  18.1 0.9 reshape.118.slot_ref
  19.0 37.5 %shard_map.174.adj_ref = bf16[1024,4096]{1,0:T(8,128)(2,1)} custom-call(s32[128,640]{1,0:T(8,128)} %reshape.118.slot_ref, f32[128,640]{1,0:T(8,128)} %reshape.127.coef_ref), custom_call_target="tpu_custom_call" | custom-call | tf_op jit(solution)/shard_map/pallas_call | solution.py:49
  56.5 19.5 %all-to-all-done = bf16[16,256,512]{2,1,0:T(8,128)(2,1)} async-done(((bf16[16,256,512]{2,1,0:T(8,128)(2,1)}), bf16[16,256,512]{2,1,0:T(8,128)(2,1)}, u32[]{:S(2)}, u32[]{:S(2)}) %all-to-all-start) | async-done | bytes 4194336 | tf_op jit(solution)/shard_map/all_to_all | solution.py:165
  76.0 0.0 copy-done.1
  76.0 11.8 %shard_map.175 = (bf16[1024,512]{1,0:T(8,128)(2,1)}, bf16[1024,512]{1,0:T(8,128)(2,1)}) custom-call(bf16[1024,4096]{1,0:T(8,128)(2,1)} %shard_map.174.adj_ref, bf16[4096,512]{1,0:T(8,128)(2,1)} %bitcast.3.table_ref, bf16[1024,512]{1,0:T(8,128)(2,1)S(1)} %convert_element_type.31.embed_ref, bf16[512,512]{1,0:T(8,128)(2,1)S(1)} %copy-done.1, ...), custom_call_target="tpu_custom_call" | custom-call | tf_op jit(solution)/shard_map/pallas_call | solution.py:92
  87.8 0.0 copy-start.11
  87.8 0.0 copy-start.8
  87.8 0.0 copy-start.5
  87.8 15.1 %all-to-all-start.1 = ((bf16[128,8,512]{2,1,0:T(8,128)(2,1)}), bf16[128,8,512]{2,1,0:T(8,128)(2,1)}, u32[]{:S(2)}, u32[]{:S(2)}) async-start(bf16[128,8,512]{2,1,0:T(8,128)(2,1)} %bitcast.7), calls=%async_computation.1 | async-start | bytes 2097152 | tf_op jit(solution)/shard_map/all_to_all | solution.py:175
  103.0 0.1 eq.63
  103.2 0.1 iota_compare_fusion.3
  103.3 1.0 fusion.20
  104.2 17.0 %all-to-all-done.1 = bf16[128,8,512]{2,1,0:T(8,128)(2,1)} async-done(((bf16[128,8,512]{2,1,0:T(8,128)(2,1)}), bf16[128,8,512]{2,1,0:T(8,128)(2,1)}, u32[]{:S(2)}, u32[]{:S(2)}) %all-to-all-start.1) | async-done | bytes 1048608 | tf_op jit(solution)/shard_map/all_to_all | solution.py:175
  121.3 2.5 %fusion.1 = f32[4,256,512]{2,1,0:T(8,128)S(1)} fusion(s32[4,256]{1,0:T(4,128)S(1)} %copy-done.8, bf16[128,8,512]{2,1,0:T(8,128)(2,1)} %all-to-all-done.1), kind=kOutput, calls=%fused_computation.7 | convolution fusion | flops 1074790400 | bytes 3149824 | tf_op jit(solution)/shard_map/dot_general | solution.py:181
  123.8 0.0 copy-start.12
  123.8 0.0 copy-start.13
  123.8 0.4 select_reduce_fusion.2
  124.2 0.2 fusion.14
  124.4 0.4 copy-done.12
  124.8 0.0 copy-done.13
  124.8 0.9 fusion.4
  125.7 0.1 fusion.25
  125.8 0.6 select_reduce_fusion.1
  126.4 0.7 all_to_all.14
  127.1 4.9 %all-to-all-start.2 = ((f32[128,1,8]{2,1,0:T(1,128)}), f32[128,1,8]{2,1,0:T(1,128)S(1)}, u32[]{:S(2)}, u32[]{:S(2)}) async-start(f32[128,1,8]{2,1,0:T(1,128)} %bitcast.12), calls=%async_computation.2 | async-start | bytes 131072 | tf_op jit(solution)/shard_map/all_to_all | solution.py:195
  132.0 0.7 divide_select_fusion
  132.7 9.0 %all-to-all-done.2 = f32[128,1,8]{2,1,0:T(1,128)S(1)} async-done(((f32[128,1,8]{2,1,0:T(1,128)}), f32[128,1,8]{2,1,0:T(1,128)S(1)}, u32[]{:S(2)}, u32[]{:S(2)}) %all-to-all-start.2) | async-done | bytes 4128 | tf_op jit(solution)/shard_map/all_to_all | solution.py:195
  141.7 0.5 broadcast.64
  142.2 0.8 reduce.3
  143.0 0.1 broadcast_in_dim.55
  143.1 1.1 select_reduce_fusion
  (24 shorter events, 0.1 us)
Async XLA Ops:
  0.6 123.6 %copy-start = (bf16[512,512]{1,0:T(8,128)(2,1)S(1)}, bf16[512,512]{1,0:T(8,128)(2,1)}, u32[]{:S(2)}) copy-start(bf16[512,512]{1,0:T(8,128)(2,1)} %param.27) | copy-start | bytes 1572868
  6.1 70.0 %all-to-all-start = ((bf16[16,256,512]{2,1,0:T(8,128)(2,1)}), bf16[16,256,512]{2,1,0:T(8,128)(2,1)}, u32[]{:S(2)}, u32[]{:S(2)}) async-start(bf16[16,256,512]{2,1,0:T(8,128)(2,1)} %bitcast.45), calls=%async_computation | async-start | bytes 8388608 | tf_op jit(solution)/shard_map/all_to_all | solution.py:165
  14.5 1.8 %copy-start.7 = (s32[1,128,8]{1,2,0:T(8,128)S(1)}, s32[1,128,8]{1,2,0:T(8,128)}, u32[]{:S(2)}) copy-start(s32[1,128,8]{1,2,0:T(8,128)} %param.19) | copy-start | bytes 12292
  14.6 1.9 %copy-start.4 = (f32[1024,80]{0,1:T(8,128)S(1)}, f32[1024,80]{0,1:T(8,128)}, u32[]{:S(2)}) copy-start(f32[1024,80]{0,1:T(8,128)} %param.17) | copy-start | bytes 983044
  16.4 1.5 %copy-start.6 = (s32[1024,80]{0,1:T(8,128)S(1)}, s32[1024,80]{0,1:T(8,128)}, u32[]{:S(2)}) copy-start(s32[1024,80]{0,1:T(8,128)} %param.16) | copy-start | bytes 983044
  19.0 57.0 %copy-start.1 = (bf16[512,512]{1,0:T(8,128)(2,1)S(1)}, bf16[512,512]{1,0:T(8,128)(2,1)}, u32[]{:S(2)}) copy-start(bf16[512,512]{1,0:T(8,128)(2,1)} %w_self_ref.1) | copy-start | bytes 1572868
  19.0 57.0 %copy-start.2 = (bf16[512,512]{1,0:T(8,128)(2,1)S(1)}, bf16[512,512]{1,0:T(8,128)(2,1)}, u32[]{:S(2)}) copy-start(bf16[512,512]{1,0:T(8,128)(2,1)} %w_nbr_ref.1) | copy-start | bytes 1572868
  19.0 57.0 %copy-start.3 = (f32[512]{0:T(512)S(1)}, f32[512]{0:T(512)}, u32[]{:S(2)}) copy-start(f32[512]{0:T(512)} %param.24) | copy-start | bytes 6148
  87.8 15.3 %copy-start.9 = (s32[4]{0:T(128)S(1)}, s32[4]{0:T(128)}, u32[]{:S(2)}) copy-start(s32[4]{0:T(128)} %param.21) | copy-start | bytes 52
  87.8 15.3 %copy-start.10 = (bf16[512]{0:T(512)(128)(2,1)S(1)}, bf16[512]{0:T(512)(128)(2,1)}, u32[]{:S(2)}) copy-start(bf16[512]{0:T(512)(128)(2,1)} %param.25) | copy-start | bytes 3076
  87.8 15.3 %copy-start.11 = (bf16[512]{0:T(512)(128)(2,1)S(1)}, bf16[512]{0:T(512)(128)(2,1)}, u32[]{:S(2)}) copy-start(bf16[512]{0:T(512)(128)(2,1)} %param.29) | copy-start | bytes 3076
  87.8 15.3 %copy-start.8 = (s32[4,256]{1,0:T(4,128)S(1)}, s32[4,256]{1,0:T(4,128)}, u32[]{:S(2)}) copy-start(s32[4,256]{1,0:T(4,128)} %param.20) | copy-start | bytes 12292
  87.8 15.4 %copy-start.5 = (bf16[1024,512]{1,0:T(8,128)(2,1)S(1)}, bf16[1024,512]{1,0:T(8,128)(2,1)}, u32[]{:S(2)}) copy-start(bf16[1024,512]{1,0:T(8,128)(2,1)} %get-tuple-element.2) | copy-start | bytes 3145732
  87.8 33.4 %all-to-all-start.1 = ((bf16[128,8,512]{2,1,0:T(8,128)(2,1)}), bf16[128,8,512]{2,1,0:T(8,128)(2,1)}, u32[]{:S(2)}, u32[]{:S(2)}) async-start(bf16[128,8,512]{2,1,0:T(8,128)(2,1)} %bitcast.7), calls=%async_computation.1 | async-start | bytes 2097152 | tf_op jit(solution)/shard_map/all_to_all | solution.py:175
  123.8 1.0 copy-start.12
  123.8 1.0 copy-start.13
  127.1 14.6 %all-to-all-start.2 = ((f32[128,1,8]{2,1,0:T(1,128)}), f32[128,1,8]{2,1,0:T(1,128)S(1)}, u32[]{:S(2)}, u32[]{:S(2)}) async-start(f32[128,1,8]{2,1,0:T(1,128)} %bitcast.12), calls=%async_computation.2 | async-start | bytes 131072 | tf_op jit(solution)/shard_map/all_to_all | solution.py:195

commit v16 on v10

--- a/solution.py
+++ b/solution.py
@@ -68,7 +68,7 @@
 def node_layer(adjacency, table, self_term, w_nbr):
     count, columns = adjacency.shape
     hidden = w_nbr.shape[1]
-    rows = 128
+    rows = 256
     return pl.pallas_call(
         node_kernel,
         grid=(count // rows,),
@@ -128,8 +128,9 @@
         column_total,
     )
     tile_count = nodes // TILE
-    embed_tiles = embed_bf.reshape(tile_count, TILE, width)
+    embed_tiles = embed.reshape(tile_count, TILE, width)
     outgoing = embed_tiles.at[tile_list[0].reshape(shard_count * list_len)].get(mode="promise_in_bounds")
+    outgoing = outgoing.astype(jnp.bfloat16)
     outgoing = outgoing.reshape(shard_count, peer_span, width)
     provided = lax.all_to_all(outgoing, "shard", split_axis=0, concat_axis=0, tiled=True)
     provided = provided.reshape(column_total, width)

time: 147 us -> 144 us (0.980)
  Pallas kernels: 60.9 us -> 56.8 us
  local copies, waits for them, and re-layouts: 7.5 us -> 9.88 us
  waiting for transfers between devices: 16.2 us -> 18.1 us
  other arithmetic: 5.57 us -> 3.78 us
    pallas_call x2, Pallas kernels: 23.5 us -> 19.4 us  [node_layer(): pl.pallas_call(node_kernel, grid=(count // rows,), in_specs=[pl.BlockSpec...]
    all_to_all x1, waiting for transfers between devices: 3.44 us -> 5.5 us  [body(): lax.all_to_all(outbound, ('grp', 'shard'), split_axis=0, concat_axis=0, t...]
    convert_element_type x1 -> x0, other arithmetic: 1.79 us -> none  [body(): embed_bf = embed.astype(jnp.bfloat16)]
    gather x1, local copies, waits for them, and re-layouts: 2.79 us -> 4.51 us  [body(): embed_tiles.at[tile_list[0].reshape(shard_count * list_len)]]
    all_to_all x1, starting transfers between devices: 6.31 us -> 4.82 us  [body(): lax.all_to_all(slot_scores, ('grp', 'shard'), split_axis=0, concat_axis=0...]
  transfers between devices with their start and end apart: 3 -> 3, of which waited for: 3 -> 3; matrix products, arithmetic and copies ran while one was open for 16% -> 17% of each run, Pallas kernels for 34% -> 33%
where the time goes in v16:
time: 144 us; the launch traced here: 143 us
  Pallas kernels  56.8 us (39%)
  starting transfers between devices  28.6 us (20%)
  matrix products  25.4 us (18%)
  waiting for transfers between devices  18.1 us (13%)
  local copies, waits for them, and re-layouts  9.88 us (7%)
  other arithmetic  3.78 us (3%)
    pallas_call x1, Pallas kernels, build_adjacency(): pl.pallas_call(adjacency_kernel, grid=(nodes // rows,), in_specs=[pl.Bloc...  37.4 us
    pallas_call x2, Pallas kernels, node_layer(): pl.pallas_call(node_kernel, grid=(count // rows,), in_specs=[pl.BlockSpec...  19.4 us
    all_to_all x1, starting transfers between devices, body(): lax.all_to_all(outbound, ('grp', 'shard'), split_axis=0, concat_axis=0, t...  15.1 us
    dot_general x1, matrix products, body(): jnp.dot(send_chooser, adjacency, preferred_element_type=jnp.float32)  14.4 us
    all_to_all x1, waiting for transfers between devices, body(): lax.all_to_all(slot_scores, ('grp', 'shard'), split_axis=0, concat_axis=0...  8.99 us
    all_to_all x1, starting transfers between devices, body(): lax.all_to_all(outgoing, 'shard', split_axis=0, concat_axis=0, tiled=True)  8.61 us
    all_to_all x1, waiting for transfers between devices, body(): lax.all_to_all(outbound, ('grp', 'shard'), split_axis=0, concat_axis=0, t...  5.5 us
    all_to_all x1, starting transfers between devices, body(): lax.all_to_all(slot_scores, ('grp', 'shard'), split_axis=0, concat_axis=0...  4.82 us
  transfers between devices with their start and end apart: 3, of which 3 were waited for; matrix products, arithmetic and copies ran while one was open for 17% of the time, Pallas kernels for 33%

profile of v16, /device:TPU:1, one launch (start us, length us, event | category | flops | bytes accessed | tf_op | source)
XLA Modules:
  0.0 143.5 jit_solution(4086392697580381081)
XLA Ops:
  0.6 0.0 copy-start
  0.6 0.8 copy.33
  1.5 0.1 reshape_squeeze.3
  1.6 4.5 %gather_fusion = bf16[32,128,512]{2,1,0:T(8,128)(2,1)} fusion(f32[8,128,512]{2,1,0:T(8,128)} %bitcast.45, s32[1024]{0:T(1024)S(1)} %pad_clamp_fusion), kind=kCustom, calls=%fused_computation | custom fusion | bytes 8388736 | tf_op jit(solution)/shard_map/gather | solution.py:132
  6.1 8.6 %all-to-all-start = ((bf16[16,256,512]{2,1,0:T(8,128)(2,1)}), bf16[16,256,512]{2,1,0:T(8,128)(2,1)}, u32[]{:S(2)}, u32[]{:S(2)}) async-start(bf16[16,256,512]{2,1,0:T(8,128)(2,1)} %bitcast.46), calls=%async_computation | async-start | bytes 8388608 | tf_op jit(solution)/shard_map/all_to_all | solution.py:135
  14.7 0.0 copy-done.5
  14.7 0.0 copy-start.6
  14.7 0.2 copy.31
  14.9 0.9 reshape.116.slot_ref
  15.9 0.2 copy.32
  16.1 1.0 reshape.124.coef_ref
  17.1 0.1 copy.34
  17.2 0.1 eq.70
  17.3 0.0 copy-start.8
  17.3 37.4 %shard_map.174.adj_ref = bf16[1024,4096]{1,0:T(8,128)(2,1)} custom-call(s32[128,640]{1,0:T(8,128)} %reshape.116.slot_ref, f32[128,640]{1,0:T(8,128)} %reshape.124.coef_ref), custom_call_target="tpu_custom_call" | custom-call | tf_op jit(solution)/shard_map/pallas_call | solution.py:49
  54.7 0.0 copy-done
  54.7 3.4 %convolution_add_fusion.self_ref = f32[1024,512]{1,0:T(8,128)S(1)} fusion(bf16[512,512]{1,0:T(8,128)(2,1)S(1)} %copy-done, f32[512]{0:T(512)S(1)} %copy-done.8, s32[1024]{0:T(1024)S(1)} %eq.70, f32[1024,512]{1,0:T(8,128)} %param.15), kind=kOutput, calls=%fused_computation.16 | convolution fusion | flops 1613234176 | bytes 4724736 | tf_op jit(solution)/shard_map/dot_general | solution.py:142
  58.1 0.0 copy-start.1
  58.1 14.4 %convolution_convert_fusion.adj_ref = bf16[1024,4096]{1,0:T(8,128)(2,1)} fusion(bf16[1024,4096]{1,0:T(8,128)(2,1)} %shard_map.174.adj_ref, s32[1024]{0:T(1024)S(1)} %eq.70), kind=kOutput, calls=%fused_computation.1 | convolution fusion | flops 8595177472 | bytes 16781312 | tf_op jit(solution)/shard_map/dot_general | solution.py:140
  72.5 3.6 %all-to-all-done = bf16[16,256,512]{2,1,0:T(8,128)(2,1)} async-done(((bf16[16,256,512]{2,1,0:T(8,128)(2,1)}), bf16[16,256,512]{2,1,0:T(8,128)(2,1)}, u32[]{:S(2)}, u32[]{:S(2)}) %all-to-all-start) | async-done | bytes 4194336 | tf_op jit(solution)/shard_map/all_to_all | solution.py:135
  76.2 0.0 copy-done.1
  76.2 9.7 %shard_map.176 = bf16[1024,512]{1,0:T(8,128)(2,1)} custom-call(bf16[1024,4096]{1,0:T(8,128)(2,1)} %convolution_convert_fusion.adj_ref, bf16[4096,512]{1,0:T(8,128)(2,1)} %bitcast.3.table_ref, f32[1024,512]{1,0:T(8,128)S(1)} %convolution_add_fusion.self_ref, bf16[512,512]{1,0:T(8,128)(2,1)S(1)} %copy-done.1), custom_call_target="tpu_custom_call" | custom-call | tf_op jit(solution)/shard_map/pallas_call | solution.py:72
  85.9 15.1 %all-to-all-start.1 = ((bf16[128,8,512]{2,1,0:T(8,128)(2,1)}), bf16[128,8,512]{2,1,0:T(8,128)(2,1)}, u32[]{:S(2)}, u32[]{:S(2)}) async-start(bf16[128,8,512]{2,1,0:T(8,128)(2,1)} %bitcast.6), calls=%async_computation.1 | async-start | bytes 2097152 | tf_op jit(solution)/shard_map/all_to_all | solution.py:151
  101.1 0.0 copy-done.10
  101.1 0.0 copy-done.11
  101.1 0.0 copy-done.9
  101.2 0.1 iota_compare_fusion.9
  101.2 0.7 convolution_add_fusion.1.self_ref
  102.0 9.7 %shard_map.175 = bf16[1024,512]{1,0:T(8,128)(2,1)} custom-call(bf16[1024,4096]{1,0:T(8,128)(2,1)} %shard_map.174.adj_ref, bf16[4096,512]{1,0:T(8,128)(2,1)} %bitcast.3.table_ref, f32[1024,512]{1,0:T(8,128)S(1)} %convolution_add_fusion.1.self_ref, bf16[512,512]{1,0:T(8,128)(2,1)S(1)} %copy-done.1), custom_call_target="tpu_custom_call" | custom-call | tf_op jit(solution)/shard_map/pallas_call | solution.py:72
  111.6 2.2 %fusion.27 = f32[1,1024]{1,0:T(1,128)} fusion(bf16[1024,512]{1,0:T(8,128)(2,1)} %shard_map.175, bf16[512,1]{0,1:T(2,128)(2,1)S(1)} %reshape.133), kind=kOutput, calls=%fused_computation.43 | convolution fusion | flops 1048576 | bytes 1053696 | tf_op jit(solution)/shard_map/dot_general | solution.py:145
  113.8 5.5 %all-to-all-done.1 = bf16[128,8,512]{2,1,0:T(8,128)(2,1)} async-done(((bf16[128,8,512]{2,1,0:T(8,128)(2,1)}), bf16[128,8,512]{2,1,0:T(8,128)(2,1)}, u32[]{:S(2)}, u32[]{:S(2)}) %all-to-all-start.1) | async-done | bytes 1048608 | tf_op jit(solution)/shard_map/all_to_all | solution.py:151
  119.3 2.5 %fusion.2 = f32[4,256,512]{2,1,0:T(8,128)S(1)} fusion(s32[4,256]{1,0:T(4,128)S(1)} %copy-done.7, bf16[128,8,512]{2,1,0:T(8,128)(2,1)} %all-to-all-done.1), kind=kOutput, calls=%fused_computation.9 | convolution fusion | flops 1074790400 | bytes 3149824 | tf_op jit(solution)/shard_map/dot_general | solution.py:157
  121.9 0.0 copy-start.4
  121.9 0.0 copy-start.12
  121.9 0.4 select_reduce_fusion.2
  122.3 0.6 copy-done.4
  122.9 0.2 fusion.21
  123.1 2.0 %fusion.8 = f32[1,4,256]{2,0,1:T(1,128)S(1)} fusion(bf16[512,1,1]{0,1,2:T(2,128)(2,1)S(1)} %reshape.137, f32[4,256,512]{2,1,0:T(8,128)S(1)} %fusion.2, f32[512]{0:T(512)S(1)} %copy-done.12, f32[4,512]{1,0:T(4,128)S(1)} %fusion.21, f32[4,512]{1,0:T(4,128)S(1)} %bitcast.48, bf16[512,512]{1,0:T(8,128)(2,1)} %param.26), kind=kOutput, calls=%fused_computation.19 | convolution fusion | flops 541065216 | bytes 2644992 | tf_op jit(solution)/shard_map/smk,k->sm/dot_general | solution.py:167
  125.1 0.1 fusion.35
  125.2 0.6 select_reduce_fusion.1
  125.7 0.7 all_to_all.14
  126.4 4.8 %all-to-all-start.2 = ((f32[128,1,8]{2,1,0:T(1,128)}), f32[128,1,8]{2,1,0:T(1,128)S(1)}, u32[]{:S(2)}, u32[]{:S(2)}) async-start(f32[128,1,8]{2,1,0:T(1,128)} %bitcast.11), calls=%async_computation.2 | async-start | bytes 131072 | tf_op jit(solution)/shard_map/all_to_all | solution.py:171
  131.3 0.7 divide_select_fusion
  131.9 9.0 %all-to-all-done.2 = f32[128,1,8]{2,1,0:T(1,128)S(1)} async-done(((f32[128,1,8]{2,1,0:T(1,128)}), f32[128,1,8]{2,1,0:T(1,128)S(1)}, u32[]{:S(2)}, u32[]{:S(2)}) %all-to-all-start.2) | async-done | bytes 4128 | tf_op jit(solution)/shard_map/all_to_all | solution.py:171
  140.9 0.5 broadcast.65
  141.4 0.8 reduce.3
  142.3 0.1 broadcast_in_dim.58
  142.3 1.1 select_reduce_fusion
  (24 shorter events, 0.1 us)
Async XLA Ops:
  0.6 54.0 %copy-start = (bf16[512,512]{1,0:T(8,128)(2,1)S(1)}, bf16[512,512]{1,0:T(8,128)(2,1)}, u32[]{:S(2)}) copy-start(bf16[512,512]{1,0:T(8,128)(2,1)} %param.22) | copy-start | bytes 1572868
  6.1 8.6 %copy-start.5 = (s32[1024,80]{0,1:T(8,128)S(1)}, s32[1024,80]{0,1:T(8,128)}, u32[]{:S(2)}) copy-start(s32[1024,80]{0,1:T(8,128)} %param.16) | copy-start | bytes 983044
  6.1 9.8 %copy-start.3 = (f32[1024,80]{0,1:T(8,128)S(1)}, f32[1024,80]{0,1:T(8,128)}, u32[]{:S(2)}) copy-start(f32[1024,80]{0,1:T(8,128)} %param.17) | copy-start | bytes 983044
  6.1 70.1 %all-to-all-start = ((bf16[16,256,512]{2,1,0:T(8,128)(2,1)}), bf16[16,256,512]{2,1,0:T(8,128)(2,1)}, u32[]{:S(2)}, u32[]{:S(2)}) async-start(bf16[16,256,512]{2,1,0:T(8,128)(2,1)} %bitcast.46), calls=%async_computation | async-start | bytes 8388608 | tf_op jit(solution)/shard_map/all_to_all | solution.py:135
  14.7 2.4 %copy-start.6 = (s32[1,128,8]{1,2,0:T(8,128)S(1)}, s32[1,128,8]{1,2,0:T(8,128)}, u32[]{:S(2)}) copy-start(s32[1,128,8]{1,2,0:T(8,128)} %param.19) | copy-start | bytes 12292
  17.3 37.4 %copy-start.8 = (f32[512]{0:T(512)S(1)}, f32[512]{0:T(512)}, u32[]{:S(2)}) copy-start(f32[512]{0:T(512)} %param.24) | copy-start | bytes 6148
  58.1 18.1 %copy-start.1 = (bf16[512,512]{1,0:T(8,128)(2,1)S(1)}, bf16[512,512]{1,0:T(8,128)(2,1)}, u32[]{:S(2)}) copy-start(bf16[512,512]{1,0:T(8,128)(2,1)} %w_nbr_ref.3) | copy-start | bytes 1572868
  76.2 24.9 %copy-start.10 = (bf16[512]{0:T(512)(128)(2,1)S(1)}, bf16[512]{0:T(512)(128)(2,1)}, u32[]{:S(2)}) copy-start(bf16[512]{0:T(512)(128)(2,1)} %param.25) | copy-start | bytes 3076
  76.2 24.9 %copy-start.11 = (bf16[512]{0:T(512)(128)(2,1)S(1)}, bf16[512]{0:T(512)(128)(2,1)}, u32[]{:S(2)}) copy-start(bf16[512]{0:T(512)(128)(2,1)} %param.29) | copy-start | bytes 3076
  85.9 15.2 %copy-start.9 = (s32[4]{0:T(128)S(1)}, s32[4]{0:T(128)}, u32[]{:S(2)}) copy-start(s32[4]{0:T(128)} %param.21) | copy-start | bytes 52
  85.9 15.2 %copy-start.7 = (s32[4,256]{1,0:T(4,128)S(1)}, s32[4,256]{1,0:T(4,128)}, u32[]{:S(2)}) copy-start(s32[4,256]{1,0:T(4,128)} %param.20) | copy-start | bytes 12292
  85.9 15.3 %copy-start.2 = (f32[1024,512]{1,0:T(8,128)S(1)}, f32[1024,512]{1,0:T(8,128)}, u32[]{:S(2)}) copy-start(f32[1024,512]{1,0:T(8,128)} %param.15) | copy-start | bytes 6291460
  85.9 33.4 %all-to-all-start.1 = ((bf16[128,8,512]{2,1,0:T(8,128)(2,1)}), bf16[128,8,512]{2,1,0:T(8,128)(2,1)}, u32[]{:S(2)}, u32[]{:S(2)}) async-start(bf16[128,8,512]{2,1,0:T(8,128)(2,1)} %bitcast.6), calls=%async_computation.1 | async-start | bytes 2097152 | tf_op jit(solution)/shard_map/all_to_all | solution.py:151
  121.9 1.0 copy-start.4
  121.9 1.2 copy-start.12
  126.4 14.5 %all-to-all-start.2 = ((f32[128,1,8]{2,1,0:T(1,128)}), f32[128,1,8]{2,1,0:T(1,128)S(1)}, u32[]{:S(2)}, u32[]{:S(2)}) async-start(f32[128,1,8]{2,1,0:T(1,128)} %bitcast.11), calls=%async_computation.2 | async-start | bytes 131072 | tf_op jit(solution)/shard_map/all_to_all | solution.py:171

commit v17 on v14

--- a/solution.py
+++ b/solution.py
@@ -59,20 +59,29 @@
     )(slot_rows, coef_rows)
 
 
-def node_kernel(adj_ref, table_ref, embed_ref, w_self_ref, w_nbr_ref, bias_ref, send_ref, out_ref, outbound_ref, held_ref):
+def node_kernel(adj_ref, table_ref, embed_ref, w_self_ref, w_nbr_ref, bias_ref, send_ref, out_ref, outbound_ref, held_ref, acc_ref):
     b = pl.program_id(0)
+    k = pl.program_id(1)
     rows = out_ref.shape[0]
-    total = jnp.dot(adj_ref[...], table_ref[...], preferred_element_type=jnp.float32)
-    pre = (
-        jnp.dot(embed_ref[...], w_self_ref[...], preferred_element_type=jnp.float32)
-        + bias_ref[...]
-        + jnp.dot(total.astype(jnp.bfloat16), w_nbr_ref[...], preferred_element_type=jnp.float32)
-    )
-    hidden = jnp.maximum(pre, 0.0).astype(out_ref.dtype)
-    out_ref[...] = hidden
-    held_ref[pl.ds(pl.multiple_of(b * rows, rows), rows), :] = hidden
-
-    @pl.when(b == pl.num_programs(0) - 1)
+
+    @pl.when(k == 0)
+    def _():
+        acc_ref[...] = jnp.zeros_like(acc_ref)
+
+    acc_ref[...] += jnp.dot(adj_ref[...], table_ref[...], preferred_element_type=jnp.float32)
+
+    @pl.when(k == pl.num_programs(1) - 1)
+    def _():
+        pre = (
+            jnp.dot(embed_ref[...], w_self_ref[...], preferred_element_type=jnp.float32)
+            + bias_ref[...]
+            + jnp.dot(acc_ref[...].astype(jnp.bfloat16), w_nbr_ref[...], preferred_element_type=jnp.float32)
+        )
+        hidden = jnp.maximum(pre, 0.0).astype(out_ref.dtype)
+        out_ref[...] = hidden
+        held_ref[pl.ds(pl.multiple_of(b * rows, rows), rows), :] = hidden
+
+    @pl.when((b == pl.num_programs(0) - 1) & (k == pl.num_programs(1) - 1))
     def _():
         nodes = held_ref.shape[0]
         chooser = jnp.where(
@@ -88,28 +97,32 @@
     hidden = w_self.shape[1]
     columns = adjacency.shape[1]
     rows = 256
+    depth = 1024
     slots = send_flat.shape[0]
     return pl.pallas_call(
         node_kernel,
-        grid=(nodes // rows,),
+        grid=(nodes // rows, columns // depth),
         in_specs=[
-            pl.BlockSpec((rows, columns), lambda b: (b, 0)),
-            pl.BlockSpec(table.shape, lambda b: (0, 0)),
-            pl.BlockSpec((rows, width), lambda b: (b, 0)),
-            pl.BlockSpec(w_self.shape, lambda b: (0, 0)),
-            pl.BlockSpec(w_nbr.shape, lambda b: (0, 0)),
-            pl.BlockSpec((1, hidden), lambda b: (0, 0)),
-            pl.BlockSpec((slots, 1), lambda b: (0, 0)),
+            pl.BlockSpec((rows, depth), lambda b, k: (b, k)),
+            pl.BlockSpec((depth, table.shape[1]), lambda b, k: (k, 0)),
+            pl.BlockSpec((rows, width), lambda b, k: (b, 0)),
+            pl.BlockSpec(w_self.shape, lambda b, k: (0, 0)),
+            pl.BlockSpec(w_nbr.shape, lambda b, k: (0, 0)),
+            pl.BlockSpec((1, hidden), lambda b, k: (0, 0)),
+            pl.BlockSpec((slots, 1), lambda b, k: (0, 0)),
         ],
         out_specs=[
-            pl.BlockSpec((rows, hidden), lambda b: (b, 0)),
-            pl.BlockSpec((slots, hidden), lambda b: (0, 0)),
+            pl.BlockSpec((rows, hidden), lambda b, k: (b, 0)),
+            pl.BlockSpec((slots, hidden), lambda b, k: (0, 0)),
         ],
         out_shape=[
             jax.ShapeDtypeStruct((nodes, hidden), jnp.bfloat16),
             jax.ShapeDtypeStruct((slots, hidden), jnp.bfloat16),
         ],
-        scratch_shapes=[pltpu.VMEM((nodes, hidden), jnp.bfloat16)],
+        scratch_shapes=[
+            pltpu.VMEM((nodes, hidden), jnp.bfloat16),
+            pltpu.VMEM((rows, table.shape[1]), jnp.float32),
+        ],
         compiler_params=pltpu.CompilerParams(vmem_limit_bytes=48 * 1024 * 1024),
     )(adjacency, table, embed_bf, w_self, w_nbr, bias.reshape(1, hidden), send_flat.reshape(slots, 1))
 

time: 145 us -> 153 us (1.055)
  Pallas kernels: 49.1 us -> 57.6 us
    pallas_call x1, Pallas kernels: 11.6 us -> 20.2 us  [node_layer(): pl.pallas_call(node_kernel, grid=(nodes // rows, columns // depth), in_sp...]
  transfers between devices with their start and end apart: 3 -> 3, of which waited for: 3 -> 3; matrix products, arithmetic and copies ran while one was open for 4% -> 4% of each run, Pallas kernels for 26% -> 25%
where the time goes in v17:
time: 153 us
  Pallas kernels  57.6 us (38%)
  waiting for transfers between devices  45.6 us (30%)
  starting transfers between devices  28.5 us (19%)
  local copies, waits for them, and re-layouts  9.83 us (6%)
  other arithmetic  5.56 us (4%)
  matrix products  4.6 us (3%)
    pallas_call x1, Pallas kernels, build_adjacency(): pl.pallas_call(adjacency_kernel, grid=(nodes // rows,), in_specs=[pl.Bloc...  37.5 us
    pallas_call x1, Pallas kernels, node_layer(): pl.pallas_call(node_kernel, grid=(nodes // rows, columns // depth), in_sp...  20.2 us
    all_to_all x1, waiting for transfers between devices, body(): lax.all_to_all(outgoing, 'shard', split_axis=0, concat_axis=0, tiled=True)  19.5 us
    all_to_all x1, waiting for transfers between devices, body(): lax.all_to_all(outbound, ('grp', 'shard'), split_axis=0, concat_axis=0, t...  17 us
    all_to_all x1, starting transfers between devices, body(): lax.all_to_all(outbound, ('grp', 'shard'), split_axis=0, concat_axis=0, t...  15.1 us
    all_to_all x1, waiting for transfers between devices, body(): lax.all_to_all(slot_scores, ('grp', 'shard'), split_axis=0, concat_axis=0...  9 us
    all_to_all x1, starting transfers between devices, body(): lax.all_to_all(outgoing, 'shard', split_axis=0, concat_axis=0, tiled=True)  8.48 us
    all_to_all x1, starting transfers between devices, body(): lax.all_to_all(slot_scores, ('grp', 'shard'), split_axis=0, concat_axis=0...  4.89 us
  transfers between devices with their start and end apart: 3, of which 3 were waited for; matrix products, arithmetic and copies ran while one was open for 4% of the time, Pallas kernels for 25%

profile of v17, /device:TPU:1, one launch (start us, length us, event | category | flops | bytes accessed | tf_op | source)
XLA Modules:
  0.0 152.7 jit_solution(508044599586781146)
XLA Ops:
  0.6 0.0 copy-start
  0.6 0.8 copy.38
  1.5 0.1 reshape_squeeze.3
  1.6 4.5 %gather_fusion = bf16[32,128,512]{2,1,0:T(8,128)(2,1)} fusion(f32[8,128,512]{2,1,0:T(8,128)} %bitcast.44, s32[1024]{0:T(1024)S(1)} %pad_clamp_fusion), kind=kCustom, calls=%fused_computation | custom fusion | bytes 8388736 | tf_op jit(solution)/shard_map/gather | solution.py:175
  6.1 8.5 %all-to-all-start = ((bf16[16,256,512]{2,1,0:T(8,128)(2,1)}), bf16[16,256,512]{2,1,0:T(8,128)(2,1)}, u32[]{:S(2)}, u32[]{:S(2)}) async-start(bf16[16,256,512]{2,1,0:T(8,128)(2,1)} %bitcast.45), calls=%async_computation | async-start | bytes 8388608 | tf_op jit(solution)/shard_map/all_to_all | solution.py:178
  14.5 0.0 copy-start.7
  14.6 0.0 copy-start.4
  14.6 1.8 %convert_element_type.31.embed_ref = bf16[1024,512]{1,0:T(8,128)(2,1)S(1)} convert(f32[1024,512]{1,0:T(8,128)} %param.15) | non-fusion elementwise | flops 524288 | bytes 3145728 | tf_op jit(solution)/shard_map/convert_element_type | solution.py:163
  16.3 0.0 copy-done.7
  16.4 0.0 copy-start.6
  16.4 0.1 copy.39
  16.5 0.0 copy-done.4
  16.6 0.2 copy.37
  16.8 0.9 reshape.127.coef_ref
  17.7 0.2 reshape_reshape_squeeze.4.send_ref
  17.9 0.0 copy-done.6
  17.9 0.2 copy.36
  18.1 0.9 reshape.118.slot_ref
  19.0 37.5 %shard_map.174.adj_ref = bf16[1024,4096]{1,0:T(8,128)(2,1)} custom-call(s32[128,640]{1,0:T(8,128)} %reshape.118.slot_ref, f32[128,640]{1,0:T(8,128)} %reshape.127.coef_ref), custom_call_target="tpu_custom_call" | custom-call | tf_op jit(solution)/shard_map/pallas_call | solution.py:49
  56.5 19.5 %all-to-all-done = bf16[16,256,512]{2,1,0:T(8,128)(2,1)} async-done(((bf16[16,256,512]{2,1,0:T(8,128)(2,1)}), bf16[16,256,512]{2,1,0:T(8,128)(2,1)}, u32[]{:S(2)}, u32[]{:S(2)}) %all-to-all-start) | async-done | bytes 4194336 | tf_op jit(solution)/shard_map/all_to_all | solution.py:178
  76.0 0.0 copy-done.1
  76.0 20.2 %shard_map.175 = (bf16[1024,512]{1,0:T(8,128)(2,1)}, bf16[1024,512]{1,0:T(8,128)(2,1)}) custom-call(bf16[1024,4096]{1,0:T(8,128)(2,1)} %shard_map.174.adj_ref, bf16[4096,512]{1,0:T(8,128)(2,1)} %bitcast.3.table_ref, bf16[1024,512]{1,0:T(8,128)(2,1)S(1)} %convert_element_type.31.embed_ref, bf16[512,512]{1,0:T(8,128)(2,1)S(1)} %copy-done.1, ...), custom_call_target="tpu_custom_call" | custom-call | tf_op jit(solution)/shard_map/pallas_call | solution.py:102
  96.2 0.0 copy-start.11
  96.2 0.0 copy-start.8
  96.2 0.0 copy-start.5
  96.2 15.1 %all-to-all-start.1 = ((bf16[128,8,512]{2,1,0:T(8,128)(2,1)}), bf16[128,8,512]{2,1,0:T(8,128)(2,1)}, u32[]{:S(2)}, u32[]{:S(2)}) async-start(bf16[128,8,512]{2,1,0:T(8,128)(2,1)} %bitcast.7), calls=%async_computation.1 | async-start | bytes 2097152 | tf_op jit(solution)/shard_map/all_to_all | solution.py:188
  111.4 0.1 eq.63
  111.6 0.1 iota_compare_fusion.3
  111.7 1.0 fusion.20
  112.6 17.0 %all-to-all-done.1 = bf16[128,8,512]{2,1,0:T(8,128)(2,1)} async-done(((bf16[128,8,512]{2,1,0:T(8,128)(2,1)}), bf16[128,8,512]{2,1,0:T(8,128)(2,1)}, u32[]{:S(2)}, u32[]{:S(2)}) %all-to-all-start.1) | async-done | bytes 1048608 | tf_op jit(solution)/shard_map/all_to_all | solution.py:188
  129.7 2.5 %fusion.1 = f32[4,256,512]{2,1,0:T(8,128)S(1)} fusion(s32[4,256]{1,0:T(4,128)S(1)} %copy-done.8, bf16[128,8,512]{2,1,0:T(8,128)(2,1)} %all-to-all-done.1), kind=kOutput, calls=%fused_computation.7 | convolution fusion | flops 1074790400 | bytes 3149824 | tf_op jit(solution)/shard_map/dot_general | solution.py:194
  132.2 0.0 copy-start.12
  132.2 0.0 copy-start.13
  132.2 0.4 select_reduce_fusion.2
  132.6 0.0 copy-done
  132.6 0.2 fusion.14
  132.8 0.4 copy-done.12
  133.2 0.9 fusion.4
  134.1 0.1 fusion.25
  134.2 0.6 select_reduce_fusion.1
  134.8 0.7 all_to_all.14
  135.5 4.9 %all-to-all-start.2 = ((f32[128,1,8]{2,1,0:T(1,128)}), f32[128,1,8]{2,1,0:T(1,128)S(1)}, u32[]{:S(2)}, u32[]{:S(2)}) async-start(f32[128,1,8]{2,1,0:T(1,128)} %bitcast.12), calls=%async_computation.2 | async-start | bytes 131072 | tf_op jit(solution)/shard_map/all_to_all | solution.py:208
  140.4 0.7 divide_select_fusion
  141.1 9.0 %all-to-all-done.2 = f32[128,1,8]{2,1,0:T(1,128)S(1)} async-done(((f32[128,1,8]{2,1,0:T(1,128)}), f32[128,1,8]{2,1,0:T(1,128)S(1)}, u32[]{:S(2)}, u32[]{:S(2)}) %all-to-all-start.2) | async-done | bytes 4128 | tf_op jit(solution)/shard_map/all_to_all | solution.py:208
  150.1 0.5 broadcast.64
  150.6 0.8 reduce.3
  151.4 0.1 broadcast_in_dim.55
  151.5 1.1 select_reduce_fusion
  (24 shorter events, 0.1 us)
Async XLA Ops:
  0.6 132.0 %copy-start = (bf16[512,512]{1,0:T(8,128)(2,1)S(1)}, bf16[512,512]{1,0:T(8,128)(2,1)}, u32[]{:S(2)}) copy-start(bf16[512,512]{1,0:T(8,128)(2,1)} %param.27) | copy-start | bytes 1572868
  6.1 70.0 %all-to-all-start = ((bf16[16,256,512]{2,1,0:T(8,128)(2,1)}), bf16[16,256,512]{2,1,0:T(8,128)(2,1)}, u32[]{:S(2)}, u32[]{:S(2)}) async-start(bf16[16,256,512]{2,1,0:T(8,128)(2,1)} %bitcast.45), calls=%async_computation | async-start | bytes 8388608 | tf_op jit(solution)/shard_map/all_to_all | solution.py:178
  14.5 1.8 %copy-start.7 = (s32[1,128,8]{1,2,0:T(8,128)S(1)}, s32[1,128,8]{1,2,0:T(8,128)}, u32[]{:S(2)}) copy-start(s32[1,128,8]{1,2,0:T(8,128)} %param.19) | copy-start | bytes 12292
  14.6 1.9 %copy-start.4 = (f32[1024,80]{0,1:T(8,128)S(1)}, f32[1024,80]{0,1:T(8,128)}, u32[]{:S(2)}) copy-start(f32[1024,80]{0,1:T(8,128)} %param.17) | copy-start | bytes 983044
  16.4 1.5 %copy-start.6 = (s32[1024,80]{0,1:T(8,128)S(1)}, s32[1024,80]{0,1:T(8,128)}, u32[]{:S(2)}) copy-start(s32[1024,80]{0,1:T(8,128)} %param.16) | copy-start | bytes 983044
  19.0 57.0 %copy-start.1 = (bf16[512,512]{1,0:T(8,128)(2,1)S(1)}, bf16[512,512]{1,0:T(8,128)(2,1)}, u32[]{:S(2)}) copy-start(bf16[512,512]{1,0:T(8,128)(2,1)} %w_self_ref.1) | copy-start | bytes 1572868
  19.0 57.0 %copy-start.2 = (bf16[512,512]{1,0:T(8,128)(2,1)S(1)}, bf16[512,512]{1,0:T(8,128)(2,1)}, u32[]{:S(2)}) copy-start(bf16[512,512]{1,0:T(8,128)(2,1)} %w_nbr_ref.1) | copy-start | bytes 1572868
  19.0 57.0 %copy-start.3 = (f32[512]{0:T(512)S(1)}, f32[512]{0:T(512)}, u32[]{:S(2)}) copy-start(f32[512]{0:T(512)} %param.24) | copy-start | bytes 6148
  96.2 15.3 %copy-start.9 = (s32[4]{0:T(128)S(1)}, s32[4]{0:T(128)}, u32[]{:S(2)}) copy-start(s32[4]{0:T(128)} %param.21) | copy-start | bytes 52
  96.2 15.3 %copy-start.10 = (bf16[512]{0:T(512)(128)(2,1)S(1)}, bf16[512]{0:T(512)(128)(2,1)}, u32[]{:S(2)}) copy-start(bf16[512]{0:T(512)(128)(2,1)} %param.25) | copy-start | bytes 3076
  96.2 15.3 %copy-start.11 = (bf16[512]{0:T(512)(128)(2,1)S(1)}, bf16[512]{0:T(512)(128)(2,1)}, u32[]{:S(2)}) copy-start(bf16[512]{0:T(512)(128)(2,1)} %param.29) | copy-start | bytes 3076
  96.2 15.3 %copy-start.8 = (s32[4,256]{1,0:T(4,128)S(1)}, s32[4,256]{1,0:T(4,128)}, u32[]{:S(2)}) copy-start(s32[4,256]{1,0:T(4,128)} %param.20) | copy-start | bytes 12292
  96.2 15.4 %copy-start.5 = (bf16[1024,512]{1,0:T(8,128)(2,1)S(1)}, bf16[1024,512]{1,0:T(8,128)(2,1)}, u32[]{:S(2)}) copy-start(bf16[1024,512]{1,0:T(8,128)(2,1)} %get-tuple-element.2) | copy-start | bytes 3145732
  96.2 33.4 %all-to-all-start.1 = ((bf16[128,8,512]{2,1,0:T(8,128)(2,1)}), bf16[128,8,512]{2,1,0:T(8,128)(2,1)}, u32[]{:S(2)}, u32[]{:S(2)}) async-start(bf16[128,8,512]{2,1,0:T(8,128)(2,1)} %bitcast.7), calls=%async_computation.1 | async-start | bytes 2097152 | tf_op jit(solution)/shard_map/all_to_all | solution.py:188
  132.2 1.0 copy-start.12
  132.2 1.0 copy-start.13
  135.5 14.6 %all-to-all-start.2 = ((f32[128,1,8]{2,1,0:T(1,128)}), f32[128,1,8]{2,1,0:T(1,128)S(1)}, u32[]{:S(2)}, u32[]{:S(2)}) async-start(f32[128,1,8]{2,1,0:T(1,128)} %bitcast.12), calls=%async_computation.2 | async-start | bytes 131072 | tf_op jit(solution)/shard_map/all_to_all | solution.py:208

commit v18 on v14

--- a/solution.py
+++ b/solution.py
@@ -74,11 +74,7 @@
 
     @pl.when(b == pl.num_programs(0) - 1)
     def _():
-        nodes = held_ref.shape[0]
-        chooser = jnp.where(
-            send_ref[...] == lax.broadcasted_iota(jnp.int32, (send_ref.shape[0], nodes), 1), 1.0, 0.0
-        ).astype(jnp.bfloat16)
-        outbound_ref[...] = jnp.dot(chooser, held_ref[...], preferred_element_type=jnp.float32).astype(
+        outbound_ref[...] = jnp.dot(send_ref[...], held_ref[...], preferred_element_type=jnp.float32).astype(
             outbound_ref.dtype
         )
 
@@ -99,7 +95,7 @@
             pl.BlockSpec(w_self.shape, lambda b: (0, 0)),
             pl.BlockSpec(w_nbr.shape, lambda b: (0, 0)),
             pl.BlockSpec((1, hidden), lambda b: (0, 0)),
-            pl.BlockSpec((slots, 1), lambda b: (0, 0)),
+            pl.BlockSpec((slots, nodes), lambda b: (0, 0)),
         ],
         out_specs=[
             pl.BlockSpec((rows, hidden), lambda b: (b, 0)),
@@ -111,7 +107,7 @@
         ],
         scratch_shapes=[pltpu.VMEM((nodes, hidden), jnp.bfloat16)],
         compiler_params=pltpu.CompilerParams(vmem_limit_bytes=48 * 1024 * 1024),
-    )(adjacency, table, embed_bf, w_self, w_nbr, bias.reshape(1, hidden), send_flat.reshape(slots, 1))
+    )(adjacency, table, embed_bf, w_self, w_nbr, bias.reshape(1, hidden), select_matrix(send_flat, nodes, jnp.bfloat16))
 
 
 def select_matrix(indices, count, dtype):
@@ -177,7 +173,7 @@
     sub_count = members.shape[0]
     member_width = members.shape[1]
     member_flat = members.reshape(sub_count * member_width)
-    member_chooser = select_matrix(member_flat, slot_total, jnp.bfloat16)
+    member_chooser = lax.optimization_barrier(select_matrix(member_flat, slot_total, jnp.bfloat16))
     member_rows = jnp.dot(member_chooser, received_rows, preferred_element_type=jnp.float32)
     member_rows = member_rows.reshape(sub_count, member_width, hidden_width)
     relative = member_rows - member_rows[:, :1, :]

time: 145 us -> 150 us (1.034)
  local copies, waits for them, and re-layouts: 9.83 us -> 13.4 us
  matrix products: 4.6 us -> 6.23 us
    unnamed x36 -> x42, local copies, waits for them, and re-layouts: 1.61 us -> 5.46 us
    convert_element_type x0 -> x2, other arithmetic: none -> 2.15 us  [select_matrix(): (indices[:, None] == jnp.arange(count, dtype=jnp.int32)[None, :]).astype(...]
  transfers between devices with their start and end apart: 3 -> 3, of which waited for: 3 -> 3; matrix products, arithmetic and copies ran while one was open for 4% -> 5% of each run, Pallas kernels for 26% -> 25%
where the time goes in v18:
time: 150 us; the launch traced here: 149 us
  Pallas kernels  48.5 us (32%)
  waiting for transfers between devices  44.8 us (30%)
  starting transfers between devices  28.2 us (19%)
  local copies, waits for them, and re-layouts  13.4 us (9%)
  other arithmetic  7.03 us (5%)
  matrix products  6.23 us (4%)
    pallas_call x1, Pallas kernels, build_adjacency(): pl.pallas_call(adjacency_kernel, grid=(nodes // rows,), in_specs=[pl.Bloc...  37.4 us
    all_to_all x1, waiting for transfers between devices, body(): lax.all_to_all(outgoing, 'shard', split_axis=0, concat_axis=0, tiled=True)  20 us
    all_to_all x1, waiting for transfers between devices, body(): lax.all_to_all(outbound, ('grp', 'shard'), split_axis=0, concat_axis=0, t...  15.8 us
    all_to_all x1, starting transfers between devices, body(): lax.all_to_all(outbound, ('grp', 'shard'), split_axis=0, concat_axis=0, t...  14.7 us
    pallas_call x1, Pallas kernels, node_layer(): pl.pallas_call(node_kernel, grid=(nodes // rows,), in_specs=[pl.BlockSpec...  11.1 us
    all_to_all x1, waiting for transfers between devices, body(): lax.all_to_all(slot_scores, ('grp', 'shard'), split_axis=0, concat_axis=0...  8.99 us
    all_to_all x1, starting transfers between devices, body(): lax.all_to_all(outgoing, 'shard', split_axis=0, concat_axis=0, tiled=True)  8.61 us
    unnamed x42, local copies, waits for them, and re-layouts  5.46 us
  transfers between devices with their start and end apart: 3, of which 3 were waited for; matrix products, arithmetic and copies ran while one was open for 5% of the time, Pallas kernels for 25%

profile of v18, /device:TPU:1, one launch (start us, length us, event | category | flops | bytes accessed | tf_op | source)
XLA Modules:
  0.0 149.0 jit_solution(575140273137801919)
XLA Ops:
  0.6 0.0 copy-start
  0.6 0.8 copy.28
  1.5 0.1 reshape_squeeze.3
  1.6 4.5 %gather_fusion = bf16[32,128,512]{2,1,0:T(8,128)(2,1)} fusion(f32[8,128,512]{2,1,0:T(8,128)} %bitcast.44, s32[1024]{0:T(1024)S(1)} %pad_clamp_fusion), kind=kCustom, calls=%fused_computation | custom fusion | bytes 8388736 | tf_op jit(solution)/shard_map/gather | solution.py:158
  6.0 8.6 %all-to-all-start = ((bf16[16,256,512]{2,1,0:T(8,128)(2,1)}), bf16[16,256,512]{2,1,0:T(8,128)(2,1)}, u32[]{:S(2)}, u32[]{:S(2)}) async-start(bf16[16,256,512]{2,1,0:T(8,128)(2,1)} %bitcast.45), calls=%async_computation | async-start | bytes 8388608 | tf_op jit(solution)/shard_map/all_to_all | solution.py:161
  14.7 0.0 copy-done.6
  14.7 0.0 copy-start.10
  14.7 0.0 copy-start.7
  14.7 1.1 convert_element_type.36.embed_ref
  15.8 0.0 copy-done.10
  15.8 0.2 copy.26
  16.0 0.9 reshape.98.slot_ref
  16.9 0.0 copy-done.7
  17.0 0.2 copy.27
  17.2 0.9 reshape.107.coef_ref
  18.1 0.1 copy.29
  18.2 0.1 eq.16
  18.3 37.4 %shard_map.174.adj_ref = bf16[1024,4096]{1,0:T(8,128)(2,1)} custom-call(s32[128,640]{1,0:T(8,128)} %reshape.98.slot_ref, f32[128,640]{1,0:T(8,128)} %reshape.107.coef_ref), custom_call_target="tpu_custom_call" | custom-call | tf_op jit(solution)/shard_map/pallas_call | solution.py:49
  55.7 0.4 fusion.1.send_ref
  56.1 20.0 %all-to-all-done = bf16[16,256,512]{2,1,0:T(8,128)(2,1)} async-done(((bf16[16,256,512]{2,1,0:T(8,128)(2,1)}), bf16[16,256,512]{2,1,0:T(8,128)(2,1)}, u32[]{:S(2)}, u32[]{:S(2)}) %all-to-all-start) | async-done | bytes 4194336 | tf_op jit(solution)/shard_map/all_to_all | solution.py:161
  76.2 0.0 copy-done.3
  76.2 1.2 copy-done.1
  77.4 1.0 copy-done.4
  78.4 11.1 %shard_map.175 = (bf16[1024,512]{1,0:T(8,128)(2,1)}, bf16[1024,512]{1,0:T(8,128)(2,1)S(1)}) custom-call(bf16[1024,4096]{1,0:T(8,128)(2,1)} %shard_map.174.adj_ref, bf16[4096,512]{1,0:T(8,128)(2,1)} %bitcast.3.table_ref, bf16[1024,512]{1,0:T(8,128)(2,1)S(1)} %copy-done.1, bf16[512,512]{1,0:T(8,128)(2,1)S(1)} %copy-done.3, bf16[512,512]{1,0:T(8,128)(2,1)S(1)} %copy-done.4, ...), custom_call_target="tpu_custom_call" | custom-call | tf_op jit(solution)/shard_map/pallas_call | solution.py:88
  89.5 1.0 copy-done.2
  90.5 0.0 copy-start.8
  90.5 14.7 %all-to-all-start.1 = ((bf16[128,8,512]{2,1,0:T(8,128)(2,1)}), bf16[128,8,512]{2,1,0:T(8,128)(2,1)S(1)}, u32[]{:S(2)}, u32[]{:S(2)}) async-start(bf16[128,8,512]{2,1,0:T(8,128)(2,1)} %bitcast.42), calls=%async_computation.1 | async-start | bytes 2097152 | tf_op jit(solution)/shard_map/all_to_all | solution.py:171
  105.3 1.7 %fusion = bf16[1024,1024]{1,0:T(8,128)(2,1)} fusion(s32[1024]{0:T(1024)S(1)} %bitcast.47), kind=kLoop, calls=%fused_computation.4 | loop fusion | flops 2097152 | bytes 2101248 | tf_op jit(solution)/shard_map/convert_element_type | solution.py:114
  107.0 0.1 iota_compare_fusion.2
  107.1 1.0 fusion.19
  108.1 15.8 %all-to-all-done.1 = bf16[128,8,512]{2,1,0:T(8,128)(2,1)S(1)} async-done(((bf16[128,8,512]{2,1,0:T(8,128)(2,1)}), bf16[128,8,512]{2,1,0:T(8,128)(2,1)S(1)}, u32[]{:S(2)}, u32[]{:S(2)}) %all-to-all-start.1) | async-done | bytes 1048608 | tf_op jit(solution)/shard_map/all_to_all | solution.py:171
  123.8 1.0 copy-done.9
  124.8 3.1 %fusion.3 = f32[4,256,512]{2,1,0:T(8,128)S(1)} fusion(bf16[4,256,1024]{2,1,0:T(8,128)(2,1)} %bitcast.46, bf16[128,8,512]{2,1,0:T(8,128)(2,1)} %copy-done.9), kind=kOutput, calls=%fused_computation.11 | convolution fusion | flops 1073741824 | bytes 5242880 | tf_op jit(solution)/shard_map/dot_general | solution.py:177
  127.9 0.0 copy-start.16
  128.0 0.4 select_reduce_fusion.2
  128.3 0.2 fusion.13
  128.6 0.0 copy-done.16
  128.6 1.9 %fusion.2 = f32[1,4,256]{2,0,1:T(1,128)S(1)} fusion(bf16[512,1,1]{0,1,2:T(2,128)(2,1)S(1)} %reshape.120, f32[4,256,512]{2,1,0:T(8,128)S(1)} %fusion.3, f32[512]{0:T(512)S(1)} %copy-done.16, f32[4,512]{1,0:T(4,128)S(1)} %fusion.13, f32[4,512]{1,0:T(4,128)S(1)} %bitcast.50, bf16[512,512]{1,0:T(8,128)(2,1)} %param.26), kind=kOutput, calls=%fused_computation.10 | convolution fusion | flops 541065216 | bytes 2644992 | tf_op jit(solution)/shard_map/smk,k->sm/dot_general | solution.py:187
  130.6 0.1 fusion.25
  130.6 0.6 select_reduce_fusion.1
  131.2 0.7 all_to_all.14
  131.9 4.9 %all-to-all-start.2 = ((f32[128,1,8]{2,1,0:T(1,128)}), f32[128,1,8]{2,1,0:T(1,128)S(1)}, u32[]{:S(2)}, u32[]{:S(2)}) async-start(f32[128,1,8]{2,1,0:T(1,128)} %bitcast.12), calls=%async_computation.2 | async-start | bytes 131072 | tf_op jit(solution)/shard_map/all_to_all | solution.py:191
  136.8 0.7 divide_select_fusion
  137.5 9.0 %all-to-all-done.2 = f32[128,1,8]{2,1,0:T(1,128)S(1)} async-done(((f32[128,1,8]{2,1,0:T(1,128)}), f32[128,1,8]{2,1,0:T(1,128)S(1)}, u32[]{:S(2)}, u32[]{:S(2)}) %all-to-all-start.2) | async-done | bytes 4128 | tf_op jit(solution)/shard_map/all_to_all | solution.py:191
  146.5 0.5 broadcast.45
  147.0 0.8 reduce.3
  147.8 0.1 broadcast_in_dim.56
  147.9 1.1 select_reduce_fusion
  (31 shorter events, 0.1 us)
Async XLA Ops:
  0.6 127.7 %copy-start = (bf16[512,512]{1,0:T(8,128)(2,1)S(1)}, bf16[512,512]{1,0:T(8,128)(2,1)}, u32[]{:S(2)}) copy-start(bf16[512,512]{1,0:T(8,128)(2,1)} %param.27) | copy-start | bytes 1572868
  6.0 8.6 %copy-start.6 = (f32[1024,512]{1,0:T(8,128)S(1)}, f32[1024,512]{1,0:T(8,128)}, u32[]{:S(2)}) copy-start(f32[1024,512]{1,0:T(8,128)} %param.15) | copy-start | bytes 6291460
  6.0 70.1 %all-to-all-start = ((bf16[16,256,512]{2,1,0:T(8,128)(2,1)}), bf16[16,256,512]{2,1,0:T(8,128)(2,1)}, u32[]{:S(2)}, u32[]{:S(2)}) async-start(bf16[16,256,512]{2,1,0:T(8,128)(2,1)} %bitcast.45), calls=%async_computation | async-start | bytes 8388608 | tf_op jit(solution)/shard_map/all_to_all | solution.py:161
  14.7 1.1 copy-start.10
  14.7 2.2 %copy-start.7 = (f32[1024,80]{0,1:T(8,128)S(1)}, f32[1024,80]{0,1:T(8,128)}, u32[]{:S(2)}) copy-start(f32[1024,80]{0,1:T(8,128)} %param.17) | copy-start | bytes 983044
  15.8 2.3 %copy-start.11 = (s32[1,128,8]{1,2,0:T(8,128)S(1)}, s32[1,128,8]{1,2,0:T(8,128)}, u32[]{:S(2)}) copy-start(s32[1,128,8]{1,2,0:T(8,128)} %param.19) | copy-start | bytes 12292
  55.7 20.4 %copy-start.3 = (bf16[512,512]{1,0:T(8,128)(2,1)S(1)}, bf16[512,512]{1,0:T(8,128)(2,1)}, u32[]{:S(2)}) copy-start(bf16[512,512]{1,0:T(8,128)(2,1)} %w_self_ref.1) | copy-start | bytes 1572868
  55.7 20.4 %copy-start.5 = (f32[512]{0:T(512)S(1)}, f32[512]{0:T(512)}, u32[]{:S(2)}) copy-start(f32[512]{0:T(512)} %param.24) | copy-start | bytes 6148
  76.2 1.2 copy-start.1
  77.4 1.0 copy-start.4
  89.5 1.0 copy-start.2
  90.5 14.7 %copy-start.14 = (bf16[512]{0:T(512)(128)(2,1)S(1)}, bf16[512]{0:T(512)(128)(2,1)}, u32[]{:S(2)}) copy-start(bf16[512]{0:T(512)(128)(2,1)} %param.25) | copy-start | bytes 3076
  90.5 14.7 %copy-start.15 = (bf16[512]{0:T(512)(128)(2,1)S(1)}, bf16[512]{0:T(512)(128)(2,1)}, u32[]{:S(2)}) copy-start(bf16[512]{0:T(512)(128)(2,1)} %param.29) | copy-start | bytes 3076
  90.5 14.7 %copy-start.12 = (s32[4,256]{1,0:T(4,128)S(1)}, s32[4,256]{1,0:T(4,128)}, u32[]{:S(2)}) copy-start(s32[4,256]{1,0:T(4,128)} %param.20) | copy-start | bytes 12292
  90.5 16.5 %copy-start.13 = (s32[4]{0:T(128)S(1)}, s32[4]{0:T(128)}, u32[]{:S(2)}) copy-start(s32[4]{0:T(128)} %param.21) | copy-start | bytes 52
  90.5 16.6 %copy-start.8 = (bf16[1024,512]{1,0:T(8,128)(2,1)S(1)}, bf16[1024,512]{1,0:T(8,128)(2,1)}, u32[]{:S(2)}) copy-start(bf16[1024,512]{1,0:T(8,128)(2,1)} %get-tuple-element.2) | copy-start | bytes 3145732
  90.5 33.3 %all-to-all-start.1 = ((bf16[128,8,512]{2,1,0:T(8,128)(2,1)}), bf16[128,8,512]{2,1,0:T(8,128)(2,1)S(1)}, u32[]{:S(2)}, u32[]{:S(2)}) async-start(bf16[128,8,512]{2,1,0:T(8,128)(2,1)} %bitcast.42), calls=%async_computation.1 | async-start | bytes 2097152 | tf_op jit(solution)/shard_map/all_to_all | solution.py:171
  123.8 1.0 copy-start.9
  127.9 0.7 copy-start.16
  131.9 14.5 %all-to-all-start.2 = ((f32[128,1,8]{2,1,0:T(1,128)}), f32[128,1,8]{2,1,0:T(1,128)S(1)}, u32[]{:S(2)}, u32[]{:S(2)}) async-start(f32[128,1,8]{2,1,0:T(1,128)} %bitcast.12), calls=%async_computation.2 | async-start | bytes 131072 | tf_op jit(solution)/shard_map/all_to_all | solution.py:191

commit v19 on v14

--- a/solution.py
+++ b/solution.py
@@ -59,10 +59,27 @@
     )(slot_rows, coef_rows)
 
 
-def node_kernel(adj_ref, table_ref, embed_ref, w_self_ref, w_nbr_ref, bias_ref, send_ref, out_ref, outbound_ref, held_ref):
+def node_kernel(adj_ref, table_hbm, embed_ref, w_self_ref, w_nbr_ref, bias_ref, send_ref, out_ref, outbound_ref, held_ref, table_ref, sems):
     b = pl.program_id(0)
     rows = out_ref.shape[0]
-    total = jnp.dot(adj_ref[...], table_ref[...], preferred_element_type=jnp.float32)
+    chunks = table_ref.shape[0]
+    depth = table_ref.shape[1]
+    copies = [pltpu.make_async_copy(table_hbm.at[c], table_ref.at[c], sems.at[c]) for c in range(chunks)]
+
+    @pl.when(b == 0)
+    def _():
+        for copy in copies:
+            copy.start()
+
+    total = jnp.zeros((rows, table_ref.shape[2]), jnp.float32)
+    for c in range(chunks):
+        @pl.when(b == 0)
+        def _():
+            copies[c].wait()
+
+        total = total + jnp.dot(
+            adj_ref[:, c * depth:(c + 1) * depth], table_ref[c], preferred_element_type=jnp.float32
+        )
     pre = (
         jnp.dot(embed_ref[...], w_self_ref[...], preferred_element_type=jnp.float32)
         + bias_ref[...]
@@ -94,7 +111,7 @@
         grid=(nodes // rows,),
         in_specs=[
             pl.BlockSpec((rows, columns), lambda b: (b, 0)),
-            pl.BlockSpec(table.shape, lambda b: (0, 0)),
+            pl.BlockSpec(memory_space=pl.ANY),
             pl.BlockSpec((rows, width), lambda b: (b, 0)),
             pl.BlockSpec(w_self.shape, lambda b: (0, 0)),
             pl.BlockSpec(w_nbr.shape, lambda b: (0, 0)),
@@ -109,9 +126,13 @@
             jax.ShapeDtypeStruct((nodes, hidden), jnp.bfloat16),
             jax.ShapeDtypeStruct((slots, hidden), jnp.bfloat16),
         ],
-        scratch_shapes=[pltpu.VMEM((nodes, hidden), jnp.bfloat16)],
+        scratch_shapes=[
+            pltpu.VMEM((nodes, hidden), jnp.bfloat16),
+            pltpu.VMEM((4, table.shape[0] // 4, table.shape[1]), jnp.bfloat16),
+            pltpu.SemaphoreType.DMA((4,)),
+        ],
         compiler_params=pltpu.CompilerParams(vmem_limit_bytes=48 * 1024 * 1024),
-    )(adjacency, table, embed_bf, w_self, w_nbr, bias.reshape(1, hidden), send_flat.reshape(slots, 1))
+    )(adjacency, table.reshape(4, table.shape[0] // 4, table.shape[1]), embed_bf, w_self, w_nbr, bias.reshape(1, hidden), send_flat.reshape(slots, 1))
 
 
 def select_matrix(indices, count, dtype):

time: 145 us -> 146 us (level)
  no operation moved by 1% of the time
where the time goes in v19:
time: 146 us; the launch traced here: 145 us
  Pallas kernels  50.1 us (34%)
  waiting for transfers between devices  45.6 us (31%)
  starting transfers between devices  28.5 us (20%)
  local copies, waits for them, and re-layouts  9.83 us (7%)
  other arithmetic  5.56 us (4%)
  matrix products  4.6 us (3%)
    pallas_call x1, Pallas kernels, build_adjacency(): pl.pallas_call(adjacency_kernel, grid=(nodes // rows,), in_specs=[pl.Bloc...  37.5 us
    all_to_all x1, waiting for transfers between devices, body(): lax.all_to_all(outgoing, 'shard', split_axis=0, concat_axis=0, tiled=True)  19.5 us
    all_to_all x1, waiting for transfers between devices, body(): lax.all_to_all(outbound, ('grp', 'shard'), split_axis=0, concat_axis=0, t...  17 us
    all_to_all x1, starting transfers between devices, body(): lax.all_to_all(outbound, ('grp', 'shard'), split_axis=0, concat_axis=0, t...  15.1 us
    pallas_call x1, Pallas kernels, node_layer(): pl.pallas_call(node_kernel, grid=(nodes // rows,), in_specs=[pl.BlockSpec...  12.6 us
    all_to_all x1, waiting for transfers between devices, body(): lax.all_to_all(slot_scores, ('grp', 'shard'), split_axis=0, concat_axis=0...  9 us
    all_to_all x1, starting transfers between devices, body(): lax.all_to_all(outgoing, 'shard', split_axis=0, concat_axis=0, tiled=True)  8.48 us
    all_to_all x1, starting transfers between devices, body(): lax.all_to_all(slot_scores, ('grp', 'shard'), split_axis=0, concat_axis=0...  4.9 us
  transfers between devices with their start and end apart: 3, of which 3 were waited for; matrix products, arithmetic and copies ran while one was open for 4% of the time, Pallas kernels for 26%

profile of v19, /device:TPU:1, one launch (start us, length us, event | category | flops | bytes accessed | tf_op | source)
XLA Modules:
  0.0 145.2 jit_solution(8568707421584103459)
XLA Ops:
  0.6 0.0 copy-start
  0.6 0.8 copy.38
  1.5 0.1 reshape_squeeze.3
  1.6 4.5 %gather_fusion = bf16[32,128,512]{2,1,0:T(8,128)(2,1)} fusion(f32[8,128,512]{2,1,0:T(8,128)} %bitcast.44, s32[1024]{0:T(1024)S(1)} %pad_clamp_fusion), kind=kCustom, calls=%fused_computation | custom fusion | bytes 8388736 | tf_op jit(solution)/shard_map/gather | solution.py:183
  6.1 8.5 %all-to-all-start = ((bf16[16,256,512]{2,1,0:T(8,128)(2,1)}), bf16[16,256,512]{2,1,0:T(8,128)(2,1)}, u32[]{:S(2)}, u32[]{:S(2)}) async-start(bf16[16,256,512]{2,1,0:T(8,128)(2,1)} %bitcast.45), calls=%async_computation | async-start | bytes 8388608 | tf_op jit(solution)/shard_map/all_to_all | solution.py:186
  14.5 0.0 copy-start.7
  14.6 0.0 copy-start.4
  14.6 1.8 %convert_element_type.31.embed_ref = bf16[1024,512]{1,0:T(8,128)(2,1)S(1)} convert(f32[1024,512]{1,0:T(8,128)} %param.15) | non-fusion elementwise | flops 524288 | bytes 3145728 | tf_op jit(solution)/shard_map/convert_element_type | solution.py:171
  16.3 0.0 copy-done.7
  16.4 0.0 copy-start.6
  16.4 0.1 copy.39
  16.5 0.0 copy-done.4
  16.6 0.2 copy.37
  16.8 0.9 reshape.123.coef_ref
  17.7 0.2 reshape_reshape_squeeze.4.send_ref
  17.9 0.2 copy.36
  18.1 0.9 reshape.115.slot_ref
  19.0 37.5 %shard_map.174.adj_ref = bf16[1024,4096]{1,0:T(8,128)(2,1)} custom-call(s32[128,640]{1,0:T(8,128)} %reshape.115.slot_ref, f32[128,640]{1,0:T(8,128)} %reshape.123.coef_ref), custom_call_target="tpu_custom_call" | custom-call | tf_op jit(solution)/shard_map/pallas_call | solution.py:49
  56.5 19.5 %all-to-all-done = bf16[16,256,512]{2,1,0:T(8,128)(2,1)} async-done(((bf16[16,256,512]{2,1,0:T(8,128)(2,1)}), bf16[16,256,512]{2,1,0:T(8,128)(2,1)}, u32[]{:S(2)}, u32[]{:S(2)}) %all-to-all-start) | async-done | bytes 4194336 | tf_op jit(solution)/shard_map/all_to_all | solution.py:186
  76.0 12.6 %shard_map.175 = (bf16[1024,512]{1,0:T(8,128)(2,1)}, bf16[1024,512]{1,0:T(8,128)(2,1)}) custom-call(bf16[1024,4096]{1,0:T(8,128)(2,1)} %shard_map.174.adj_ref, bf16[4,1024,512]{2,1,0:T(8,128)(2,1)} %bitcast.3.table_hbm, bf16[1024,512]{1,0:T(8,128)(2,1)S(1)} %convert_element_type.31.embed_ref, bf16[512,512]{1,0:T(8,128)(2,1)S(1)} %copy-done.1, ...), custom_call_target="tpu_custom_call" | custom-call | tf_op jit(solution)/shard_map/pallas_call | solution.py:109
  88.7 0.0 copy-start.9
  88.7 0.0 copy-start.10
  88.7 0.0 copy-start.11
  88.7 0.0 copy-start.8
  88.7 0.0 copy-start.5
  88.7 15.1 %all-to-all-start.1 = ((bf16[128,8,512]{2,1,0:T(8,128)(2,1)}), bf16[128,8,512]{2,1,0:T(8,128)(2,1)}, u32[]{:S(2)}, u32[]{:S(2)}) async-start(bf16[128,8,512]{2,1,0:T(8,128)(2,1)} %bitcast.7), calls=%async_computation.1 | async-start | bytes 2097152 | tf_op jit(solution)/shard_map/all_to_all | solution.py:196
  103.9 0.1 eq.63
  104.0 0.0 copy-done.9
  104.1 0.1 iota_compare_fusion.3
  104.2 1.0 fusion.20
  105.1 17.0 %all-to-all-done.1 = bf16[128,8,512]{2,1,0:T(8,128)(2,1)} async-done(((bf16[128,8,512]{2,1,0:T(8,128)(2,1)}), bf16[128,8,512]{2,1,0:T(8,128)(2,1)}, u32[]{:S(2)}, u32[]{:S(2)}) %all-to-all-start.1) | async-done | bytes 1048608 | tf_op jit(solution)/shard_map/all_to_all | solution.py:196
  122.2 2.5 %fusion.1 = f32[4,256,512]{2,1,0:T(8,128)S(1)} fusion(s32[4,256]{1,0:T(4,128)S(1)} %copy-done.8, bf16[128,8,512]{2,1,0:T(8,128)(2,1)} %all-to-all-done.1), kind=kOutput, calls=%fused_computation.7 | convolution fusion | flops 1074790400 | bytes 3149824 | tf_op jit(solution)/shard_map/dot_general | solution.py:202
  124.7 0.0 copy-start.12
  124.7 0.0 copy-start.13
  124.7 0.4 select_reduce_fusion.2
  125.1 0.2 fusion.14
  125.3 0.4 copy-done.12
  125.7 0.9 fusion.4
  126.6 0.1 fusion.25
  126.7 0.6 select_reduce_fusion.1
  127.3 0.7 all_to_all.14
  128.0 4.9 %all-to-all-start.2 = ((f32[128,1,8]{2,1,0:T(1,128)}), f32[128,1,8]{2,1,0:T(1,128)S(1)}, u32[]{:S(2)}, u32[]{:S(2)}) async-start(f32[128,1,8]{2,1,0:T(1,128)} %bitcast.12), calls=%async_computation.2 | async-start | bytes 131072 | tf_op jit(solution)/shard_map/all_to_all | solution.py:216
  132.9 0.7 divide_select_fusion
  133.6 9.0 %all-to-all-done.2 = f32[128,1,8]{2,1,0:T(1,128)S(1)} async-done(((f32[128,1,8]{2,1,0:T(1,128)}), f32[128,1,8]{2,1,0:T(1,128)S(1)}, u32[]{:S(2)}, u32[]{:S(2)}) %all-to-all-start.2) | async-done | bytes 4128 | tf_op jit(solution)/shard_map/all_to_all | solution.py:216
  142.6 0.5 broadcast.64
  143.1 0.8 reduce.3
  143.9 0.1 broadcast_in_dim.55
  144.0 1.1 select_reduce_fusion
  (24 shorter events, 0.1 us)
Async XLA Ops:
  0.6 124.5 %copy-start = (bf16[512,512]{1,0:T(8,128)(2,1)S(1)}, bf16[512,512]{1,0:T(8,128)(2,1)}, u32[]{:S(2)}) copy-start(bf16[512,512]{1,0:T(8,128)(2,1)} %param.27) | copy-start | bytes 1572868
  6.1 70.0 %all-to-all-start = ((bf16[16,256,512]{2,1,0:T(8,128)(2,1)}), bf16[16,256,512]{2,1,0:T(8,128)(2,1)}, u32[]{:S(2)}, u32[]{:S(2)}) async-start(bf16[16,256,512]{2,1,0:T(8,128)(2,1)} %bitcast.45), calls=%async_computation | async-start | bytes 8388608 | tf_op jit(solution)/shard_map/all_to_all | solution.py:186
  14.5 1.8 %copy-start.7 = (s32[1,128,8]{1,2,0:T(8,128)S(1)}, s32[1,128,8]{1,2,0:T(8,128)}, u32[]{:S(2)}) copy-start(s32[1,128,8]{1,2,0:T(8,128)} %param.19) | copy-start | bytes 12292
  14.6 1.9 %copy-start.4 = (f32[1024,80]{0,1:T(8,128)S(1)}, f32[1024,80]{0,1:T(8,128)}, u32[]{:S(2)}) copy-start(f32[1024,80]{0,1:T(8,128)} %param.17) | copy-start | bytes 983044
  16.4 1.5 %copy-start.6 = (s32[1024,80]{0,1:T(8,128)S(1)}, s32[1024,80]{0,1:T(8,128)}, u32[]{:S(2)}) copy-start(s32[1024,80]{0,1:T(8,128)} %param.16) | copy-start | bytes 983044
  19.0 57.0 %copy-start.1 = (bf16[512,512]{1,0:T(8,128)(2,1)S(1)}, bf16[512,512]{1,0:T(8,128)(2,1)}, u32[]{:S(2)}) copy-start(bf16[512,512]{1,0:T(8,128)(2,1)} %w_self_ref.1) | copy-start | bytes 1572868
  19.0 57.0 %copy-start.2 = (bf16[512,512]{1,0:T(8,128)(2,1)S(1)}, bf16[512,512]{1,0:T(8,128)(2,1)}, u32[]{:S(2)}) copy-start(bf16[512,512]{1,0:T(8,128)(2,1)} %w_nbr_ref.1) | copy-start | bytes 1572868
  19.0 57.0 %copy-start.3 = (f32[512]{0:T(512)S(1)}, f32[512]{0:T(512)}, u32[]{:S(2)}) copy-start(f32[512]{0:T(512)} %param.24) | copy-start | bytes 6148
  88.7 15.3 %copy-start.9 = (s32[4]{0:T(128)S(1)}, s32[4]{0:T(128)}, u32[]{:S(2)}) copy-start(s32[4]{0:T(128)} %param.21) | copy-start | bytes 52
  88.7 15.3 %copy-start.10 = (bf16[512]{0:T(512)(128)(2,1)S(1)}, bf16[512]{0:T(512)(128)(2,1)}, u32[]{:S(2)}) copy-start(bf16[512]{0:T(512)(128)(2,1)} %param.25) | copy-start | bytes 3076
  88.7 15.3 %copy-start.11 = (bf16[512]{0:T(512)(128)(2,1)S(1)}, bf16[512]{0:T(512)(128)(2,1)}, u32[]{:S(2)}) copy-start(bf16[512]{0:T(512)(128)(2,1)} %param.29) | copy-start | bytes 3076
  88.7 15.3 %copy-start.8 = (s32[4,256]{1,0:T(4,128)S(1)}, s32[4,256]{1,0:T(4,128)}, u32[]{:S(2)}) copy-start(s32[4,256]{1,0:T(4,128)} %param.20) | copy-start | bytes 12292
  88.7 15.4 %copy-start.5 = (bf16[1024,512]{1,0:T(8,128)(2,1)S(1)}, bf16[1024,512]{1,0:T(8,128)(2,1)}, u32[]{:S(2)}) copy-start(bf16[1024,512]{1,0:T(8,128)(2,1)} %get-tuple-element.2) | copy-start | bytes 3145732
  88.7 33.4 %all-to-all-start.1 = ((bf16[128,8,512]{2,1,0:T(8,128)(2,1)}), bf16[128,8,512]{2,1,0:T(8,128)(2,1)}, u32[]{:S(2)}, u32[]{:S(2)}) async-start(bf16[128,8,512]{2,1,0:T(8,128)(2,1)} %bitcast.7), calls=%async_computation.1 | async-start | bytes 2097152 | tf_op jit(solution)/shard_map/all_to_all | solution.py:196
  124.7 1.0 copy-start.12
  124.7 1.0 copy-start.13
  128.0 14.6 %all-to-all-start.2 = ((f32[128,1,8]{2,1,0:T(1,128)}), f32[128,1,8]{2,1,0:T(1,128)S(1)}, u32[]{:S(2)}, u32[]{:S(2)}) async-start(f32[128,1,8]{2,1,0:T(1,128)} %bitcast.12), calls=%async_computation.2 | async-start | bytes 131072 | tf_op jit(solution)/shard_map/all_to_all | solution.py:216

commit v20 on v14

--- a/solution.py
+++ b/solution.py
@@ -59,8 +59,15 @@
     )(slot_rows, coef_rows)
 
 
-def node_kernel(adj_ref, table_ref, embed_ref, w_self_ref, w_nbr_ref, bias_ref, send_ref, out_ref, outbound_ref, held_ref):
+def node_kernel(adj_ref, table_ref, embed_ref, w_self_ref, w_nbr_ref, bias_ref, send_ref, out_ref, outbound_ref, held_ref, chooser_ref):
     b = pl.program_id(0)
+
+    @pl.when(b == 0)
+    def _():
+        chooser_ref[...] = jnp.where(
+            send_ref[...] == lax.broadcasted_iota(jnp.int32, chooser_ref.shape, 1), 1.0, 0.0
+        ).astype(jnp.bfloat16)
+
     rows = out_ref.shape[0]
     total = jnp.dot(adj_ref[...], table_ref[...], preferred_element_type=jnp.float32)
     pre = (
@@ -74,11 +81,7 @@
 
     @pl.when(b == pl.num_programs(0) - 1)
     def _():
-        nodes = held_ref.shape[0]
-        chooser = jnp.where(
-            send_ref[...] == lax.broadcasted_iota(jnp.int32, (send_ref.shape[0], nodes), 1), 1.0, 0.0
-        ).astype(jnp.bfloat16)
-        outbound_ref[...] = jnp.dot(chooser, held_ref[...], preferred_element_type=jnp.float32).astype(
+        outbound_ref[...] = jnp.dot(chooser_ref[...], held_ref[...], preferred_element_type=jnp.float32).astype(
             outbound_ref.dtype
         )
 
@@ -109,7 +112,7 @@
             jax.ShapeDtypeStruct((nodes, hidden), jnp.bfloat16),
             jax.ShapeDtypeStruct((slots, hidden), jnp.bfloat16),
         ],
-        scratch_shapes=[pltpu.VMEM((nodes, hidden), jnp.bfloat16)],
+        scratch_shapes=[pltpu.VMEM((nodes, hidden), jnp.bfloat16), pltpu.VMEM((slots, nodes), jnp.bfloat16)],
         compiler_params=pltpu.CompilerParams(vmem_limit_bytes=48 * 1024 * 1024),
     )(adjacency, table, embed_bf, w_self, w_nbr, bias.reshape(1, hidden), send_flat.reshape(slots, 1))
 

time: 145 us -> 145 us (level)
  no operation moved by 1% of the time
where the time goes in v20:
time: 145 us; the launch traced here: 144 us
  Pallas kernels  49.4 us (34%)
  waiting for transfers between devices  45.6 us (31%)
  starting transfers between devices  28.5 us (20%)
  local copies, waits for them, and re-layouts  9.83 us (7%)
  other arithmetic  5.56 us (4%)
  matrix products  4.61 us (3%)
    pallas_call x1, Pallas kernels, build_adjacency(): pl.pallas_call(adjacency_kernel, grid=(nodes // rows,), in_specs=[pl.Bloc...  37.5 us
    all_to_all x1, waiting for transfers between devices, body(): lax.all_to_all(outgoing, 'shard', split_axis=0, concat_axis=0, tiled=True)  19.5 us
    all_to_all x1, waiting for transfers between devices, body(): lax.all_to_all(outbound, ('grp', 'shard'), split_axis=0, concat_axis=0, t...  17 us
    all_to_all x1, starting transfers between devices, body(): lax.all_to_all(outbound, ('grp', 'shard'), split_axis=0, concat_axis=0, t...  15.1 us
    pallas_call x1, Pallas kernels, node_layer(): pl.pallas_call(node_kernel, grid=(nodes // rows,), in_specs=[pl.BlockSpec...  11.9 us
    all_to_all x1, waiting for transfers between devices, body(): lax.all_to_all(slot_scores, ('grp', 'shard'), split_axis=0, concat_axis=0...  9 us
    all_to_all x1, starting transfers between devices, body(): lax.all_to_all(outgoing, 'shard', split_axis=0, concat_axis=0, tiled=True)  8.48 us
    all_to_all x1, starting transfers between devices, body(): lax.all_to_all(slot_scores, ('grp', 'shard'), split_axis=0, concat_axis=0...  4.9 us
  transfers between devices with their start and end apart: 3, of which 3 were waited for; matrix products, arithmetic and copies ran while one was open for 4% of the time, Pallas kernels for 26%

profile of v20, /device:TPU:1, one launch (start us, length us, event | category | flops | bytes accessed | tf_op | source)
XLA Modules:
  0.0 144.5 jit_solution(12499850219169737862)
XLA Ops:
  0.6 0.0 copy-start
  0.6 0.8 copy.38
  1.5 0.1 reshape_squeeze.3
  1.6 4.5 %gather_fusion = bf16[32,128,512]{2,1,0:T(8,128)(2,1)} fusion(f32[8,128,512]{2,1,0:T(8,128)} %bitcast.44, s32[1024]{0:T(1024)S(1)} %pad_clamp_fusion), kind=kCustom, calls=%fused_computation | custom fusion | bytes 8388736 | tf_op jit(solution)/shard_map/gather | solution.py:165
  6.1 8.5 %all-to-all-start = ((bf16[16,256,512]{2,1,0:T(8,128)(2,1)}), bf16[16,256,512]{2,1,0:T(8,128)(2,1)}, u32[]{:S(2)}, u32[]{:S(2)}) async-start(bf16[16,256,512]{2,1,0:T(8,128)(2,1)} %bitcast.45), calls=%async_computation | async-start | bytes 8388608 | tf_op jit(solution)/shard_map/all_to_all | solution.py:168
  14.5 0.0 copy-start.7
  14.6 0.0 copy-start.4
  14.6 1.8 %convert_element_type.31.embed_ref = bf16[1024,512]{1,0:T(8,128)(2,1)S(1)} convert(f32[1024,512]{1,0:T(8,128)} %param.15) | non-fusion elementwise | flops 524288 | bytes 3145728 | tf_op jit(solution)/shard_map/convert_element_type | solution.py:153
  16.3 0.0 copy-done.7
  16.4 0.0 copy-start.6
  16.4 0.1 copy.39
  16.5 0.0 copy-done.4
  16.6 0.2 copy.37
  16.8 0.9 reshape.127.coef_ref
  17.7 0.2 reshape_reshape_squeeze.4.send_ref
  17.9 0.0 copy-done.6
  17.9 0.2 copy.36
  18.1 0.9 reshape.118.slot_ref
  19.0 37.5 %shard_map.174.adj_ref = bf16[1024,4096]{1,0:T(8,128)(2,1)} custom-call(s32[128,640]{1,0:T(8,128)} %reshape.118.slot_ref, f32[128,640]{1,0:T(8,128)} %reshape.127.coef_ref), custom_call_target="tpu_custom_call" | custom-call | tf_op jit(solution)/shard_map/pallas_call | solution.py:49
  56.5 19.5 %all-to-all-done = bf16[16,256,512]{2,1,0:T(8,128)(2,1)} async-done(((bf16[16,256,512]{2,1,0:T(8,128)(2,1)}), bf16[16,256,512]{2,1,0:T(8,128)(2,1)}, u32[]{:S(2)}, u32[]{:S(2)}) %all-to-all-start) | async-done | bytes 4194336 | tf_op jit(solution)/shard_map/all_to_all | solution.py:168
  76.0 11.9 %shard_map.175 = (bf16[1024,512]{1,0:T(8,128)(2,1)}, bf16[1024,512]{1,0:T(8,128)(2,1)}) custom-call(bf16[1024,4096]{1,0:T(8,128)(2,1)} %shard_map.174.adj_ref, bf16[4096,512]{1,0:T(8,128)(2,1)} %bitcast.3.table_ref, bf16[1024,512]{1,0:T(8,128)(2,1)S(1)} %convert_element_type.31.embed_ref, bf16[512,512]{1,0:T(8,128)(2,1)S(1)} %copy-done.1, ...), custom_call_target="tpu_custom_call" | custom-call | tf_op jit(solution)/shard_map/pallas_call | solution.py:95
  88.0 0.0 copy-start.11
  88.0 0.0 copy-start.8
  88.0 0.0 copy-start.5
  88.0 15.1 %all-to-all-start.1 = ((bf16[128,8,512]{2,1,0:T(8,128)(2,1)}), bf16[128,8,512]{2,1,0:T(8,128)(2,1)}, u32[]{:S(2)}, u32[]{:S(2)}) async-start(bf16[128,8,512]{2,1,0:T(8,128)(2,1)} %bitcast.7), calls=%async_computation.1 | async-start | bytes 2097152 | tf_op jit(solution)/shard_map/all_to_all | solution.py:178
  103.2 0.1 eq.63
  103.4 0.1 iota_compare_fusion.3
  103.4 0.0 copy-done.5
  103.4 1.0 fusion.20
  104.4 17.0 %all-to-all-done.1 = bf16[128,8,512]{2,1,0:T(8,128)(2,1)} async-done(((bf16[128,8,512]{2,1,0:T(8,128)(2,1)}), bf16[128,8,512]{2,1,0:T(8,128)(2,1)}, u32[]{:S(2)}, u32[]{:S(2)}) %all-to-all-start.1) | async-done | bytes 1048608 | tf_op jit(solution)/shard_map/all_to_all | solution.py:178
  121.5 2.5 %fusion.1 = f32[4,256,512]{2,1,0:T(8,128)S(1)} fusion(s32[4,256]{1,0:T(4,128)S(1)} %copy-done.8, bf16[128,8,512]{2,1,0:T(8,128)(2,1)} %all-to-all-done.1), kind=kOutput, calls=%fused_computation.7 | convolution fusion | flops 1074790400 | bytes 3149824 | tf_op jit(solution)/shard_map/dot_general | solution.py:184
  124.0 0.0 copy-start.12
  124.0 0.0 copy-start.13
  124.0 0.4 select_reduce_fusion.2
  124.4 0.0 copy-done
  124.4 0.2 fusion.14
  124.6 0.4 copy-done.12
  125.0 0.9 fusion.4
  125.9 0.1 fusion.25
  126.0 0.6 select_reduce_fusion.1
  126.6 0.7 all_to_all.14
  127.3 4.9 %all-to-all-start.2 = ((f32[128,1,8]{2,1,0:T(1,128)}), f32[128,1,8]{2,1,0:T(1,128)S(1)}, u32[]{:S(2)}, u32[]{:S(2)}) async-start(f32[128,1,8]{2,1,0:T(1,128)} %bitcast.12), calls=%async_computation.2 | async-start | bytes 131072 | tf_op jit(solution)/shard_map/all_to_all | solution.py:198
  132.2 0.7 divide_select_fusion
  132.9 9.0 %all-to-all-done.2 = f32[128,1,8]{2,1,0:T(1,128)S(1)} async-done(((f32[128,1,8]{2,1,0:T(1,128)}), f32[128,1,8]{2,1,0:T(1,128)S(1)}, u32[]{:S(2)}, u32[]{:S(2)}) %all-to-all-start.2) | async-done | bytes 4128 | tf_op jit(solution)/shard_map/all_to_all | solution.py:198
  141.9 0.5 broadcast.64
  142.4 0.8 reduce.3
  143.2 0.1 broadcast_in_dim.55
  143.3 1.1 select_reduce_fusion
  (24 shorter events, 0.1 us)
Async XLA Ops:
  0.6 123.8 %copy-start = (bf16[512,512]{1,0:T(8,128)(2,1)S(1)}, bf16[512,512]{1,0:T(8,128)(2,1)}, u32[]{:S(2)}) copy-start(bf16[512,512]{1,0:T(8,128)(2,1)} %param.27) | copy-start | bytes 1572868
  6.1 70.0 %all-to-all-start = ((bf16[16,256,512]{2,1,0:T(8,128)(2,1)}), bf16[16,256,512]{2,1,0:T(8,128)(2,1)}, u32[]{:S(2)}, u32[]{:S(2)}) async-start(bf16[16,256,512]{2,1,0:T(8,128)(2,1)} %bitcast.45), calls=%async_computation | async-start | bytes 8388608 | tf_op jit(solution)/shard_map/all_to_all | solution.py:168
  14.5 1.8 %copy-start.7 = (s32[1,128,8]{1,2,0:T(8,128)S(1)}, s32[1,128,8]{1,2,0:T(8,128)}, u32[]{:S(2)}) copy-start(s32[1,128,8]{1,2,0:T(8,128)} %param.19) | copy-start | bytes 12292
  14.6 1.9 %copy-start.4 = (f32[1024,80]{0,1:T(8,128)S(1)}, f32[1024,80]{0,1:T(8,128)}, u32[]{:S(2)}) copy-start(f32[1024,80]{0,1:T(8,128)} %param.17) | copy-start | bytes 983044
  16.4 1.5 %copy-start.6 = (s32[1024,80]{0,1:T(8,128)S(1)}, s32[1024,80]{0,1:T(8,128)}, u32[]{:S(2)}) copy-start(s32[1024,80]{0,1:T(8,128)} %param.16) | copy-start | bytes 983044
  19.0 57.0 %copy-start.1 = (bf16[512,512]{1,0:T(8,128)(2,1)S(1)}, bf16[512,512]{1,0:T(8,128)(2,1)}, u32[]{:S(2)}) copy-start(bf16[512,512]{1,0:T(8,128)(2,1)} %w_self_ref.1) | copy-start | bytes 1572868
  19.0 57.0 %copy-start.2 = (bf16[512,512]{1,0:T(8,128)(2,1)S(1)}, bf16[512,512]{1,0:T(8,128)(2,1)}, u32[]{:S(2)}) copy-start(bf16[512,512]{1,0:T(8,128)(2,1)} %w_nbr_ref.1) | copy-start | bytes 1572868
  19.0 57.0 %copy-start.3 = (f32[512]{0:T(512)S(1)}, f32[512]{0:T(512)}, u32[]{:S(2)}) copy-start(f32[512]{0:T(512)} %param.24) | copy-start | bytes 6148
  88.0 15.3 %copy-start.9 = (s32[4]{0:T(128)S(1)}, s32[4]{0:T(128)}, u32[]{:S(2)}) copy-start(s32[4]{0:T(128)} %param.21) | copy-start | bytes 52
  88.0 15.3 %copy-start.10 = (bf16[512]{0:T(512)(128)(2,1)S(1)}, bf16[512]{0:T(512)(128)(2,1)}, u32[]{:S(2)}) copy-start(bf16[512]{0:T(512)(128)(2,1)} %param.25) | copy-start | bytes 3076
  88.0 15.3 %copy-start.11 = (bf16[512]{0:T(512)(128)(2,1)S(1)}, bf16[512]{0:T(512)(128)(2,1)}, u32[]{:S(2)}) copy-start(bf16[512]{0:T(512)(128)(2,1)} %param.29) | copy-start | bytes 3076
  88.0 15.3 %copy-start.8 = (s32[4,256]{1,0:T(4,128)S(1)}, s32[4,256]{1,0:T(4,128)}, u32[]{:S(2)}) copy-start(s32[4,256]{1,0:T(4,128)} %param.20) | copy-start | bytes 12292
  88.0 15.4 %copy-start.5 = (bf16[1024,512]{1,0:T(8,128)(2,1)S(1)}, bf16[1024,512]{1,0:T(8,128)(2,1)}, u32[]{:S(2)}) copy-start(bf16[1024,512]{1,0:T(8,128)(2,1)} %get-tuple-element.2) | copy-start | bytes 3145732
  88.0 33.4 %all-to-all-start.1 = ((bf16[128,8,512]{2,1,0:T(8,128)(2,1)}), bf16[128,8,512]{2,1,0:T(8,128)(2,1)}, u32[]{:S(2)}, u32[]{:S(2)}) async-start(bf16[128,8,512]{2,1,0:T(8,128)(2,1)} %bitcast.7), calls=%async_computation.1 | async-start | bytes 2097152 | tf_op jit(solution)/shard_map/all_to_all | solution.py:178
  124.0 1.0 copy-start.12
  124.0 1.0 copy-start.13
  127.3 14.6 %all-to-all-start.2 = ((f32[128,1,8]{2,1,0:T(1,128)}), f32[128,1,8]{2,1,0:T(1,128)S(1)}, u32[]{:S(2)}, u32[]{:S(2)}) async-start(f32[128,1,8]{2,1,0:T(1,128)} %bitcast.12), calls=%async_computation.2 | async-start | bytes 131072 | tf_op jit(solution)/shard_map/all_to_all | solution.py:198

commit v21 on v14

--- a/solution.py
+++ b/solution.py
@@ -178,7 +178,8 @@
     member_width = members.shape[1]
     member_flat = members.reshape(sub_count * member_width)
     member_chooser = select_matrix(member_flat, slot_total, jnp.bfloat16)
-    member_rows = jnp.dot(member_chooser, received_rows, preferred_element_type=jnp.float32)
+    member_rows = jnp.dot(member_chooser, received_rows, preferred_element_type=jnp.float32).astype(jnp.bfloat16)
+    member_rows = lax.reduce_precision(member_rows, exponent_bits=8, mantissa_bits=7).astype(jnp.float32)
     member_rows = member_rows.reshape(sub_count, member_width, hidden_width)
     relative = member_rows - member_rows[:, :1, :]
     alive = jnp.arange(member_width, dtype=jnp.int32)[None, :] < sub_len[:, None]

time: 145 us -> 143 us (0.986)
  transfers between devices with their start and end apart: 3 -> 3, of which waited for: 3 -> 3; matrix products, arithmetic and copies ran while one was open for 4% -> 5% of each run, Pallas kernels for 26% -> 26%
where the time goes in v21:
time: 143 us; the launch traced here: 142 us
  Pallas kernels  49.1 us (34%)
  waiting for transfers between devices  44.7 us (31%)
  starting transfers between devices  28.1 us (20%)
  local copies, waits for them, and re-layouts  9.39 us (7%)
  other arithmetic  5.53 us (4%)
  matrix products  4.62 us (3%)
    pallas_call x1, Pallas kernels, build_adjacency(): pl.pallas_call(adjacency_kernel, grid=(nodes // rows,), in_specs=[pl.Bloc...  37.5 us
    all_to_all x1, waiting for transfers between devices, body(): lax.all_to_all(outgoing, 'shard', split_axis=0, concat_axis=0, tiled=True)  19.6 us
    all_to_all x1, waiting for transfers between devices, body(): lax.all_to_all(outbound, ('grp', 'shard'), split_axis=0, concat_axis=0, t...  16.2 us
    all_to_all x1, starting transfers between devices, body(): lax.all_to_all(outbound, ('grp', 'shard'), split_axis=0, concat_axis=0, t...  14.7 us
    pallas_call x1, Pallas kernels, node_layer(): pl.pallas_call(node_kernel, grid=(nodes // rows,), in_specs=[pl.BlockSpec...  11.6 us
    all_to_all x1, waiting for transfers between devices, body(): lax.all_to_all(slot_scores, ('grp', 'shard'), split_axis=0, concat_axis=0...  8.99 us
    all_to_all x1, starting transfers between devices, body(): lax.all_to_all(outgoing, 'shard', split_axis=0, concat_axis=0, tiled=True)  8.61 us
    all_to_all x1, starting transfers between devices, body(): lax.all_to_all(slot_scores, ('grp', 'shard'), split_axis=0, concat_axis=0...  4.81 us
  transfers between devices with their start and end apart: 3, of which 3 were waited for; matrix products, arithmetic and copies ran while one was open for 5% of the time, Pallas kernels for 26%

profile of v21, /device:TPU:1, one launch (start us, length us, event | category | flops | bytes accessed | tf_op | source)
XLA Modules:
  0.0 142.3 jit_solution(16951682594790901885)
XLA Ops:
  0.6 0.0 copy-start
  0.6 0.8 copy.38
  1.5 0.1 reshape_squeeze.3
  1.6 4.5 %gather_fusion = bf16[32,128,512]{2,1,0:T(8,128)(2,1)} fusion(f32[8,128,512]{2,1,0:T(8,128)} %bitcast.42, s32[1024]{0:T(1024)S(1)} %pad_clamp_fusion), kind=kCustom, calls=%fused_computation | custom fusion | bytes 8388736 | tf_op jit(solution)/shard_map/gather | solution.py:162
  6.1 8.6 %all-to-all-start = ((bf16[16,256,512]{2,1,0:T(8,128)(2,1)}), bf16[16,256,512]{2,1,0:T(8,128)(2,1)}, u32[]{:S(2)}, u32[]{:S(2)}) async-start(bf16[16,256,512]{2,1,0:T(8,128)(2,1)} %bitcast.43), calls=%async_computation | async-start | bytes 8388608 | tf_op jit(solution)/shard_map/all_to_all | solution.py:165
  14.7 0.0 copy-start.5
  14.7 1.8 %convert_element_type.35.embed_ref = bf16[1024,512]{1,0:T(8,128)(2,1)S(1)} convert(f32[1024,512]{1,0:T(8,128)} %param.15) | non-fusion elementwise | flops 524288 | bytes 3145728 | tf_op jit(solution)/shard_map/convert_element_type | solution.py:150
  16.5 0.0 copy-done.6
  16.5 0.1 copy.39
  16.6 0.0 copy-done.4
  16.7 0.2 copy.37
  16.9 0.9 reshape.113.coef_ref
  17.8 0.2 reshape_reshape_squeeze.4.send_ref
  18.0 0.0 copy-done.5
  18.0 0.2 copy.36
  18.2 0.9 reshape.102.slot_ref
  19.1 37.5 %shard_map.174.adj_ref = bf16[1024,4096]{1,0:T(8,128)(2,1)} custom-call(s32[128,640]{1,0:T(8,128)} %reshape.102.slot_ref, f32[128,640]{1,0:T(8,128)} %reshape.113.coef_ref), custom_call_target="tpu_custom_call" | custom-call | tf_op jit(solution)/shard_map/pallas_call | solution.py:49
  56.6 19.6 %all-to-all-done = bf16[16,256,512]{2,1,0:T(8,128)(2,1)} async-done(((bf16[16,256,512]{2,1,0:T(8,128)(2,1)}), bf16[16,256,512]{2,1,0:T(8,128)(2,1)}, u32[]{:S(2)}, u32[]{:S(2)}) %all-to-all-start) | async-done | bytes 4194336 | tf_op jit(solution)/shard_map/all_to_all | solution.py:165
  76.2 0.0 copy-done.1
  76.2 0.0 copy-done.2
  76.2 0.0 copy-done.3
  76.2 0.0 copy-start.9
  76.2 0.0 copy-start.10
  76.2 0.0 copy-start.7
  76.2 11.6 %shard_map.175 = (bf16[1024,512]{1,0:T(8,128)(2,1)}, bf16[1024,512]{1,0:T(8,128)(2,1)}) custom-call(bf16[1024,4096]{1,0:T(8,128)(2,1)} %shard_map.174.adj_ref, bf16[4096,512]{1,0:T(8,128)(2,1)} %bitcast.3.table_ref, bf16[1024,512]{1,0:T(8,128)(2,1)S(1)} %convert_element_type.35.embed_ref, bf16[512,512]{1,0:T(8,128)(2,1)S(1)} %copy-done.1, ...), custom_call_target="tpu_custom_call" | custom-call | tf_op jit(solution)/shard_map/pallas_call | solution.py:92
  87.8 14.7 %all-to-all-start.1 = ((bf16[128,8,512]{2,1,0:T(8,128)(2,1)}), bf16[128,8,512]{2,1,0:T(8,128)(2,1)S(1)}, u32[]{:S(2)}, u32[]{:S(2)}) async-start(bf16[128,8,512]{2,1,0:T(8,128)(2,1)} %bitcast.6), calls=%async_computation.1 | async-start | bytes 2097152 | tf_op jit(solution)/shard_map/all_to_all | solution.py:175
  102.5 0.1 eq.20
  102.6 0.0 copy-done.8
  102.6 0.0 copy-done.9
  102.6 0.0 copy-done.10
  102.7 0.1 iota_compare_fusion.7
  102.7 2.2 %fusion.22 = f32[1,1024]{1,0:T(1,128)} fusion(bf16[1024,512]{1,0:T(8,128)(2,1)} %get-tuple-element.2, bf16[512,1]{0,1:T(2,128)(2,1)S(1)} %reshape.124), kind=kOutput, calls=%fused_computation.35 | convolution fusion | flops 1048576 | bytes 1053696 | tf_op jit(solution)/shard_map/dot_general | solution.py:169
  104.9 16.2 %all-to-all-done.1 = bf16[128,8,512]{2,1,0:T(8,128)(2,1)S(1)} async-done(((bf16[128,8,512]{2,1,0:T(8,128)(2,1)}), bf16[128,8,512]{2,1,0:T(8,128)(2,1)S(1)}, u32[]{:S(2)}, u32[]{:S(2)}) %all-to-all-start.1) | async-done | bytes 1048608 | tf_op jit(solution)/shard_map/all_to_all | solution.py:175
  121.1 1.3 fusion.3
  122.4 0.4 select_reduce_fusion.2
  122.8 0.2 fusion.16
  123.0 0.0 copy-done.11
  123.0 0.9 fusion.4
  123.9 0.1 fusion.27
  124.0 0.6 select_reduce_fusion.1
  124.6 0.7 all_to_all.14
  125.3 4.8 %all-to-all-start.2 = ((f32[128,1,8]{2,1,0:T(1,128)}), f32[128,1,8]{2,1,0:T(1,128)S(1)}, u32[]{:S(2)}, u32[]{:S(2)}) async-start(f32[128,1,8]{2,1,0:T(1,128)} %bitcast.12), calls=%async_computation.2 | async-start | bytes 131072 | tf_op jit(solution)/shard_map/all_to_all | solution.py:196
  130.1 0.7 divide_select_fusion
  130.8 9.0 %all-to-all-done.2 = f32[128,1,8]{2,1,0:T(1,128)S(1)} async-done(((f32[128,1,8]{2,1,0:T(1,128)}), f32[128,1,8]{2,1,0:T(1,128)S(1)}, u32[]{:S(2)}, u32[]{:S(2)}) %all-to-all-start.2) | async-done | bytes 4128 | tf_op jit(solution)/shard_map/all_to_all | solution.py:196
  139.8 0.5 broadcast.45
  140.3 0.8 reduce.3
  141.1 0.1 broadcast_in_dim.55
  141.2 1.1 select_reduce_fusion
  (22 shorter events, 0.1 us)
Async XLA Ops:
  0.6 122.2 %copy-start = (bf16[512,512]{1,0:T(8,128)(2,1)S(1)}, bf16[512,512]{1,0:T(8,128)(2,1)}, u32[]{:S(2)}) copy-start(bf16[512,512]{1,0:T(8,128)(2,1)} %param.27) | copy-start | bytes 1572868
  6.1 10.4 %copy-start.6 = (s32[1,128,8]{1,2,0:T(8,128)S(1)}, s32[1,128,8]{1,2,0:T(8,128)}, u32[]{:S(2)}) copy-start(s32[1,128,8]{1,2,0:T(8,128)} %param.19) | copy-start | bytes 12292
  6.1 10.5 %copy-start.4 = (f32[1024,80]{0,1:T(8,128)S(1)}, f32[1024,80]{0,1:T(8,128)}, u32[]{:S(2)}) copy-start(f32[1024,80]{0,1:T(8,128)} %param.17) | copy-start | bytes 983044
  6.1 70.1 %all-to-all-start = ((bf16[16,256,512]{2,1,0:T(8,128)(2,1)}), bf16[16,256,512]{2,1,0:T(8,128)(2,1)}, u32[]{:S(2)}, u32[]{:S(2)}) async-start(bf16[16,256,512]{2,1,0:T(8,128)(2,1)} %bitcast.43), calls=%async_computation | async-start | bytes 8388608 | tf_op jit(solution)/shard_map/all_to_all | solution.py:165
  14.7 3.3 %copy-start.5 = (s32[1024,80]{0,1:T(8,128)S(1)}, s32[1024,80]{0,1:T(8,128)}, u32[]{:S(2)}) copy-start(s32[1024,80]{0,1:T(8,128)} %param.16) | copy-start | bytes 983044
  19.1 57.1 %copy-start.1 = (bf16[512,512]{1,0:T(8,128)(2,1)S(1)}, bf16[512,512]{1,0:T(8,128)(2,1)}, u32[]{:S(2)}) copy-start(bf16[512,512]{1,0:T(8,128)(2,1)} %w_self_ref.1) | copy-start | bytes 1572868
  19.1 57.1 %copy-start.2 = (bf16[512,512]{1,0:T(8,128)(2,1)S(1)}, bf16[512,512]{1,0:T(8,128)(2,1)}, u32[]{:S(2)}) copy-start(bf16[512,512]{1,0:T(8,128)(2,1)} %w_nbr_ref.1) | copy-start | bytes 1572868
  19.1 57.1 %copy-start.3 = (f32[512]{0:T(512)S(1)}, f32[512]{0:T(512)}, u32[]{:S(2)}) copy-start(f32[512]{0:T(512)} %param.24) | copy-start | bytes 6148
  76.2 26.4 %copy-start.8 = (s32[4]{0:T(128)S(1)}, s32[4]{0:T(128)}, u32[]{:S(2)}) copy-start(s32[4]{0:T(128)} %param.21) | copy-start | bytes 52
  76.2 26.4 %copy-start.9 = (bf16[512]{0:T(512)(128)(2,1)S(1)}, bf16[512]{0:T(512)(128)(2,1)}, u32[]{:S(2)}) copy-start(bf16[512]{0:T(512)(128)(2,1)} %param.25) | copy-start | bytes 3076
  76.2 26.4 %copy-start.10 = (bf16[512]{0:T(512)(128)(2,1)S(1)}, bf16[512]{0:T(512)(128)(2,1)}, u32[]{:S(2)}) copy-start(bf16[512]{0:T(512)(128)(2,1)} %param.29) | copy-start | bytes 3076
  76.2 26.4 %copy-start.7 = (s32[4,256]{1,0:T(4,128)S(1)}, s32[4,256]{1,0:T(4,128)}, u32[]{:S(2)}) copy-start(s32[4,256]{1,0:T(4,128)} %param.20) | copy-start | bytes 12292
  87.8 33.3 %all-to-all-start.1 = ((bf16[128,8,512]{2,1,0:T(8,128)(2,1)}), bf16[128,8,512]{2,1,0:T(8,128)(2,1)S(1)}, u32[]{:S(2)}, u32[]{:S(2)}) async-start(bf16[128,8,512]{2,1,0:T(8,128)(2,1)} %bitcast.6), calls=%async_computation.1 | async-start | bytes 2097152 | tf_op jit(solution)/shard_map/all_to_all | solution.py:175
  121.1 1.9 %copy-start.11 = (bf16[512,512]{1,0:T(8,128)(2,1)S(1)}, bf16[512,512]{1,0:T(8,128)(2,1)}, u32[]{:S(2)}) copy-start(bf16[512,512]{1,0:T(8,128)(2,1)} %param.26) | copy-start | bytes 1572868
  121.1 1.9 %copy-start.12 = (f32[512]{0:T(512)S(1)}, f32[512]{0:T(512)}, u32[]{:S(2)}) copy-start(f32[512]{0:T(512)} %param.28) | copy-start | bytes 6148
  125.3 14.5 %all-to-all-start.2 = ((f32[128,1,8]{2,1,0:T(1,128)}), f32[128,1,8]{2,1,0:T(1,128)S(1)}, u32[]{:S(2)}, u32[]{:S(2)}) async-start(f32[128,1,8]{2,1,0:T(1,128)} %bitcast.12), calls=%async_computation.2 | async-start | bytes 131072 | tf_op jit(solution)/shard_map/all_to_all | solution.py:196
